TPU v7x, 32 devices: a whole 2x2x4 slice. The times are simulated.
32 devices in a mesh: expert: 8 (over y, x, core), dp: 4 (over z).
Axes of the slice: x: 2, y: 2, z: 4, core: 2. Of those that a mesh axis runs over, the one named last changes fastest.
Arguments:
- tokens: bfloat16 [6144, 1024], P(('expert', 'dp')), may hold values from -6 to 6
- grad_out: bfloat16 [6144, 1024], P(('expert', 'dp')), may hold values from -6 to 6
- routes: int32 [6144, 2], P(('expert', 'dp')), may hold values from 0 to 7, all different within a row
- keep_second: int32 [6144], P(('expert', 'dp')), may hold values 0 or 1
- combine: bfloat16 [6144, 2], P(('expert', 'dp')), may hold values from 0.099609375 to 0.8984375
- w_in: bfloat16 [8, 2048, 1024], P('expert'), may hold values from -0.1875 to 0.1875
- w_out: bfloat16 [8, 2048, 1024], P('expert'), may hold values from -0.125 to 0.125
Outputs:
- grad_tokens: bfloat16 [6144, 1024], P(('expert', 'dp'))
- grad_combine: bfloat16 [6144, 2], P(('expert', 'dp'))
- grad_w_in: float32 [8, 2048, 1024], P('expert', 'dp')
- grad_w_out: float32 [8, 2048, 1024], P('expert', 'dp')
Inputs may be any that keep to these rules, and one draw needn't show every extreme that they name: `routes`: each token names two different experts.
All inputs are finite; a program needn't handle non-finite values. No bound on the sum of `keep_second` on one device may be relied on, other than what follows from the above.
Results may differ from a plain program's by a relative error of at most 0.011.
Values may be sent and summed in bfloat16 or wider, within the bound.
No kernel may reach another device: no remote copies, remote signals or barrier semaphores. Data moves between devices by JAX's collectives and lax.ppermute only.
A program may use at most 128 MiB of HBM per device.

v0:
```python
import jax
import jax.numpy as jnp
from jax import lax
from jax.sharding import PartitionSpec as P

root_coef = 0.7978845608
cube_coef = 0.044715


def gelu_slope(hidden):
    inner_arg = root_coef * (hidden + cube_coef * hidden * hidden * hidden)
    tanh_val = jnp.tanh(inner_arg)
    active = 0.5 * hidden * (1.0 + tanh_val)
    derivative = 0.5 * (1.0 + tanh_val) + 0.5 * hidden * (1.0 - tanh_val * tanh_val) * root_coef * (
        1.0 + 3.0 * cube_coef * hidden * hidden
    )
    return (active, derivative)


def slot_index(routes, keep_second, expert_count, capacity):
    expert_ids = jnp.arange(expert_count, dtype=jnp.int32)
    first_hot = (routes[:, 0:1] == expert_ids[None, :]).astype(jnp.int32)
    second_hot = (routes[:, 1:2] == expert_ids[None, :]).astype(jnp.int32) * keep_second[:, None]
    first_pos = jnp.cumsum(first_hot, axis=0) - first_hot
    second_pos = jnp.cumsum(second_hot, axis=0) - second_hot + jnp.sum(first_hot, axis=0)[None, :]
    first_slot = jnp.sum(first_pos * first_hot, axis=1)
    second_slot = jnp.sum(second_pos * second_hot, axis=1)
    first_flat = jnp.where(first_slot < capacity, routes[:, 0] * capacity + first_slot, -1)
    second_live = (keep_second > 0) & (second_slot < capacity)
    second_flat = jnp.where(second_live, routes[:, 1] * capacity + second_slot, -1)
    slot_ids = jnp.arange(expert_count * capacity, dtype=jnp.int32)
    first_pick = slot_ids[:, None] == first_flat[None, :]
    second_pick = slot_ids[:, None] == second_flat[None, :]
    return (first_pick, second_pick)


def dispatch(tokens, grad_out, combine, first_pick, second_pick):
    chosen = (first_pick | second_pick).astype(jnp.bfloat16)
    sent_x = jnp.dot(chosen, tokens, preferred_element_type=jnp.float32).astype(jnp.bfloat16)
    sent_dy = jnp.dot(chosen, grad_out, preferred_element_type=jnp.float32).astype(jnp.bfloat16)
    weights = combine.astype(jnp.float32)
    sent_c = jnp.sum(
        jnp.where(first_pick, weights[None, :, 0], 0.0)
        + jnp.where(second_pick, weights[None, :, 1], 0.0),
        axis=1,
    ).astype(jnp.bfloat16)
    return (sent_x, sent_dy, sent_c)


def expert_rows(rows_x, rows_dy, rows_c, weight_in, weight_out):
    hidden = lax.dot_general(
        rows_x, weight_in, (((1,), (1,)), ((), ())), preferred_element_type=jnp.float32
    )
    active, derivative = gelu_slope(hidden)
    active_b = active.astype(jnp.bfloat16)
    output = jnp.dot(active_b, weight_out, preferred_element_type=jnp.float32)
    gate_grad = jnp.sum(output * rows_dy.astype(jnp.float32), axis=1).astype(jnp.bfloat16)
    scaled = (rows_c.astype(jnp.float32)[:, None] * rows_dy.astype(jnp.float32)).astype(
        jnp.bfloat16
    )
    active_grad = lax.dot_general(
        scaled, weight_out, (((1,), (1,)), ((), ())), preferred_element_type=jnp.float32
    )
    hidden_grad = (active_grad * derivative).astype(jnp.bfloat16)
    token_grad = jnp.dot(hidden_grad, weight_in, preferred_element_type=jnp.float32).astype(
        jnp.bfloat16
    )
    return (token_grad, gate_grad, hidden_grad, active_b, scaled)


def collect(token_back, gate_back, first_pick, second_pick):
    chosen = (first_pick | second_pick).astype(jnp.bfloat16)
    grad_tokens = lax.dot_general(
        chosen, token_back, (((0,), (0,)), ((), ())), preferred_element_type=jnp.float32
    ).astype(jnp.bfloat16)
    gate_float = gate_back.astype(jnp.float32)[:, None]
    first_grad = jnp.sum(jnp.where(first_pick, gate_float, 0.0), axis=0)
    second_grad = jnp.sum(jnp.where(second_pick, gate_float, 0.0), axis=0)
    grad_combine = jnp.stack([first_grad, second_grad], axis=1).astype(jnp.bfloat16)
    return (grad_tokens, grad_combine)


def per_device(tokens, grad_out, routes, keep_second, combine, w_in, w_out):
    expert_count = lax.axis_size("expert")
    tok_rows = tokens.shape[0]
    model_width = tokens.shape[1]
    capacity = 5 * tok_rows // (2 * expert_count)
    first_pick, second_pick = slot_index(routes, keep_second, expert_count, capacity)
    sent_x, sent_dy, sent_c = dispatch(tokens, grad_out, combine, first_pick, second_pick)
    sent_x = sent_x.reshape(expert_count, capacity, model_width)
    sent_dy = sent_dy.reshape(expert_count, capacity, model_width)
    sent_c = sent_c.reshape(expert_count, capacity)
    weight_in = w_in[0]
    weight_out = w_out[0]
    got_x, got_dy, got_c = (
        lax.all_to_all(sent_x, "expert", split_axis=0, concat_axis=0, tiled=True),
        lax.all_to_all(sent_dy, "expert", split_axis=0, concat_axis=0, tiled=True),
        lax.all_to_all(sent_c, "expert", split_axis=0, concat_axis=0, tiled=True),
    )
    sources = got_c.shape[0]
    rows_x = got_x.reshape(sources * capacity, model_width)
    token_grad, gate_grad, hidden_grad, active_b, scaled = expert_rows(
        rows_x,
        got_dy.reshape(sources * capacity, model_width),
        got_c.reshape(sources * capacity),
        weight_in,
        weight_out,
    )
    token_back, gate_back = (
        lax.all_to_all(
            token_grad.reshape(sources, capacity, model_width),
            "expert",
            split_axis=0,
            concat_axis=0,
            tiled=True,
        ),
        lax.all_to_all(
            gate_grad.reshape(sources, capacity), "expert", split_axis=0, concat_axis=0, tiled=True
        ),
    )
    token_back = token_back.reshape(expert_count * capacity, model_width)
    gate_back = gate_back.reshape(expert_count * capacity)
    all_x, all_scaled = (
        lax.all_gather(rows_x, "dp", axis=0, tiled=True),
        lax.all_gather(scaled, "dp", axis=0, tiled=True),
    )
    part_hidden, part_active = (
        lax.all_to_all(hidden_grad, "dp", split_axis=1, concat_axis=0, tiled=True),
        lax.all_to_all(active_b, "dp", split_axis=1, concat_axis=0, tiled=True),
    )
    grad_in = lax.dot_general(
        part_hidden, all_x, (((0,), (0,)), ((), ())), preferred_element_type=jnp.float32
    )
    grad_outw = lax.dot_general(
        part_active, all_scaled, (((0,), (0,)), ((), ())), preferred_element_type=jnp.float32
    )
    grad_tokens, grad_combine = collect(token_back, gate_back, first_pick, second_pick)
    return (grad_tokens, grad_combine, grad_in[None], grad_outw[None])


def solution(mesh):
    return jax.shard_map(
        per_device,
        mesh=mesh,
        in_specs=(
            P(("expert", "dp"), None),
            P(("expert", "dp"), None),
            P(("expert", "dp"), None),
            P(("expert", "dp")),
            P(("expert", "dp"), None),
            P("expert", None, None),
            P("expert", None, None),
        ),
        out_specs=(
            P(("expert", "dp"), None),
            P(("expert", "dp"), None),
            P("expert", "dp", None),
            P("expert", "dp", None),
        ),
        check_vma=False,
    )
```

profile of v0, /device:TPU:2, one launch (start us, length us, event | category | flops | bytes accessed | tf_op | source)
XLA Modules:
  0.0 280.0 jit_solution(2785787398814354813)
XLA Ops:
  7.2 0.0 copy-start
  7.2 0.0 all-gather.3.cloned.1.call-start
  7.2 0.8 fusion.37
  8.0 0.7 fusion.36
  8.7 0.6 reduce-window.16
  9.3 0.2 slice_reduce_fusion
  9.5 0.1 add_bitcast_fusion
  9.6 0.6 reduce-window.14
  10.2 0.2 slice_reduce_fusion.1
  10.5 0.1 add_bitcast_fusion.1
  10.5 0.1 fusion.33
  10.7 0.8 fusion.35
  11.4 0.7 and_select_fusion
  12.1 0.0 copy-done
  12.1 0.0 copy-start.3
  12.1 0.6 convolution_convert_fusion
  12.7 0.2 reshape.130
  12.9 17.9 %all_to_all.65 = bf16[8,60,1024]{2,1,0:T(8,128)(2,1)S(1)} all-to-all(bf16[8,60,1024]{2,1,0:T(8,128)(2,1)S(1)} %reshape.130), channel_id=1, replica_groups=mesh['expert'=8,'dp'=4] {'expert'}, dimensions={0} | all-to-all | bytes 1966080 | tf_op jit(solution)/shard_map/all_to_all | solution.py:96
  30.8 1.2 reshape.131
  32.0 0.0 all-gather.3.cloned.1.call-update
  32.0 0.0 copy-done.3
  32.0 0.6 convolution_convert_fusion.1
  32.6 0.2 reshape.129
  32.8 17.7 %all_to_all.66 = bf16[8,60,1024]{2,1,0:T(8,128)(2,1)S(1)} all-to-all(bf16[8,60,1024]{2,1,0:T(8,128)(2,1)S(1)} %reshape.129), channel_id=1, replica_groups=mesh['expert'=8,'dp'=4] {'expert'}, dimensions={0} | all-to-all | bytes 1966080 | tf_op jit(solution)/shard_map/all_to_all | solution.py:97
  50.5 0.2 reshape.136
  50.7 0.0 copy-start.5
  50.7 7.5 %multiply_convert_fusion = (bf16[480,2048]{1,0:T(8,128)(2,1)S(1)}, f32[480,2048]{1,0:T(8,128)}) fusion(bf16[480,1024]{1,0:T(8,128)(2,1)} %reshape.131, bf16[1,2048,1024]{2,1,0:T(8,128)(2,1)} %param.12), kind=kOutput, calls=%fused_computation.17 | convolution fusion | flops 2022113280 | bytes 11075584 | tf_op jit(solution)/shard_map/dot_general | solution.py:51
  58.2 1.4 copy-done.1
  59.6 0.0 copy-done.5
  59.6 2.3 multiply_reduce_fusion
  61.9 0.7 convert_element_type.130
  62.6 4.7 %all-to-all-start.4 = ((bf16[8,1,60]{2,1,0:T(2,128)(2,1)}), bf16[8,1,60]{2,1,0:T(2,128)(2,1)S(1)}, u32[]{:S(2)}, u32[]{:S(2)}) async-start(bf16[8,1,60]{2,1,0:T(2,128)(2,1)} %convert_element_type.130), calls=%async_computation.4 | async-start | bytes 8192 | tf_op jit(solution)/shard_map/all_to_all | solution.py:117
  67.3 0.0 copy-done.4
  67.3 3.2 %all-to-all-done.4 = bf16[8,1,60]{2,1,0:T(2,128)(2,1)S(1)} async-done(((bf16[8,1,60]{2,1,0:T(2,128)(2,1)}), bf16[8,1,60]{2,1,0:T(2,128)(2,1)S(1)}, u32[]{:S(2)}, u32[]{:S(2)}) %all-to-all-start.4) | async-done | bytes 992 | tf_op jit(solution)/shard_map/all_to_all | solution.py:117
  70.5 0.1 reshape.137
  70.6 0.4 select_reduce_fusion.1
  70.9 0.1 convert_element_type.129
  71.0 7.1 %all_to_all.67 = bf16[8,1,60]{2,1,0:T(2,128)(2,1)S(1)} all-to-all(bf16[8,1,60]{2,1,0:T(2,128)(2,1)S(1)} %convert_element_type.129), channel_id=1, replica_groups=mesh['expert'=8,'dp'=4] {'expert'}, dimensions={0} | all-to-all | bytes 1920 | tf_op jit(solution)/shard_map/all_to_all | solution.py:98
  78.1 1.2 multiply_convert_fusion.1
  79.3 1.4 convert_element_type.110
  80.6 0.0 copy-start.6
  80.7 7.4 %fusion.14 = bf16[480,2048]{1,0:T(8,128)(2,1)S(1)} fusion(f32[480,2048]{1,0:T(8,128)} %get-tuple-element.14, bf16[480,1024]{1,0:T(8,128)(2,1)S(1)} %convert_element_type.110, bf16[1,2048,1024]{2,1,0:T(8,128)(2,1)} %param.13), kind=kOutput, calls=%fused_computation.16 | convolution fusion | flops 2031943680 | bytes 11075584 | tf_op jit(solution)/shard_map/dot_general | solution.py:61
  88.1 0.0 copy-start.2
  88.1 1.3 copy-done.2
  89.3 0.0 copy-done.6
  89.3 2.2 fusion.19
  91.6 1.2 reshape.132
  92.7 4.9 %all-to-all-start.3 = ((bf16[8,60,1024]{2,1,0:T(8,128)(2,1)}), bf16[8,60,1024]{2,1,0:T(8,128)(2,1)S(1)}, u32[]{:S(2)}, u32[]{:S(2)}) async-start(bf16[8,60,1024]{2,1,0:T(8,128)(2,1)} %reshape.132), calls=%async_computation.3 | async-start | bytes 2097152 | tf_op jit(solution)/shard_map/all_to_all | solution.py:110
  97.7 3.0 %copy.29 = bf16[60,4,8,512]{3,2,0,1:T(8,128)(2,1)} copy(bf16[60,4,8,512]{3,2,1,0:T(8,128)(2,1)} %bitcast.67) | data formatting | bytes 3932160 | tf_op jit(solution)/shard_map/all_to_all | solution.py:128
  100.7 0.1 reshape.138
  100.8 10.8 %all-to-all-done.3 = bf16[8,60,1024]{2,1,0:T(8,128)(2,1)S(1)} async-done(((bf16[8,60,1024]{2,1,0:T(8,128)(2,1)}), bf16[8,60,1024]{2,1,0:T(8,128)(2,1)S(1)}, u32[]{:S(2)}, u32[]{:S(2)}) %all-to-all-start.3) | async-done | bytes 983072 | tf_op jit(solution)/shard_map/all_to_all | solution.py:110
  111.6 4.8 %all-to-all-start.5 = ((bf16[480,4,512]{2,0,1:T(8,128)(2,1)}), bf16[480,4,512]{2,0,1:T(8,128)(2,1)}, u32[]{:S(2)}, u32[]{:S(2)}) async-start(bf16[480,4,512]{2,0,1:T(8,128)(2,1)} %bitcast.64), calls=%async_computation.5 | async-start | bytes 3932160 | tf_op jit(solution)/shard_map/all_to_all | solution.py:128
  116.4 0.0 all-gather.5.cloned.1.call-start
  116.4 1.2 multiply_convert_fusion.2
  117.6 0.0 all-gather.5.cloned.1.call-update
  117.6 3.0 %copy.28 = bf16[60,4,8,512]{3,2,0,1:T(8,128)(2,1)} copy(bf16[60,4,8,512]{3,2,1,0:T(8,128)(2,1)} %bitcast.65) | data formatting | bytes 3932160 | tf_op jit(solution)/shard_map/all_to_all | solution.py:129
  120.6 88.2 %all-to-all-done.5 = bf16[480,4,512]{2,0,1:T(8,128)(2,1)} async-done(((bf16[480,4,512]{2,0,1:T(8,128)(2,1)}), bf16[480,4,512]{2,0,1:T(8,128)(2,1)}, u32[]{:S(2)}, u32[]{:S(2)}) %all-to-all-start.5) | async-done | bytes 1966112 | tf_op jit(solution)/shard_map/all_to_all | solution.py:128
  208.8 3.6 %all-to-all-start.6 = ((bf16[480,4,512]{2,0,1:T(8,128)(2,1)}), bf16[480,4,512]{2,0,1:T(8,128)(2,1)S(1)}, u32[]{:S(2)}, u32[]{:S(2)}) async-start(bf16[480,4,512]{2,0,1:T(8,128)(2,1)} %bitcast.62), calls=%async_computation.6 | async-start | bytes 3932160 | tf_op jit(solution)/shard_map/all_to_all | solution.py:129
  212.5 0.6 pad_maximum_fusion
  213.0 1.1 reshape.133
  214.2 2.4 convolution_convert_fusion.2
  216.5 6.4 %convolution_bitcast_fusion.1 = f32[1,512,1024]{2,1,0:T(8,128)} fusion(bf16[1920,512]{1,0:T(8,128)(2,1)} %bitcast.14, bf16[1920,1024]{1,0:T(8,128)(2,1)} %all-gather.3.cloned.1.call-done), kind=kOutput, calls=%fused_computation.24 | convolution fusion | flops 2013265920 | bytes 7995392 | tf_op jit(solution)/shard_map/dot_general | solution.py:131
  222.9 44.5 %all-to-all-done.6 = bf16[480,4,512]{2,0,1:T(8,128)(2,1)S(1)} async-done(((bf16[480,4,512]{2,0,1:T(8,128)(2,1)}), bf16[480,4,512]{2,0,1:T(8,128)(2,1)S(1)}, u32[]{:S(2)}, u32[]{:S(2)}) %all-to-all-start.6) | async-done | bytes 1966112 | tf_op jit(solution)/shard_map/all_to_all | solution.py:129
  267.4 5.8 %convolution_bitcast_fusion = f32[1,512,1024]{2,1,0:T(8,128)} fusion(bf16[1920,512]{1,0:T(8,128)(2,1)S(1)} %bitcast.66, bf16[1920,1024]{1,0:T(8,128)(2,1)} %all-gather.5.cloned.1.call-done), kind=kOutput, calls=%fused_computation.23 | convolution fusion | flops 2013265920 | bytes 7995392 | tf_op jit(solution)/shard_map/dot_general | solution.py:134
  (17 shorter events, 0.2 us)
Async XLA Ops:
  7.2 4.9 %copy-start = (bf16[192,1024]{1,0:T(8,128)(2,1)S(1)}, bf16[192,1024]{1,0:T(8,128)(2,1)}, u32[]{:S(2)}) copy-start(bf16[192,1024]{1,0:T(8,128)(2,1)} %param.7) | copy-start | bytes 1179652
  7.2 209.4 %all-gather.3.cloned.1.call-start = ((), (), s32[]{:S(2)}) async-start(), calls=%async_computation.7 | async-start | bytes 4915200 | tf_op jit(solution)/shard_map/all_gather | solution.py:124
  12.1 19.9 %copy-start.3 = (bf16[192,1024]{1,0:T(8,128)(2,1)S(1)}, bf16[192,1024]{1,0:T(8,128)(2,1)}, u32[]{:S(2)}) copy-start(bf16[192,1024]{1,0:T(8,128)(2,1)} %param.8) | copy-start | bytes 1179652
  50.7 8.9 %copy-start.5 = (bf16[1,2048,1024]{2,1,0:T(8,128)(2,1)S(1)}, bf16[1,2048,1024]{2,1,0:T(8,128)(2,1)}, u32[]{:S(2)}) copy-start(bf16[1,2048,1024]{2,1,0:T(8,128)(2,1)} %param.13) | copy-start | bytes 12582916
  58.2 1.4 copy-start.1
  59.6 7.7 %copy-start.4 = (bf16[192,2]{0,1:T(2,128)(2,1)S(1)}, bf16[192,2]{0,1:T(2,128)(2,1)}, u32[]{:S(2)}) copy-start(bf16[192,2]{0,1:T(2,128)(2,1)} %param.11) | copy-start | bytes 2308
  62.6 7.9 %all-to-all-start.4 = ((bf16[8,1,60]{2,1,0:T(2,128)(2,1)}), bf16[8,1,60]{2,1,0:T(2,128)(2,1)S(1)}, u32[]{:S(2)}, u32[]{:S(2)}) async-start(bf16[8,1,60]{2,1,0:T(2,128)(2,1)} %convert_element_type.130), calls=%async_computation.4 | async-start | bytes 8192 | tf_op jit(solution)/shard_map/all_to_all | solution.py:117
  80.6 8.7 %copy-start.6 = (bf16[1,2048,1024]{2,1,0:T(8,128)(2,1)S(1)}, bf16[1,2048,1024]{2,1,0:T(8,128)(2,1)}, u32[]{:S(2)}) copy-start(bf16[1,2048,1024]{2,1,0:T(8,128)(2,1)} %param.12) | copy-start | bytes 12582916
  88.1 1.3 copy-start.2
  92.7 18.8 %all-to-all-start.3 = ((bf16[8,60,1024]{2,1,0:T(8,128)(2,1)}), bf16[8,60,1024]{2,1,0:T(8,128)(2,1)S(1)}, u32[]{:S(2)}, u32[]{:S(2)}) async-start(bf16[8,60,1024]{2,1,0:T(8,128)(2,1)} %reshape.132), calls=%async_computation.3 | async-start | bytes 2097152 | tf_op jit(solution)/shard_map/all_to_all | solution.py:110
  111.6 97.3 %all-to-all-start.5 = ((bf16[480,4,512]{2,0,1:T(8,128)(2,1)}), bf16[480,4,512]{2,0,1:T(8,128)(2,1)}, u32[]{:S(2)}, u32[]{:S(2)}) async-start(bf16[480,4,512]{2,0,1:T(8,128)(2,1)} %bitcast.64), calls=%async_computation.5 | async-start | bytes 3932160 | tf_op jit(solution)/shard_map/all_to_all | solution.py:128
  116.4 151.0 %all-gather.5.cloned.1.call-start = ((), (), s32[]{:S(2)}) async-start(), calls=%async_computation.8 | async-start | bytes 4915200 | tf_op jit(solution)/shard_map/all_gather | solution.py:125
  208.8 58.6 %all-to-all-start.6 = ((bf16[480,4,512]{2,0,1:T(8,128)(2,1)}), bf16[480,4,512]{2,0,1:T(8,128)(2,1)S(1)}, u32[]{:S(2)}, u32[]{:S(2)}) async-start(bf16[480,4,512]{2,0,1:T(8,128)(2,1)} %bitcast.62), calls=%async_computation.6 | async-start | bytes 3932160 | tf_op jit(solution)/shard_map/all_to_all | solution.py:129
Sparse Core Ops, SparseCore 0:
  32.1 76.6 all-gather.2
  118.8 137.1 all-gather.4
where the time goes:
time: 281 us; the launch traced here: 280 us
  waiting for transfers between devices  147 us (52%)
  blocking collectives  42.7 us (15%)
  matrix products  35.1 us (12%)
  starting transfers between devices  18.1 us (6%)
  local copies, waits for them, and re-layouts  16.1 us (6%)
  between operations  14.2 us (5%)
  other arithmetic  7.03 us (3%)
    all_to_all x1, waiting for transfers between devices, per_device(): lax.all_to_all(hidden_grad, 'dp', split_axis=1, concat_axis=0, tiled=True)  88.2 us
    all_to_all x1, waiting for transfers between devices, per_device(): lax.all_to_all(active_b, 'dp', split_axis=1, concat_axis=0, tiled=True)  44.5 us
    all_to_all x1, blocking collectives, per_device(): lax.all_to_all(sent_x, 'expert', split_axis=0, concat_axis=0, tiled=True)  17.9 us
    all_to_all x1, blocking collectives, per_device(): lax.all_to_all(sent_dy, 'expert', split_axis=0, concat_axis=0, tiled=True)  17.7 us
    all_to_all x1, waiting for transfers between devices, per_device(): lax.all_to_all(token_grad.reshape(sources, capacity, model_width), 'exper...  10.8 us
    dot_general x1, matrix products, expert_rows(): lax.dot_general(rows_x, weight_in, (((1,), (1,)), ((), ())), preferred_el...  7.52 us
    dot_general x1, matrix products, expert_rows(): lax.dot_general(scaled, weight_out, (((1,), (1,)), ((), ())), preferred_e...  7.39 us
    all_to_all x1, blocking collectives, per_device(): lax.all_to_all(sent_c, 'expert', split_axis=0, concat_axis=0, tiled=True)  7.05 us
  transfers between devices with their start and end apart: 6, of which 4 were waited for; matrix products, arithmetic and copies ran while one was open for 15% of the time, Pallas kernels for 0%

commit v1 on v0

v1 whole, which is shorter than its diff:
```python
import functools

import jax
import jax.numpy as jnp
from jax import lax
from jax.experimental import pallas as pl
from jax.experimental.pallas import tpu as pltpu
from jax.sharding import PartitionSpec as P


root_coef = 0.7978845608
cube_coef = 0.044715
bf16 = jnp.bfloat16
f32 = jnp.float32

NN = (((1,), (0,)), ((), ()))
NT = (((1,), (1,)), ((), ()))
TN = (((0,), (0,)), ((), ()))


def dot(a, b, dims=NN):
    return lax.dot_general(a, b, dims, preferred_element_type=f32)


def gelu_slope(hidden):
    square = hidden * hidden
    tanh_val = jnp.tanh(hidden * (root_coef + (root_coef * cube_coef) * square))
    half_up = 0.5 + 0.5 * tanh_val
    active = hidden * half_up
    derivative = half_up + active * (1.0 - half_up) * (
        2.0 * root_coef + (6.0 * root_coef * cube_coef) * square
    )
    return active, derivative


def steps(extent, most):
    size = min(extent, most)
    return [(at, size) for at in range(0, extent, size)]


def stack(refs, part, block):
    return jnp.concatenate([ref[part * block : (part + 1) * block, :] for ref in refs], axis=0)


def slot_rows(routes, keep, combine, me, experts, block, capacity):
    count = routes.shape[1]
    kept = keep > 0
    first, second = routes[0:1, :] ^ me, routes[1:2, :] ^ me
    ids = lax.broadcasted_iota(jnp.int32, (experts, count), 0)
    first_hot = jnp.where(first == ids, 1.0, 0.0)
    second_hot = jnp.where((second == ids) & kept, 1.0, 0.0)
    earlier = jnp.where(
        lax.broadcasted_iota(jnp.int32, (count, count), 0)
        < lax.broadcasted_iota(jnp.int32, (count, count), 1),
        1.0,
        0.0,
    ).astype(bf16)
    first_pos = dot(first_hot.astype(bf16), earlier)
    second_pos = dot(second_hot.astype(bf16), earlier) + jnp.sum(first_hot, axis=1, keepdims=True)
    first_slot = jnp.sum(first_pos * first_hot, axis=0, keepdims=True)
    second_slot = jnp.sum(second_pos * second_hot, axis=0, keepdims=True)
    first_flat = jnp.where(first_slot < capacity, first.astype(f32) * block + first_slot, -1.0)
    second_flat = jnp.where(
        kept & (second_slot < capacity), second.astype(f32) * block + second_slot, -1.0
    )
    weights = combine.astype(f32)
    return first_flat, second_flat, weights[0:1, :], weights[1:2, :]


def picks(first_flat, second_flat, rows):
    ids = lax.broadcasted_iota(jnp.int32, (rows, first_flat.shape[1]), 0)
    return ids == first_flat.astype(jnp.int32), ids == second_flat.astype(jnp.int32)


def place(pick, source, out_refs, block):
    for at, size in steps(source.shape[1], 256):
        rows = dot(pick, source[:, at : at + size]).astype(bf16)
        for k, out in enumerate(out_refs):
            out[:, at : at + size] = rows[k * block : (k + 1) * block]


def own_send_kernel(
    experts, block, capacity, routes, keep, combine, tokens, grad_out, meta, *refs
):
    outs, weighted = refs[:experts], refs[experts]

    @pl.when(pl.program_id(0) == 0)
    def _():
        me = lax.axis_index("expert")
        a, b, c, d = slot_rows(
            routes[...], keep[...], combine[...], me, experts, block, capacity
        )
        meta[0:1, :] = a
        meta[1:2, :] = b
        meta[2:3, :] = c
        meta[3:4, :] = d
        meta[4:8, :] = jnp.zeros((4, a.shape[1]), f32)
        first, second = picks(a, b, experts * block)
        weighted[...] = jnp.where(first, c, jnp.where(second, d, 0.0)).astype(bf16)
        chosen = jnp.where(first | second, 1.0, 0.0).astype(bf16)
        place(chosen, tokens, outs, block)

    @pl.when(pl.program_id(0) == 1)
    def _():
        place(weighted[...], grad_out, outs, block)


def send_x_kernel(experts, block, meta, tokens, *outs):
    first, second = picks(meta[0:1, :], meta[1:2, :], experts * block)
    place(jnp.where(first | second, 1.0, 0.0).astype(bf16), tokens, outs, block)


def send_s_kernel(experts, block, meta, grad_out, *outs):
    first, second = picks(meta[0:1, :], meta[1:2, :], experts * block)
    weighted = jnp.where(first, meta[2:3, :], jnp.where(second, meta[3:4, :], 0.0)).astype(bf16)
    place(weighted, grad_out, outs, block)


def add_tokens(grad, w_in, total, gates, outs, block, capacity):
    step, last = pl.program_id(0), pl.num_programs(0) - 1
    more = dot(grad, w_in, TN)

    @pl.when(step == 0)
    def _():
        total[...] = more

    @pl.when((step > 0) & (step < last))
    def _():
        total[...] += more

    @pl.when(step == last)
    def _():
        rows = (total[...] + more).astype(bf16)
        gate_rows = gates[0:1, :].astype(bf16)
        for k, out in enumerate(outs):
            out[...] = rows[k * block : (k + 1) * block]
            out[capacity : capacity + 1, 0:block] = gate_rows[:, k * block : (k + 1) * block]


def add_gates(active, up, gates):
    more = jnp.sum(active.astype(f32) * up, axis=0, keepdims=True)

    @pl.when(pl.program_id(0) == 0)
    def _():
        gates[0:1, :] = more

    @pl.when(pl.program_id(0) > 0)
    def _():
        gates[0:1, :] += more


def own_expert_kernel(experts, block, capacity, pos, w_in, w_out, *refs):
    blocks, (act, grad), outs = refs[:experts], refs[experts : experts + 2], refs[experts + 2 : -2]
    total, gates = refs[-2:]
    x, s = stack(blocks, 0, block), stack(blocks, 1, block)
    active, slope = gelu_slope(dot(w_in[0], x, NT))
    active = active.astype(bf16)
    act[...] = active
    up = dot(w_out[0], s, NT)
    add_gates(active, up, gates)
    hidden_grad = (up * slope).astype(bf16)
    grad[...] = hidden_grad
    add_tokens(hidden_grad, w_in[0], total, gates, outs, block, capacity)


def act_kernel(experts, block, pos, w_in, *refs):
    blocks, (act, slope) = refs[:experts], refs[experts:]
    active, derivative = gelu_slope(dot(w_in[0], stack(blocks, 0, block), NT))
    act[...] = active.astype(bf16)
    slope[...] = derivative.astype(bf16)


def grad_kernel(experts, block, capacity, pos, w_in, w_out, act, slope, *refs):
    blocks, grad, outs = refs[:experts], refs[experts], refs[experts + 1 : -2]
    total, gates = refs[-2:]
    up = dot(w_out[0], stack(blocks, 0, block), NT)
    add_gates(act[...], up, gates)
    hidden_grad = (up * slope[...].astype(f32)).astype(bf16)
    grad[...] = hidden_grad
    add_tokens(hidden_grad, w_in[0], total, gates, outs, block, capacity)


def outer_rows(own_ref, other_ref, own_rows, other_rows, at, size):
    return dot(own_ref[pl.ds(at, size), :], own_rows) + dot(other_ref[pl.ds(at, size), :], other_rows)


def away_kernel(experts, block, owners, pos, own, other, *refs):
    own_blocks, other_blocks, outs = refs[:experts], refs[experts : 2 * experts], refs[2 * experts :]
    own_rows, other_rows = stack(own_blocks, 0, block), stack(other_blocks, 0, block)
    size = own.shape[0] // owners
    for r, out in enumerate(outs):
        at = pl.multiple_of(lax.rem(pos[1] + r + 1, owners) * size, size)
        out[...] = outer_rows(own, other, own_rows, other_rows, at, size).astype(bf16)


def home_kernel(experts, block, owners, pos, own, other, *refs):
    own_blocks, other_blocks = refs[:experts], refs[experts : 2 * experts]
    got, out = refs[2 * experts : 2 * experts + owners - 1], refs[-1]
    own_rows, other_rows = stack(own_blocks, 0, block), stack(other_blocks, 0, block)
    size = own.shape[0] // owners
    at = pl.multiple_of(pos[1] * size, size)
    total = outer_rows(own, other, own_rows, other_rows, at, size)
    for ref in got:
        total = total + ref[...].astype(f32)
    out[0] = total


def gathered(meta, refs, experts, block):
    first, second = picks(meta[0:1, :], meta[1:2, :], experts * block)
    chosen = jnp.where(first | second, 1.0, 0.0).astype(bf16)
    return dot(chosen, stack(refs, 0, block), TN)


def gate_rows(meta, refs, block, capacity):
    values = jnp.concatenate([ref[capacity : capacity + 1, 0:block] for ref in refs], axis=0)
    out = []
    for at in (0, 1):
        flat = meta[at : at + 1, :].astype(jnp.int32)
        live = flat >= 0
        which = jnp.where(live, flat, 0) // block
        where = flat - which * block
        lane = lax.broadcasted_iota(jnp.int32, (block, flat.shape[1]), 0)
        hit = jnp.where((lane == where) & live, 1.0, 0.0).astype(bf16)
        by_block = dot(values, hit)
        mine = lax.broadcasted_iota(jnp.int32, by_block.shape, 0) == which
        gate = jnp.sum(jnp.where(mine, by_block, 0.0), axis=0, keepdims=True)
        out.append(jnp.where(live, gate / meta[at + 2 : at + 3, :], 0.0))
    return out


def other_collect_kernel(experts, block, capacity, meta, *refs):
    blocks, (out, gates) = refs[:experts], refs[experts:]
    out[...] = gathered(meta, blocks, experts, block).astype(bf16)

    @pl.when(pl.program_id(0) == 0)
    def _():
        first, second = gate_rows(meta, blocks, block, capacity)
        gates[0:1, :] = first
        gates[1:2, :] = second
        gates[2:8, :] = jnp.zeros((6, first.shape[1]), f32)


def own_collect_kernel(experts, block, capacity, meta, got, got_gates, *refs):
    blocks, (grad_tokens, grad_combine) = refs[:experts], refs[experts:]
    tokens = gathered(meta, blocks, experts, block)
    grad_tokens[...] = (tokens + got[...].astype(f32)).astype(bf16)

    @pl.when(pl.program_id(0) == 0)
    def _():
        gates = gate_rows(meta, blocks, block, capacity)
        grad_combine[...] = (jnp.concatenate(gates, axis=0) + got_gates[0:2, :]).astype(bf16)


def shaped(shape, dtype=bf16):
    return jax.ShapeDtypeStruct(shape, dtype)


def full(array):
    return pl.BlockSpec(array.shape, lambda g, *pos, rank=array.ndim: (0,) * rank)


def columns(array, parts, first=0):
    size = array.shape[-1] // parts
    lead = array.shape[:-1]
    return pl.BlockSpec(
        lead + (size,), lambda g, *pos, rank=array.ndim: (0,) * (rank - 1) + (first + g,)
    )


def rows(array, size):
    return pl.BlockSpec((size, array.shape[1]), lambda g, *pos: (g, 0))


def half_rows(array, parts):
    size = array.shape[1] // 2 // parts
    return pl.BlockSpec((1, size, array.shape[2]), lambda g, pos: (0, pos[0] * parts + g, 0))


def call(kernel, grid, scalars, operands, results, scratch=(), flops=0, alias=None):
    arrays, in_specs = [a for a, _ in operands], [s for _, s in operands]
    outs, out_specs = [a for a, _ in results], [s for _, s in results]
    moved = sum(a.size * a.dtype.itemsize for a in arrays + outs)
    return pl.pallas_call(
        kernel,
        out_shape=outs,
        grid_spec=pltpu.PrefetchScalarGridSpec(
            num_scalar_prefetch=len(scalars),
            grid=(grid,),
            in_specs=in_specs,
            out_specs=out_specs,
            scratch_shapes=list(scratch),
        ),
        input_output_aliases=alias or {},
        compiler_params=pltpu.CompilerParams(vmem_limit_bytes=28 << 20),
        cost_estimate=pl.CostEstimate(flops=int(flops), transcendentals=0, bytes_accessed=moved),
    )(*scalars, *arrays)


def part_of(array, part, block, parts, first=0):
    return pl.BlockSpec((block, array.shape[1] // parts), lambda g, *pos: (part, first + g))


def per_device(tokens, grad_out, routes, keep_second, combine, w_in, w_out):
    experts, planes = lax.axis_size("expert"), lax.axis_size("dp")
    count, width = tokens.shape
    capacity = 5 * count // (2 * experts)
    block = -(-(capacity + 1) // 16) * 16
    owners = planes // 2
    units = w_in.shape[1] // 2
    share = units // owners
    slots = experts * block
    if planes % 2 or experts & (experts - 1):
        raise ValueError("mesh sizes")
    plane = lax.axis_index("dp")
    pos = jnp.stack([plane // owners, plane % owners]).astype(jnp.int32)
    bind = functools.partial

    def across(value):
        return lax.ppermute(value, "dp", [(j, (j + owners) % planes) for j in range(planes)])

    def exchange(values):
        return [values[0]] + [
            lax.ppermute(values[k], "expert", [(i, i ^ k) for i in range(experts)])
            for k in range(1, experts)
        ]

    def to_owners(values):
        return [
            lax.ppermute(
                value,
                "dp",
                [(j, j // owners * owners + (j + r + 1) % owners) for j in range(planes)],
            )
            for r, value in enumerate(values)
        ]

    def each(arrays, spec, *more):
        return [(a, spec(a, *more)) for a in arrays]

    routes_t, keep_t, combine_t = routes.T, keep_second.reshape(1, count), combine.T

    def stay(array):
        return pltpu.with_memory_space_constraint(array, pltpu.HBM)

    w_in, w_out = stay(w_in), stay(w_out)
    other_x = across(tokens)
    other_dy = across(grad_out)
    blocks2 = [shaped((2 * block, width))] * experts
    blocks1 = [shaped((block, width))] * experts
    act_shape = shaped((units, slots))
    unit_parts = max(units // 256, 1)
    unit_rows = units // unit_parts
    sums = [pltpu.VMEM((slots, width), f32), pltpu.VMEM((8, slots), f32)]
    meta_shape = shaped((8, count), f32)
    meta, *own_blocks = call(
        bind(own_send_kernel, experts, block, capacity),
        2,
        [],
        each([stay(a) for a in (routes_t, keep_t, combine_t, tokens, grad_out)], full),
        each([meta_shape], full) + each(blocks2, rows, block),
        [pltpu.VMEM((slots, count), bf16)],
        4 * slots * count * width,
    )
    own_blocks = exchange(own_blocks)
    other_meta = across(meta)
    other_xb = call(
        bind(send_x_kernel, experts, block),
        2,
        [],
        each([other_meta], full) + each([other_x], columns, 2),
        each(blocks1, columns, 2),
        flops=2 * slots * count * width,
    )
    other_xb = exchange(other_xb)
    other_sb = call(
        bind(send_s_kernel, experts, block),
        2,
        [],
        each([other_meta], full) + each([other_dy], columns, 2),
        each(blocks1, columns, 2),
        flops=2 * slots * count * width,
    )
    other_sb = exchange(other_sb)
    own_act, own_grad, *own_back = call(
        bind(own_expert_kernel, experts, block, capacity),
        unit_parts,
        [pos],
        each([w_in, w_out], half_rows, unit_parts) + each(own_blocks, full),
        each([act_shape] * 2, rows, unit_rows) + each(blocks1, full),
        sums,
        6 * slots * units * width,
    )
    other_act, other_slope = call(
        bind(act_kernel, experts, block),
        unit_parts,
        [pos],
        each([w_in], half_rows, unit_parts) + each(other_xb, full),
        each([act_shape] * 2, rows, unit_rows),
        flops=2 * slots * units * width,
    )
    runs = 4
    fed = slots * share * width

    def away(acts, left, part, right, first, many):
        extent = width // runs * many
        return call(
            bind(away_kernel, experts, block, owners),
            many,
            [pos],
            each(acts, full)
            + each(left, part_of, part, block, runs, first)
            + each(right, part_of, 0, block, runs, first),
            each([shaped((share, extent))] * (owners - 1), columns, many),
            flops=4 * fed * (owners - 1) * many // runs,
        )

    def home(acts, left, part, right, got, first, many, into=None):
        goal = shaped((1, share, width), f32)
        operands = (
            each(acts, full)
            + each(left, part_of, part, block, runs, first)
            + each(right, part_of, 0, block, runs, first)
            + each(got, columns, many)
        )
        alias = None
        if into is not None:
            operands.append((into, pl.BlockSpec(memory_space=pl.ANY)))
            alias = {len(operands): 0}
        return call(
            bind(home_kernel, experts, block, owners),
            many,
            [pos],
            operands,
            each([goal], columns, runs, first),
            flops=4 * fed * many // runs,
            alias=alias,
        )[0]

    away_out = away([own_act, other_act], own_blocks, 1, other_sb, 0, runs)
    got_out = to_owners(away_out)
    other_grad, *other_back = call(
        bind(grad_kernel, experts, block, capacity),
        unit_parts,
        [pos],
        each([w_in, w_out], half_rows, unit_parts)
        + each([other_act, other_slope], rows, unit_rows)
        + each(other_sb, full),
        each([act_shape], rows, unit_rows) + each(blocks1, full),
        sums,
        4 * slots * units * width,
    )
    other_back = exchange(other_back)
    in_args = [own_grad, other_grad], own_blocks, 0, other_xb
    away_a = away(*in_args, 0, 3)
    got_a = to_owners(away_a)
    away_b = away(*in_args, 3, 1)
    got_b = to_owners(away_b)
    own_back = exchange(own_back)
    other_part, other_gates = call(
        bind(other_collect_kernel, experts, block, capacity),
        2,
        [],
        each([other_meta], full) + each(other_back, columns, 2),
        each([shaped((count, width))], columns, 2) + each([meta_shape], full),
        flops=2 * slots * count * width,
    )
    part = across(other_part)
    part_gates = across(other_gates)
    grad_outw = home([own_act, other_act], own_blocks, 1, other_sb, got_out, 0, runs)
    grad_tokens, grad_combine = call(
        bind(own_collect_kernel, experts, block, capacity),
        2,
        [],
        each([meta], full)
        + each([part], columns, 2)
        + each([part_gates], full)
        + each(own_back, columns, 2),
        each([shaped((count, width))], columns, 2) + each([shaped((2, count))], full),
        flops=2 * slots * count * width,
    )
    grad_in = home(*in_args, got_a, 0, 3)
    grad_in = home(*in_args, got_b, 3, 1, grad_in)
    return grad_tokens, grad_combine.T, grad_in, grad_outw


def solution(mesh):
    return jax.shard_map(
        per_device,
        mesh=mesh,
        in_specs=(
            P(("expert", "dp"), None),
            P(("expert", "dp"), None),
            P(("expert", "dp"), None),
            P(("expert", "dp")),
            P(("expert", "dp"), None),
            P("expert", None, None),
            P("expert", None, None),
        ),
        out_specs=(
            P(("expert", "dp"), None),
            P(("expert", "dp"), None),
            P("expert", "dp", None),
            P("expert", "dp", None),
        ),
        check_vma=False,
    )
```

time: 281 us -> 170 us (0.60)
  the two profiles are of different devices: /device:TPU:2 before, /device:TPU:8 now
where the time goes in v1:
time: 170 us; the launch traced here: 169 us
  waiting for transfers between devices  77 us (45%)
  starting transfers between devices  48 us (28%)
  Pallas kernels  42 us (25%)
    ppermute x35, waiting for transfers between devices, exchange(): lax.ppermute(values[k], 'expert', [(i, i ^ k) for i in range(experts)])  44.6 us
    pallas_call x14, Pallas kernels, call(): pl.pallas_call(kernel, out_shape=outs, grid_spec=pltpu.PrefetchScalarGrid...  42 us
    ppermute x35, starting transfers between devices, exchange(): lax.ppermute(values[k], 'expert', [(i, i ^ k) for i in range(experts)])  33 us
    ppermute x5, waiting for transfers between devices, across(): lax.ppermute(value, 'dp', [(j, (j + owners) % planes) for j in range(plan...  32.3 us
    ppermute x5, starting transfers between devices, across(): lax.ppermute(value, 'dp', [(j, (j + owners) % planes) for j in range(plan...  11.2 us
    ppermute x3, starting transfers between devices, to_owners(): lax.ppermute(value, 'dp', [(j, j // owners * owners + (j + r + 1) % owner...  3.76 us
  transfers between devices with their start and end apart: 43, of which 15 were waited for; matrix products, arithmetic and copies ran while one was open for 0% of the time, Pallas kernels for 22%

profile of v1, /device:TPU:8, one launch (start us, length us, event | category | flops | bytes accessed | tf_op | source)
XLA Modules:
  0.0 169.2 jit_solution(15615017285654350771)
XLA Ops:
  0.6 2.7 %collective-permute-start.1 = (bf16[192,1024]{1,0:T(8,128)(2,1)}, bf16[192,1024]{1,0:T(8,128)(2,1)S(1)}, u32[]{:S(2)}, u32[]{:S(2)}) collective-permute-start(bf16[192,1024]{1,0:T(8,128)(2,1)} %tokens.1), channel_id=1, source_target_pairs={{0,2},{1,3},{2,0},{3,1},{4,6},{5,7},{6,4},{7,5},{8,10},{9,11},{10,... | collective-permute-start | bytes 1179656 | tf_op jit(solution)/shard_map/ppermute | solution.py:319
  3.6 2.3 %shard_map.102 = (f32[8,192]{1,0:T(8,128)S(1)}, bf16[128,1024]{1,0:T(8,128)(2,1)S(1)}, bf16[128,1024]{1,0:T(8,128)(2,1)S(1)}, bf16[128,1024]{1,0:T(8,128)(2,1)S(...) custom-call(s32[2,192]{1,0:T(2,128)} %bitcast.6, ...), custom_call_target="tpu_custom_call" | custom-call | flops 402653184 | bytes 2892800 | tf_op jit(solution)/shard_map/pallas_call | solution.py:283
  6.0 1.6 collective-permute-start.27
  7.6 2.6 %collective-permute-start = (f32[8,192]{1,0:T(8,128)S(1)}, f32[8,192]{1,0:T(8,128)S(1)}, u32[]{:S(2)}, u32[]{:S(2)}) collective-permute-start(f32[8,192]{1,0:T(8,128)S(1)} %get-tuple-element.54.meta), channel_id=1, source_target_pairs={{0,2},{1,3},{2,0},{3,1},{4,6},{5,7},{6,4},{7,5},{8,10},{9,11},{10,... | collective-permute-start | bytes 18440 | tf_op jit(solution)/shard_map/ppermute | solution.py:319
  10.2 27.2 %collective-permute-done.meta = f32[8,192]{1,0:T(8,128)S(1)} collective-permute-done((f32[8,192]{1,0:T(8,128)S(1)}, f32[8,192]{1,0:T(8,128)S(1)}, u32[]{:S(2)}, u32[]{:S(2)}) %collective-permute-start) | collective-permute-done | bytes 6176 | tf_op jit(solution)/shard_map/ppermute | solution.py:319
  37.4 1.1 collective-permute-start.28
  38.5 1.5 collective-permute-start.29
  40.4 1.5 collective-permute-start.31
  41.9 1.0 collective-permute-start.32
  42.9 0.7 shard_map.105
  43.7 0.7 copy-done
  44.3 0.7 copy-done.4
  45.0 1.5 shard_map.103
  46.5 0.6 collective-permute-start.10
  47.0 11.9 %collective-permute-done.29.refs_4_ = bf16[128,1024]{1,0:T(8,128)(2,1)S(1)} collective-permute-done((bf16[128,1024]{1,0:T(8,128)(2,1)S(1)}, bf16[128,1024]{1,0:T(8,128)(2,1)S(1)}, u32[]{:S(2)}, u32[]{:S(2)}) %collective-permute-start.29) | collective-permute-done | bytes 262176 | tf_op jit(solution)/shard_map/ppermute | solution.py:323
  58.9 4.7 %collective-permute-done.30.refs_5_ = bf16[128,1024]{1,0:T(8,128)(2,1)S(1)} collective-permute-done((bf16[128,1024]{1,0:T(8,128)(2,1)S(1)}, bf16[128,1024]{1,0:T(8,128)(2,1)S(1)}, u32[]{:S(2)}, u32[]{:S(2)}) %collective-permute-start.30) | collective-permute-done | bytes 262176 | tf_op jit(solution)/shard_map/ppermute | solution.py:323
  64.4 1.0 collective-permute-start.4
  65.5 1.5 collective-permute-start.5
  67.0 0.5 collective-permute-start.6
  67.5 1.5 collective-permute-start.7
  69.0 1.4 collective-permute-done.3.refs_2_.refs_10_
  70.5 1.0 collective-permute-done.4.refs_3_.refs_11_
  71.5 1.8 %collective-permute-start.12 = (bf16[64,1024]{1,0:T(8,128)(2,1)}, bf16[64,1024]{1,0:T(8,128)(2,1)S(1)}, u32[]{:S(2)}, u32[]{:S(2)}) collective-permute-start(bf16[64,1024]{1,0:T(8,128)(2,1)} %copy-done.4), channel_id=1, source_target_pairs={{0,12},{4,8},{8,4},{12,0},{16,28},{20,24},{24,20},{28,16},{1,13},{... | collective-permute-start | bytes 393224 | tf_op jit(solution)/shard_map/ppermute | solution.py:323
  73.3 1.6 collective-permute-start.13
  75.0 4.9 %collective-permute-done.6.refs_5_.refs_13_ = bf16[64,1024]{1,0:T(8,128)(2,1)S(1)} collective-permute-done((bf16[64,1024]{1,0:T(8,128)(2,1)}, bf16[64,1024]{1,0:T(8,128)(2,1)S(1)}, u32[]{:S(2)}, u32[]{:S(2)}) %collective-permute-start.6) | collective-permute-done | bytes 131104 | tf_op jit(solution)/shard_map/ppermute | solution.py:323
  79.9 1.6 collective-permute-start.14
  81.5 0.6 collective-permute-start.15
  82.0 1.8 %collective-permute-start.16 = (bf16[64,1024]{1,0:T(8,128)(2,1)}, bf16[64,1024]{1,0:T(8,128)(2,1)S(1)}, u32[]{:S(2)}, u32[]{:S(2)}) collective-permute-start(bf16[64,1024]{1,0:T(8,128)(2,1)} %copy-done), channel_id=1, source_target_pairs={{0,28},{4,24},{8,20},{12,16},{16,12},{20,8},{24,4},{28,0},{1,29},{... | collective-permute-start | bytes 393224 | tf_op jit(solution)/shard_map/ppermute | solution.py:323
  83.8 8.4 %shard_map.108 = (bf16[1024,512]{1,0:T(8,128)(2,1)S(1)}, bf16[1024,512]{1,0:T(8,128)(2,1)S(1)}, bf16[64,1024]{1,0:T(8,128)(2,1)S(1)}, bf16[64,1024]{1,0:T(8,128)...) custom-call(s32[2]{0:T(128)S(1)} %pad_add_fusion.pos, ...), custom_call_target="tpu_custom_call" | custom-call | flops 3221225472 | bytes 13631488 | tf_op jit(solution)/shard_map/pallas_call | solution.py:283
  92.2 4.7 %shard_map.104 = (bf16[1024,512]{1,0:T(8,128)(2,1)S(1)}, bf16[1024,512]{1,0:T(8,128)(2,1)S(1)}) custom-call(s32[2]{0:T(128)S(1)} %pad_add_fusion.pos, bf16[1,2048,1024]{2,1,0:T(8,128)(2,1)} %w_in.5, bf16[64,1024]{1,0:T(8,128)(2,1)S(1)} %get-tuple-element.55.refs_0_.refs_8_, bf16[64,1024]{1,0:T(8,128)(2,1)S(1)} %collective-permute-done.2.refs_1_.refs_9_, ...), custom_call_target="tpu_custom_call" | custom-call | flops 1073741824 | bytes 7340032 | tf_op jit(solution)/shard_map/pallas_call | solution.py:283
  96.9 0.8 collective-permute-start.33
  97.7 2.9 %shard_map.114 = bf16[512,1024]{1,0:T(8,128)(2,1)S(1)} custom-call(s32[2]{0:T(128)S(1)} %pad_add_fusion.pos, bf16[1024,512]{1,0:T(8,128)(2,1)S(1)} %get-tuple-element.103.own, bf16[1024,512]{1,0:T(8,128)(2,1)S(1)} %get-tuple-element.63.act.other, bf16[128,1024]{1,0:T(8,128)(2,1)S(1)} %get-tuple-element.83.refs_0_, ...), custom_call_target="tpu_custom_call" | custom-call | flops 1073741824 | bytes 6291456 | tf_op jit(solution)/shard_map/pallas_call | solution.py:283
  100.7 1.5 collective-permute-start.42
  102.1 6.6 %shard_map.106 = (bf16[1024,512]{1,0:T(8,128)(2,1)S(1)}, bf16[64,1024]{1,0:T(8,128)(2,1)S(1)}, bf16[64,1024]{1,0:T(8,128)(2,1)S(1)}, bf16[64,1024]{1,0:T(8,128)(...) custom-call(s32[2]{0:T(128)S(1)} %pad_add_fusion.pos, ...), custom_call_target="tpu_custom_call" | custom-call | flops 2147483648 | bytes 13631488 | tf_op jit(solution)/shard_map/pallas_call | solution.py:283
  108.8 0.7 collective-permute-start.18
  109.5 2.3 %shard_map.111 = bf16[512,768]{1,0:T(8,128)(2,1)S(1)} custom-call(s32[2]{0:T(128)S(1)} %pad_add_fusion.pos, bf16[1024,512]{1,0:T(8,128)(2,1)S(1)} %get-tuple-element.101.own, bf16[1024,512]{1,0:T(8,128)(2,1)S(1)} %get-tuple-element.102.other, bf16[128,1024]{1,0:T(8,128)(2,1)S(1)} %get-tuple-element.83.refs_0_, ...), custom_call_target="tpu_custom_call" | custom-call | flops 805306368 | bytes 6029312 | tf_op jit(solution)/shard_map/pallas_call | solution.py:283
  111.8 0.7 collective-permute-start.41
  112.5 0.9 collective-permute-start.19
  113.4 0.5 collective-permute-start.20
  113.9 0.8 collective-permute-done.18.refs_2_
  114.7 0.7 collective-permute-start.21
  115.4 2.9 %collective-permute-done.19.refs_3_ = bf16[64,1024]{1,0:T(8,128)(2,1)S(1)} collective-permute-done((bf16[64,1024]{1,0:T(8,128)(2,1)S(1)}, bf16[64,1024]{1,0:T(8,128)(2,1)S(1)}, u32[]{:S(2)}, u32[]{:S(2)}) %collective-permute-start.19) | collective-permute-done | bytes 131104 | tf_op jit(solution)/shard_map/ppermute | solution.py:323
  118.2 1.4 collective-permute-start.22
  119.7 0.9 collective-permute-start.23
  120.6 5.3 %collective-permute-done.21.refs_5_ = bf16[64,1024]{1,0:T(8,128)(2,1)S(1)} collective-permute-done((bf16[64,1024]{1,0:T(8,128)(2,1)S(1)}, bf16[64,1024]{1,0:T(8,128)(2,1)S(1)}, u32[]{:S(2)}, u32[]{:S(2)}) %collective-permute-start.21) | collective-permute-done | bytes 131104 | tf_op jit(solution)/shard_map/ppermute | solution.py:323
  125.9 3.4 %collective-permute-start.35 = (bf16[64,1024]{1,0:T(8,128)(2,1)S(1)}, bf16[64,1024]{1,0:T(8,128)(2,1)S(1)}, u32[]{:S(2)}, u32[]{:S(2)}) collective-permute-start(bf16[64,1024]{1,0:T(8,128)(2,1)S(1)} %get-tuple-element.94), channel_id=1, source_target_pairs={{0,12},{4,8},{8,4},{12,0},{16,28},{20,24},{24,20},{28,16},{1,13},{... | collective-permute-start | bytes 393224 | tf_op jit(solution)/shard_map/ppermute | solution.py:323
  129.3 0.5 collective-permute-start.36
  129.8 0.9 shard_map.107
  130.7 0.4 collective-permute-done.34.refs_2_
  131.2 3.3 %collective-permute-start.24 = (bf16[192,1024]{1,0:T(8,128)(2,1)S(1)}, bf16[192,1024]{1,0:T(8,128)(2,1)S(1)}, u32[]{:S(2)}, u32[]{:S(2)}) collective-permute-start(bf16[192,1024]{1,0:T(8,128)(2,1)S(1)} %get-tuple-element.81), channel_id=1, source_target_pairs={{0,2},{1,3},{2,0},{3,1},{4,6},{5,7},{6,4},{7,5},{8,10},{9,11},{10,... | collective-permute-start | bytes 1179656 | tf_op jit(solution)/shard_map/ppermute | solution.py:319
  134.5 0.6 collective-permute-done.35.refs_3_
  135.1 1.6 collective-permute-start.37
  136.7 0.5 collective-permute-start.38
  137.2 1.0 shard_map.110
  138.2 5.0 %collective-permute-done.37.refs_5_ = bf16[64,1024]{1,0:T(8,128)(2,1)S(1)} collective-permute-done((bf16[64,1024]{1,0:T(8,128)(2,1)S(1)}, bf16[64,1024]{1,0:T(8,128)(2,1)S(1)}, u32[]{:S(2)}, u32[]{:S(2)}) %collective-permute-start.37) | collective-permute-done | bytes 131104 | tf_op jit(solution)/shard_map/ppermute | solution.py:323
  143.2 1.6 collective-permute-start.40
  144.8 0.8 collective-permute-start.39
  145.6 5.5 %collective-permute-done.39.refs_7_ = bf16[64,1024]{1,0:T(8,128)(2,1)S(1)} collective-permute-done((bf16[64,1024]{1,0:T(8,128)(2,1)S(1)}, bf16[64,1024]{1,0:T(8,128)(2,1)S(1)}, u32[]{:S(2)}, u32[]{:S(2)}) %collective-permute-start.39) | collective-permute-done | bytes 131104 | tf_op jit(solution)/shard_map/ppermute | solution.py:323
  151.1 2.3 %collective-permute-start.25 = (f32[8,192]{1,0:T(8,128)S(1)}, f32[8,192]{1,0:T(8,128)S(1)}, u32[]{:S(2)}, u32[]{:S(2)}) collective-permute-start(f32[8,192]{1,0:T(8,128)S(1)} %get-tuple-element.82), channel_id=1, source_target_pairs={{0,2},{1,3},{2,0},{3,1},{4,6},{5,7},{6,4},{7,5},{8,10},{9,11},{10,... | collective-permute-start | bytes 18440 | tf_op jit(solution)/shard_map/ppermute | solution.py:319
  153.4 5.1 %collective-permute-done.25.got_gates = f32[8,192]{1,0:T(8,128)S(1)} collective-permute-done((f32[8,192]{1,0:T(8,128)S(1)}, f32[8,192]{1,0:T(8,128)S(1)}, u32[]{:S(2)}, u32[]{:S(2)}) %collective-permute-start.25) | collective-permute-done | bytes 6176 | tf_op jit(solution)/shard_map/ppermute | solution.py:319
  158.5 1.6 shard_map.109
  160.1 3.3 %shard_map.112.refs_17_ = f32[1,512,1024]{2,1,0:T(8,128)} custom-call(s32[2]{0:T(128)S(1)} %pad_add_fusion.pos, bf16[1024,512]{1,0:T(8,128)(2,1)S(1)} %get-tuple-element.101.own, bf16[1024,512]{1,0:T(8,128)(2,1)S(1)} %get-tuple-element.102.other, bf16[128,1024]{1,0:T(8,128)(2,1)S(1)} %get-tuple-element.83.refs_0_, ...), custom_call_target="tpu_custom_call" | custom-call | flops 805306368 | bytes 8126464 | tf_op jit(solution)/shard_map/pallas_call | solution.py:283
  163.5 1.8 %shard_map.113 = f32[1,512,1024]{2,1,0:T(8,128)} custom-call(s32[2]{0:T(128)S(1)} %pad_add_fusion.pos, bf16[1024,512]{1,0:T(8,128)(2,1)S(1)} %get-tuple-element.101.own, bf16[1024,512]{1,0:T(8,128)(2,1)S(1)} %get-tuple-element.102.other, bf16[128,1024]{1,0:T(8,128)(2,1)S(1)} %get-tuple-element.83.refs_0_, ...), custom_call_target="tpu_custom_call", output_to_operand_aliasing={{}: (20, {})} | custom-call | flops 268435456 | bytes 9699328 | tf_op jit(solution)/shard_map/pallas_call | solution.py:283
  165.2 4.0 %shard_map.115 = f32[1,512,1024]{2,1,0:T(8,128)} custom-call(s32[2]{0:T(128)S(1)} %pad_add_fusion.pos, bf16[1024,512]{1,0:T(8,128)(2,1)S(1)} %get-tuple-element.103.own, bf16[1024,512]{1,0:T(8,128)(2,1)S(1)} %get-tuple-element.63.act.other, bf16[128,1024]{1,0:T(8,128)(2,1)S(1)} %get-tuple-element.83.refs_0_, ...), custom_call_target="tpu_custom_call" | custom-call | flops 1073741824 | bytes 8388608 | tf_op jit(solution)/shard_map/pallas_call | solution.py:283
  (47 shorter events, 2.0 us)
Async XLA Ops:
  0.6 39.7 %collective-permute-start.1 = (bf16[192,1024]{1,0:T(8,128)(2,1)}, bf16[192,1024]{1,0:T(8,128)(2,1)S(1)}, u32[]{:S(2)}, u32[]{:S(2)}) collective-permute-start(bf16[192,1024]{1,0:T(8,128)(2,1)} %tokens.1), channel_id=1, source_target_pairs={{0,2},{1,3},{2,0},{3,1},{4,6},{5,7},{6,4},{7,5},{8,10},{9,11},{10,... | collective-permute-start | bytes 1179656 | tf_op jit(solution)/shard_map/ppermute | solution.py:319
  3.3 38.6 %collective-permute-start.9 = (bf16[192,1024]{1,0:T(8,128)(2,1)}, bf16[192,1024]{1,0:T(8,128)(2,1)S(1)}, u32[]{:S(2)}, u32[]{:S(2)}) collective-permute-start(bf16[192,1024]{1,0:T(8,128)(2,1)} %grad_out.1), channel_id=1, source_target_pairs={{0,2},{1,3},{2,0},{3,1},{4,6},{5,7},{6,4},{7,5},{8,10},{9,11},{10,... | collective-permute-start | bytes 1179656 | tf_op jit(solution)/shard_map/ppermute | solution.py:319
  5.9 32.6 %collective-permute-start.26 = (bf16[128,1024]{1,0:T(8,128)(2,1)S(1)}, bf16[128,1024]{1,0:T(8,128)(2,1)S(1)}, u32[]{:S(2)}, u32[]{:S(2)}) collective-permute-start(bf16[128,1024]{1,0:T(8,128)(2,1)S(1)} %get-tuple-element.84), channel_id=1, source_target_pairs={{0,4},{4,0},{8,12},{12,8},{16,20},{20,16},{24,28},{28,24},{1,5},{5... | collective-permute-start | bytes 786440 | tf_op jit(solution)/shard_map/ppermute | solution.py:323
  6.0 34.0 %collective-permute-start.27 = (bf16[128,1024]{1,0:T(8,128)(2,1)S(1)}, bf16[128,1024]{1,0:T(8,128)(2,1)S(1)}, u32[]{:S(2)}, u32[]{:S(2)}) collective-permute-start(bf16[128,1024]{1,0:T(8,128)(2,1)S(1)} %get-tuple-element.85), channel_id=1, source_target_pairs={{0,8},{4,12},{8,0},{12,4},{16,24},{20,28},{24,16},{28,20},{1,9},{5... | collective-permute-start | bytes 786440 | tf_op jit(solution)/shard_map/ppermute | solution.py:323
  7.6 29.8 %collective-permute-start = (f32[8,192]{1,0:T(8,128)S(1)}, f32[8,192]{1,0:T(8,128)S(1)}, u32[]{:S(2)}, u32[]{:S(2)}) collective-permute-start(f32[8,192]{1,0:T(8,128)S(1)} %get-tuple-element.54.meta), channel_id=1, source_target_pairs={{0,2},{1,3},{2,0},{3,1},{4,6},{5,7},{6,4},{7,5},{8,10},{9,11},{10,... | collective-permute-start | bytes 18440 | tf_op jit(solution)/shard_map/ppermute | solution.py:319
  37.4 9.0 %collective-permute-start.28 = (bf16[128,1024]{1,0:T(8,128)(2,1)S(1)}, bf16[128,1024]{1,0:T(8,128)(2,1)S(1)}, u32[]{:S(2)}, u32[]{:S(2)}) collective-permute-start(bf16[128,1024]{1,0:T(8,128)(2,1)S(1)} %get-tuple-element.86), channel_id=1, source_target_pairs={{0,12},{4,8},{8,4},{12,0},{16,28},{20,24},{24,20},{28,16},{1,13},{... | collective-permute-start | bytes 786440 | tf_op jit(solution)/shard_map/ppermute | solution.py:323
  38.5 20.4 %collective-permute-start.29 = (bf16[128,1024]{1,0:T(8,128)(2,1)S(1)}, bf16[128,1024]{1,0:T(8,128)(2,1)S(1)}, u32[]{:S(2)}, u32[]{:S(2)}) collective-permute-start(bf16[128,1024]{1,0:T(8,128)(2,1)S(1)} %get-tuple-element.87), channel_id=1, source_target_pairs={{0,16},{4,20},{8,24},{12,28},{16,0},{20,4},{24,8},{28,12},{1,17},{... | collective-permute-start | bytes 786440 | tf_op jit(solution)/shard_map/ppermute | solution.py:323
  40.0 23.6 %collective-permute-start.30 = (bf16[128,1024]{1,0:T(8,128)(2,1)S(1)}, bf16[128,1024]{1,0:T(8,128)(2,1)S(1)}, u32[]{:S(2)}, u32[]{:S(2)}) collective-permute-start(bf16[128,1024]{1,0:T(8,128)(2,1)S(1)} %get-tuple-element.88), channel_id=1, source_target_pairs={{0,20},{4,16},{8,28},{12,24},{16,4},{20,0},{24,12},{28,8},{1,21},{... | collective-permute-start | bytes 786440 | tf_op jit(solution)/shard_map/ppermute | solution.py:323
  40.4 23.6 %collective-permute-start.31 = (bf16[128,1024]{1,0:T(8,128)(2,1)S(1)}, bf16[128,1024]{1,0:T(8,128)(2,1)S(1)}, u32[]{:S(2)}, u32[]{:S(2)}) collective-permute-start(bf16[128,1024]{1,0:T(8,128)(2,1)S(1)} %get-tuple-element.89), channel_id=1, source_target_pairs={{0,24},{4,28},{8,16},{12,20},{16,8},{20,12},{24,0},{28,4},{1,25},{... | collective-permute-start | bytes 786440 | tf_op jit(solution)/shard_map/ppermute | solution.py:323
  41.9 22.6 %collective-permute-start.32 = (bf16[128,1024]{1,0:T(8,128)(2,1)S(1)}, bf16[128,1024]{1,0:T(8,128)(2,1)S(1)}, u32[]{:S(2)}, u32[]{:S(2)}) collective-permute-start(bf16[128,1024]{1,0:T(8,128)(2,1)S(1)} %get-tuple-element.90), channel_id=1, source_target_pairs={{0,28},{4,24},{8,20},{12,16},{16,12},{20,8},{24,4},{28,0},{1,29},{... | collective-permute-start | bytes 786440 | tf_op jit(solution)/shard_map/ppermute | solution.py:323
  43.7 0.7 copy-start
  44.3 0.7 copy-start.4
  45.0 25.4 %copy-start.1 = (bf16[64,1024]{1,0:T(8,128)(2,1)}, bf16[64,1024]{1,0:T(8,128)(2,1)S(1)}, u32[]{:S(2)}) copy-start(bf16[64,1024]{1,0:T(8,128)(2,1)S(1)} %get-tuple-element.71) | copy-start | bytes 393220
  45.0 25.4 %copy-start.2 = (bf16[64,1024]{1,0:T(8,128)(2,1)}, bf16[64,1024]{1,0:T(8,128)(2,1)S(1)}, u32[]{:S(2)}) copy-start(bf16[64,1024]{1,0:T(8,128)(2,1)S(1)} %get-tuple-element.70) | copy-start | bytes 393220
  45.0 25.4 %copy-start.3 = (bf16[64,1024]{1,0:T(8,128)(2,1)}, bf16[64,1024]{1,0:T(8,128)(2,1)S(1)}, u32[]{:S(2)}) copy-start(bf16[64,1024]{1,0:T(8,128)(2,1)S(1)} %get-tuple-element.69) | copy-start | bytes 393220
  46.5 19.0 %collective-permute-start.10 = (bf16[64,1024]{1,0:T(8,128)(2,1)S(1)}, bf16[64,1024]{1,0:T(8,128)(2,1)S(1)}, u32[]{:S(2)}, u32[]{:S(2)}) collective-permute-start(bf16[64,1024]{1,0:T(8,128)(2,1)S(1)} %get-tuple-element.66), channel_id=1, source_target_pairs={{0,4},{4,0},{8,12},{12,8},{16,20},{20,16},{24,28},{28,24},{1,5},{5... | collective-permute-start | bytes 393224 | tf_op jit(solution)/shard_map/ppermute | solution.py:323
  58.9 8.1 %collective-permute-start.11 = (bf16[64,1024]{1,0:T(8,128)(2,1)S(1)}, bf16[64,1024]{1,0:T(8,128)(2,1)S(1)}, u32[]{:S(2)}, u32[]{:S(2)}) collective-permute-start(bf16[64,1024]{1,0:T(8,128)(2,1)S(1)} %get-tuple-element.67), channel_id=1, source_target_pairs={{0,8},{4,12},{8,0},{12,4},{16,24},{20,28},{24,16},{28,20},{1,9},{5... | collective-permute-start | bytes 393224 | tf_op jit(solution)/shard_map/ppermute | solution.py:323
  63.6 3.9 %collective-permute-start.2 = (bf16[64,1024]{1,0:T(8,128)(2,1)S(1)}, bf16[64,1024]{1,0:T(8,128)(2,1)S(1)}, u32[]{:S(2)}, u32[]{:S(2)}) collective-permute-start(bf16[64,1024]{1,0:T(8,128)(2,1)S(1)} %get-tuple-element.56), channel_id=1, source_target_pairs={{0,4},{4,0},{8,12},{12,8},{16,20},{20,16},{24,28},{28,24},{1,5},{5... | collective-permute-start | bytes 393224 | tf_op jit(solution)/shard_map/ppermute | solution.py:323
  64.0 6.4 %collective-permute-start.3 = (bf16[64,1024]{1,0:T(8,128)(2,1)S(1)}, bf16[64,1024]{1,0:T(8,128)(2,1)S(1)}, u32[]{:S(2)}, u32[]{:S(2)}) collective-permute-start(bf16[64,1024]{1,0:T(8,128)(2,1)S(1)} %get-tuple-element.57), channel_id=1, source_target_pairs={{0,8},{4,12},{8,0},{12,4},{16,24},{20,28},{24,16},{28,20},{1,9},{5... | collective-permute-start | bytes 393224 | tf_op jit(solution)/shard_map/ppermute | solution.py:323
  64.4 7.1 %collective-permute-start.4 = (bf16[64,1024]{1,0:T(8,128)(2,1)}, bf16[64,1024]{1,0:T(8,128)(2,1)S(1)}, u32[]{:S(2)}, u32[]{:S(2)}) collective-permute-start(bf16[64,1024]{1,0:T(8,128)(2,1)} %get-tuple-element.58), channel_id=1, source_target_pairs={{0,12},{4,8},{8,4},{12,0},{16,28},{20,24},{24,20},{28,16},{1,13},{... | collective-permute-start | bytes 393224 | tf_op jit(solution)/shard_map/ppermute | solution.py:323
  65.5 7.9 %collective-permute-start.5 = (bf16[64,1024]{1,0:T(8,128)(2,1)}, bf16[64,1024]{1,0:T(8,128)(2,1)S(1)}, u32[]{:S(2)}, u32[]{:S(2)}) collective-permute-start(bf16[64,1024]{1,0:T(8,128)(2,1)} %get-tuple-element.59), channel_id=1, source_target_pairs={{0,16},{4,20},{8,24},{12,28},{16,0},{20,4},{24,8},{28,12},{1,17},{... | collective-permute-start | bytes 393224 | tf_op jit(solution)/shard_map/ppermute | solution.py:323
  67.0 12.9 %collective-permute-start.6 = (bf16[64,1024]{1,0:T(8,128)(2,1)}, bf16[64,1024]{1,0:T(8,128)(2,1)S(1)}, u32[]{:S(2)}, u32[]{:S(2)}) collective-permute-start(bf16[64,1024]{1,0:T(8,128)(2,1)} %get-tuple-element.60), channel_id=1, source_target_pairs={{0,20},{4,16},{8,28},{12,24},{16,4},{20,0},{24,12},{28,8},{1,21},{... | collective-permute-start | bytes 393224 | tf_op jit(solution)/shard_map/ppermute | solution.py:323
  67.5 13.9 %collective-permute-start.7 = (bf16[64,1024]{1,0:T(8,128)(2,1)}, bf16[64,1024]{1,0:T(8,128)(2,1)S(1)}, u32[]{:S(2)}, u32[]{:S(2)}) collective-permute-start(bf16[64,1024]{1,0:T(8,128)(2,1)} %get-tuple-element.61), channel_id=1, source_target_pairs={{0,24},{4,28},{8,16},{12,20},{16,8},{20,12},{24,0},{28,4},{1,25},{... | collective-permute-start | bytes 393224 | tf_op jit(solution)/shard_map/ppermute | solution.py:323
  70.4 11.6 %collective-permute-start.8 = (bf16[64,1024]{1,0:T(8,128)(2,1)}, bf16[64,1024]{1,0:T(8,128)(2,1)S(1)}, u32[]{:S(2)}, u32[]{:S(2)}) collective-permute-start(bf16[64,1024]{1,0:T(8,128)(2,1)} %get-tuple-element.62), channel_id=1, source_target_pairs={{0,28},{4,24},{8,20},{12,16},{16,12},{20,8},{24,4},{28,0},{1,29},{... | collective-permute-start | bytes 393224 | tf_op jit(solution)/shard_map/ppermute | solution.py:323
  71.5 25.4 %collective-permute-start.12 = (bf16[64,1024]{1,0:T(8,128)(2,1)}, bf16[64,1024]{1,0:T(8,128)(2,1)S(1)}, u32[]{:S(2)}, u32[]{:S(2)}) collective-permute-start(bf16[64,1024]{1,0:T(8,128)(2,1)} %copy-done.4), channel_id=1, source_target_pairs={{0,12},{4,8},{8,4},{12,0},{16,28},{20,24},{24,20},{28,16},{1,13},{... | collective-permute-start | bytes 393224 | tf_op jit(solution)/shard_map/ppermute | solution.py:323
  73.3 24.4 %collective-permute-start.13 = (bf16[64,1024]{1,0:T(8,128)(2,1)}, bf16[64,1024]{1,0:T(8,128)(2,1)S(1)}, u32[]{:S(2)}, u32[]{:S(2)}) collective-permute-start(bf16[64,1024]{1,0:T(8,128)(2,1)} %copy-done.3), channel_id=1, source_target_pairs={{0,16},{4,20},{8,24},{12,28},{16,0},{20,4},{24,8},{28,12},{1,17},{... | collective-permute-start | bytes 393224 | tf_op jit(solution)/shard_map/ppermute | solution.py:323
  79.9 17.8 %collective-permute-start.14 = (bf16[64,1024]{1,0:T(8,128)(2,1)}, bf16[64,1024]{1,0:T(8,128)(2,1)S(1)}, u32[]{:S(2)}, u32[]{:S(2)}) collective-permute-start(bf16[64,1024]{1,0:T(8,128)(2,1)} %copy-done.2), channel_id=1, source_target_pairs={{0,20},{4,16},{8,28},{12,24},{16,4},{20,0},{24,12},{28,8},{1,21},{... | collective-permute-start | bytes 393224 | tf_op jit(solution)/shard_map/ppermute | solution.py:323
  81.5 16.3 %collective-permute-start.15 = (bf16[64,1024]{1,0:T(8,128)(2,1)}, bf16[64,1024]{1,0:T(8,128)(2,1)S(1)}, u32[]{:S(2)}, u32[]{:S(2)}) collective-permute-start(bf16[64,1024]{1,0:T(8,128)(2,1)} %copy-done.1), channel_id=1, source_target_pairs={{0,24},{4,28},{8,16},{12,20},{16,8},{20,12},{24,0},{28,4},{1,25},{... | collective-permute-start | bytes 393224 | tf_op jit(solution)/shard_map/ppermute | solution.py:323
  82.0 15.7 %collective-permute-start.16 = (bf16[64,1024]{1,0:T(8,128)(2,1)}, bf16[64,1024]{1,0:T(8,128)(2,1)S(1)}, u32[]{:S(2)}, u32[]{:S(2)}) collective-permute-start(bf16[64,1024]{1,0:T(8,128)(2,1)} %copy-done), channel_id=1, source_target_pairs={{0,28},{4,24},{8,20},{12,16},{16,12},{20,8},{24,4},{28,0},{1,29},{... | collective-permute-start | bytes 393224 | tf_op jit(solution)/shard_map/ppermute | solution.py:323
  96.9 15.6 %collective-permute-start.33 = (bf16[64,1024]{1,0:T(8,128)(2,1)S(1)}, bf16[64,1024]{1,0:T(8,128)(2,1)S(1)}, u32[]{:S(2)}, u32[]{:S(2)}) collective-permute-start(bf16[64,1024]{1,0:T(8,128)(2,1)S(1)} %get-tuple-element.92), channel_id=1, source_target_pairs={{0,4},{4,0},{8,12},{12,8},{16,20},{20,16},{24,28},{28,24},{1,5},{5... | collective-permute-start | bytes 393224 | tf_op jit(solution)/shard_map/ppermute | solution.py:323
  100.7 64.6 %collective-permute-start.42 = (bf16[512,1024]{1,0:T(8,128)(2,1)S(1)}, bf16[512,1024]{1,0:T(8,128)(2,1)S(1)}, u32[]{:S(2)}, u32[]{:S(2)}) collective-permute-start(bf16[512,1024]{1,0:T(8,128)(2,1)S(1)} %shard_map.114), channel_id=1, source_target_pairs={{0,1},{1,0},{2,3},{3,2},{4,5},{5,4},{6,7},{7,6},{8,9},{9,8},{10,11... | collective-permute-start | bytes 3145736 | tf_op jit(solution)/shard_map/ppermute | solution.py:329
  108.7 4.6 %collective-permute-start.17 = (bf16[64,1024]{1,0:T(8,128)(2,1)S(1)}, bf16[64,1024]{1,0:T(8,128)(2,1)S(1)}, u32[]{:S(2)}, u32[]{:S(2)}) collective-permute-start(bf16[64,1024]{1,0:T(8,128)(2,1)S(1)} %get-tuple-element.74), channel_id=1, source_target_pairs={{0,4},{4,0},{8,12},{12,8},{16,20},{20,16},{24,28},{28,24},{1,5},{5... | collective-permute-start | bytes 393224 | tf_op jit(solution)/shard_map/ppermute | solution.py:323
  108.8 5.9 %collective-permute-start.18 = (bf16[64,1024]{1,0:T(8,128)(2,1)S(1)}, bf16[64,1024]{1,0:T(8,128)(2,1)S(1)}, u32[]{:S(2)}, u32[]{:S(2)}) collective-permute-start(bf16[64,1024]{1,0:T(8,128)(2,1)S(1)} %get-tuple-element.75), channel_id=1, source_target_pairs={{0,8},{4,12},{8,0},{12,4},{16,24},{20,28},{24,16},{28,20},{1,9},{5... | collective-permute-start | bytes 393224 | tf_op jit(solution)/shard_map/ppermute | solution.py:323
  111.8 48.4 %collective-permute-start.41 = (bf16[512,768]{1,0:T(8,128)(2,1)S(1)}, bf16[512,768]{1,0:T(8,128)(2,1)S(1)}, u32[]{:S(2)}, u32[]{:S(2)}) collective-permute-start(bf16[512,768]{1,0:T(8,128)(2,1)S(1)} %shard_map.111), channel_id=1, source_target_pairs={{0,1},{1,0},{2,3},{3,2},{4,5},{5,4},{6,7},{7,6},{8,9},{9,8},{10,11... | collective-permute-start | bytes 2359304 | tf_op jit(solution)/shard_map/ppermute | solution.py:329
  112.5 5.7 %collective-permute-start.19 = (bf16[64,1024]{1,0:T(8,128)(2,1)S(1)}, bf16[64,1024]{1,0:T(8,128)(2,1)S(1)}, u32[]{:S(2)}, u32[]{:S(2)}) collective-permute-start(bf16[64,1024]{1,0:T(8,128)(2,1)S(1)} %get-tuple-element.76), channel_id=1, source_target_pairs={{0,12},{4,8},{8,4},{12,0},{16,28},{20,24},{24,20},{28,16},{1,13},{... | collective-permute-start | bytes 393224 | tf_op jit(solution)/shard_map/ppermute | solution.py:323
  113.4 6.4 %collective-permute-start.20 = (bf16[64,1024]{1,0:T(8,128)(2,1)S(1)}, bf16[64,1024]{1,0:T(8,128)(2,1)S(1)}, u32[]{:S(2)}, u32[]{:S(2)}) collective-permute-start(bf16[64,1024]{1,0:T(8,128)(2,1)S(1)} %get-tuple-element.77), channel_id=1, source_target_pairs={{0,16},{4,20},{8,24},{12,28},{16,0},{20,4},{24,8},{28,12},{1,17},{... | collective-permute-start | bytes 393224 | tf_op jit(solution)/shard_map/ppermute | solution.py:323
  114.7 11.2 %collective-permute-start.21 = (bf16[64,1024]{1,0:T(8,128)(2,1)S(1)}, bf16[64,1024]{1,0:T(8,128)(2,1)S(1)}, u32[]{:S(2)}, u32[]{:S(2)}) collective-permute-start(bf16[64,1024]{1,0:T(8,128)(2,1)S(1)} %get-tuple-element.78), channel_id=1, source_target_pairs={{0,20},{4,16},{8,28},{12,24},{16,4},{20,0},{24,12},{28,8},{1,21},{... | collective-permute-start | bytes 393224 | tf_op jit(solution)/shard_map/ppermute | solution.py:323
  118.2 7.7 %collective-permute-start.22 = (bf16[64,1024]{1,0:T(8,128)(2,1)S(1)}, bf16[64,1024]{1,0:T(8,128)(2,1)S(1)}, u32[]{:S(2)}, u32[]{:S(2)}) collective-permute-start(bf16[64,1024]{1,0:T(8,128)(2,1)S(1)} %get-tuple-element.79), channel_id=1, source_target_pairs={{0,24},{4,28},{8,16},{12,20},{16,8},{20,12},{24,0},{28,4},{1,25},{... | collective-permute-start | bytes 393224 | tf_op jit(solution)/shard_map/ppermute | solution.py:323
  119.7 9.6 %collective-permute-start.23 = (bf16[64,1024]{1,0:T(8,128)(2,1)S(1)}, bf16[64,1024]{1,0:T(8,128)(2,1)S(1)}, u32[]{:S(2)}, u32[]{:S(2)}) collective-permute-start(bf16[64,1024]{1,0:T(8,128)(2,1)S(1)} %get-tuple-element.80), channel_id=1, source_target_pairs={{0,28},{4,24},{8,20},{12,16},{16,12},{20,8},{24,4},{28,0},{1,29},{... | collective-permute-start | bytes 393224 | tf_op jit(solution)/shard_map/ppermute | solution.py:323
  125.9 5.3 %collective-permute-start.34 = (bf16[64,1024]{1,0:T(8,128)(2,1)S(1)}, bf16[64,1024]{1,0:T(8,128)(2,1)S(1)}, u32[]{:S(2)}, u32[]{:S(2)}) collective-permute-start(bf16[64,1024]{1,0:T(8,128)(2,1)S(1)} %get-tuple-element.93), channel_id=1, source_target_pairs={{0,8},{4,12},{8,0},{12,4},{16,24},{20,28},{24,16},{28,20},{1,9},{5... | collective-permute-start | bytes 393224 | tf_op jit(solution)/shard_map/ppermute | solution.py:323
  125.9 9.2 %collective-permute-start.35 = (bf16[64,1024]{1,0:T(8,128)(2,1)S(1)}, bf16[64,1024]{1,0:T(8,128)(2,1)S(1)}, u32[]{:S(2)}, u32[]{:S(2)}) collective-permute-start(bf16[64,1024]{1,0:T(8,128)(2,1)S(1)} %get-tuple-element.94), channel_id=1, source_target_pairs={{0,12},{4,8},{8,4},{12,0},{16,28},{20,24},{24,20},{28,16},{1,13},{... | collective-permute-start | bytes 393224 | tf_op jit(solution)/shard_map/ppermute | solution.py:323
  129.3 7.3 %collective-permute-start.36 = (bf16[64,1024]{1,0:T(8,128)(2,1)S(1)}, bf16[64,1024]{1,0:T(8,128)(2,1)S(1)}, u32[]{:S(2)}, u32[]{:S(2)}) collective-permute-start(bf16[64,1024]{1,0:T(8,128)(2,1)S(1)} %get-tuple-element.95), channel_id=1, source_target_pairs={{0,16},{4,20},{8,24},{12,28},{16,0},{20,4},{24,8},{28,12},{1,17},{... | collective-permute-start | bytes 393224 | tf_op jit(solution)/shard_map/ppermute | solution.py:323
  131.2 27.3 %collective-permute-start.24 = (bf16[192,1024]{1,0:T(8,128)(2,1)S(1)}, bf16[192,1024]{1,0:T(8,128)(2,1)S(1)}, u32[]{:S(2)}, u32[]{:S(2)}) collective-permute-start(bf16[192,1024]{1,0:T(8,128)(2,1)S(1)} %get-tuple-element.81), channel_id=1, source_target_pairs={{0,2},{1,3},{2,0},{3,1},{4,6},{5,7},{6,4},{7,5},{8,10},{9,11},{10,... | collective-permute-start | bytes 1179656 | tf_op jit(solution)/shard_map/ppermute | solution.py:319
  135.1 8.1 %collective-permute-start.37 = (bf16[64,1024]{1,0:T(8,128)(2,1)S(1)}, bf16[64,1024]{1,0:T(8,128)(2,1)S(1)}, u32[]{:S(2)}, u32[]{:S(2)}) collective-permute-start(bf16[64,1024]{1,0:T(8,128)(2,1)S(1)} %get-tuple-element.96), channel_id=1, source_target_pairs={{0,20},{4,16},{8,28},{12,24},{16,4},{20,0},{24,12},{28,8},{1,21},{... | collective-permute-start | bytes 393224 | tf_op jit(solution)/shard_map/ppermute | solution.py:323
  136.7 8.1 %collective-permute-start.38 = (bf16[64,1024]{1,0:T(8,128)(2,1)S(1)}, bf16[64,1024]{1,0:T(8,128)(2,1)S(1)}, u32[]{:S(2)}, u32[]{:S(2)}) collective-permute-start(bf16[64,1024]{1,0:T(8,128)(2,1)S(1)} %get-tuple-element.97), channel_id=1, source_target_pairs={{0,24},{4,28},{8,16},{12,20},{16,8},{20,12},{24,0},{28,4},{1,25},{... | collective-permute-start | bytes 393224 | tf_op jit(solution)/shard_map/ppermute | solution.py:323
  143.2 20.3 %collective-permute-start.40 = (bf16[512,256]{1,0:T(8,128)(2,1)S(1)}, bf16[512,256]{1,0:T(8,128)(2,1)S(1)}, u32[]{:S(2)}, u32[]{:S(2)}) collective-permute-start(bf16[512,256]{1,0:T(8,128)(2,1)S(1)} %shard_map.110), channel_id=1, source_target_pairs={{0,1},{1,0},{2,3},{3,2},{4,5},{5,4},{6,7},{7,6},{8,9},{9,8},{10,11... | collective-permute-start | bytes 786440 | tf_op jit(solution)/shard_map/ppermute | solution.py:329
  144.8 6.4 %collective-permute-start.39 = (bf16[64,1024]{1,0:T(8,128)(2,1)S(1)}, bf16[64,1024]{1,0:T(8,128)(2,1)S(1)}, u32[]{:S(2)}, u32[]{:S(2)}) collective-permute-start(bf16[64,1024]{1,0:T(8,128)(2,1)S(1)} %get-tuple-element.98), channel_id=1, source_target_pairs={{0,28},{4,24},{8,20},{12,16},{16,12},{20,8},{24,4},{28,0},{1,29},{... | collective-permute-start | bytes 393224 | tf_op jit(solution)/shard_map/ppermute | solution.py:323
  151.1 7.4 %collective-permute-start.25 = (f32[8,192]{1,0:T(8,128)S(1)}, f32[8,192]{1,0:T(8,128)S(1)}, u32[]{:S(2)}, u32[]{:S(2)}) collective-permute-start(f32[8,192]{1,0:T(8,128)S(1)} %get-tuple-element.82), channel_id=1, source_target_pairs={{0,2},{1,3},{2,0},{3,1},{4,6},{5,7},{6,4},{7,5},{8,10},{9,11},{10,... | collective-permute-start | bytes 18440 | tf_op jit(solution)/shard_map/ppermute | solution.py:319

commit v2 on v1

v2 whole, which is shorter than its diff:
```python
import functools

import jax
import jax.numpy as jnp
from jax import lax
from jax.experimental import pallas as pl
from jax.experimental.pallas import tpu as pltpu
from jax.sharding import PartitionSpec as P


root_coef = 0.7978845608
cube_coef = 0.044715
bf16 = jnp.bfloat16
f32 = jnp.float32

NN = (((1,), (0,)), ((), ()))
NT = (((1,), (1,)), ((), ()))
TN = (((0,), (0,)), ((), ()))


def dot(a, b, dims=NN):
    return lax.dot_general(a, b, dims, preferred_element_type=f32)


def gelu_slope(hidden):
    square = hidden * hidden
    tanh_val = jnp.tanh(hidden * (root_coef + (root_coef * cube_coef) * square))
    half_up = 0.5 + 0.5 * tanh_val
    active = hidden * half_up
    derivative = half_up + active * (1.0 - half_up) * (
        2.0 * root_coef + (6.0 * root_coef * cube_coef) * square
    )
    return active, derivative


def steps(extent, most):
    size = min(extent, most)
    return [(at, size) for at in range(0, extent, size)]


def stack(refs, experts):
    runs = [
        jnp.concatenate([ref[...] for ref in refs[at : at + experts]], axis=0)
        for at in range(0, len(refs), experts)
    ]
    return runs[0] if len(runs) == 1 else jnp.concatenate(runs, axis=1)


def slot_rows(routes, keep, combine, me, experts, block, capacity):
    count = routes.shape[1]
    kept = keep > 0
    first, second = routes[0:1, :] ^ me, routes[1:2, :] ^ me
    ids = lax.broadcasted_iota(jnp.int32, (experts, count), 0)
    first_hot = jnp.where(first == ids, 1.0, 0.0)
    second_hot = jnp.where((second == ids) & kept, 1.0, 0.0)
    earlier = jnp.where(
        lax.broadcasted_iota(jnp.int32, (count, count), 0)
        < lax.broadcasted_iota(jnp.int32, (count, count), 1),
        1.0,
        0.0,
    ).astype(bf16)
    first_pos = dot(first_hot.astype(bf16), earlier)
    second_pos = dot(second_hot.astype(bf16), earlier) + jnp.sum(first_hot, axis=1, keepdims=True)
    first_slot = jnp.sum(first_pos * first_hot, axis=0, keepdims=True)
    second_slot = jnp.sum(second_pos * second_hot, axis=0, keepdims=True)
    first_flat = jnp.where(first_slot < capacity, first.astype(f32) * block + first_slot, -1.0)
    second_flat = jnp.where(
        kept & (second_slot < capacity), second.astype(f32) * block + second_slot, -1.0
    )
    weights = combine.astype(f32)
    return first_flat, second_flat, weights[0:1, :], weights[1:2, :]


def picks(first_flat, second_flat, rows):
    ids = lax.broadcasted_iota(jnp.int32, (rows, first_flat.shape[1]), 0)
    return ids == first_flat.astype(jnp.int32), ids == second_flat.astype(jnp.int32)


def place(pick, source, out_refs, block, left=0):
    for at, size in steps(source.shape[1], 256):
        rows = dot(pick, source[:, at : at + size]).astype(bf16)
        for k, out in enumerate(out_refs):
            out[:, left + at : left + at + size] = rows[k * block : (k + 1) * block]


def own_send_kernel(experts, block, capacity, routes, keep, combine, tokens, grad_out, meta, *outs):
    me = lax.axis_index("expert")
    a, b, c, d = slot_rows(routes[...], keep[...], combine[...], me, experts, block, capacity)
    meta[0:1, :] = a
    meta[1:2, :] = b
    meta[2:3, :] = c
    meta[3:4, :] = d
    meta[4:8, :] = jnp.zeros((4, a.shape[1]), f32)
    first, second = picks(a, b, experts * block)
    place(jnp.where(first | second, 1.0, 0.0).astype(bf16), tokens, outs, block)
    weighted = jnp.where(first, c, jnp.where(second, d, 0.0)).astype(bf16)
    place(weighted, grad_out, outs, block, tokens.shape[1])


def load_kernel(pos, w_in, w_out, in_half, out_half):
    in_half[...] = w_in[0]
    out_half[...] = w_out[0]


def send_x_kernel(experts, block, meta, tokens, *outs):
    first, second = picks(meta[0:1, :], meta[1:2, :], experts * block)
    place(jnp.where(first | second, 1.0, 0.0).astype(bf16), tokens, outs, block)


def send_s_kernel(experts, block, meta, grad_out, *outs):
    first, second = picks(meta[0:1, :], meta[1:2, :], experts * block)
    weighted = jnp.where(first, meta[2:3, :], jnp.where(second, meta[3:4, :], 0.0))
    place(weighted.astype(bf16), grad_out, outs, block)


def add_tokens(grad, w_in, total, gates, outs, block, capacity):
    step, last = pl.program_id(0), pl.num_programs(0) - 1
    more = dot(grad, w_in, TN)

    @pl.when(step == 0)
    def _():
        total[...] = more

    @pl.when((step > 0) & (step < last))
    def _():
        total[...] += more

    @pl.when(step == last)
    def _():
        rows = (total[...] + more).astype(bf16)
        gate_rows = gates[0:1, :].astype(bf16)
        for k, out in enumerate(outs):
            out[...] = rows[k * block : (k + 1) * block]
            out[capacity : capacity + 1, 0:block] = gate_rows[:, k * block : (k + 1) * block]


def add_gates(active, up, gates):
    more = jnp.sum(active.astype(f32) * up, axis=0, keepdims=True)

    @pl.when(pl.program_id(0) == 0)
    def _():
        gates[0:1, :] = more

    @pl.when(pl.program_id(0) > 0)
    def _():
        gates[0:1, :] += more


def act_kernel(experts, w_in, *refs):
    blocks, (act, slope) = refs[:-2], refs[-2:]
    active, derivative = gelu_slope(dot(w_in[...], stack(blocks, experts), NT))
    act[...] = active.astype(bf16)
    slope[...] = derivative.astype(bf16)


def grad_kernel(experts, block, capacity, w_in, w_out, act, slope, *refs):
    (total, gates), outs = refs[-2:], refs[-2 - experts : -2]
    grad, blocks = refs[-3 - experts], refs[: -3 - experts]
    up = dot(w_out[...], stack(blocks, experts), NT)
    add_gates(act[...], up, gates)
    hidden_grad = (up * slope[...].astype(f32)).astype(bf16)
    grad[...] = hidden_grad
    add_tokens(hidden_grad, w_in[...], total, gates, outs, block, capacity)


def outer_rows(own_ref, other_ref, own_rows, other_rows, at, size):
    return dot(own_ref[pl.ds(at, size), :], own_rows) + dot(other_ref[pl.ds(at, size), :], other_rows)


def away_kernel(experts, owners, pos, own, other, *refs):
    own_blocks, other_blocks, outs = refs[:experts], refs[experts : 2 * experts], refs[2 * experts :]
    own_rows, other_rows = stack(own_blocks, experts), stack(other_blocks, experts)
    size = own.shape[0] // owners
    for r, out in enumerate(outs):
        at = pl.multiple_of(lax.rem(pos[1] + r + 1, owners) * size, size)
        out[...] = outer_rows(own, other, own_rows, other_rows, at, size).astype(bf16)


def home_kernel(experts, owners, pos, own, other, *refs):
    own_blocks, other_blocks = refs[:experts], refs[experts : 2 * experts]
    got, out = refs[2 * experts : 2 * experts + owners - 1], refs[-1]
    size = own.shape[0] // owners
    at = pl.multiple_of(pos[1] * size, size)
    total = outer_rows(
        own, other, stack(own_blocks, experts), stack(other_blocks, experts), at, size
    )
    for ref in got:
        total = total + ref[...].astype(f32)
    out[0] = total


def before_kernel(experts, owners, pos, own, other, *refs):
    own_blocks, other_blocks, out = refs[:experts], refs[experts : 2 * experts], refs[-1]
    size = own.shape[0] // owners
    at = pl.multiple_of(pos[1] * size, size)
    out[...] = outer_rows(
        own, other, stack(own_blocks, experts), stack(other_blocks, experts), at, size
    )


def after_kernel(owners, before, *refs):
    total = before[...]
    for ref in refs[: owners - 1]:
        total = total + ref[...].astype(f32)
    refs[-1][0] = total


def gathered(meta, refs, experts, block):
    first, second = picks(meta[0:1, :], meta[1:2, :], experts * block)
    chosen = jnp.where(first | second, 1.0, 0.0).astype(bf16)
    return dot(chosen, stack(refs, experts), TN)


def gate_rows(meta, refs, block, capacity):
    values = jnp.concatenate([ref[capacity : capacity + 1, 0:block] for ref in refs], axis=0)
    out = []
    for at in (0, 1):
        flat = meta[at : at + 1, :].astype(jnp.int32)
        live = flat >= 0
        which = jnp.where(live, flat, 0) // block
        where = flat - which * block
        lane = lax.broadcasted_iota(jnp.int32, (block, flat.shape[1]), 0)
        hit = jnp.where((lane == where) & live, 1.0, 0.0).astype(bf16)
        by_block = dot(values, hit)
        mine = lax.broadcasted_iota(jnp.int32, by_block.shape, 0) == which
        gate = jnp.sum(jnp.where(mine, by_block, 0.0), axis=0, keepdims=True)
        out.append(jnp.where(live, gate / meta[at + 2 : at + 3, :], 0.0))
    return out


def collect_kernel(experts, block, capacity, meta, *refs):
    blocks, (out, gates) = refs[:experts], refs[experts:]
    out[...] = gathered(meta, blocks, experts, block).astype(out.dtype)

    @pl.when(pl.program_id(0) == 0)
    def _():
        first, second = gate_rows(meta, blocks, block, capacity)
        gates[0:1, :] = first
        gates[1:2, :] = second
        gates[2:8, :] = jnp.zeros((6, first.shape[1]), f32)


def join_kernel(own, own_gates, got, got_gates, grad_tokens, grad_combine):
    grad_tokens[...] = (own[...] + got[...].astype(f32)).astype(bf16)
    grad_combine[...] = (own_gates[0:2, :] + got_gates[0:2, :]).astype(bf16)


def shaped(shape, dtype=bf16):
    return jax.ShapeDtypeStruct(shape, dtype)


def full(array):
    return pl.BlockSpec(array.shape, lambda g, *pos, rank=array.ndim: (0,) * rank)


def columns(array, parts, first=0):
    size = array.shape[-1] // parts
    lead = array.shape[:-1]
    return pl.BlockSpec(
        lead + (size,), lambda g, *pos, rank=array.ndim: (0,) * (rank - 1) + (first + g,)
    )


def rows(array, size):
    return pl.BlockSpec((size, array.shape[1]), lambda g, *pos: (g, 0))


def half_rows(array, parts):
    size = array.shape[1] // 2 // parts
    return pl.BlockSpec((1, size, array.shape[2]), lambda g, pos: (0, pos[0] * parts + g, 0))


def call(kernel, grid, scalars, operands, results, scratch=(), flops=0, alias=None):
    arrays, in_specs = [a for a, _ in operands], [s for _, s in operands]
    outs, out_specs = [a for a, _ in results], [s for _, s in results]
    moved = sum(a.size * a.dtype.itemsize for a in arrays + outs)
    return pl.pallas_call(
        kernel,
        out_shape=outs,
        grid_spec=pltpu.PrefetchScalarGridSpec(
            num_scalar_prefetch=len(scalars),
            grid=(grid,),
            in_specs=in_specs,
            out_specs=out_specs,
            scratch_shapes=list(scratch),
        ),
        input_output_aliases=alias or {},
        compiler_params=pltpu.CompilerParams(vmem_limit_bytes=28 << 20),
        cost_estimate=pl.CostEstimate(flops=int(flops), transcendentals=0, bytes_accessed=moved),
    )(*scalars, *arrays)


def window(arrays, start, size):
    return [
        (a, pl.BlockSpec((a.shape[0], size), lambda g, *pos: (0, start // size))) for a in arrays
    ]


def runs_of(arrays, start, run):
    return [
        (a, pl.BlockSpec((a.shape[0], run), lambda g, *pos: (0, start // run + g))) for a in arrays
    ]


def per_device(tokens, grad_out, routes, keep_second, combine, w_in, w_out):
    experts, planes = lax.axis_size("expert"), lax.axis_size("dp")
    count, width = tokens.shape
    capacity = 5 * count // (2 * experts)
    block = -(-(capacity + 1) // 16) * 16
    owners = planes // 2
    units = w_in.shape[1] // 2
    share = units // owners
    slots = experts * block
    if planes % 2 or experts & (experts - 1):
        raise ValueError("mesh sizes")
    plane = lax.axis_index("dp")
    pos = jnp.stack([plane // owners, plane % owners]).astype(jnp.int32)
    bind = functools.partial

    def across(value):
        return lax.ppermute(value, "dp", [(j, (j + owners) % planes) for j in range(planes)])

    def exchange(values):
        return [values[0]] + [
            lax.ppermute(values[k], "expert", [(i, i ^ k) for i in range(experts)])
            for k in range(1, experts)
        ]

    def to_owners(values):
        return [
            lax.ppermute(
                value,
                "dp",
                [(j, j // owners * owners + (j + r + 1) % owners) for j in range(planes)],
            )
            for r, value in enumerate(values)
        ]

    def each(arrays, spec, *more):
        return [(a, spec(a, *more)) for a in arrays]

    routes_t, keep_t, combine_t = routes.T, keep_second.reshape(1, count), combine.T

    def stay(array):
        return pltpu.with_memory_space_constraint(array, pltpu.HBM)

    other_x = across(tokens)
    half = width // 2
    other_dya = across(grad_out[:, :half])
    other_dyb = across(grad_out[:, half:])

    def blocks(columns_of):
        return [shaped((block, columns_of))] * experts

    act_shape = shaped((units, slots))
    unit_parts = max(units // 256, 1)
    unit_rows = units // unit_parts
    sums = [pltpu.VMEM((slots, width), f32), pltpu.VMEM((8, slots), f32)]
    meta_shape = shaped((8, count), f32)
    meta, *own_xs = call(
        bind(own_send_kernel, experts, block, capacity),
        1,
        [],
        each([stay(a) for a in (routes_t, keep_t, combine_t, tokens, grad_out)], full),
        each([meta_shape] + blocks(2 * width), full),
        flops=4 * slots * count * width,
    )
    own_xs = exchange(own_xs)
    half_in, half_out = call(
        load_kernel,
        4,
        [pos],
        each([stay(w_in), stay(w_out)], half_rows, 4),
        each([shaped((units, width))] * 2, rows, units // 4),
    )
    other_meta = across(meta)
    other_xb = call(
        bind(send_x_kernel, experts, block),
        2,
        [],
        each([other_meta], full) + each([other_x], columns, 2),
        each(blocks(width), columns, 2),
        flops=2 * slots * count * width,
    )
    x_out = exchange(other_xb)
    sent = []
    for values in (other_dya, other_dyb):
        out = call(
            bind(send_s_kernel, experts, block),
            1,
            [],
            each([other_meta, values], full),
            each(blocks(half), full),
            flops=slots * count * width,
        )
        sent.append(exchange(out))
    own_x, other_x = (own_xs, 0), (x_out, 0)
    own_sa, other_sa = (own_xs, width), (sent[0], 0)
    own_sb, other_sb = (own_xs, width + half), (sent[1], 0)

    def act(x):
        return call(
            bind(act_kernel, experts),
            unit_parts,
            [],
            each([half_in], rows, unit_rows) + window(*x, width),
            each([act_shape] * 2, rows, unit_rows),
            flops=2 * slots * units * width,
        )

    def grad(acts, sa, sb):
        result, *back = call(
            bind(grad_kernel, experts, block, capacity),
            unit_parts,
            [],
            each([half_in, half_out], rows, unit_rows)
            + each(acts, rows, unit_rows)
            + window(*sa, half)
            + window(*sb, half),
            each([act_shape], rows, unit_rows) + each(blocks(width), full),
            sums,
            4 * slots * units * width,
        )
        return result, back

    own_act, own_slope = act(own_x)
    other_act, other_slope = act(other_x)
    run = width // 4
    fed = slots * share * run

    def away(acts, left, right, first, many):
        return call(
            bind(away_kernel, experts, owners),
            many,
            [pos],
            each(acts, full)
            + runs_of(left[0], left[1] + first * run, run)
            + runs_of(right[0], right[1] + first * run, run),
            each([shaped((share, many * run))] * (owners - 1), columns, many),
            flops=4 * fed * (owners - 1) * many,
        )

    goal = shaped((1, share, width), f32)

    def into(array, operands, prefetched):
        if array is None:
            return operands, None
        return operands + [(array, pl.BlockSpec(memory_space=pl.ANY))], {
            len(operands) + prefetched: 0
        }

    def home(acts, left, right, got, first, many, array=None):
        operands, alias = into(
            array,
            each(acts, full)
            + runs_of(*left, run)
            + runs_of(*right, run)
            + each(got, columns, many),
            1,
        )
        return call(
            bind(home_kernel, experts, owners),
            many,
            [pos],
            operands,
            each([goal], columns, 4, first),
            flops=4 * fed * many,
            alias=alias,
        )[0]

    def after(before, got, first, many, array=None):
        operands, alias = into(
            array, runs_of([before], first * run, run) + each(got, columns, many), 0
        )
        return call(
            bind(after_kernel, owners),
            many,
            [],
            operands,
            each([goal], columns, 4, first),
            alias=alias,
        )[0]

    out_acts = [own_act, other_act]
    away_oa = away(out_acts, own_sa, other_sa, 0, 2)
    got_oa = to_owners(away_oa)
    away_ob = away(out_acts, own_sb, other_sb, 0, 2)
    got_ob = to_owners(away_ob)
    other_grad, other_back = grad([other_act, other_slope], other_sa, other_sb)
    other_back = exchange(other_back)
    own_grad, own_back = grad([own_act, own_slope], own_sa, own_sb)
    in_acts = [own_grad, other_grad]
    away_a = away(in_acts, own_x, other_x, 0, 3)
    got_a = to_owners(away_a)
    away_b = away(in_acts, own_x, other_x, 3, 1)
    got_b = to_owners(away_b)
    own_back = exchange(own_back)

    def collect(rows_of, back, kind):
        return call(
            bind(collect_kernel, experts, block, capacity),
            2,
            [],
            each([rows_of], full) + each(back, columns, 2),
            each([shaped((count, width), kind)], columns, 2) + each([meta_shape], full),
            flops=2 * slots * count * width,
        )

    other_part, other_gates = collect(other_meta, other_back, bf16)
    part = across(other_part)
    part_gates = across(other_gates)
    grad_outw = home(out_acts, own_sa, other_sa, got_oa, 0, 2)
    grad_outw = home(out_acts, own_sb, other_sb, got_ob, 2, 2, grad_outw)
    own_part, own_gates = collect(meta, own_back, f32)
    before = call(
        bind(before_kernel, experts, owners),
        4,
        [pos],
        each(in_acts, full) + runs_of(*own_x, run) + runs_of(*other_x, run),
        each([shaped((share, width), f32)], columns, 4),
        flops=16 * fed,
    )[0]
    grad_tokens, grad_combine = call(
        join_kernel,
        1,
        [],
        each([own_part, own_gates, part, part_gates], full),
        each([shaped((count, width)), shaped((2, count))], full),
    )
    grad_in = after(before, got_a, 0, 3)
    grad_in = after(before, got_b, 3, 1, grad_in)
    return grad_tokens, grad_combine.T, grad_in, grad_outw


def solution(mesh):
    return jax.shard_map(
        per_device,
        mesh=mesh,
        in_specs=(
            P(("expert", "dp"), None),
            P(("expert", "dp"), None),
            P(("expert", "dp"), None),
            P(("expert", "dp")),
            P(("expert", "dp"), None),
            P("expert", None, None),
            P("expert", None, None),
        ),
        out_specs=(
            P(("expert", "dp"), None),
            P(("expert", "dp"), None),
            P("expert", "dp", None),
            P("expert", "dp", None),
        ),
        check_vma=False,
    )
```

time: 170 us -> 174 us (1.024)
  the two profiles are of different devices: /device:TPU:8 before, /device:TPU:2 now
where the time goes in v2:
time: 174 us; the launch traced here: 172 us
  waiting for transfers between devices  70.2 us (40%)
  starting transfers between devices  55.1 us (32%)
  Pallas kernels  43 us (25%)
  local copies, waits for them, and re-layouts  2.98 us (2%)
    pallas_call x21, Pallas kernels, call(): pl.pallas_call(kernel, out_shape=outs, grid_spec=pltpu.PrefetchScalarGrid...  43 us
    ppermute x6, waiting for transfers between devices, across(): lax.ppermute(value, 'dp', [(j, (j + owners) % planes) for j in range(plan...  41.9 us
    ppermute x42, starting transfers between devices, exchange(): lax.ppermute(values[k], 'expert', [(i, i ^ k) for i in range(experts)])  41.2 us
    ppermute x42, waiting for transfers between devices, exchange(): lax.ppermute(values[k], 'expert', [(i, i ^ k) for i in range(experts)])  28.4 us
    ppermute x6, starting transfers between devices, across(): lax.ppermute(value, 'dp', [(j, (j + owners) % planes) for j in range(plan...  9.07 us
    ppermute x4, starting transfers between devices, to_owners(): lax.ppermute(value, 'dp', [(j, j // owners * owners + (j + r + 1) % owner...  4.84 us
  transfers between devices with their start and end apart: 52, of which 11 were waited for; matrix products, arithmetic and copies ran while one was open for 0% of the time, Pallas kernels for 24%

profile of v2, /device:TPU:2, one launch (start us, length us, event | category | flops | bytes accessed | tf_op | source)
XLA Modules:
  0.0 172.2 jit_solution(8289940966769317765)
XLA Ops:
  0.6 1.1 fusion
  1.7 2.7 %collective-permute-start.31 = (bf16[192,512]{1,0:T(8,128)(2,1)S(1)}, bf16[192,512]{1,0:T(8,128)(2,1)S(1)}, u32[]{:S(2)}, u32[]{:S(2)}) collective-permute-start(bf16[192,512]{1,0:T(8,128)(2,1)S(1)} %get-tuple-element.130), channel_id=1, source_target_pairs={{0,2},{1,3},{2,0},{3,1},{4,6},{5,7},{6,4},{7,5},{8,10},{9,11},{10,... | collective-permute-start | bytes 589832 | tf_op jit(solution)/shard_map/ppermute | solution.py:321
  4.4 2.1 %shard_map.102 = (f32[8,192]{1,0:T(8,128)S(1)}, bf16[64,2048]{1,0:T(8,128)(2,1)S(1)}, bf16[64,2048]{1,0:T(8,128)(2,1)S(1)}, bf16[64,2048]{1,0:T(8,128)(2,1)S(1)}...) custom-call(s32[2,192]{1,0:T(2,128)} %bitcast.6, ...), custom_call_target="tpu_custom_call" | custom-call | flops 402653184 | bytes 2892800 | tf_op jit(solution)/shard_map/pallas_call | solution.py:277
  7.3 1.2 collective-permute-start.2
  8.5 5.4 %collective-permute-done.14.meta = f32[8,192]{1,0:T(8,128)S(1)} collective-permute-done((f32[8,192]{1,0:T(8,128)S(1)}, f32[8,192]{1,0:T(8,128)S(1)}, u32[]{:S(2)}, u32[]{:S(2)}) %collective-permute-start.14) | collective-permute-done | bytes 6176 | tf_op jit(solution)/shard_map/ppermute | solution.py:321
  13.9 2.9 %collective-permute-start.15 = (bf16[192,1024]{1,0:T(8,128)(2,1)S(1)}, bf16[192,1024]{1,0:T(8,128)(2,1)S(1)}, u32[]{:S(2)}, u32[]{:S(2)}) collective-permute-start(bf16[192,1024]{1,0:T(8,128)(2,1)S(1)} %copy-done.3), channel_id=1, source_target_pairs={{0,2},{1,3},{2,0},{3,1},{4,6},{5,7},{6,4},{7,5},{8,10},{9,11},{10,... | collective-permute-start | bytes 1179656 | tf_op jit(solution)/shard_map/ppermute | solution.py:321
  16.8 18.4 %collective-permute-done.23.grad_out = bf16[192,512]{1,0:T(8,128)(2,1)S(1)} collective-permute-done((bf16[192,512]{1,0:T(8,128)(2,1)S(1)}, bf16[192,512]{1,0:T(8,128)(2,1)S(1)}, u32[]{:S(2)}, u32[]{:S(2)}) %collective-permute-start.23) | collective-permute-done | bytes 196640 | tf_op jit(solution)/shard_map/ppermute | solution.py:321
  35.2 1.5 collective-permute-start.3
  37.2 2.4 %collective-permute-start.6 = (bf16[64,2048]{1,0:T(8,128)(2,1)S(1)}, bf16[64,2048]{1,0:T(8,128)(2,1)S(1)}, u32[]{:S(2)}, u32[]{:S(2)}) collective-permute-start(bf16[64,2048]{1,0:T(8,128)(2,1)S(1)} %get-tuple-element.77), channel_id=1, source_target_pairs={{0,28},{4,24},{8,20},{12,16},{16,12},{20,8},{24,4},{28,0},{1,29},{... | collective-permute-start | bytes 786440 | tf_op jit(solution)/shard_map/ppermute | solution.py:325
  39.6 0.9 shard_map.110
  40.5 0.6 copy-done
  41.7 0.6 copy-done.2
  42.4 12.3 %collective-permute-done.3.refs_4_.refs_12_ = bf16[64,2048]{1,0:T(8,128)(2,1)S(1)} collective-permute-done((bf16[64,2048]{1,0:T(8,128)(2,1)S(1)}, bf16[64,2048]{1,0:T(8,128)(2,1)S(1)}, u32[]{:S(2)}, u32[]{:S(2)}) %collective-permute-start.3) | collective-permute-done | bytes 262176 | tf_op jit(solution)/shard_map/ppermute | solution.py:325
  54.7 2.7 %collective-permute-done.4.refs_5_.refs_13_ = bf16[64,2048]{1,0:T(8,128)(2,1)S(1)} collective-permute-done((bf16[64,2048]{1,0:T(8,128)(2,1)S(1)}, bf16[64,2048]{1,0:T(8,128)(2,1)S(1)}, u32[]{:S(2)}, u32[]{:S(2)}) %collective-permute-start.4) | collective-permute-done | bytes 262176 | tf_op jit(solution)/shard_map/ppermute | solution.py:325
  57.9 1.7 collective-permute-start.34
  59.6 0.8 shard_map.107
  60.4 1.5 collective-permute-start.35
  61.9 1.2 collective-permute-start.37
  63.8 1.5 collective-permute-start.17
  65.3 3.5 %shard_map.103 = (bf16[1024,1024]{1,0:T(8,128)(2,1)S(1)}, bf16[1024,1024]{1,0:T(8,128)(2,1)S(1)}) custom-call(s32[2]{0:T(128)S(1)} %pad_add_fusion.pos, bf16[1,2048,1024]{2,1,0:T(8,128)(2,1)} %w_in.1, bf16[1,2048,1024]{2,1,0:T(8,128)(2,1)} %w_out.1), custom_call_target="tpu_custom_call" | custom-call | bytes 12582912 | tf_op jit(solution)/shard_map/pallas_call | solution.py:277
  69.4 0.7 collective-permute-start.24
  70.1 1.3 collective-permute-start.25
  71.4 2.9 %shard_map.104 = (bf16[1024,512]{1,0:T(8,128)(2,1)S(1)}, bf16[1024,512]{1,0:T(8,128)(2,1)S(1)}) custom-call(bf16[1024,1024]{1,0:T(8,128)(2,1)S(1)} %get-tuple-element.68.w_in, bf16[64,2048]{1,0:T(8,128)(2,1)S(1)} %get-tuple-element.70.refs_0_.refs_8_, bf16[64,2048]{1,0:T(8,128)(2,1)S(1)} %collective-permute-done.refs_1_.refs_9_, ...), custom_call_target="tpu_custom_call" | custom-call | flops 1073741824 | bytes 6291456 | tf_op jit(solution)/shard_map/pallas_call | solution.py:277
  74.7 1.2 collective-permute-start.19
  75.9 0.7 collective-permute-start.20
  76.6 2.2 %collective-permute-start.21 = (bf16[64,1024]{1,0:T(8,128)(2,1)S(1)}, bf16[64,1024]{1,0:T(8,128)(2,1)S(1)}, u32[]{:S(2)}, u32[]{:S(2)}) collective-permute-start(bf16[64,1024]{1,0:T(8,128)(2,1)S(1)} %get-tuple-element.96), channel_id=1, source_target_pairs={{0,24},{4,28},{8,16},{12,20},{16,8},{20,12},{24,0},{28,4},{1,25},{... | collective-permute-start | bytes 393224 | tf_op jit(solution)/shard_map/ppermute | solution.py:325
  79.1 5.0 %shard_map.105 = (bf16[1024,512]{1,0:T(8,128)(2,1)S(1)}, bf16[64,1024]{1,0:T(8,128)(2,1)S(1)}, bf16[64,1024]{1,0:T(8,128)(2,1)S(1)}, bf16[64,1024]{1,0:T(8,128)(...) custom-call(bf16[1024,1024]{1,0:T(8,128)(2,1)S(1)} %get-tuple-elemen, ...), custom_call_target="tpu_custom_call" | custom-call | flops 2147483648 | bytes 12582912 | tf_op jit(solution)/shard_map/pallas_call | solution.py:277
  84.2 1.6 collective-permute-start.26
  85.8 2.1 %collective-permute-start.27 = (bf16[64,512]{1,0:T(8,128)(2,1)S(1)}, bf16[64,512]{1,0:T(8,128)(2,1)S(1)}, u32[]{:S(2)}, u32[]{:S(2)}) collective-permute-start(bf16[64,512]{1,0:T(8,128)(2,1)S(1)} %get-tuple-element.104), channel_id=1, source_target_pairs={{0,16},{4,20},{8,24},{12,28},{16,0},{20,4},{24,8},{28,12},{1,17},{... | collective-permute-start | bytes 196616 | tf_op jit(solution)/shard_map/ppermute | solution.py:325
  87.9 0.7 collective-permute-done.20.refs_5_.refs_13_
  88.5 1.6 collective-permute-start.28
  90.1 1.8 %collective-permute-start.29 = (bf16[64,512]{1,0:T(8,128)(2,1)S(1)}, bf16[64,512]{1,0:T(8,128)(2,1)S(1)}, u32[]{:S(2)}, u32[]{:S(2)}) collective-permute-start(bf16[64,512]{1,0:T(8,128)(2,1)S(1)} %get-tuple-element.106), channel_id=1, source_target_pairs={{0,24},{4,28},{8,16},{12,20},{16,8},{20,12},{24,0},{28,4},{1,25},{... | collective-permute-start | bytes 196616 | tf_op jit(solution)/shard_map/ppermute | solution.py:325
  92.2 2.7 %shard_map.108 = (bf16[1024,512]{1,0:T(8,128)(2,1)S(1)}, bf16[1024,512]{1,0:T(8,128)(2,1)S(1)}) custom-call(bf16[1024,1024]{1,0:T(8,128)(2,1)S(1)} %get-tuple-element.68.w_in, bf16[64,1024]{1,0:T(8,128)(2,1)S(1)} %get-tuple-element.90.refs_0_.refs_8_, bf16[64,1024]{1,0:T(8,128)(2,1)S(1)} %collective-permute-done.16.refs_1_.refs_9_, ...), custom_call_target="tpu_custom_call" | custom-call | flops 1073741824 | bytes 5242880 | tf_op jit(solution)/shard_map/pallas_call | solution.py:277
  95.0 1.0 collective-permute-start.7
  96.0 1.3 collective-permute-start.8
  97.4 1.0 collective-permute-start.10
  98.4 4.8 %shard_map.111 = (bf16[1024,512]{1,0:T(8,128)(2,1)S(1)}, bf16[64,1024]{1,0:T(8,128)(2,1)S(1)}, bf16[64,1024]{1,0:T(8,128)(2,1)S(1)}, bf16[64,1024]{1,0:T(8,128)(...) custom-call(bf16[1024,1024]{1,0:T(8,128)(2,1)S(1)} %get-tuple-elemen, ...), custom_call_target="tpu_custom_call" | custom-call | flops 2147483648 | bytes 9437184 | tf_op jit(solution)/shard_map/pallas_call | solution.py:277
  103.6 1.5 collective-permute-start.40
  105.1 1.1 collective-permute-start.42
  106.2 2.3 %shard_map.116 = bf16[512,768]{1,0:T(8,128)(2,1)S(1)} custom-call(s32[2]{0:T(128)S(1)} %pad_add_fusion.pos, bf16[1024,512]{1,0:T(8,128)(2,1)S(1)} %get-tuple-element.128.own, bf16[1024,512]{1,0:T(8,128)(2,1)S(1)} %get-tuple-element.129.other, bf16[64,2048]{1,0:T(8,128)(2,1)S(1)} %get-tuple-element.70.refs_0_.refs_8_, ...), custom_call_target="tpu_custom_call" | custom-call | flops 805306368 | bytes 6029312 | tf_op jit(solution)/shard_map/pallas_call | solution.py:277
  108.6 1.0 collective-permute-start.43
  109.9 1.9 %collective-permute-start.44 = (bf16[64,1024]{1,0:T(8,128)(2,1)S(1)}, bf16[64,1024]{1,0:T(8,128)(2,1)S(1)}, u32[]{:S(2)}, u32[]{:S(2)}) collective-permute-start(bf16[64,1024]{1,0:T(8,128)(2,1)S(1)} %get-tuple-element.122), channel_id=1, source_target_pairs={{0,24},{4,28},{8,16},{12,20},{16,8},{20,12},{24,0},{28,4},{1,25},{... | collective-permute-start | bytes 393224 | tf_op jit(solution)/shard_map/ppermute | solution.py:325
  111.9 1.6 collective-permute-start.45
  113.7 1.7 shard_map.120
  115.5 4.0 %collective-permute-done.43.refs_5_ = bf16[64,1024]{1,0:T(8,128)(2,1)S(1)} collective-permute-done((bf16[64,1024]{1,0:T(8,128)(2,1)S(1)}, bf16[64,1024]{1,0:T(8,128)(2,1)S(1)}, u32[]{:S(2)}, u32[]{:S(2)}) %collective-permute-start.43) | collective-permute-done | bytes 131104 | tf_op jit(solution)/shard_map/ppermute | solution.py:325
  119.4 2.2 %collective-permute-start.51 = (bf16[512,512]{1,0:T(8,128)(2,1)S(1)}, bf16[512,512]{1,0:T(8,128)(2,1)S(1)}, u32[]{:S(2)}, u32[]{:S(2)}) collective-permute-start(bf16[512,512]{1,0:T(8,128)(2,1)S(1)} %shard_map.120), channel_id=1, source_target_pairs={{0,1},{1,0},{2,3},{3,2},{4,5},{5,4},{6,7},{7,6},{8,9},{9,8},{10,11... | collective-permute-start | bytes 1572872 | tf_op jit(solution)/shard_map/ppermute | solution.py:331
  121.7 1.7 shard_map.119
  123.5 1.8 %collective-permute-start.12 = (bf16[64,1024]{1,0:T(8,128)(2,1)S(1)}, bf16[64,1024]{1,0:T(8,128)(2,1)S(1)}, u32[]{:S(2)}, u32[]{:S(2)}) collective-permute-start(bf16[64,1024]{1,0:T(8,128)(2,1)S(1)} %get-tuple-element.86), channel_id=1, source_target_pairs={{0,24},{4,28},{8,16},{12,20},{16,8},{20,12},{24,0},{28,4},{1,25},{... | collective-permute-start | bytes 393224 | tf_op jit(solution)/shard_map/ppermute | solution.py:325
  125.3 0.9 shard_map.112
  126.2 1.7 collective-permute-start.46
  127.9 2.4 %collective-permute-done.12.refs_6_ = bf16[64,1024]{1,0:T(8,128)(2,1)S(1)} collective-permute-done((bf16[64,1024]{1,0:T(8,128)(2,1)S(1)}, bf16[64,1024]{1,0:T(8,128)(2,1)S(1)}, u32[]{:S(2)}, u32[]{:S(2)}) %collective-permute-start.12) | collective-permute-done | bytes 131104 | tf_op jit(solution)/shard_map/ppermute | solution.py:325
  130.3 1.0 collective-permute-start.13
  131.3 5.5 %collective-permute-done.13.refs_7_ = bf16[64,1024]{1,0:T(8,128)(2,1)S(1)} collective-permute-done((bf16[64,1024]{1,0:T(8,128)(2,1)S(1)}, bf16[64,1024]{1,0:T(8,128)(2,1)S(1)}, u32[]{:S(2)}, u32[]{:S(2)}) %collective-permute-start.13) | collective-permute-done | bytes 131104 | tf_op jit(solution)/shard_map/ppermute | solution.py:325
  136.8 1.4 collective-permute-start.47
  138.2 1.0 shard_map.115
  139.2 18.1 %collective-permute-done.47.got_gates = f32[8,192]{1,0:T(8,128)S(1)} collective-permute-done((f32[8,192]{1,0:T(8,128)S(1)}, f32[8,192]{1,0:T(8,128)S(1)}, u32[]{:S(2)}, u32[]{:S(2)}) %collective-permute-start.47) | collective-permute-done | bytes 6176 | tf_op jit(solution)/shard_map/ppermute | solution.py:321
  157.3 2.5 %collective-permute-start.48 = (bf16[512,256]{1,0:T(8,128)(2,1)S(1)}, bf16[512,256]{1,0:T(8,128)(2,1)S(1)}, u32[]{:S(2)}, u32[]{:S(2)}) collective-permute-start(bf16[512,256]{1,0:T(8,128)(2,1)S(1)} %shard_map.115), channel_id=1, source_target_pairs={{0,1},{1,0},{2,3},{3,2},{4,5},{5,4},{6,7},{7,6},{8,9},{9,8},{10,11... | collective-permute-start | bytes 786440 | tf_op jit(solution)/shard_map/ppermute | solution.py:331
  159.8 0.9 shard_map.106
  160.7 2.9 %shard_map.114.before = f32[512,1024]{1,0:T(8,128)S(1)} custom-call(s32[2]{0:T(128)S(1)} %pad_add_fusion.pos, bf16[1024,512]{1,0:T(8,128)(2,1)S(1)} %get-tuple-element.128.own, bf16[1024,512]{1,0:T(8,128)(2,1)S(1)} %get-tuple-element.129.other, bf16[64,2048]{1,0:T(8,128)(2,1)S(1)} %get-tuple-element.70.refs_0_.refs_8_, ...), custom_call_target="tpu_custom_call" | custom-call | flops 1073741824 | bytes 7340032 | tf_op jit(solution)/shard_map/pallas_call | solution.py:277
  163.7 0.8 shard_map.113
  164.5 2.5 %shard_map.121.refs_17_ = f32[1,512,1024]{2,1,0:T(8,128)} custom-call(s32[2]{0:T(128)S(1)} %pad_add_fusion.pos, bf16[1024,512]{1,0:T(8,128)(2,1)S(1)} %get-tuple-element.78.act.own, bf16[1024,512]{1,0:T(8,128)(2,1)S(1)} %get-tuple-element.98.act.other, bf16[64,2048]{1,0:T(8,128)(2,1)S(1)} %get-tuple-element.70.refs_0_.refs_8_, ...), custom_call_target="tpu_custom_call" | custom-call | flops 536870912 | bytes 7340032 | tf_op jit(solution)/shard_map/pallas_call | solution.py:277
  167.0 2.5 %shard_map.122 = f32[1,512,1024]{2,1,0:T(8,128)} custom-call(s32[2]{0:T(128)S(1)} %pad_add_fusion.pos, bf16[1024,512]{1,0:T(8,128)(2,1)S(1)} %get-tuple-element.78.act.own, bf16[1024,512]{1,0:T(8,128)(2,1)S(1)} %get-tuple-element.98.act.other, bf16[64,2048]{1,0:T(8,128)(2,1)S(1)} %get-tuple-element.70.refs_0_.refs_8_, ...), custom_call_target="tpu_custom_call", output_to_operand_aliasing={{}: (20, {})} | custom-call | flops 536870912 | bytes 9437184 | tf_op jit(solution)/shard_map/pallas_call | solution.py:277
  169.6 1.8 %shard_map.117.refs_1_ = f32[1,512,1024]{2,1,0:T(8,128)} custom-call(f32[512,1024]{1,0:T(8,128)S(1)} %shard_map.114.before, bf16[512,768]{1,0:T(8,128)(2,1)S(1)} %collective-permute-done.49.refs_0_), custom_call_target="tpu_custom_call" | custom-call | bytes 4980736 | tf_op jit(solution)/shard_map/pallas_call | solution.py:277
  171.4 0.8 shard_map.118
  (71 shorter events, 6.3 us)
Async XLA Ops:
  0.6 13.3 %copy-start.3 = (bf16[192,1024]{1,0:T(8,128)(2,1)S(1)}, bf16[192,1024]{1,0:T(8,128)(2,1)}, u32[]{:S(2)}) copy-start(bf16[192,1024]{1,0:T(8,128)(2,1)} %tokens.1) | copy-start | bytes 1179652
  1.7 12.2 %collective-permute-start.31 = (bf16[192,512]{1,0:T(8,128)(2,1)S(1)}, bf16[192,512]{1,0:T(8,128)(2,1)S(1)}, u32[]{:S(2)}, u32[]{:S(2)}) collective-permute-start(bf16[192,512]{1,0:T(8,128)(2,1)S(1)} %get-tuple-element.130), channel_id=1, source_target_pairs={{0,2},{1,3},{2,0},{3,1},{4,6},{5,7},{6,4},{7,5},{8,10},{9,11},{10,... | collective-permute-start | bytes 589832 | tf_op jit(solution)/shard_map/ppermute | solution.py:321
  6.5 30.2 %collective-permute-start = (bf16[64,2048]{1,0:T(8,128)(2,1)S(1)}, bf16[64,2048]{1,0:T(8,128)(2,1)S(1)}, u32[]{:S(2)}, u32[]{:S(2)}) collective-permute-start(bf16[64,2048]{1,0:T(8,128)(2,1)S(1)} %get-tuple-element.71), channel_id=1, source_target_pairs={{0,4},{4,0},{8,12},{12,8},{16,20},{20,16},{24,28},{28,24},{1,5},{5... | collective-permute-start | bytes 786440 | tf_op jit(solution)/shard_map/ppermute | solution.py:325
  6.6 7.3 %collective-permute-start.14 = (f32[8,192]{1,0:T(8,128)S(1)}, f32[8,192]{1,0:T(8,128)S(1)}, u32[]{:S(2)}, u32[]{:S(2)}) collective-permute-start(f32[8,192]{1,0:T(8,128)S(1)} %get-tuple-element.67.meta), channel_id=1, source_target_pairs={{0,2},{1,3},{2,0},{3,1},{4,6},{5,7},{6,4},{7,5},{8,10},{9,11},{10,... | collective-permute-start | bytes 18440 | tf_op jit(solution)/shard_map/ppermute | solution.py:321
  7.0 29.7 %collective-permute-start.1 = (bf16[64,2048]{1,0:T(8,128)(2,1)S(1)}, bf16[64,2048]{1,0:T(8,128)(2,1)S(1)}, u32[]{:S(2)}, u32[]{:S(2)}) collective-permute-start(bf16[64,2048]{1,0:T(8,128)(2,1)S(1)} %get-tuple-element.72), channel_id=1, source_target_pairs={{0,8},{4,12},{8,0},{12,4},{16,24},{20,28},{24,16},{28,20},{1,9},{5... | collective-permute-start | bytes 786440 | tf_op jit(solution)/shard_map/ppermute | solution.py:325
  7.3 30.0 %collective-permute-start.2 = (bf16[64,2048]{1,0:T(8,128)(2,1)S(1)}, bf16[64,2048]{1,0:T(8,128)(2,1)S(1)}, u32[]{:S(2)}, u32[]{:S(2)}) collective-permute-start(bf16[64,2048]{1,0:T(8,128)(2,1)S(1)} %get-tuple-element.73), channel_id=1, source_target_pairs={{0,12},{4,8},{8,4},{12,0},{16,28},{20,24},{24,20},{28,16},{1,13},{... | collective-permute-start | bytes 786440 | tf_op jit(solution)/shard_map/ppermute | solution.py:325
  13.9 21.3 %collective-permute-start.23 = (bf16[192,512]{1,0:T(8,128)(2,1)S(1)}, bf16[192,512]{1,0:T(8,128)(2,1)S(1)}, u32[]{:S(2)}, u32[]{:S(2)}) collective-permute-start(bf16[192,512]{1,0:T(8,128)(2,1)S(1)} %get-tuple-element.131), channel_id=1, source_target_pairs={{0,2},{1,3},{2,0},{3,1},{4,6},{5,7},{6,4},{7,5},{8,10},{9,11},{10,... | collective-permute-start | bytes 589832 | tf_op jit(solution)/shard_map/ppermute | solution.py:321
  13.9 44.0 %collective-permute-start.15 = (bf16[192,1024]{1,0:T(8,128)(2,1)S(1)}, bf16[192,1024]{1,0:T(8,128)(2,1)S(1)}, u32[]{:S(2)}, u32[]{:S(2)}) collective-permute-start(bf16[192,1024]{1,0:T(8,128)(2,1)S(1)} %copy-done.3), channel_id=1, source_target_pairs={{0,2},{1,3},{2,0},{3,1},{4,6},{5,7},{6,4},{7,5},{8,10},{9,11},{10,... | collective-permute-start | bytes 1179656 | tf_op jit(solution)/shard_map/ppermute | solution.py:321
  35.2 19.5 %collective-permute-start.3 = (bf16[64,2048]{1,0:T(8,128)(2,1)S(1)}, bf16[64,2048]{1,0:T(8,128)(2,1)S(1)}, u32[]{:S(2)}, u32[]{:S(2)}) collective-permute-start(bf16[64,2048]{1,0:T(8,128)(2,1)S(1)} %get-tuple-element.74), channel_id=1, source_target_pairs={{0,16},{4,20},{8,24},{12,28},{16,0},{20,4},{24,8},{28,12},{1,17},{... | collective-permute-start | bytes 786440 | tf_op jit(solution)/shard_map/ppermute | solution.py:325
  36.7 20.7 %collective-permute-start.4 = (bf16[64,2048]{1,0:T(8,128)(2,1)S(1)}, bf16[64,2048]{1,0:T(8,128)(2,1)S(1)}, u32[]{:S(2)}, u32[]{:S(2)}) collective-permute-start(bf16[64,2048]{1,0:T(8,128)(2,1)S(1)} %get-tuple-element.75), channel_id=1, source_target_pairs={{0,20},{4,16},{8,28},{12,24},{16,4},{20,0},{24,12},{28,8},{1,21},{... | collective-permute-start | bytes 786440 | tf_op jit(solution)/shard_map/ppermute | solution.py:325
  36.7 23.6 %collective-permute-start.5 = (bf16[64,2048]{1,0:T(8,128)(2,1)S(1)}, bf16[64,2048]{1,0:T(8,128)(2,1)S(1)}, u32[]{:S(2)}, u32[]{:S(2)}) collective-permute-start(bf16[64,2048]{1,0:T(8,128)(2,1)S(1)} %get-tuple-element.76), channel_id=1, source_target_pairs={{0,24},{4,28},{8,16},{12,20},{16,8},{20,12},{24,0},{28,4},{1,25},{... | collective-permute-start | bytes 786440 | tf_op jit(solution)/shard_map/ppermute | solution.py:325
  37.2 24.7 %collective-permute-start.6 = (bf16[64,2048]{1,0:T(8,128)(2,1)S(1)}, bf16[64,2048]{1,0:T(8,128)(2,1)S(1)}, u32[]{:S(2)}, u32[]{:S(2)}) collective-permute-start(bf16[64,2048]{1,0:T(8,128)(2,1)S(1)} %get-tuple-element.77), channel_id=1, source_target_pairs={{0,28},{4,24},{8,20},{12,16},{16,12},{20,8},{24,4},{28,0},{1,29},{... | collective-permute-start | bytes 786440 | tf_op jit(solution)/shard_map/ppermute | solution.py:325
  40.5 0.6 copy-start
  41.1 0.6 copy-start.1
  41.7 0.6 copy-start.2
  54.7 7.2 %collective-permute-start.32 = (bf16[64,512]{1,0:T(8,128)(2,1)}, bf16[64,512]{1,0:T(8,128)(2,1)S(1)}, u32[]{:S(2)}, u32[]{:S(2)}) collective-permute-start(bf16[64,512]{1,0:T(8,128)(2,1)} %get-tuple-element.109), channel_id=1, source_target_pairs={{0,4},{4,0},{8,12},{12,8},{16,20},{20,16},{24,28},{28,24},{1,5},{5... | collective-permute-start | bytes 196616 | tf_op jit(solution)/shard_map/ppermute | solution.py:325
  57.4 5.7 %collective-permute-start.33 = (bf16[64,512]{1,0:T(8,128)(2,1)}, bf16[64,512]{1,0:T(8,128)(2,1)S(1)}, u32[]{:S(2)}, u32[]{:S(2)}) collective-permute-start(bf16[64,512]{1,0:T(8,128)(2,1)} %get-tuple-element.110), channel_id=1, source_target_pairs={{0,8},{4,12},{8,0},{12,4},{16,24},{20,28},{24,16},{28,20},{1,9},{5... | collective-permute-start | bytes 196616 | tf_op jit(solution)/shard_map/ppermute | solution.py:325
  57.9 5.8 %collective-permute-start.34 = (bf16[64,512]{1,0:T(8,128)(2,1)}, bf16[64,512]{1,0:T(8,128)(2,1)S(1)}, u32[]{:S(2)}, u32[]{:S(2)}) collective-permute-start(bf16[64,512]{1,0:T(8,128)(2,1)} %get-tuple-element.111), channel_id=1, source_target_pairs={{0,12},{4,8},{8,4},{12,0},{16,28},{20,24},{24,20},{28,16},{1,13},{... | collective-permute-start | bytes 196616 | tf_op jit(solution)/shard_map/ppermute | solution.py:325
  60.4 8.8 %collective-permute-start.35 = (bf16[64,512]{1,0:T(8,128)(2,1)}, bf16[64,512]{1,0:T(8,128)(2,1)S(1)}, u32[]{:S(2)}, u32[]{:S(2)}) collective-permute-start(bf16[64,512]{1,0:T(8,128)(2,1)} %copy-done.2), channel_id=1, source_target_pairs={{0,16},{4,20},{8,24},{12,28},{16,0},{20,4},{24,8},{28,12},{1,17},{... | collective-permute-start | bytes 196616 | tf_op jit(solution)/shard_map/ppermute | solution.py:325
  61.9 7.5 %collective-permute-start.36 = (bf16[64,512]{1,0:T(8,128)(2,1)}, bf16[64,512]{1,0:T(8,128)(2,1)S(1)}, u32[]{:S(2)}, u32[]{:S(2)}) collective-permute-start(bf16[64,512]{1,0:T(8,128)(2,1)} %copy-done.1), channel_id=1, source_target_pairs={{0,20},{4,16},{8,28},{12,24},{16,4},{20,0},{24,12},{28,8},{1,21},{... | collective-permute-start | bytes 196616 | tf_op jit(solution)/shard_map/ppermute | solution.py:325
  61.9 8.2 %collective-permute-start.37 = (bf16[64,512]{1,0:T(8,128)(2,1)}, bf16[64,512]{1,0:T(8,128)(2,1)S(1)}, u32[]{:S(2)}, u32[]{:S(2)}) collective-permute-start(bf16[64,512]{1,0:T(8,128)(2,1)} %copy-done), channel_id=1, source_target_pairs={{0,24},{4,28},{8,16},{12,20},{16,8},{20,12},{24,0},{28,4},{1,25},{... | collective-permute-start | bytes 196616 | tf_op jit(solution)/shard_map/ppermute | solution.py:325
  63.1 13.5 %collective-permute-start.16 = (bf16[64,1024]{1,0:T(8,128)(2,1)S(1)}, bf16[64,1024]{1,0:T(8,128)(2,1)S(1)}, u32[]{:S(2)}, u32[]{:S(2)}) collective-permute-start(bf16[64,1024]{1,0:T(8,128)(2,1)S(1)} %get-tuple-element.91), channel_id=1, source_target_pairs={{0,4},{4,0},{8,12},{12,8},{16,20},{20,16},{24,28},{28,24},{1,5},{5... | collective-permute-start | bytes 393224 | tf_op jit(solution)/shard_map/ppermute | solution.py:325
  63.8 15.0 %collective-permute-start.17 = (bf16[64,1024]{1,0:T(8,128)(2,1)S(1)}, bf16[64,1024]{1,0:T(8,128)(2,1)S(1)}, u32[]{:S(2)}, u32[]{:S(2)}) collective-permute-start(bf16[64,1024]{1,0:T(8,128)(2,1)S(1)} %get-tuple-element.92), channel_id=1, source_target_pairs={{0,8},{4,12},{8,0},{12,4},{16,24},{20,28},{24,16},{28,20},{1,9},{5... | collective-permute-start | bytes 393224 | tf_op jit(solution)/shard_map/ppermute | solution.py:325
  69.2 5.4 %collective-permute-start.38 = (bf16[64,512]{1,0:T(8,128)(2,1)S(1)}, bf16[64,512]{1,0:T(8,128)(2,1)S(1)}, u32[]{:S(2)}, u32[]{:S(2)}) collective-permute-start(bf16[64,512]{1,0:T(8,128)(2,1)S(1)} %get-tuple-element.115), channel_id=1, source_target_pairs={{0,28},{4,24},{8,20},{12,16},{16,12},{20,8},{24,4},{28,0},{1,29},{... | collective-permute-start | bytes 196616 | tf_op jit(solution)/shard_map/ppermute | solution.py:325
  69.4 5.3 %collective-permute-start.24 = (bf16[64,512]{1,0:T(8,128)(2,1)S(1)}, bf16[64,512]{1,0:T(8,128)(2,1)S(1)}, u32[]{:S(2)}, u32[]{:S(2)}) collective-permute-start(bf16[64,512]{1,0:T(8,128)(2,1)S(1)} %get-tuple-element.101), channel_id=1, source_target_pairs={{0,4},{4,0},{8,12},{12,8},{16,20},{20,16},{24,28},{28,24},{1,5},{5... | collective-permute-start | bytes 196616 | tf_op jit(solution)/shard_map/ppermute | solution.py:325
  70.1 5.8 %collective-permute-start.25 = (bf16[64,512]{1,0:T(8,128)(2,1)S(1)}, bf16[64,512]{1,0:T(8,128)(2,1)S(1)}, u32[]{:S(2)}, u32[]{:S(2)}) collective-permute-start(bf16[64,512]{1,0:T(8,128)(2,1)S(1)} %get-tuple-element.102), channel_id=1, source_target_pairs={{0,8},{4,12},{8,0},{12,4},{16,24},{20,28},{24,16},{28,20},{1,9},{5... | collective-permute-start | bytes 196616 | tf_op jit(solution)/shard_map/ppermute | solution.py:325
  74.5 9.7 %collective-permute-start.18 = (bf16[64,1024]{1,0:T(8,128)(2,1)S(1)}, bf16[64,1024]{1,0:T(8,128)(2,1)S(1)}, u32[]{:S(2)}, u32[]{:S(2)}) collective-permute-start(bf16[64,1024]{1,0:T(8,128)(2,1)S(1)} %get-tuple-element.93), channel_id=1, source_target_pairs={{0,12},{4,8},{8,4},{12,0},{16,28},{20,24},{24,20},{28,16},{1,13},{... | collective-permute-start | bytes 393224 | tf_op jit(solution)/shard_map/ppermute | solution.py:325
  74.7 11.1 %collective-permute-start.19 = (bf16[64,1024]{1,0:T(8,128)(2,1)S(1)}, bf16[64,1024]{1,0:T(8,128)(2,1)S(1)}, u32[]{:S(2)}, u32[]{:S(2)}) collective-permute-start(bf16[64,1024]{1,0:T(8,128)(2,1)S(1)} %get-tuple-element.94), channel_id=1, source_target_pairs={{0,16},{4,20},{8,24},{12,28},{16,0},{20,4},{24,8},{28,12},{1,17},{... | collective-permute-start | bytes 393224 | tf_op jit(solution)/shard_map/ppermute | solution.py:325
  75.9 12.6 %collective-permute-start.20 = (bf16[64,1024]{1,0:T(8,128)(2,1)S(1)}, bf16[64,1024]{1,0:T(8,128)(2,1)S(1)}, u32[]{:S(2)}, u32[]{:S(2)}) collective-permute-start(bf16[64,1024]{1,0:T(8,128)(2,1)S(1)} %get-tuple-element.95), channel_id=1, source_target_pairs={{0,20},{4,16},{8,28},{12,24},{16,4},{20,0},{24,12},{28,8},{1,21},{... | collective-permute-start | bytes 393224 | tf_op jit(solution)/shard_map/ppermute | solution.py:325
  76.6 13.5 %collective-permute-start.21 = (bf16[64,1024]{1,0:T(8,128)(2,1)S(1)}, bf16[64,1024]{1,0:T(8,128)(2,1)S(1)}, u32[]{:S(2)}, u32[]{:S(2)}) collective-permute-start(bf16[64,1024]{1,0:T(8,128)(2,1)S(1)} %get-tuple-element.96), channel_id=1, source_target_pairs={{0,24},{4,28},{8,16},{12,20},{16,8},{20,12},{24,0},{28,4},{1,25},{... | collective-permute-start | bytes 393224 | tf_op jit(solution)/shard_map/ppermute | solution.py:325
  78.8 13.1 %collective-permute-start.22 = (bf16[64,1024]{1,0:T(8,128)(2,1)S(1)}, bf16[64,1024]{1,0:T(8,128)(2,1)S(1)}, u32[]{:S(2)}, u32[]{:S(2)}) collective-permute-start(bf16[64,1024]{1,0:T(8,128)(2,1)S(1)} %get-tuple-element.97), channel_id=1, source_target_pairs={{0,28},{4,24},{8,20},{12,16},{16,12},{20,8},{24,4},{28,0},{1,29},{... | collective-permute-start | bytes 393224 | tf_op jit(solution)/shard_map/ppermute | solution.py:325
  84.2 10.7 %collective-permute-start.26 = (bf16[64,512]{1,0:T(8,128)(2,1)S(1)}, bf16[64,512]{1,0:T(8,128)(2,1)S(1)}, u32[]{:S(2)}, u32[]{:S(2)}) collective-permute-start(bf16[64,512]{1,0:T(8,128)(2,1)S(1)} %get-tuple-element.103), channel_id=1, source_target_pairs={{0,12},{4,8},{8,4},{12,0},{16,28},{20,24},{24,20},{28,16},{1,13},{... | collective-permute-start | bytes 196616 | tf_op jit(solution)/shard_map/ppermute | solution.py:325
  85.8 10.2 %collective-permute-start.27 = (bf16[64,512]{1,0:T(8,128)(2,1)S(1)}, bf16[64,512]{1,0:T(8,128)(2,1)S(1)}, u32[]{:S(2)}, u32[]{:S(2)}) collective-permute-start(bf16[64,512]{1,0:T(8,128)(2,1)S(1)} %get-tuple-element.104), channel_id=1, source_target_pairs={{0,16},{4,20},{8,24},{12,28},{16,0},{20,4},{24,8},{28,12},{1,17},{... | collective-permute-start | bytes 196616 | tf_op jit(solution)/shard_map/ppermute | solution.py:325
  88.5 8.8 %collective-permute-start.28 = (bf16[64,512]{1,0:T(8,128)(2,1)S(1)}, bf16[64,512]{1,0:T(8,128)(2,1)S(1)}, u32[]{:S(2)}, u32[]{:S(2)}) collective-permute-start(bf16[64,512]{1,0:T(8,128)(2,1)S(1)} %get-tuple-element.105), channel_id=1, source_target_pairs={{0,20},{4,16},{8,28},{12,24},{16,4},{20,0},{24,12},{28,8},{1,21},{... | collective-permute-start | bytes 196616 | tf_op jit(solution)/shard_map/ppermute | solution.py:325
  90.1 7.3 %collective-permute-start.29 = (bf16[64,512]{1,0:T(8,128)(2,1)S(1)}, bf16[64,512]{1,0:T(8,128)(2,1)S(1)}, u32[]{:S(2)}, u32[]{:S(2)}) collective-permute-start(bf16[64,512]{1,0:T(8,128)(2,1)S(1)} %get-tuple-element.106), channel_id=1, source_target_pairs={{0,24},{4,28},{8,16},{12,20},{16,8},{20,12},{24,0},{28,4},{1,25},{... | collective-permute-start | bytes 196616 | tf_op jit(solution)/shard_map/ppermute | solution.py:325
  91.9 6.5 %collective-permute-start.30 = (bf16[64,512]{1,0:T(8,128)(2,1)S(1)}, bf16[64,512]{1,0:T(8,128)(2,1)S(1)}, u32[]{:S(2)}, u32[]{:S(2)}) collective-permute-start(bf16[64,512]{1,0:T(8,128)(2,1)S(1)} %get-tuple-element.107), channel_id=1, source_target_pairs={{0,28},{4,24},{8,20},{12,16},{16,12},{20,8},{24,4},{28,0},{1,29},{... | collective-permute-start | bytes 196616 | tf_op jit(solution)/shard_map/ppermute | solution.py:325
  95.0 8.6 %collective-permute-start.7 = (bf16[64,1024]{1,0:T(8,128)(2,1)S(1)}, bf16[64,1024]{1,0:T(8,128)(2,1)S(1)}, u32[]{:S(2)}, u32[]{:S(2)}) collective-permute-start(bf16[64,1024]{1,0:T(8,128)(2,1)S(1)} %get-tuple-element.81), channel_id=1, source_target_pairs={{0,4},{4,0},{8,12},{12,8},{16,20},{20,16},{24,28},{28,24},{1,5},{5... | collective-permute-start | bytes 393224 | tf_op jit(solution)/shard_map/ppermute | solution.py:325
  96.0 9.1 %collective-permute-start.8 = (bf16[64,1024]{1,0:T(8,128)(2,1)S(1)}, bf16[64,1024]{1,0:T(8,128)(2,1)S(1)}, u32[]{:S(2)}, u32[]{:S(2)}) collective-permute-start(bf16[64,1024]{1,0:T(8,128)(2,1)S(1)} %get-tuple-element.82), channel_id=1, source_target_pairs={{0,8},{4,12},{8,0},{12,4},{16,24},{20,28},{24,16},{28,20},{1,9},{5... | collective-permute-start | bytes 393224 | tf_op jit(solution)/shard_map/ppermute | solution.py:325
  97.3 7.8 %collective-permute-start.9 = (bf16[64,1024]{1,0:T(8,128)(2,1)S(1)}, bf16[64,1024]{1,0:T(8,128)(2,1)S(1)}, u32[]{:S(2)}, u32[]{:S(2)}) collective-permute-start(bf16[64,1024]{1,0:T(8,128)(2,1)S(1)} %get-tuple-element.83), channel_id=1, source_target_pairs={{0,12},{4,8},{8,4},{12,0},{16,28},{20,24},{24,20},{28,16},{1,13},{... | collective-permute-start | bytes 393224 | tf_op jit(solution)/shard_map/ppermute | solution.py:325
  97.4 11.1 %collective-permute-start.10 = (bf16[64,1024]{1,0:T(8,128)(2,1)S(1)}, bf16[64,1024]{1,0:T(8,128)(2,1)S(1)}, u32[]{:S(2)}, u32[]{:S(2)}) collective-permute-start(bf16[64,1024]{1,0:T(8,128)(2,1)S(1)} %get-tuple-element.84), channel_id=1, source_target_pairs={{0,16},{4,20},{8,24},{12,28},{16,0},{20,4},{24,8},{28,12},{1,17},{... | collective-permute-start | bytes 393224 | tf_op jit(solution)/shard_map/ppermute | solution.py:325
  103.2 5.4 %collective-permute-start.39 = (bf16[64,1024]{1,0:T(8,128)(2,1)S(1)}, bf16[64,1024]{1,0:T(8,128)(2,1)S(1)}, u32[]{:S(2)}, u32[]{:S(2)}) collective-permute-start(bf16[64,1024]{1,0:T(8,128)(2,1)S(1)} %get-tuple-element.117), channel_id=1, source_target_pairs={{0,4},{4,0},{8,12},{12,8},{16,20},{20,16},{24,28},{28,24},{1,5},{5... | collective-permute-start | bytes 393224 | tf_op jit(solution)/shard_map/ppermute | solution.py:325
  103.6 6.4 %collective-permute-start.40 = (bf16[64,1024]{1,0:T(8,128)(2,1)S(1)}, bf16[64,1024]{1,0:T(8,128)(2,1)S(1)}, u32[]{:S(2)}, u32[]{:S(2)}) collective-permute-start(bf16[64,1024]{1,0:T(8,128)(2,1)S(1)} %get-tuple-element.118), channel_id=1, source_target_pairs={{0,8},{4,12},{8,0},{12,4},{16,24},{20,28},{24,16},{28,20},{1,9},{5... | collective-permute-start | bytes 393224 | tf_op jit(solution)/shard_map/ppermute | solution.py:325
  105.0 6.8 %collective-permute-start.41 = (bf16[64,1024]{1,0:T(8,128)(2,1)S(1)}, bf16[64,1024]{1,0:T(8,128)(2,1)S(1)}, u32[]{:S(2)}, u32[]{:S(2)}) collective-permute-start(bf16[64,1024]{1,0:T(8,128)(2,1)S(1)} %get-tuple-element.119), channel_id=1, source_target_pairs={{0,12},{4,8},{8,4},{12,0},{16,28},{20,24},{24,20},{28,16},{1,13},{... | collective-permute-start | bytes 393224 | tf_op jit(solution)/shard_map/ppermute | solution.py:325
  105.1 8.4 %collective-permute-start.42 = (bf16[64,1024]{1,0:T(8,128)(2,1)S(1)}, bf16[64,1024]{1,0:T(8,128)(2,1)S(1)}, u32[]{:S(2)}, u32[]{:S(2)}) collective-permute-start(bf16[64,1024]{1,0:T(8,128)(2,1)S(1)} %get-tuple-element.120), channel_id=1, source_target_pairs={{0,16},{4,20},{8,24},{12,28},{16,0},{20,4},{24,8},{28,12},{1,17},{... | collective-permute-start | bytes 393224 | tf_op jit(solution)/shard_map/ppermute | solution.py:325
  108.5 61.1 %collective-permute-start.49 = (bf16[512,768]{1,0:T(8,128)(2,1)S(1)}, bf16[512,768]{1,0:T(8,128)(2,1)S(1)}, u32[]{:S(2)}, u32[]{:S(2)}) collective-permute-start(bf16[512,768]{1,0:T(8,128)(2,1)S(1)} %shard_map.116), channel_id=1, source_target_pairs={{0,1},{1,0},{2,3},{3,2},{4,5},{5,4},{6,7},{7,6},{8,9},{9,8},{10,11... | collective-permute-start | bytes 2359304 | tf_op jit(solution)/shard_map/ppermute | solution.py:331
  108.6 10.9 %collective-permute-start.43 = (bf16[64,1024]{1,0:T(8,128)(2,1)S(1)}, bf16[64,1024]{1,0:T(8,128)(2,1)S(1)}, u32[]{:S(2)}, u32[]{:S(2)}) collective-permute-start(bf16[64,1024]{1,0:T(8,128)(2,1)S(1)} %get-tuple-element.121), channel_id=1, source_target_pairs={{0,20},{4,16},{8,28},{12,24},{16,4},{20,0},{24,12},{28,8},{1,21},{... | collective-permute-start | bytes 393224 | tf_op jit(solution)/shard_map/ppermute | solution.py:325
  109.9 13.4 %collective-permute-start.44 = (bf16[64,1024]{1,0:T(8,128)(2,1)S(1)}, bf16[64,1024]{1,0:T(8,128)(2,1)S(1)}, u32[]{:S(2)}, u32[]{:S(2)}) collective-permute-start(bf16[64,1024]{1,0:T(8,128)(2,1)S(1)} %get-tuple-element.122), channel_id=1, source_target_pairs={{0,24},{4,28},{8,16},{12,20},{16,8},{20,12},{24,0},{28,4},{1,25},{... | collective-permute-start | bytes 393224 | tf_op jit(solution)/shard_map/ppermute | solution.py:325
  111.9 11.6 %collective-permute-start.45 = (bf16[64,1024]{1,0:T(8,128)(2,1)S(1)}, bf16[64,1024]{1,0:T(8,128)(2,1)S(1)}, u32[]{:S(2)}, u32[]{:S(2)}) collective-permute-start(bf16[64,1024]{1,0:T(8,128)(2,1)S(1)} %get-tuple-element.123), channel_id=1, source_target_pairs={{0,28},{4,24},{8,20},{12,16},{16,12},{20,8},{24,4},{28,0},{1,29},{... | collective-permute-start | bytes 393224 | tf_op jit(solution)/shard_map/ppermute | solution.py:325
  113.5 12.7 %collective-permute-start.11 = (bf16[64,1024]{1,0:T(8,128)(2,1)S(1)}, bf16[64,1024]{1,0:T(8,128)(2,1)S(1)}, u32[]{:S(2)}, u32[]{:S(2)}) collective-permute-start(bf16[64,1024]{1,0:T(8,128)(2,1)S(1)} %get-tuple-element.85), channel_id=1, source_target_pairs={{0,20},{4,16},{8,28},{12,24},{16,4},{20,0},{24,12},{28,8},{1,21},{... | collective-permute-start | bytes 393224 | tf_op jit(solution)/shard_map/ppermute | solution.py:325
  119.4 45.0 %collective-permute-start.51 = (bf16[512,512]{1,0:T(8,128)(2,1)S(1)}, bf16[512,512]{1,0:T(8,128)(2,1)S(1)}, u32[]{:S(2)}, u32[]{:S(2)}) collective-permute-start(bf16[512,512]{1,0:T(8,128)(2,1)S(1)} %shard_map.120), channel_id=1, source_target_pairs={{0,1},{1,0},{2,3},{3,2},{4,5},{5,4},{6,7},{7,6},{8,9},{9,8},{10,11... | collective-permute-start | bytes 1572872 | tf_op jit(solution)/shard_map/ppermute | solution.py:331
  123.4 43.6 %collective-permute-start.50 = (bf16[512,512]{1,0:T(8,128)(2,1)S(1)}, bf16[512,512]{1,0:T(8,128)(2,1)S(1)}, u32[]{:S(2)}, u32[]{:S(2)}) collective-permute-start(bf16[512,512]{1,0:T(8,128)(2,1)S(1)} %shard_map.119), channel_id=1, source_target_pairs={{0,1},{1,0},{2,3},{3,2},{4,5},{5,4},{6,7},{7,6},{8,9},{9,8},{10,11... | collective-permute-start | bytes 1572872 | tf_op jit(solution)/shard_map/ppermute | solution.py:331
  123.5 6.9 %collective-permute-start.12 = (bf16[64,1024]{1,0:T(8,128)(2,1)S(1)}, bf16[64,1024]{1,0:T(8,128)(2,1)S(1)}, u32[]{:S(2)}, u32[]{:S(2)}) collective-permute-start(bf16[64,1024]{1,0:T(8,128)(2,1)S(1)} %get-tuple-element.86), channel_id=1, source_target_pairs={{0,24},{4,28},{8,16},{12,20},{16,8},{20,12},{24,0},{28,4},{1,25},{... | collective-permute-start | bytes 393224 | tf_op jit(solution)/shard_map/ppermute | solution.py:325
  126.2 37.4 %collective-permute-start.46 = (bf16[192,1024]{1,0:T(8,128)(2,1)S(1)}, bf16[192,1024]{1,0:T(8,128)(2,1)S(1)}, u32[]{:S(2)}, u32[]{:S(2)}) collective-permute-start(bf16[192,1024]{1,0:T(8,128)(2,1)S(1)} %get-tuple-element.124), channel_id=1, source_target_pairs={{0,2},{1,3},{2,0},{3,1},{4,6},{5,7},{6,4},{7,5},{8,10},{9,11},{10,... | collective-permute-start | bytes 1179656 | tf_op jit(solution)/shard_map/ppermute | solution.py:321
  130.3 6.5 %collective-permute-start.13 = (bf16[64,1024]{1,0:T(8,128)(2,1)S(1)}, bf16[64,1024]{1,0:T(8,128)(2,1)S(1)}, u32[]{:S(2)}, u32[]{:S(2)}) collective-permute-start(bf16[64,1024]{1,0:T(8,128)(2,1)S(1)} %get-tuple-element.87), channel_id=1, source_target_pairs={{0,28},{4,24},{8,20},{12,16},{16,12},{20,8},{24,4},{28,0},{1,29},{... | collective-permute-start | bytes 393224 | tf_op jit(solution)/shard_map/ppermute | solution.py:325
  136.8 20.5 %collective-permute-start.47 = (f32[8,192]{1,0:T(8,128)S(1)}, f32[8,192]{1,0:T(8,128)S(1)}, u32[]{:S(2)}, u32[]{:S(2)}) collective-permute-start(f32[8,192]{1,0:T(8,128)S(1)} %get-tuple-element.125), channel_id=1, source_target_pairs={{0,2},{1,3},{2,0},{3,1},{4,6},{5,7},{6,4},{7,5},{8,10},{9,11},{10,... | collective-permute-start | bytes 18440 | tf_op jit(solution)/shard_map/ppermute | solution.py:321
  157.3 14.1 %collective-permute-start.48 = (bf16[512,256]{1,0:T(8,128)(2,1)S(1)}, bf16[512,256]{1,0:T(8,128)(2,1)S(1)}, u32[]{:S(2)}, u32[]{:S(2)}) collective-permute-start(bf16[512,256]{1,0:T(8,128)(2,1)S(1)} %shard_map.115), channel_id=1, source_target_pairs={{0,1},{1,0},{2,3},{3,2},{4,5},{5,4},{6,7},{7,6},{8,9},{9,8},{10,11... | collective-permute-start | bytes 786440 | tf_op jit(solution)/shard_map/ppermute | solution.py:331

commit v3 on v2

--- a/solution.py
+++ b/solution.py
@@ -113,37 +113,18 @@
     place(weighted.astype(bf16), grad_out, outs, block)
 
 
-def add_tokens(grad, w_in, total, gates, outs, block, capacity):
-    step, last = pl.program_id(0), pl.num_programs(0) - 1
-    more = dot(grad, w_in, TN)
-
-    @pl.when(step == 0)
-    def _():
-        total[...] = more
-
-    @pl.when((step > 0) & (step < last))
-    def _():
-        total[...] += more
-
-    @pl.when(step == last)
-    def _():
-        rows = (total[...] + more).astype(bf16)
-        gate_rows = gates[0:1, :].astype(bf16)
-        for k, out in enumerate(outs):
-            out[...] = rows[k * block : (k + 1) * block]
-            out[capacity : capacity + 1, 0:block] = gate_rows[:, k * block : (k + 1) * block]
-
-
-def add_gates(active, up, gates):
-    more = jnp.sum(active.astype(f32) * up, axis=0, keepdims=True)
-
+def accumulate(ref, more):
     @pl.when(pl.program_id(0) == 0)
     def _():
-        gates[0:1, :] = more
+        ref[...] = more
 
     @pl.when(pl.program_id(0) > 0)
     def _():
-        gates[0:1, :] += more
+        ref[...] += more
+
+
+def gate_sums(active, up):
+    return jnp.sum(active.astype(f32) * up, axis=0, keepdims=True)
 
 
 def act_kernel(experts, w_in, *refs):
@@ -153,14 +134,42 @@
     slope[...] = derivative.astype(bf16)
 
 
-def grad_kernel(experts, block, capacity, w_in, w_out, act, slope, *refs):
-    (total, gates), outs = refs[-2:], refs[-2 - experts : -2]
-    grad, blocks = refs[-3 - experts], refs[: -3 - experts]
+def other_grad_kernel(experts, w_out, slope, *refs):
+    up = dot(w_out[...], stack(refs[:-1], experts), NT)
+    refs[-1][...] = (up * slope[...].astype(f32)).astype(bf16)
+
+
+def own_grad_kernel(experts, w_in, w_out, act, slope, *refs):
+    blocks, (grad, total, gates) = refs[:-3], refs[-3:]
     up = dot(w_out[...], stack(blocks, experts), NT)
-    add_gates(act[...], up, gates)
+    accumulate(gates, gate_sums(act[...], up))
     hidden_grad = (up * slope[...].astype(f32)).astype(bf16)
     grad[...] = hidden_grad
-    add_tokens(hidden_grad, w_in[...], total, gates, outs, block, capacity)
+    accumulate(total, dot(hidden_grad, w_in[...], TN))
+
+
+def far_kernel(experts, block, capacity, pos, w_in, w_out, near_total, near_gates, *refs):
+    x_blocks, s_blocks = refs[:experts], refs[experts : 3 * experts]
+    outs, (total, gates) = refs[3 * experts : -2], refs[-2:]
+    step, last = pl.program_id(0), pl.num_programs(0) - 1
+
+    @pl.when(step == 0)
+    def _():
+        total[...] = near_total[...]
+        gates[...] = near_gates[...]
+
+    active, slope = gelu_slope(dot(w_in[0], stack(x_blocks, experts), NT))
+    up = dot(w_out[0], stack(s_blocks, experts), NT)
+    gates[...] += gate_sums(active.astype(bf16), up)
+    total[...] += dot((up * slope).astype(bf16), w_in[0], TN)
+
+    @pl.when(step == last)
+    def _():
+        rows = total[...].astype(bf16)
+        gate_rows = gates[...].astype(bf16)
+        for k, out in enumerate(outs):
+            out[...] = rows[k * block : (k + 1) * block]
+            out[capacity : capacity + 1, 0:block] = gate_rows[:, k * block : (k + 1) * block]
 
 
 def outer_rows(own_ref, other_ref, own_rows, other_rows, at, size):
@@ -229,20 +238,13 @@
 
 
 def collect_kernel(experts, block, capacity, meta, *refs):
-    blocks, (out, gates) = refs[:experts], refs[experts:]
-    out[...] = gathered(meta, blocks, experts, block).astype(out.dtype)
+    blocks, (grad_tokens, grad_combine) = refs[:experts], refs[experts:]
+    grad_tokens[...] = gathered(meta, blocks, experts, block).astype(bf16)
 
     @pl.when(pl.program_id(0) == 0)
     def _():
-        first, second = gate_rows(meta, blocks, block, capacity)
-        gates[0:1, :] = first
-        gates[1:2, :] = second
-        gates[2:8, :] = jnp.zeros((6, first.shape[1]), f32)
-
-
-def join_kernel(own, own_gates, got, got_gates, grad_tokens, grad_combine):
-    grad_tokens[...] = (own[...] + got[...].astype(f32)).astype(bf16)
-    grad_combine[...] = (own_gates[0:2, :] + got_gates[0:2, :]).astype(bf16)
+        gates = gate_rows(meta, blocks, block, capacity)
+        grad_combine[...] = jnp.concatenate(gates, axis=0).astype(bf16)
 
 
 def shaped(shape, dtype=bf16):
@@ -265,9 +267,11 @@
     return pl.BlockSpec((size, array.shape[1]), lambda g, *pos: (g, 0))
 
 
-def half_rows(array, parts):
+def half_rows(array, parts, far=0):
     size = array.shape[1] // 2 // parts
-    return pl.BlockSpec((1, size, array.shape[2]), lambda g, pos: (0, pos[0] * parts + g, 0))
+    return pl.BlockSpec(
+        (1, size, array.shape[2]), lambda g, pos: (0, (pos[0] ^ far) * parts + g, 0)
+    )
 
 
 def call(kernel, grid, scalars, operands, results, scratch=(), flops=0, alias=None):
@@ -355,7 +359,6 @@
     act_shape = shaped((units, slots))
     unit_parts = max(units // 256, 1)
     unit_rows = units // unit_parts
-    sums = [pltpu.VMEM((slots, width), f32), pltpu.VMEM((8, slots), f32)]
     meta_shape = shaped((8, count), f32)
     meta, *own_xs = call(
         bind(own_send_kernel, experts, block, capacity),
@@ -407,21 +410,6 @@
             each([act_shape] * 2, rows, unit_rows),
             flops=2 * slots * units * width,
         )
-
-    def grad(acts, sa, sb):
-        result, *back = call(
-            bind(grad_kernel, experts, block, capacity),
-            unit_parts,
-            [],
-            each([half_in, half_out], rows, unit_rows)
-            + each(acts, rows, unit_rows)
-            + window(*sa, half)
-            + window(*sb, half),
-            each([act_shape], rows, unit_rows) + each(blocks(width), full),
-            sums,
-            4 * slots * units * width,
-        )
-        return result, back
 
     own_act, own_slope = act(own_x)
     other_act, other_slope = act(other_x)
@@ -486,9 +474,40 @@
     got_oa = to_owners(away_oa)
     away_ob = away(out_acts, own_sb, other_sb, 0, 2)
     got_ob = to_owners(away_ob)
-    other_grad, other_back = grad([other_act, other_slope], other_sa, other_sb)
-    other_back = exchange(other_back)
-    own_grad, own_back = grad([own_act, own_slope], own_sa, own_sb)
+    total_shape, gate_shape = shaped((slots, width), f32), shaped((1, slots), f32)
+    own_grad, near_total, near_gates = call(
+        bind(own_grad_kernel, experts),
+        unit_parts,
+        [],
+        each([half_in, half_out, own_act, own_slope], rows, unit_rows)
+        + window(*own_sa, half)
+        + window(*own_sb, half),
+        each([act_shape], rows, unit_rows) + each([total_shape, gate_shape], full),
+        flops=4 * slots * units * width,
+    )
+    other_grad = call(
+        bind(other_grad_kernel, experts),
+        unit_parts,
+        [],
+        each([half_out, other_slope], rows, unit_rows)
+        + window(*other_sa, half)
+        + window(*other_sb, half),
+        each([act_shape], rows, unit_rows),
+        flops=2 * slots * units * width,
+    )[0]
+    own_back = call(
+        bind(far_kernel, experts, block, capacity),
+        unit_parts,
+        [pos],
+        each([stay(w_in), stay(w_out)], half_rows, unit_parts, 1)
+        + each([near_total, near_gates], full)
+        + window(*own_x, width)
+        + window(*own_sa, half)
+        + window(*own_sb, half),
+        each(blocks(width), full),
+        [pltpu.VMEM((slots, width), f32), pltpu.VMEM((1, slots), f32)],
+        6 * slots * units * width,
+    )
     in_acts = [own_grad, other_grad]
     away_a = away(in_acts, own_x, other_x, 0, 3)
     got_a = to_owners(away_a)
@@ -496,22 +515,16 @@
     got_b = to_owners(away_b)
     own_back = exchange(own_back)
 
-    def collect(rows_of, back, kind):
-        return call(
-            bind(collect_kernel, experts, block, capacity),
-            2,
-            [],
-            each([rows_of], full) + each(back, columns, 2),
-            each([shaped((count, width), kind)], columns, 2) + each([meta_shape], full),
-            flops=2 * slots * count * width,
-        )
-
-    other_part, other_gates = collect(other_meta, other_back, bf16)
-    part = across(other_part)
-    part_gates = across(other_gates)
     grad_outw = home(out_acts, own_sa, other_sa, got_oa, 0, 2)
     grad_outw = home(out_acts, own_sb, other_sb, got_ob, 2, 2, grad_outw)
-    own_part, own_gates = collect(meta, own_back, f32)
+    grad_tokens, grad_combine = call(
+        bind(collect_kernel, experts, block, capacity),
+        2,
+        [],
+        each([meta], full) + each(own_back, columns, 2),
+        each([shaped((count, width))], columns, 2) + each([shaped((2, count))], full),
+        flops=2 * slots * count * width,
+    )
     before = call(
         bind(before_kernel, experts, owners),
         4,
@@ -520,13 +533,6 @@
         each([shaped((share, width), f32)], columns, 4),
         flops=16 * fed,
     )[0]
-    grad_tokens, grad_combine = call(
-        join_kernel,
-        1,
-        [],
-        each([own_part, own_gates, part, part_gates], full),
-        each([shaped((count, width)), shaped((2, count))], full),
-    )
     grad_in = after(before, got_a, 0, 3)
     grad_in = after(before, got_b, 3, 1, grad_in)
     return grad_tokens, grad_combine.T, grad_in, grad_outw

time: 174 us -> 152 us (0.87)
  waiting for transfers between devices: 70.2 us -> 55.3 us
  starting transfers between devices: 55.1 us -> 43.2 us
  Pallas kernels: 43 us -> 46.8 us
    ppermute x6 -> x4, waiting for transfers between devices: 41.9 us -> 23.8 us  [across(): lax.ppermute(value, 'dp', [(j, (j + owners) % planes) for j in range(plan...]
    ppermute x42 -> x35, starting transfers between devices: 41.2 us -> 33.7 us  [exchange(): lax.ppermute(values[k], 'expert', [(i, i ^ k) for i in range(experts)])]
    ppermute x4, waiting for transfers between devices: 0.01 us -> 5.92 us  [to_owners(): lax.ppermute(value, 'dp', [(j, j // owners * owners + (j + r + 1) % owner...]
    pallas_call x21 -> x20, Pallas kernels: 43 us -> 46.8 us  [call(): pl.pallas_call(kernel, out_shape=outs, grid_spec=pltpu.PrefetchScalarGrid...]
    ppermute x6 -> x4, starting transfers between devices: 9.07 us -> 6 us  [across(): lax.ppermute(value, 'dp', [(j, (j + owners) % planes) for j in range(plan...]
    ppermute x42 -> x35, waiting for transfers between devices: 28.4 us -> 25.6 us  [exchange(): lax.ppermute(values[k], 'expert', [(i, i ^ k) for i in range(experts)])]
  transfers between devices with their start and end apart: 52 -> 43, of which waited for: 11 -> 13; matrix products, arithmetic and copies ran while one was open for 0% -> 0% of each run, Pallas kernels for 24% -> 28%
where the time goes in v3:
time: 152 us; the launch traced here: 149 us
  waiting for transfers between devices  55.3 us (36%)
  Pallas kernels  46.8 us (31%)
  starting transfers between devices  43.2 us (28%)
  local copies, waits for them, and re-layouts  2.98 us (2%)
    pallas_call x20, Pallas kernels, call(): pl.pallas_call(kernel, out_shape=outs, grid_spec=pltpu.PrefetchScalarGrid...  46.8 us
    ppermute x35, starting transfers between devices, exchange(): lax.ppermute(values[k], 'expert', [(i, i ^ k) for i in range(experts)])  33.7 us
    ppermute x35, waiting for transfers between devices, exchange(): lax.ppermute(values[k], 'expert', [(i, i ^ k) for i in range(experts)])  25.6 us
    ppermute x4, waiting for transfers between devices, across(): lax.ppermute(value, 'dp', [(j, (j + owners) % planes) for j in range(plan...  23.8 us
    ppermute x4, starting transfers between devices, across(): lax.ppermute(value, 'dp', [(j, (j + owners) % planes) for j in range(plan...  6 us
    ppermute x4, waiting for transfers between devices, to_owners(): lax.ppermute(value, 'dp', [(j, j // owners * owners + (j + r + 1) % owner...  5.92 us
    ppermute x4, starting transfers between devices, to_owners(): lax.ppermute(value, 'dp', [(j, j // owners * owners + (j + r + 1) % owner...  3.45 us
  transfers between devices with their start and end apart: 43, of which 13 were waited for; matrix products, arithmetic and copies ran while one was open for 0% of the time, Pallas kernels for 28%

profile of v3, /device:TPU:2, one launch (start us, length us, event | category | flops | bytes accessed | tf_op | source)
XLA Modules:
  0.0 149.2 jit_solution(9883861862168380621)
XLA Ops:
  0.6 1.1 fusion
  1.7 2.7 %collective-permute-start.23 = (bf16[192,512]{1,0:T(8,128)(2,1)S(1)}, bf16[192,512]{1,0:T(8,128)(2,1)S(1)}, u32[]{:S(2)}, u32[]{:S(2)}) collective-permute-start(bf16[192,512]{1,0:T(8,128)(2,1)S(1)} %get-tuple-element.109), channel_id=1, source_target_pairs={{0,2},{1,3},{2,0},{3,1},{4,6},{5,7},{6,4},{7,5},{8,10},{9,11},{10,... | collective-permute-start | bytes 589832 | tf_op jit(solution)/shard_map/ppermute | solution.py:325
  4.4 2.1 %shard_map.102 = (f32[8,192]{1,0:T(8,128)S(1)}, bf16[64,2048]{1,0:T(8,128)(2,1)S(1)}, bf16[64,2048]{1,0:T(8,128)(2,1)S(1)}, bf16[64,2048]{1,0:T(8,128)(2,1)S(1)}...) custom-call(s32[2,192]{1,0:T(2,128)} %bitcast.6, ...), custom_call_target="tpu_custom_call" | custom-call | flops 402653184 | bytes 2892800 | tf_op jit(solution)/shard_map/pallas_call | solution.py:281
  6.6 0.4 collective-permute-start.14
  7.3 1.2 collective-permute-start.2
  8.5 5.4 %collective-permute-done.14.meta = f32[8,192]{1,0:T(8,128)S(1)} collective-permute-done((f32[8,192]{1,0:T(8,128)S(1)}, f32[8,192]{1,0:T(8,128)S(1)}, u32[]{:S(2)}, u32[]{:S(2)}) %collective-permute-start.14) | collective-permute-done | bytes 6176 | tf_op jit(solution)/shard_map/ppermute | solution.py:325
  13.9 2.9 %collective-permute-start.15 = (bf16[192,1024]{1,0:T(8,128)(2,1)S(1)}, bf16[192,1024]{1,0:T(8,128)(2,1)S(1)}, u32[]{:S(2)}, u32[]{:S(2)}) collective-permute-start(bf16[192,1024]{1,0:T(8,128)(2,1)S(1)} %copy-done.3), channel_id=1, source_target_pairs={{0,2},{1,3},{2,0},{3,1},{4,6},{5,7},{6,4},{7,5},{8,10},{9,11},{10,... | collective-permute-start | bytes 1179656 | tf_op jit(solution)/shard_map/ppermute | solution.py:325
  16.8 18.4 %collective-permute-done.31.grad_out = bf16[192,512]{1,0:T(8,128)(2,1)S(1)} collective-permute-done((bf16[192,512]{1,0:T(8,128)(2,1)S(1)}, bf16[192,512]{1,0:T(8,128)(2,1)S(1)}, u32[]{:S(2)}, u32[]{:S(2)}) %collective-permute-start.31) | collective-permute-done | bytes 196640 | tf_op jit(solution)/shard_map/ppermute | solution.py:325
  35.2 1.5 %collective-permute-start.3 = (bf16[64,2048]{1,0:T(8,128)(2,1)S(1)}, bf16[64,2048]{1,0:T(8,128)(2,1)S(1)}, u32[]{:S(2)}, u32[]{:S(2)}) collective-permute-start(bf16[64,2048]{1,0:T(8,128)(2,1)S(1)} %get-tuple-element.63), channel_id=1, source_target_pairs={{0,16},{4,20},{8,24},{12,28},{16,0},{20,4},{24,8},{28,12},{1,17},{... | collective-permute-start | bytes 786440 | tf_op jit(solution)/shard_map/ppermute | solution.py:329
  36.7 0.5 collective-permute-start.5
  37.2 2.4 %collective-permute-start.6 = (bf16[64,2048]{1,0:T(8,128)(2,1)S(1)}, bf16[64,2048]{1,0:T(8,128)(2,1)S(1)}, u32[]{:S(2)}, u32[]{:S(2)}) collective-permute-start(bf16[64,2048]{1,0:T(8,128)(2,1)S(1)} %get-tuple-element.66), channel_id=1, source_target_pairs={{0,28},{4,24},{8,20},{12,16},{16,12},{20,8},{24,4},{28,0},{1,29},{... | collective-permute-start | bytes 786440 | tf_op jit(solution)/shard_map/ppermute | solution.py:329
  39.6 0.9 shard_map.110
  40.5 0.6 copy-done
  41.1 0.6 copy-done.1
  41.7 0.6 copy-done.2
  42.4 12.3 %collective-permute-done.3.refs_4_.refs_12_.refs_20_ = bf16[64,2048]{1,0:T(8,128)(2,1)S(1)} collective-permute-done((bf16[64,2048]{1,0:T(8,128)(2,1)S(1)}, bf16[64,2048]{1,0:T(8,128)(2,1)S(1)}, u32[]{:S(2)}, u32[]{:S(2)}) %collective-permute-start.3) | collective-permute-done | bytes 262176 | tf_op jit(solution)/shard_map/ppermute | solution.py:329
  54.7 2.7 %collective-permute-done.4.refs_5_.refs_13_.refs_21_ = bf16[64,2048]{1,0:T(8,128)(2,1)S(1)} collective-permute-done((bf16[64,2048]{1,0:T(8,128)(2,1)S(1)}, bf16[64,2048]{1,0:T(8,128)(2,1)S(1)}, u32[]{:S(2)}, u32[]{:S(2)}) %collective-permute-start.4) | collective-permute-done | bytes 262176 | tf_op jit(solution)/shard_map/ppermute | solution.py:329
  57.4 0.5 collective-permute-start.25
  57.9 1.7 %collective-permute-start.26 = (bf16[64,512]{1,0:T(8,128)(2,1)}, bf16[64,512]{1,0:T(8,128)(2,1)S(1)}, u32[]{:S(2)}, u32[]{:S(2)}) collective-permute-start(bf16[64,512]{1,0:T(8,128)(2,1)} %get-tuple-element.94), channel_id=1, source_target_pairs={{0,12},{4,8},{8,4},{12,0},{16,28},{20,24},{24,20},{28,16},{1,13},{... | collective-permute-start | bytes 196616 | tf_op jit(solution)/shard_map/ppermute | solution.py:329
  59.6 0.8 shard_map.108
  60.4 1.5 %collective-permute-start.27 = (bf16[64,512]{1,0:T(8,128)(2,1)}, bf16[64,512]{1,0:T(8,128)(2,1)S(1)}, u32[]{:S(2)}, u32[]{:S(2)}) collective-permute-start(bf16[64,512]{1,0:T(8,128)(2,1)} %copy-done.2), channel_id=1, source_target_pairs={{0,16},{4,20},{8,24},{12,28},{16,0},{20,4},{24,8},{28,12},{1,17},{... | collective-permute-start | bytes 196616 | tf_op jit(solution)/shard_map/ppermute | solution.py:329
  61.9 1.2 collective-permute-start.29
  63.1 0.6 collective-permute-start.16
  63.8 1.5 %collective-permute-start.17 = (bf16[64,1024]{1,0:T(8,128)(2,1)S(1)}, bf16[64,1024]{1,0:T(8,128)(2,1)S(1)}, u32[]{:S(2)}, u32[]{:S(2)}) collective-permute-start(bf16[64,1024]{1,0:T(8,128)(2,1)S(1)} %get-tuple-element.84), channel_id=1, source_target_pairs={{0,8},{4,12},{8,0},{12,4},{16,24},{20,28},{24,16},{28,20},{1,9},{5... | collective-permute-start | bytes 393224 | tf_op jit(solution)/shard_map/ppermute | solution.py:329
  65.3 3.5 %shard_map.103 = (bf16[1024,1024]{1,0:T(8,128)(2,1)S(1)}, bf16[1024,1024]{1,0:T(8,128)(2,1)S(1)}) custom-call(s32[2]{0:T(128)S(1)} %pad_add_fusion.pos, bf16[1,2048,1024]{2,1,0:T(8,128)(2,1)} %w_in.3, bf16[1,2048,1024]{2,1,0:T(8,128)(2,1)} %w_out.3), custom_call_target="tpu_custom_call" | custom-call | bytes 12582912 | tf_op jit(solution)/shard_map/pallas_call | solution.py:281
  69.4 0.7 collective-permute-start.32
  70.1 1.3 collective-permute-start.33
  71.4 2.9 %shard_map.104 = (bf16[1024,512]{1,0:T(8,128)(2,1)S(1)}, bf16[1024,512]{1,0:T(8,128)(2,1)S(1)}) custom-call(bf16[1024,1024]{1,0:T(8,128)(2,1)S(1)} %get-tuple-element.57.w_in, bf16[64,2048]{1,0:T(8,128)(2,1)S(1)} %get-tuple-element.59.refs_0_.refs_8_.refs_16_, bf16[64,2048]{1,0:T(8,128)(2,1)S(1)} %collective-permute-done.refs_1_.refs_9_.refs_17_, ...), custom_call_target="tpu_custom_call" | custom-call | flops 1073741824 | bytes 6291456 | tf_op jit(solution)/shard_map/pallas_call | solution.py:281
  74.7 1.1 collective-permute-start.19
  75.9 0.7 collective-permute-start.20
  76.6 2.2 %collective-permute-start.21 = (bf16[64,1024]{1,0:T(8,128)(2,1)S(1)}, bf16[64,1024]{1,0:T(8,128)(2,1)S(1)}, u32[]{:S(2)}, u32[]{:S(2)}) collective-permute-start(bf16[64,1024]{1,0:T(8,128)(2,1)S(1)} %get-tuple-element.88), channel_id=1, source_target_pairs={{0,24},{4,28},{8,16},{12,20},{16,8},{20,12},{24,0},{28,4},{1,25},{... | collective-permute-start | bytes 393224 | tf_op jit(solution)/shard_map/ppermute | solution.py:329
  79.1 5.1 %shard_map.105 = (bf16[1024,512]{1,0:T(8,128)(2,1)S(1)}, f32[512,1024]{1,0:T(8,128)S(1)}, f32[1,512]{1,0:T(1,128)S(1)}) custom-call(bf16[1024,1024]{1,0:T(8,128)(2,1)S(1)} %get-tuple-element.57.w_in, bf16[1024,1024]{1,0:T(8,128)(2,1)S(1)} %get-tuple-element.58.w_out, bf16[1024,512]{1,0:T(8,128)(2,1)S(1)} %get-tuple-element.67.act.own, ...), custom_call_target="tpu_custom_call" | custom-call | flops 2147483648 | bytes 13633536 | tf_op jit(solution)/shard_map/pallas_call | solution.py:281
  84.2 1.6 %collective-permute-start.34 = (bf16[64,512]{1,0:T(8,128)(2,1)S(1)}, bf16[64,512]{1,0:T(8,128)(2,1)S(1)}, u32[]{:S(2)}, u32[]{:S(2)}) collective-permute-start(bf16[64,512]{1,0:T(8,128)(2,1)S(1)} %get-tuple-element.102), channel_id=1, source_target_pairs={{0,12},{4,8},{8,4},{12,0},{16,28},{20,24},{24,20},{28,16},{1,13},{... | collective-permute-start | bytes 196616 | tf_op jit(solution)/shard_map/ppermute | solution.py:329
  85.8 0.9 collective-permute-done.19.refs_4_.refs_12_
  86.7 1.1 collective-permute-start.35
  87.9 0.7 collective-permute-done.20.refs_5_.refs_13_
  88.5 1.6 %collective-permute-start.36 = (bf16[64,512]{1,0:T(8,128)(2,1)S(1)}, bf16[64,512]{1,0:T(8,128)(2,1)S(1)}, u32[]{:S(2)}, u32[]{:S(2)}) collective-permute-start(bf16[64,512]{1,0:T(8,128)(2,1)S(1)} %get-tuple-element.104), channel_id=1, source_target_pairs={{0,20},{4,16},{8,28},{12,24},{16,4},{20,0},{24,12},{28,8},{1,21},{... | collective-permute-start | bytes 196616 | tf_op jit(solution)/shard_map/ppermute | solution.py:329
  90.1 1.8 %collective-permute-start.37 = (bf16[64,512]{1,0:T(8,128)(2,1)S(1)}, bf16[64,512]{1,0:T(8,128)(2,1)S(1)}, u32[]{:S(2)}, u32[]{:S(2)}) collective-permute-start(bf16[64,512]{1,0:T(8,128)(2,1)S(1)} %get-tuple-element.105), channel_id=1, source_target_pairs={{0,24},{4,28},{8,16},{12,20},{16,8},{20,12},{24,0},{28,4},{1,25},{... | collective-permute-start | bytes 196616 | tf_op jit(solution)/shard_map/ppermute | solution.py:329
  92.2 2.7 %shard_map.109 = (bf16[1024,512]{1,0:T(8,128)(2,1)S(1)}, bf16[1024,512]{1,0:T(8,128)(2,1)S(1)}) custom-call(bf16[1024,1024]{1,0:T(8,128)(2,1)S(1)} %get-tuple-element.57.w_in, bf16[64,1024]{1,0:T(8,128)(2,1)S(1)} %get-tuple-element.82.refs_0_.refs_8_, bf16[64,1024]{1,0:T(8,128)(2,1)S(1)} %collective-permute-done.16.refs_1_.refs_9_, ...), custom_call_target="tpu_custom_call" | custom-call | flops 1073741824 | bytes 5242880 | tf_op jit(solution)/shard_map/pallas_call | solution.py:281
  95.3 1.5 collective-permute-done.38.refs_15_
  96.8 1.9 %shard_map.112.other = bf16[1024,512]{1,0:T(8,128)(2,1)S(1)} custom-call(bf16[1024,1024]{1,0:T(8,128)(2,1)S(1)} %get-tuple-element.58.w_out, bf16[1024,512]{1,0:T(8,128)(2,1)S(1)} %get-tuple-element.90.slope, bf16[64,512]{1,0:T(8,128)(2,1)S(1)} %get-tuple-element.91.refs_0_.refs_8_, bf16[64,512]{1,0:T(8,128)(2,1)S(1)} %collective-permute-done.24.refs_1_.refs_9_, ...), custom_call_target="tpu_custom_call" | custom-call | flops 1073741824 | bytes 5242880 | tf_op jit(solution)/shard_map/pallas_call | solution.py:281
  98.7 2.3 %shard_map.115 = bf16[512,768]{1,0:T(8,128)(2,1)S(1)} custom-call(s32[2]{0:T(128)S(1)} %pad_add_fusion.pos, bf16[1024,512]{1,0:T(8,128)(2,1)S(1)} %get-tuple-element.81.own, bf16[1024,512]{1,0:T(8,128)(2,1)S(1)} %shard_map.112.other, bf16[64,2048]{1,0:T(8,128)(2,1)S(1)} %get-tuple-element.59.refs_0_.refs_8_.refs_16_, ...), custom_call_target="tpu_custom_call" | custom-call | flops 805306368 | bytes 6029312 | tf_op jit(solution)/shard_map/pallas_call | solution.py:281
  101.1 7.7 %shard_map.106 = (bf16[64,1024]{1,0:T(8,128)(2,1)S(1)}, bf16[64,1024]{1,0:T(8,128)(2,1)S(1)}, bf16[64,1024]{1,0:T(8,128)(2,1)S(1)}, bf16[64,1024]{1,0:T(8,128)(2...) custom-call(s32[2]{0:T(128)S(1)} %pad_add_fusion.pos, ...), custom_call_target="tpu_custom_call" | custom-call | flops 3221225472 | bytes 17827840 | tf_op jit(solution)/shard_map/pallas_call | solution.py:281
  108.9 1.1 collective-permute-start.8
  110.0 0.7 collective-permute-start.9
  110.7 1.7 %shard_map.119 = bf16[512,512]{1,0:T(8,128)(2,1)S(1)} custom-call(s32[2]{0:T(128)S(1)} %pad_add_fusion.pos, bf16[1024,512]{1,0:T(8,128)(2,1)S(1)} %get-tuple-element.67.act.own, bf16[1024,512]{1,0:T(8,128)(2,1)S(1)} %get-tuple-element.107.other, bf16[64,2048]{1,0:T(8,128)(2,1)S(1)} %get-tuple-element.59.refs_0_.refs_8_.refs_16_, ...), custom_call_target="tpu_custom_call" | custom-call | flops 536870912 | bytes 5242880 | tf_op jit(solution)/shard_map/pallas_call | solution.py:281
  112.4 2.0 %collective-permute-start.42 = (bf16[512,512]{1,0:T(8,128)(2,1)S(1)}, bf16[512,512]{1,0:T(8,128)(2,1)S(1)}, u32[]{:S(2)}, u32[]{:S(2)}) collective-permute-start(bf16[512,512]{1,0:T(8,128)(2,1)S(1)} %shard_map.119), channel_id=1, source_target_pairs={{0,1},{1,0},{2,3},{3,2},{4,5},{5,4},{6,7},{7,6},{8,9},{9,8},{10,11... | collective-permute-start | bytes 1572872 | tf_op jit(solution)/shard_map/ppermute | solution.py:335
  114.5 1.7 %shard_map.118 = bf16[512,512]{1,0:T(8,128)(2,1)S(1)} custom-call(s32[2]{0:T(128)S(1)} %pad_add_fusion.pos, bf16[1024,512]{1,0:T(8,128)(2,1)S(1)} %get-tuple-element.67.act.own, bf16[1024,512]{1,0:T(8,128)(2,1)S(1)} %get-tuple-element.107.other, bf16[64,2048]{1,0:T(8,128)(2,1)S(1)} %get-tuple-element.59.refs_0_.refs_8_.refs_16_, ...), custom_call_target="tpu_custom_call" | custom-call | flops 536870912 | bytes 5242880 | tf_op jit(solution)/shard_map/pallas_call | solution.py:281
  116.3 1.4 collective-permute-start.10
  117.7 1.0 collective-permute-start.11
  118.7 4.0 %collective-permute-done.10.refs_4_ = bf16[64,1024]{1,0:T(8,128)(2,1)S(1)} collective-permute-done((bf16[64,1024]{1,0:T(8,128)(2,1)S(1)}, bf16[64,1024]{1,0:T(8,128)(2,1)S(1)}, u32[]{:S(2)}, u32[]{:S(2)}) %collective-permute-start.10) | collective-permute-done | bytes 131104 | tf_op jit(solution)/shard_map/ppermute | solution.py:329
  122.7 1.6 %collective-permute-start.12 = (bf16[64,1024]{1,0:T(8,128)(2,1)S(1)}, bf16[64,1024]{1,0:T(8,128)(2,1)S(1)}, u32[]{:S(2)}, u32[]{:S(2)}) collective-permute-start(bf16[64,1024]{1,0:T(8,128)(2,1)S(1)} %get-tuple-element.77), channel_id=1, source_target_pairs={{0,24},{4,28},{8,16},{12,20},{16,8},{20,12},{24,0},{28,4},{1,25},{... | collective-permute-start | bytes 393224 | tf_op jit(solution)/shard_map/ppermute | solution.py:329
  124.3 1.6 %collective-permute-start.13 = (bf16[64,1024]{1,0:T(8,128)(2,1)S(1)}, bf16[64,1024]{1,0:T(8,128)(2,1)S(1)}, u32[]{:S(2)}, u32[]{:S(2)}) collective-permute-start(bf16[64,1024]{1,0:T(8,128)(2,1)S(1)} %get-tuple-element.78), channel_id=1, source_target_pairs={{0,28},{4,24},{8,20},{12,16},{16,12},{20,8},{24,4},{28,0},{1,29},{... | collective-permute-start | bytes 393224 | tf_op jit(solution)/shard_map/ppermute | solution.py:329
  125.9 1.0 shard_map.114
  126.9 2.0 %collective-permute-done.12.refs_6_ = bf16[64,1024]{1,0:T(8,128)(2,1)S(1)} collective-permute-done((bf16[64,1024]{1,0:T(8,128)(2,1)S(1)}, bf16[64,1024]{1,0:T(8,128)(2,1)S(1)}, u32[]{:S(2)}, u32[]{:S(2)}) %collective-permute-start.12) | collective-permute-done | bytes 131104 | tf_op jit(solution)/shard_map/ppermute | solution.py:329
  129.0 1.2 collective-permute-start.39
  130.2 0.8 collective-permute-done.13.refs_7_
  131.0 1.6 %shard_map.107 = (bf16[192,1024]{1,0:T(8,128)(2,1)}, bf16[2,192]{1,0:T(2,128)(2,1)}) custom-call(f32[8,192]{1,0:T(8,128)S(1)} %get-tuple-element.56.meta, bf16[64,1024]{1,0:T(8,128)(2,1)S(1)} %get-tuple-element.71.refs_0_, bf16[64,1024]{1,0:T(8,128)(2,1)S(1)} %collective-permute-done.7.refs_1_, bf16[64,1024]{1,0:T(8,128)(2,1)S(1)} %collective-permute-done.8.refs_2_, ...), custom_call_target="tpu_custom_call" | custom-call | flops 201326592 | bytes 1448704 | tf_op jit(solution)/shard_map/pallas_call | solution.py:281
  132.5 2.9 %shard_map.113.before = f32[512,1024]{1,0:T(8,128)S(1)} custom-call(s32[2]{0:T(128)S(1)} %pad_add_fusion.pos, bf16[1024,512]{1,0:T(8,128)(2,1)S(1)} %get-tuple-element.81.own, bf16[1024,512]{1,0:T(8,128)(2,1)S(1)} %shard_map.112.other, bf16[64,2048]{1,0:T(8,128)(2,1)S(1)} %get-tuple-element.59.refs_0_.refs_8_.refs_16_, ...), custom_call_target="tpu_custom_call" | custom-call | flops 1073741824 | bytes 7340032 | tf_op jit(solution)/shard_map/pallas_call | solution.py:281
  135.5 2.5 %shard_map.120.refs_17_ = f32[1,512,1024]{2,1,0:T(8,128)} custom-call(s32[2]{0:T(128)S(1)} %pad_add_fusion.pos, bf16[1024,512]{1,0:T(8,128)(2,1)S(1)} %get-tuple-element.67.act.own, bf16[1024,512]{1,0:T(8,128)(2,1)S(1)} %get-tuple-element.107.other, bf16[64,2048]{1,0:T(8,128)(2,1)S(1)} %get-tuple-element.59.refs_0_.refs_8_.refs_16_, ...), custom_call_target="tpu_custom_call" | custom-call | flops 536870912 | bytes 7340032 | tf_op jit(solution)/shard_map/pallas_call | solution.py:281
  138.0 5.9 %collective-permute-done.41.refs_16_ = bf16[512,512]{1,0:T(8,128)(2,1)S(1)} collective-permute-done((bf16[512,512]{1,0:T(8,128)(2,1)S(1)}, bf16[512,512]{1,0:T(8,128)(2,1)S(1)}, u32[]{:S(2)}, u32[]{:S(2)}) %collective-permute-start.41) | collective-permute-done | bytes 524320 | tf_op jit(solution)/shard_map/ppermute | solution.py:335
  144.0 2.5 %shard_map.121 = f32[1,512,1024]{2,1,0:T(8,128)} custom-call(s32[2]{0:T(128)S(1)} %pad_add_fusion.pos, bf16[1024,512]{1,0:T(8,128)(2,1)S(1)} %get-tuple-element.67.act.own, bf16[1024,512]{1,0:T(8,128)(2,1)S(1)} %get-tuple-element.107.other, bf16[64,2048]{1,0:T(8,128)(2,1)S(1)} %get-tuple-element.59.refs_0_.refs_8_.refs_16_, ...), custom_call_target="tpu_custom_call", output_to_operand_aliasing={{}: (20, {})} | custom-call | flops 536870912 | bytes 9437184 | tf_op jit(solution)/shard_map/pallas_call | solution.py:281
  146.5 1.8 %shard_map.116.refs_1_ = f32[1,512,1024]{2,1,0:T(8,128)} custom-call(f32[512,1024]{1,0:T(8,128)S(1)} %shard_map.113.before, bf16[512,768]{1,0:T(8,128)(2,1)S(1)} %collective-permute-done.40.refs_0_), custom_call_target="tpu_custom_call" | custom-call | bytes 4980736 | tf_op jit(solution)/shard_map/pallas_call | solution.py:281
  148.3 0.8 shard_map.117
  (52 shorter events, 2.9 us)
Async XLA Ops:
  0.6 13.3 %copy-start.3 = (bf16[192,1024]{1,0:T(8,128)(2,1)S(1)}, bf16[192,1024]{1,0:T(8,128)(2,1)}, u32[]{:S(2)}) copy-start(bf16[192,1024]{1,0:T(8,128)(2,1)} %tokens.1) | copy-start | bytes 1179652
  1.7 12.2 %collective-permute-start.23 = (bf16[192,512]{1,0:T(8,128)(2,1)S(1)}, bf16[192,512]{1,0:T(8,128)(2,1)S(1)}, u32[]{:S(2)}, u32[]{:S(2)}) collective-permute-start(bf16[192,512]{1,0:T(8,128)(2,1)S(1)} %get-tuple-element.109), channel_id=1, source_target_pairs={{0,2},{1,3},{2,0},{3,1},{4,6},{5,7},{6,4},{7,5},{8,10},{9,11},{10,... | collective-permute-start | bytes 589832 | tf_op jit(solution)/shard_map/ppermute | solution.py:325
  6.5 30.2 %collective-permute-start = (bf16[64,2048]{1,0:T(8,128)(2,1)S(1)}, bf16[64,2048]{1,0:T(8,128)(2,1)S(1)}, u32[]{:S(2)}, u32[]{:S(2)}) collective-permute-start(bf16[64,2048]{1,0:T(8,128)(2,1)S(1)} %get-tuple-element.60), channel_id=1, source_target_pairs={{0,4},{4,0},{8,12},{12,8},{16,20},{20,16},{24,28},{28,24},{1,5},{5... | collective-permute-start | bytes 786440 | tf_op jit(solution)/shard_map/ppermute | solution.py:329
  6.6 7.3 %collective-permute-start.14 = (f32[8,192]{1,0:T(8,128)S(1)}, f32[8,192]{1,0:T(8,128)S(1)}, u32[]{:S(2)}, u32[]{:S(2)}) collective-permute-start(f32[8,192]{1,0:T(8,128)S(1)} %get-tuple-element.56.meta), channel_id=1, source_target_pairs={{0,2},{1,3},{2,0},{3,1},{4,6},{5,7},{6,4},{7,5},{8,10},{9,11},{10,... | collective-permute-start | bytes 18440 | tf_op jit(solution)/shard_map/ppermute | solution.py:325
  7.0 29.7 %collective-permute-start.1 = (bf16[64,2048]{1,0:T(8,128)(2,1)S(1)}, bf16[64,2048]{1,0:T(8,128)(2,1)S(1)}, u32[]{:S(2)}, u32[]{:S(2)}) collective-permute-start(bf16[64,2048]{1,0:T(8,128)(2,1)S(1)} %get-tuple-element.61), channel_id=1, source_target_pairs={{0,8},{4,12},{8,0},{12,4},{16,24},{20,28},{24,16},{28,20},{1,9},{5... | collective-permute-start | bytes 786440 | tf_op jit(solution)/shard_map/ppermute | solution.py:329
  7.3 30.0 %collective-permute-start.2 = (bf16[64,2048]{1,0:T(8,128)(2,1)S(1)}, bf16[64,2048]{1,0:T(8,128)(2,1)S(1)}, u32[]{:S(2)}, u32[]{:S(2)}) collective-permute-start(bf16[64,2048]{1,0:T(8,128)(2,1)S(1)} %get-tuple-element.62), channel_id=1, source_target_pairs={{0,12},{4,8},{8,4},{12,0},{16,28},{20,24},{24,20},{28,16},{1,13},{... | collective-permute-start | bytes 786440 | tf_op jit(solution)/shard_map/ppermute | solution.py:329
  13.9 21.3 %collective-permute-start.31 = (bf16[192,512]{1,0:T(8,128)(2,1)S(1)}, bf16[192,512]{1,0:T(8,128)(2,1)S(1)}, u32[]{:S(2)}, u32[]{:S(2)}) collective-permute-start(bf16[192,512]{1,0:T(8,128)(2,1)S(1)} %get-tuple-element.108), channel_id=1, source_target_pairs={{0,2},{1,3},{2,0},{3,1},{4,6},{5,7},{6,4},{7,5},{8,10},{9,11},{10,... | collective-permute-start | bytes 589832 | tf_op jit(solution)/shard_map/ppermute | solution.py:325
  13.9 44.0 %collective-permute-start.15 = (bf16[192,1024]{1,0:T(8,128)(2,1)S(1)}, bf16[192,1024]{1,0:T(8,128)(2,1)S(1)}, u32[]{:S(2)}, u32[]{:S(2)}) collective-permute-start(bf16[192,1024]{1,0:T(8,128)(2,1)S(1)} %copy-done.3), channel_id=1, source_target_pairs={{0,2},{1,3},{2,0},{3,1},{4,6},{5,7},{6,4},{7,5},{8,10},{9,11},{10,... | collective-permute-start | bytes 1179656 | tf_op jit(solution)/shard_map/ppermute | solution.py:325
  35.2 19.5 %collective-permute-start.3 = (bf16[64,2048]{1,0:T(8,128)(2,1)S(1)}, bf16[64,2048]{1,0:T(8,128)(2,1)S(1)}, u32[]{:S(2)}, u32[]{:S(2)}) collective-permute-start(bf16[64,2048]{1,0:T(8,128)(2,1)S(1)} %get-tuple-element.63), channel_id=1, source_target_pairs={{0,16},{4,20},{8,24},{12,28},{16,0},{20,4},{24,8},{28,12},{1,17},{... | collective-permute-start | bytes 786440 | tf_op jit(solution)/shard_map/ppermute | solution.py:329
  36.7 20.7 %collective-permute-start.4 = (bf16[64,2048]{1,0:T(8,128)(2,1)S(1)}, bf16[64,2048]{1,0:T(8,128)(2,1)S(1)}, u32[]{:S(2)}, u32[]{:S(2)}) collective-permute-start(bf16[64,2048]{1,0:T(8,128)(2,1)S(1)} %get-tuple-element.64), channel_id=1, source_target_pairs={{0,20},{4,16},{8,28},{12,24},{16,4},{20,0},{24,12},{28,8},{1,21},{... | collective-permute-start | bytes 786440 | tf_op jit(solution)/shard_map/ppermute | solution.py:329
  36.7 23.6 %collective-permute-start.5 = (bf16[64,2048]{1,0:T(8,128)(2,1)S(1)}, bf16[64,2048]{1,0:T(8,128)(2,1)S(1)}, u32[]{:S(2)}, u32[]{:S(2)}) collective-permute-start(bf16[64,2048]{1,0:T(8,128)(2,1)S(1)} %get-tuple-element.65), channel_id=1, source_target_pairs={{0,24},{4,28},{8,16},{12,20},{16,8},{20,12},{24,0},{28,4},{1,25},{... | collective-permute-start | bytes 786440 | tf_op jit(solution)/shard_map/ppermute | solution.py:329
  37.2 24.7 %collective-permute-start.6 = (bf16[64,2048]{1,0:T(8,128)(2,1)S(1)}, bf16[64,2048]{1,0:T(8,128)(2,1)S(1)}, u32[]{:S(2)}, u32[]{:S(2)}) collective-permute-start(bf16[64,2048]{1,0:T(8,128)(2,1)S(1)} %get-tuple-element.66), channel_id=1, source_target_pairs={{0,28},{4,24},{8,20},{12,16},{16,12},{20,8},{24,4},{28,0},{1,29},{... | collective-permute-start | bytes 786440 | tf_op jit(solution)/shard_map/ppermute | solution.py:329
  40.5 0.6 copy-start
  41.1 0.6 copy-start.1
  41.7 0.6 copy-start.2
  54.7 7.2 %collective-permute-start.24 = (bf16[64,512]{1,0:T(8,128)(2,1)}, bf16[64,512]{1,0:T(8,128)(2,1)S(1)}, u32[]{:S(2)}, u32[]{:S(2)}) collective-permute-start(bf16[64,512]{1,0:T(8,128)(2,1)} %get-tuple-element.92), channel_id=1, source_target_pairs={{0,4},{4,0},{8,12},{12,8},{16,20},{20,16},{24,28},{28,24},{1,5},{5... | collective-permute-start | bytes 196616 | tf_op jit(solution)/shard_map/ppermute | solution.py:329
  57.4 5.7 %collective-permute-start.25 = (bf16[64,512]{1,0:T(8,128)(2,1)}, bf16[64,512]{1,0:T(8,128)(2,1)S(1)}, u32[]{:S(2)}, u32[]{:S(2)}) collective-permute-start(bf16[64,512]{1,0:T(8,128)(2,1)} %get-tuple-element.93), channel_id=1, source_target_pairs={{0,8},{4,12},{8,0},{12,4},{16,24},{20,28},{24,16},{28,20},{1,9},{5... | collective-permute-start | bytes 196616 | tf_op jit(solution)/shard_map/ppermute | solution.py:329
  57.9 5.8 %collective-permute-start.26 = (bf16[64,512]{1,0:T(8,128)(2,1)}, bf16[64,512]{1,0:T(8,128)(2,1)S(1)}, u32[]{:S(2)}, u32[]{:S(2)}) collective-permute-start(bf16[64,512]{1,0:T(8,128)(2,1)} %get-tuple-element.94), channel_id=1, source_target_pairs={{0,12},{4,8},{8,4},{12,0},{16,28},{20,24},{24,20},{28,16},{1,13},{... | collective-permute-start | bytes 196616 | tf_op jit(solution)/shard_map/ppermute | solution.py:329
  60.4 8.8 %collective-permute-start.27 = (bf16[64,512]{1,0:T(8,128)(2,1)}, bf16[64,512]{1,0:T(8,128)(2,1)S(1)}, u32[]{:S(2)}, u32[]{:S(2)}) collective-permute-start(bf16[64,512]{1,0:T(8,128)(2,1)} %copy-done.2), channel_id=1, source_target_pairs={{0,16},{4,20},{8,24},{12,28},{16,0},{20,4},{24,8},{28,12},{1,17},{... | collective-permute-start | bytes 196616 | tf_op jit(solution)/shard_map/ppermute | solution.py:329
  61.9 7.5 %collective-permute-start.28 = (bf16[64,512]{1,0:T(8,128)(2,1)}, bf16[64,512]{1,0:T(8,128)(2,1)S(1)}, u32[]{:S(2)}, u32[]{:S(2)}) collective-permute-start(bf16[64,512]{1,0:T(8,128)(2,1)} %copy-done.1), channel_id=1, source_target_pairs={{0,20},{4,16},{8,28},{12,24},{16,4},{20,0},{24,12},{28,8},{1,21},{... | collective-permute-start | bytes 196616 | tf_op jit(solution)/shard_map/ppermute | solution.py:329
  61.9 8.2 %collective-permute-start.29 = (bf16[64,512]{1,0:T(8,128)(2,1)}, bf16[64,512]{1,0:T(8,128)(2,1)S(1)}, u32[]{:S(2)}, u32[]{:S(2)}) collective-permute-start(bf16[64,512]{1,0:T(8,128)(2,1)} %copy-done), channel_id=1, source_target_pairs={{0,24},{4,28},{8,16},{12,20},{16,8},{20,12},{24,0},{28,4},{1,25},{... | collective-permute-start | bytes 196616 | tf_op jit(solution)/shard_map/ppermute | solution.py:329
  63.1 13.4 %collective-permute-start.16 = (bf16[64,1024]{1,0:T(8,128)(2,1)S(1)}, bf16[64,1024]{1,0:T(8,128)(2,1)S(1)}, u32[]{:S(2)}, u32[]{:S(2)}) collective-permute-start(bf16[64,1024]{1,0:T(8,128)(2,1)S(1)} %get-tuple-element.83), channel_id=1, source_target_pairs={{0,4},{4,0},{8,12},{12,8},{16,20},{20,16},{24,28},{28,24},{1,5},{5... | collective-permute-start | bytes 393224 | tf_op jit(solution)/shard_map/ppermute | solution.py:329
  63.8 15.0 %collective-permute-start.17 = (bf16[64,1024]{1,0:T(8,128)(2,1)S(1)}, bf16[64,1024]{1,0:T(8,128)(2,1)S(1)}, u32[]{:S(2)}, u32[]{:S(2)}) collective-permute-start(bf16[64,1024]{1,0:T(8,128)(2,1)S(1)} %get-tuple-element.84), channel_id=1, source_target_pairs={{0,8},{4,12},{8,0},{12,4},{16,24},{20,28},{24,16},{28,20},{1,9},{5... | collective-permute-start | bytes 393224 | tf_op jit(solution)/shard_map/ppermute | solution.py:329
  69.2 5.4 %collective-permute-start.30 = (bf16[64,512]{1,0:T(8,128)(2,1)S(1)}, bf16[64,512]{1,0:T(8,128)(2,1)S(1)}, u32[]{:S(2)}, u32[]{:S(2)}) collective-permute-start(bf16[64,512]{1,0:T(8,128)(2,1)S(1)} %get-tuple-element.98), channel_id=1, source_target_pairs={{0,28},{4,24},{8,20},{12,16},{16,12},{20,8},{24,4},{28,0},{1,29},{... | collective-permute-start | bytes 196616 | tf_op jit(solution)/shard_map/ppermute | solution.py:329
  69.4 5.3 %collective-permute-start.32 = (bf16[64,512]{1,0:T(8,128)(2,1)S(1)}, bf16[64,512]{1,0:T(8,128)(2,1)S(1)}, u32[]{:S(2)}, u32[]{:S(2)}) collective-permute-start(bf16[64,512]{1,0:T(8,128)(2,1)S(1)} %get-tuple-element.100), channel_id=1, source_target_pairs={{0,4},{4,0},{8,12},{12,8},{16,20},{20,16},{24,28},{28,24},{1,5},{5... | collective-permute-start | bytes 196616 | tf_op jit(solution)/shard_map/ppermute | solution.py:329
  70.1 5.8 %collective-permute-start.33 = (bf16[64,512]{1,0:T(8,128)(2,1)S(1)}, bf16[64,512]{1,0:T(8,128)(2,1)S(1)}, u32[]{:S(2)}, u32[]{:S(2)}) collective-permute-start(bf16[64,512]{1,0:T(8,128)(2,1)S(1)} %get-tuple-element.101), channel_id=1, source_target_pairs={{0,8},{4,12},{8,0},{12,4},{16,24},{20,28},{24,16},{28,20},{1,9},{5... | collective-permute-start | bytes 196616 | tf_op jit(solution)/shard_map/ppermute | solution.py:329
  74.5 9.7 %collective-permute-start.18 = (bf16[64,1024]{1,0:T(8,128)(2,1)S(1)}, bf16[64,1024]{1,0:T(8,128)(2,1)S(1)}, u32[]{:S(2)}, u32[]{:S(2)}) collective-permute-start(bf16[64,1024]{1,0:T(8,128)(2,1)S(1)} %get-tuple-element.85), channel_id=1, source_target_pairs={{0,12},{4,8},{8,4},{12,0},{16,28},{20,24},{24,20},{28,16},{1,13},{... | collective-permute-start | bytes 393224 | tf_op jit(solution)/shard_map/ppermute | solution.py:329
  74.7 12.0 %collective-permute-start.19 = (bf16[64,1024]{1,0:T(8,128)(2,1)S(1)}, bf16[64,1024]{1,0:T(8,128)(2,1)S(1)}, u32[]{:S(2)}, u32[]{:S(2)}) collective-permute-start(bf16[64,1024]{1,0:T(8,128)(2,1)S(1)} %get-tuple-element.86), channel_id=1, source_target_pairs={{0,16},{4,20},{8,24},{12,28},{16,0},{20,4},{24,8},{28,12},{1,17},{... | collective-permute-start | bytes 393224 | tf_op jit(solution)/shard_map/ppermute | solution.py:329
  75.9 12.6 %collective-permute-start.20 = (bf16[64,1024]{1,0:T(8,128)(2,1)S(1)}, bf16[64,1024]{1,0:T(8,128)(2,1)S(1)}, u32[]{:S(2)}, u32[]{:S(2)}) collective-permute-start(bf16[64,1024]{1,0:T(8,128)(2,1)S(1)} %get-tuple-element.87), channel_id=1, source_target_pairs={{0,20},{4,16},{8,28},{12,24},{16,4},{20,0},{24,12},{28,8},{1,21},{... | collective-permute-start | bytes 393224 | tf_op jit(solution)/shard_map/ppermute | solution.py:329
  76.6 13.5 %collective-permute-start.21 = (bf16[64,1024]{1,0:T(8,128)(2,1)S(1)}, bf16[64,1024]{1,0:T(8,128)(2,1)S(1)}, u32[]{:S(2)}, u32[]{:S(2)}) collective-permute-start(bf16[64,1024]{1,0:T(8,128)(2,1)S(1)} %get-tuple-element.88), channel_id=1, source_target_pairs={{0,24},{4,28},{8,16},{12,20},{16,8},{20,12},{24,0},{28,4},{1,25},{... | collective-permute-start | bytes 393224 | tf_op jit(solution)/shard_map/ppermute | solution.py:329
  78.7 13.1 %collective-permute-start.22 = (bf16[64,1024]{1,0:T(8,128)(2,1)S(1)}, bf16[64,1024]{1,0:T(8,128)(2,1)S(1)}, u32[]{:S(2)}, u32[]{:S(2)}) collective-permute-start(bf16[64,1024]{1,0:T(8,128)(2,1)S(1)} %get-tuple-element.89), channel_id=1, source_target_pairs={{0,28},{4,24},{8,20},{12,16},{16,12},{20,8},{24,4},{28,0},{1,29},{... | collective-permute-start | bytes 393224 | tf_op jit(solution)/shard_map/ppermute | solution.py:329
  84.2 10.7 %collective-permute-start.34 = (bf16[64,512]{1,0:T(8,128)(2,1)S(1)}, bf16[64,512]{1,0:T(8,128)(2,1)S(1)}, u32[]{:S(2)}, u32[]{:S(2)}) collective-permute-start(bf16[64,512]{1,0:T(8,128)(2,1)S(1)} %get-tuple-element.102), channel_id=1, source_target_pairs={{0,12},{4,8},{8,4},{12,0},{16,28},{20,24},{24,20},{28,16},{1,13},{... | collective-permute-start | bytes 196616 | tf_op jit(solution)/shard_map/ppermute | solution.py:329
  86.7 8.2 %collective-permute-start.35 = (bf16[64,512]{1,0:T(8,128)(2,1)S(1)}, bf16[64,512]{1,0:T(8,128)(2,1)S(1)}, u32[]{:S(2)}, u32[]{:S(2)}) collective-permute-start(bf16[64,512]{1,0:T(8,128)(2,1)S(1)} %get-tuple-element.103), channel_id=1, source_target_pairs={{0,16},{4,20},{8,24},{12,28},{16,0},{20,4},{24,8},{28,12},{1,17},{... | collective-permute-start | bytes 196616 | tf_op jit(solution)/shard_map/ppermute | solution.py:329
  88.5 6.4 %collective-permute-start.36 = (bf16[64,512]{1,0:T(8,128)(2,1)S(1)}, bf16[64,512]{1,0:T(8,128)(2,1)S(1)}, u32[]{:S(2)}, u32[]{:S(2)}) collective-permute-start(bf16[64,512]{1,0:T(8,128)(2,1)S(1)} %get-tuple-element.104), channel_id=1, source_target_pairs={{0,20},{4,16},{8,28},{12,24},{16,4},{20,0},{24,12},{28,8},{1,21},{... | collective-permute-start | bytes 196616 | tf_op jit(solution)/shard_map/ppermute | solution.py:329
  90.1 5.2 %collective-permute-start.37 = (bf16[64,512]{1,0:T(8,128)(2,1)S(1)}, bf16[64,512]{1,0:T(8,128)(2,1)S(1)}, u32[]{:S(2)}, u32[]{:S(2)}) collective-permute-start(bf16[64,512]{1,0:T(8,128)(2,1)S(1)} %get-tuple-element.105), channel_id=1, source_target_pairs={{0,24},{4,28},{8,16},{12,20},{16,8},{20,12},{24,0},{28,4},{1,25},{... | collective-permute-start | bytes 196616 | tf_op jit(solution)/shard_map/ppermute | solution.py:329
  91.9 4.9 %collective-permute-start.38 = (bf16[64,512]{1,0:T(8,128)(2,1)S(1)}, bf16[64,512]{1,0:T(8,128)(2,1)S(1)}, u32[]{:S(2)}, u32[]{:S(2)}) collective-permute-start(bf16[64,512]{1,0:T(8,128)(2,1)S(1)} %get-tuple-element.106), channel_id=1, source_target_pairs={{0,28},{4,24},{8,20},{12,16},{16,12},{20,8},{24,4},{28,0},{1,29},{... | collective-permute-start | bytes 196616 | tf_op jit(solution)/shard_map/ppermute | solution.py:329
  101.0 45.5 %collective-permute-start.40 = (bf16[512,768]{1,0:T(8,128)(2,1)S(1)}, bf16[512,768]{1,0:T(8,128)(2,1)S(1)}, u32[]{:S(2)}, u32[]{:S(2)}) collective-permute-start(bf16[512,768]{1,0:T(8,128)(2,1)S(1)} %shard_map.115), channel_id=1, source_target_pairs={{0,1},{1,0},{2,3},{3,2},{4,5},{5,4},{6,7},{7,6},{8,9},{9,8},{10,11... | collective-permute-start | bytes 2359304 | tf_op jit(solution)/shard_map/ppermute | solution.py:335
  108.8 7.4 %collective-permute-start.7 = (bf16[64,1024]{1,0:T(8,128)(2,1)S(1)}, bf16[64,1024]{1,0:T(8,128)(2,1)S(1)}, u32[]{:S(2)}, u32[]{:S(2)}) collective-permute-start(bf16[64,1024]{1,0:T(8,128)(2,1)S(1)} %get-tuple-element.72), channel_id=1, source_target_pairs={{0,4},{4,0},{8,12},{12,8},{16,20},{20,16},{24,28},{28,24},{1,5},{5... | collective-permute-start | bytes 393224 | tf_op jit(solution)/shard_map/ppermute | solution.py:329
  108.9 7.4 %collective-permute-start.8 = (bf16[64,1024]{1,0:T(8,128)(2,1)S(1)}, bf16[64,1024]{1,0:T(8,128)(2,1)S(1)}, u32[]{:S(2)}, u32[]{:S(2)}) collective-permute-start(bf16[64,1024]{1,0:T(8,128)(2,1)S(1)} %get-tuple-element.73), channel_id=1, source_target_pairs={{0,8},{4,12},{8,0},{12,4},{16,24},{20,28},{24,16},{28,20},{1,9},{5... | collective-permute-start | bytes 393224 | tf_op jit(solution)/shard_map/ppermute | solution.py:329
  110.0 7.7 %collective-permute-start.9 = (bf16[64,1024]{1,0:T(8,128)(2,1)S(1)}, bf16[64,1024]{1,0:T(8,128)(2,1)S(1)}, u32[]{:S(2)}, u32[]{:S(2)}) collective-permute-start(bf16[64,1024]{1,0:T(8,128)(2,1)S(1)} %get-tuple-element.74), channel_id=1, source_target_pairs={{0,12},{4,8},{8,4},{12,0},{16,28},{20,24},{24,20},{28,16},{1,13},{... | collective-permute-start | bytes 393224 | tf_op jit(solution)/shard_map/ppermute | solution.py:329
  112.4 23.0 %collective-permute-start.42 = (bf16[512,512]{1,0:T(8,128)(2,1)S(1)}, bf16[512,512]{1,0:T(8,128)(2,1)S(1)}, u32[]{:S(2)}, u32[]{:S(2)}) collective-permute-start(bf16[512,512]{1,0:T(8,128)(2,1)S(1)} %shard_map.119), channel_id=1, source_target_pairs={{0,1},{1,0},{2,3},{3,2},{4,5},{5,4},{6,7},{7,6},{8,9},{9,8},{10,11... | collective-permute-start | bytes 1572872 | tf_op jit(solution)/shard_map/ppermute | solution.py:335
  116.2 27.8 %collective-permute-start.41 = (bf16[512,512]{1,0:T(8,128)(2,1)S(1)}, bf16[512,512]{1,0:T(8,128)(2,1)S(1)}, u32[]{:S(2)}, u32[]{:S(2)}) collective-permute-start(bf16[512,512]{1,0:T(8,128)(2,1)S(1)} %shard_map.118), channel_id=1, source_target_pairs={{0,1},{1,0},{2,3},{3,2},{4,5},{5,4},{6,7},{7,6},{8,9},{9,8},{10,11... | collective-permute-start | bytes 1572872 | tf_op jit(solution)/shard_map/ppermute | solution.py:335
  116.3 6.4 %collective-permute-start.10 = (bf16[64,1024]{1,0:T(8,128)(2,1)S(1)}, bf16[64,1024]{1,0:T(8,128)(2,1)S(1)}, u32[]{:S(2)}, u32[]{:S(2)}) collective-permute-start(bf16[64,1024]{1,0:T(8,128)(2,1)S(1)} %get-tuple-element.75), channel_id=1, source_target_pairs={{0,16},{4,20},{8,24},{12,28},{16,0},{20,4},{24,8},{28,12},{1,17},{... | collective-permute-start | bytes 393224 | tf_op jit(solution)/shard_map/ppermute | solution.py:329
  117.7 6.6 %collective-permute-start.11 = (bf16[64,1024]{1,0:T(8,128)(2,1)S(1)}, bf16[64,1024]{1,0:T(8,128)(2,1)S(1)}, u32[]{:S(2)}, u32[]{:S(2)}) collective-permute-start(bf16[64,1024]{1,0:T(8,128)(2,1)S(1)} %get-tuple-element.76), channel_id=1, source_target_pairs={{0,20},{4,16},{8,28},{12,24},{16,4},{20,0},{24,12},{28,8},{1,21},{... | collective-permute-start | bytes 393224 | tf_op jit(solution)/shard_map/ppermute | solution.py:329
  122.7 6.3 %collective-permute-start.12 = (bf16[64,1024]{1,0:T(8,128)(2,1)S(1)}, bf16[64,1024]{1,0:T(8,128)(2,1)S(1)}, u32[]{:S(2)}, u32[]{:S(2)}) collective-permute-start(bf16[64,1024]{1,0:T(8,128)(2,1)S(1)} %get-tuple-element.77), channel_id=1, source_target_pairs={{0,24},{4,28},{8,16},{12,20},{16,8},{20,12},{24,0},{28,4},{1,25},{... | collective-permute-start | bytes 393224 | tf_op jit(solution)/shard_map/ppermute | solution.py:329
  124.3 6.7 %collective-permute-start.13 = (bf16[64,1024]{1,0:T(8,128)(2,1)S(1)}, bf16[64,1024]{1,0:T(8,128)(2,1)S(1)}, u32[]{:S(2)}, u32[]{:S(2)}) collective-permute-start(bf16[64,1024]{1,0:T(8,128)(2,1)S(1)} %get-tuple-element.78), channel_id=1, source_target_pairs={{0,28},{4,24},{8,20},{12,16},{16,12},{20,8},{24,4},{28,0},{1,29},{... | collective-permute-start | bytes 393224 | tf_op jit(solution)/shard_map/ppermute | solution.py:329
  129.0 19.4 %collective-permute-start.39 = (bf16[512,256]{1,0:T(8,128)(2,1)S(1)}, bf16[512,256]{1,0:T(8,128)(2,1)S(1)}, u32[]{:S(2)}, u32[]{:S(2)}) collective-permute-start(bf16[512,256]{1,0:T(8,128)(2,1)S(1)} %shard_map.114), channel_id=1, source_target_pairs={{0,1},{1,0},{2,3},{3,2},{4,5},{5,4},{6,7},{7,6},{8,9},{9,8},{10,11... | collective-permute-start | bytes 786440 | tf_op jit(solution)/shard_map/ppermute | solution.py:335

commit v4 on v3

--- a/solution.py
+++ b/solution.py
@@ -98,8 +98,8 @@
 
 
 def load_kernel(pos, w_in, w_out, in_half, out_half):
-    in_half[...] = w_in[0]
-    out_half[...] = w_out[0]
+    in_half[...] = w_in[...]
+    out_half[...] = w_out[...]
 
 
 def send_x_kernel(experts, block, meta, tokens, *outs):
@@ -107,50 +107,61 @@
     place(jnp.where(first | second, 1.0, 0.0).astype(bf16), tokens, outs, block)
 
 
-def send_s_kernel(experts, block, meta, grad_out, *outs):
+def send_s_kernel(experts, block, meta, grad_out, *refs):
     first, second = picks(meta[0:1, :], meta[1:2, :], experts * block)
     weighted = jnp.where(first, meta[2:3, :], jnp.where(second, meta[3:4, :], 0.0))
-    place(weighted.astype(bf16), grad_out, outs, block)
-
-
-def accumulate(ref, more):
-    @pl.when(pl.program_id(0) == 0)
-    def _():
-        ref[...] = more
-
-    @pl.when(pl.program_id(0) > 0)
-    def _():
-        ref[...] += more
+    place(weighted.astype(bf16), grad_out, refs[-experts:], block)
 
 
 def gate_sums(active, up):
     return jnp.sum(active.astype(f32) * up, axis=0, keepdims=True)
 
 
-def act_kernel(experts, w_in, *refs):
+def act_rows(weights, x, act, slope, at, size):
+    active, derivative = gelu_slope(dot(weights, x, NT))
+    act[at : at + size, :] = active.astype(bf16)
+    slope[at : at + size, :] = derivative.astype(bf16)
+
+
+def act_kernel(left, w_in, *refs):
     blocks, (act, slope) = refs[:-2], refs[-2:]
-    active, derivative = gelu_slope(dot(w_in[...], stack(blocks, experts), NT))
-    act[...] = active.astype(bf16)
-    slope[...] = derivative.astype(bf16)
-
-
-def other_grad_kernel(experts, w_out, slope, *refs):
-    up = dot(w_out[...], stack(refs[:-1], experts), NT)
-    refs[-1][...] = (up * slope[...].astype(f32)).astype(bf16)
-
-
-def own_grad_kernel(experts, w_in, w_out, act, slope, *refs):
+    x = cut(blocks, left, w_in.shape[1])
+    for at, size in steps(w_in.shape[0], 256):
+        act_rows(w_in[at : at + size, :], x, act, slope, at, size)
+
+
+def far_act_kernel(experts, pos, w_in, *refs):
+    act_rows(w_in[...], stack(refs[:-2], experts), *refs[-2:], 0, w_in.shape[0])
+
+
+def other_grad_kernel(experts, lefts, w_out, slope, *refs):
+    run = w_out.shape[1] // 2
+    s = jnp.concatenate(
+        [cut(refs[:experts], lefts[0], run), cut(refs[experts : 2 * experts], lefts[1], run)], axis=1
+    )
+    for at, size in steps(w_out.shape[0], 256):
+        up = dot(w_out[at : at + size, :], s, NT)
+        refs[-1][at : at + size, :] = (up * slope[at : at + size, :].astype(f32)).astype(bf16)
+
+
+def own_grad_kernel(experts, lefts, w_in, w_out, act, slope, *refs):
     blocks, (grad, total, gates) = refs[:-3], refs[-3:]
-    up = dot(w_out[...], stack(blocks, experts), NT)
-    accumulate(gates, gate_sums(act[...], up))
-    hidden_grad = (up * slope[...].astype(f32)).astype(bf16)
-    grad[...] = hidden_grad
-    accumulate(total, dot(hidden_grad, w_in[...], TN))
-
-
-def far_kernel(experts, block, capacity, pos, w_in, w_out, near_total, near_gates, *refs):
-    x_blocks, s_blocks = refs[:experts], refs[experts : 3 * experts]
-    outs, (total, gates) = refs[3 * experts : -2], refs[-2:]
+    run = w_out.shape[1] // 2
+    s = jnp.concatenate(
+        [cut(blocks[:experts], lefts[0], run), cut(blocks[experts:], lefts[1], run)], axis=1
+    )
+    sums = 0.0
+    for at, size in steps(w_out.shape[0], 256):
+        up = dot(w_out[at : at + size, :], s, NT)
+        sums = sums + gate_sums(act[at : at + size, :], up)
+        grad[at : at + size, :] = (up * slope[at : at + size, :].astype(f32)).astype(bf16)
+    gates[...] = sums
+    for at, size in steps(w_in.shape[1], 256):
+        total[:, at : at + size] = dot(grad[...], w_in[:, at : at + size], TN)
+
+
+def far_kernel(experts, block, capacity, pos, w_in, w_out, act, slope, near_total, near_gates, *refs):
+    blocks, outs, (total, gates) = refs[: 2 * experts], refs[2 * experts : -2], refs[-2:]
     step, last = pl.program_id(0), pl.num_programs(0) - 1
 
     @pl.when(step == 0)
@@ -158,10 +169,9 @@
         total[...] = near_total[...]
         gates[...] = near_gates[...]
 
-    active, slope = gelu_slope(dot(w_in[0], stack(x_blocks, experts), NT))
-    up = dot(w_out[0], stack(s_blocks, experts), NT)
-    gates[...] += gate_sums(active.astype(bf16), up)
-    total[...] += dot((up * slope).astype(bf16), w_in[0], TN)
+    up = dot(w_out[...], stack(blocks, experts), NT)
+    gates[...] += gate_sums(act[...], up)
+    total[...] += dot((up * slope[...].astype(f32)).astype(bf16), w_in[...], TN)
 
     @pl.when(step == last)
     def _():
@@ -172,39 +182,31 @@
             out[capacity : capacity + 1, 0:block] = gate_rows[:, k * block : (k + 1) * block]
 
 
-def outer_rows(own_ref, other_ref, own_rows, other_rows, at, size):
-    return dot(own_ref[pl.ds(at, size), :], own_rows) + dot(other_ref[pl.ds(at, size), :], other_rows)
-
-
-def away_kernel(experts, owners, pos, own, other, *refs):
-    own_blocks, other_blocks, outs = refs[:experts], refs[experts : 2 * experts], refs[2 * experts :]
-    own_rows, other_rows = stack(own_blocks, experts), stack(other_blocks, experts)
+def cut(refs, left, size):
+    return jnp.concatenate([ref[:, left : left + size] for ref in refs], axis=0)
+
+
+def outer_rows(experts, own, other, refs):
+    return dot(own[...], stack(refs[:experts], experts)) + dot(
+        other[...], stack(refs[experts : 2 * experts], experts)
+    )
+
+
+def away_kernel(experts, owners, r, left, right, pos, own, other, *refs):
+    out = refs[-1]
     size = own.shape[0] // owners
-    for r, out in enumerate(outs):
-        at = pl.multiple_of(lax.rem(pos[1] + r + 1, owners) * size, size)
-        out[...] = outer_rows(own, other, own_rows, other_rows, at, size).astype(bf16)
+    mine = pl.ds(pl.multiple_of(lax.rem(pos[1] + r, owners) * size, size), size)
+    for at, run in steps(out.shape[1], 256):
+        total = dot(own[mine, :], cut(refs[:experts], left + at, run))
+        total += dot(other[mine, :], cut(refs[experts : 2 * experts], right + at, run))
+        out[:, at : at + run] = total.astype(out.dtype)
 
 
 def home_kernel(experts, owners, pos, own, other, *refs):
-    own_blocks, other_blocks = refs[:experts], refs[experts : 2 * experts]
-    got, out = refs[2 * experts : 2 * experts + owners - 1], refs[-1]
-    size = own.shape[0] // owners
-    at = pl.multiple_of(pos[1] * size, size)
-    total = outer_rows(
-        own, other, stack(own_blocks, experts), stack(other_blocks, experts), at, size
-    )
-    for ref in got:
+    total = outer_rows(experts, own, other, refs)
+    for ref in refs[2 * experts : 2 * experts + owners - 1]:
         total = total + ref[...].astype(f32)
-    out[0] = total
-
-
-def before_kernel(experts, owners, pos, own, other, *refs):
-    own_blocks, other_blocks, out = refs[:experts], refs[experts : 2 * experts], refs[-1]
-    size = own.shape[0] // owners
-    at = pl.multiple_of(pos[1] * size, size)
-    out[...] = outer_rows(
-        own, other, stack(own_blocks, experts), stack(other_blocks, experts), at, size
-    )
+    refs[-1][0] = total
 
 
 def after_kernel(owners, before, *refs):
@@ -267,10 +269,16 @@
     return pl.BlockSpec((size, array.shape[1]), lambda g, *pos: (g, 0))
 
 
+def share_rows(array, owners, r):
+    return pl.BlockSpec(
+        (array.shape[0] // owners, array.shape[1]), lambda g, pos: (lax.rem(pos[1] + r, owners), 0)
+    )
+
+
 def half_rows(array, parts, far=0):
     size = array.shape[1] // 2 // parts
     return pl.BlockSpec(
-        (1, size, array.shape[2]), lambda g, pos: (0, (pos[0] ^ far) * parts + g, 0)
+        (None, size, array.shape[2]), lambda g, pos: (0, (pos[0] ^ far) * parts + g, 0)
     )
 
 
@@ -294,6 +302,19 @@
     )(*scalars, *arrays)
 
 
+def direct(kernel, scalars, arrays, outs, flops=0):
+    moved = sum(a.size * a.dtype.itemsize for a in list(arrays) + outs)
+    return pl.pallas_call(
+        kernel,
+        out_shape=outs,
+        in_specs=[pl.BlockSpec(memory_space=pltpu.SMEM)] * len(scalars)
+        + [pl.BlockSpec(memory_space=pltpu.VMEM)] * len(arrays),
+        out_specs=[pl.BlockSpec(memory_space=pltpu.VMEM)] * len(outs),
+        compiler_params=pltpu.CompilerParams(vmem_limit_bytes=28 << 20),
+        cost_estimate=pl.CostEstimate(flops=int(flops), transcendentals=0, bytes_accessed=moved),
+    )(*scalars, *arrays)
+
+
 def window(arrays, start, size):
     return [
         (a, pl.BlockSpec((a.shape[0], size), lambda g, *pos: (0, start // size))) for a in arrays
@@ -364,9 +385,10 @@
         bind(own_send_kernel, experts, block, capacity),
         1,
         [],
-        each([stay(a) for a in (routes_t, keep_t, combine_t, tokens, grad_out)], full),
-        each([meta_shape] + blocks(2 * width), full),
-        flops=4 * slots * count * width,
+        each([stay(a) for a in (routes_t, keep_t, combine_t, tokens)], full)
+        + window([stay(grad_out)], 0, half),
+        each([meta_shape] + blocks(width + half), full),
+        flops=3 * slots * count * width,
     )
     own_xs = exchange(own_xs)
     half_in, half_out = call(
@@ -386,47 +408,69 @@
         flops=2 * slots * count * width,
     )
     x_out = exchange(other_xb)
-    sent = []
-    for values in (other_dya, other_dyb):
-        out = call(
-            bind(send_s_kernel, experts, block),
-            1,
-            [],
-            each([other_meta, values], full),
-            each(blocks(half), full),
-            flops=slots * count * width,
-        )
-        sent.append(exchange(out))
+    sb_out = call(
+        bind(send_s_kernel, experts, block),
+        1,
+        [],
+        each([meta], full) + window([stay(grad_out)], half, half),
+        window(blocks(2 * half), 0, half),
+        flops=slots * count * width,
+    )
+    sa_out = call(
+        bind(send_s_kernel, experts, block),
+        1,
+        [],
+        each([other_meta, other_dya], full),
+        each(blocks(half), full),
+        flops=slots * count * width,
+    )
+    sa_out = exchange(sa_out)
+    sb_out = call(
+        bind(send_s_kernel, experts, block),
+        1,
+        [],
+        each([other_meta, other_dyb], full)
+        + [(a, pl.BlockSpec(memory_space=pl.ANY)) for a in sb_out],
+        window(blocks(2 * half), half, half),
+        flops=slots * count * width,
+        alias={2 + k: k for k in range(experts)},
+    )
+    sb_out = exchange(sb_out)
     own_x, other_x = (own_xs, 0), (x_out, 0)
-    own_sa, other_sa = (own_xs, width), (sent[0], 0)
-    own_sb, other_sb = (own_xs, width + half), (sent[1], 0)
+    own_sa, other_sa = (own_xs, width), (sa_out, 0)
+    own_sb, other_sb = (sb_out, 0), (sb_out, half)
 
     def act(x):
-        return call(
-            bind(act_kernel, experts),
-            unit_parts,
-            [],
-            each([half_in], rows, unit_rows) + window(*x, width),
-            each([act_shape] * 2, rows, unit_rows),
-            flops=2 * slots * units * width,
+        return direct(
+            bind(act_kernel, x[1]), [], [half_in] + x[0], [act_shape] * 2, 2 * slots * units * width
         )
 
     own_act, own_slope = act(own_x)
     other_act, other_slope = act(other_x)
+    far_act, far_slope = call(
+        bind(far_act_kernel, experts),
+        unit_parts,
+        [pos],
+        each([stay(w_in)], half_rows, unit_parts, 1) + window(*own_x, width),
+        each([act_shape] * 2, rows, unit_rows),
+        flops=2 * slots * units * width,
+    )
     run = width // 4
     fed = slots * share * run
 
     def away(acts, left, right, first, many):
-        return call(
-            bind(away_kernel, experts, owners),
-            many,
-            [pos],
-            each(acts, full)
-            + runs_of(left[0], left[1] + first * run, run)
-            + runs_of(right[0], right[1] + first * run, run),
-            each([shaped((share, many * run))] * (owners - 1), columns, many),
-            flops=4 * fed * (owners - 1) * many,
-        )
+        return [
+            direct(
+                bind(
+                    away_kernel, experts, owners, r, left[1] + first * run, right[1] + first * run
+                ),
+                [pos],
+                acts + left[0] + right[0],
+                [shaped((share, many * run))],
+                4 * fed * many,
+            )[0]
+            for r in range(1, owners)
+        ]
 
     goal = shaped((1, share, width), f32)
 
@@ -440,7 +484,7 @@
     def home(acts, left, right, got, first, many, array=None):
         operands, alias = into(
             array,
-            each(acts, full)
+            each(acts, share_rows, owners, 0)
             + runs_of(*left, run)
             + runs_of(*right, run)
             + each(got, columns, many),
@@ -475,38 +519,32 @@
     away_ob = away(out_acts, own_sb, other_sb, 0, 2)
     got_ob = to_owners(away_ob)
     total_shape, gate_shape = shaped((slots, width), f32), shaped((1, slots), f32)
-    own_grad, near_total, near_gates = call(
-        bind(own_grad_kernel, experts),
-        unit_parts,
-        [],
-        each([half_in, half_out, own_act, own_slope], rows, unit_rows)
-        + window(*own_sa, half)
-        + window(*own_sb, half),
-        each([act_shape], rows, unit_rows) + each([total_shape, gate_shape], full),
-        flops=4 * slots * units * width,
-    )
-    other_grad = call(
-        bind(other_grad_kernel, experts),
-        unit_parts,
-        [],
-        each([half_out, other_slope], rows, unit_rows)
-        + window(*other_sa, half)
-        + window(*other_sb, half),
-        each([act_shape], rows, unit_rows),
-        flops=2 * slots * units * width,
+    own_grad, near_total, near_gates = direct(
+        bind(own_grad_kernel, experts, (own_sa[1], own_sb[1])),
+        [],
+        [half_in, half_out, own_act, own_slope] + own_sa[0] + own_sb[0],
+        [act_shape, total_shape, gate_shape],
+        4 * slots * units * width,
+    )
+    other_grad = direct(
+        bind(other_grad_kernel, experts, (other_sa[1], other_sb[1])),
+        [],
+        [half_out, other_slope] + other_sa[0] + other_sb[0],
+        [act_shape],
+        2 * slots * units * width,
     )[0]
     own_back = call(
         bind(far_kernel, experts, block, capacity),
         unit_parts,
         [pos],
         each([stay(w_in), stay(w_out)], half_rows, unit_parts, 1)
+        + each([far_act, far_slope], rows, unit_rows)
         + each([near_total, near_gates], full)
-        + window(*own_x, width)
         + window(*own_sa, half)
         + window(*own_sb, half),
         each(blocks(width), full),
         [pltpu.VMEM((slots, width), f32), pltpu.VMEM((1, slots), f32)],
-        6 * slots * units * width,
+        4 * slots * units * width,
     )
     in_acts = [own_grad, other_grad]
     away_a = away(in_acts, own_x, other_x, 0, 3)
@@ -525,13 +563,12 @@
         each([shaped((count, width))], columns, 2) + each([shaped((2, count))], full),
         flops=2 * slots * count * width,
     )
-    before = call(
-        bind(before_kernel, experts, owners),
-        4,
+    before = direct(
+        bind(away_kernel, experts, owners, 0, own_x[1], other_x[1]),
         [pos],
-        each(in_acts, full) + runs_of(*own_x, run) + runs_of(*other_x, run),
-        each([shaped((share, width), f32)], columns, 4),
-        flops=16 * fed,
+        in_acts + own_x[0] + other_x[0],
+        [shaped((share, width), f32)],
+        16 * fed,
     )[0]
     grad_in = after(before, got_a, 0, 3)
     grad_in = after(before, got_b, 3, 1, grad_in)

time: 152 us -> 146 us (0.961)
  Pallas kernels: 46.8 us -> 43.7 us
  local copies, waits for them, and re-layouts: 2.98 us -> 1.05 us
    pallas_call x20 -> x13, Pallas kernels: 46.8 us -> 28.7 us  [call(): pl.pallas_call(kernel, out_shape=outs, grid_spec=pltpu.PrefetchScalarGrid...]
    pallas_call x0 -> x9, Pallas kernels: none -> 15 us  [direct(): pl.pallas_call(kernel, out_shape=outs, in_specs=[pl.BlockSpec(memory_spac...]
    ppermute x35, waiting for transfers between devices: 25.6 us -> 13.4 us  [exchange(): lax.ppermute(values[k], 'expert', [(i, i ^ k) for i in range(experts)])]
    ppermute x4, waiting for transfers between devices: 23.8 us -> 30.7 us  [across(): lax.ppermute(value, 'dp', [(j, (j + owners) % planes) for j in range(plan...]
    ppermute x4, waiting for transfers between devices: 5.92 us -> 10.5 us  [to_owners(): lax.ppermute(value, 'dp', [(j, j // owners * owners + (j + r + 1) % owner...]
    ppermute x35, starting transfers between devices: 33.7 us -> 31 us  [exchange(): lax.ppermute(values[k], 'expert', [(i, i ^ k) for i in range(experts)])]
    ppermute x4, starting transfers between devices: 6 us -> 8.1 us  [across(): lax.ppermute(value, 'dp', [(j, (j + owners) % planes) for j in range(plan...]
    unnamed x8 -> x0, local copies, waits for them, and re-layouts: 1.88 us -> none
  transfers between devices with their start and end apart: 43 -> 43, of which waited for: 13 -> 16; matrix products, arithmetic and copies ran while one was open for 0% -> 1% of each run, Pallas kernels for 28% -> 27%
where the time goes in v4:
time: 146 us; the launch traced here: 144 us
  waiting for transfers between devices  54.5 us (37%)
  Pallas kernels  43.7 us (30%)
  starting transfers between devices  43.4 us (30%)
    ppermute x35, starting transfers between devices, exchange(): lax.ppermute(values[k], 'expert', [(i, i ^ k) for i in range(experts)])  31 us
    ppermute x4, waiting for transfers between devices, across(): lax.ppermute(value, 'dp', [(j, (j + owners) % planes) for j in range(plan...  30.7 us
    pallas_call x13, Pallas kernels, call(): pl.pallas_call(kernel, out_shape=outs, grid_spec=pltpu.PrefetchScalarGrid...  28.7 us
    pallas_call x9, Pallas kernels, direct(): pl.pallas_call(kernel, out_shape=outs, in_specs=[pl.BlockSpec(memory_spac...  15 us
    ppermute x35, waiting for transfers between devices, exchange(): lax.ppermute(values[k], 'expert', [(i, i ^ k) for i in range(experts)])  13.4 us
    ppermute x4, waiting for transfers between devices, to_owners(): lax.ppermute(value, 'dp', [(j, j // owners * owners + (j + r + 1) % owner...  10.5 us
    ppermute x4, starting transfers between devices, across(): lax.ppermute(value, 'dp', [(j, (j + owners) % planes) for j in range(plan...  8.1 us
    ppermute x4, starting transfers between devices, to_owners(): lax.ppermute(value, 'dp', [(j, j // owners * owners + (j + r + 1) % owner...  4.26 us
  transfers between devices with their start and end apart: 43, of which 16 were waited for; matrix products, arithmetic and copies ran while one was open for 1% of the time, Pallas kernels for 27%

profile of v4, /device:TPU:2, one launch (start us, length us, event | category | flops | bytes accessed | tf_op | source)
XLA Modules:
  0.0 143.6 jit_solution(2062273366971911922)
XLA Ops:
  0.6 1.9 %shard_map.102 = (f32[8,192]{1,0:T(8,128)S(1)}, bf16[64,1536]{1,0:T(8,128)(2,1)S(1)}, bf16[64,1536]{1,0:T(8,128)(2,1)S(1)}, bf16[64,1536]{1,0:T(8,128)(2,1)S(1)}...) custom-call(s32[2,192]{1,0:T(2,128)} %bitcast.6, ...), custom_call_target="tpu_custom_call" | custom-call | flops 301989888 | bytes 2368512 | tf_op jit(solution)/shard_map/pallas_call | solution.py:289
  2.7 1.8 %collective-permute-start.2 = (bf16[64,1536]{1,0:T(8,128)(2,1)S(1)}, bf16[64,1536]{1,0:T(8,128)(2,1)S(1)}, u32[]{:S(2)}, u32[]{:S(2)}) collective-permute-start(bf16[64,1536]{1,0:T(8,128)(2,1)S(1)} %get-tuple-element.70), channel_id=1, source_target_pairs={{0,12},{4,8},{8,4},{12,0},{16,28},{20,24},{24,20},{28,16},{1,13},{... | collective-permute-start | bytes 589832 | tf_op jit(solution)/shard_map/ppermute | solution.py:350
  4.5 1.5 %collective-permute-start.3 = (bf16[64,1536]{1,0:T(8,128)(2,1)S(1)}, bf16[64,1536]{1,0:T(8,128)(2,1)S(1)}, u32[]{:S(2)}, u32[]{:S(2)}) collective-permute-start(bf16[64,1536]{1,0:T(8,128)(2,1)S(1)} %get-tuple-element.71), channel_id=1, source_target_pairs={{0,16},{4,20},{8,24},{12,28},{16,0},{20,4},{24,8},{28,12},{1,17},{... | collective-permute-start | bytes 589832 | tf_op jit(solution)/shard_map/ppermute | solution.py:350
  6.0 2.6 %collective-permute-start.7 = (f32[8,192]{1,0:T(8,128)S(1)}, f32[8,192]{1,0:T(8,128)S(1)}, u32[]{:S(2)}, u32[]{:S(2)}) collective-permute-start(f32[8,192]{1,0:T(8,128)S(1)} %get-tuple-element.66.meta), channel_id=1, source_target_pairs={{0,2},{1,3},{2,0},{3,1},{4,6},{5,7},{6,4},{7,5},{8,10},{9,11},{10,... | collective-permute-start | bytes 18440 | tf_op jit(solution)/shard_map/ppermute | solution.py:346
  8.6 1.0 fusion
  9.6 0.9 collective-permute-done.7.meta
  10.5 2.6 %collective-permute-start.31 = (bf16[192,512]{1,0:T(8,128)(2,1)S(1)}, bf16[192,512]{1,0:T(8,128)(2,1)S(1)}, u32[]{:S(2)}, u32[]{:S(2)}) collective-permute-start(bf16[192,512]{1,0:T(8,128)(2,1)S(1)} %get-tuple-element.128), channel_id=1, source_target_pairs={{0,2},{1,3},{2,0},{3,1},{4,6},{5,7},{6,4},{7,5},{8,10},{9,11},{10,... | collective-permute-start | bytes 589832 | tf_op jit(solution)/shard_map/ppermute | solution.py:346
  13.5 2.6 %collective-permute-start.8 = (bf16[192,512]{1,0:T(8,128)(2,1)S(1)}, bf16[192,512]{1,0:T(8,128)(2,1)S(1)}, u32[]{:S(2)}, u32[]{:S(2)}) collective-permute-start(bf16[192,512]{1,0:T(8,128)(2,1)S(1)} %get-tuple-element.129), channel_id=1, source_target_pairs={{0,2},{1,3},{2,0},{3,1},{4,6},{5,7},{6,4},{7,5},{8,10},{9,11},{10,... | collective-permute-start | bytes 589832 | tf_op jit(solution)/shard_map/ppermute | solution.py:346
  16.1 0.5 collective-permute-start.5
  16.6 18.5 %collective-permute-done.31.grad_out = bf16[192,512]{1,0:T(8,128)(2,1)S(1)} collective-permute-done((bf16[192,512]{1,0:T(8,128)(2,1)S(1)}, bf16[192,512]{1,0:T(8,128)(2,1)S(1)}, u32[]{:S(2)}, u32[]{:S(2)}) %collective-permute-start.31) | collective-permute-done | bytes 196640 | tf_op jit(solution)/shard_map/ppermute | solution.py:346
  35.5 11.2 %collective-permute-done.8.grad_out = bf16[192,512]{1,0:T(8,128)(2,1)S(1)} collective-permute-done((bf16[192,512]{1,0:T(8,128)(2,1)S(1)}, bf16[192,512]{1,0:T(8,128)(2,1)S(1)}, u32[]{:S(2)}, u32[]{:S(2)}) %collective-permute-start.8) | collective-permute-done | bytes 196640 | tf_op jit(solution)/shard_map/ppermute | solution.py:346
  46.7 1.2 shard_map.106
  48.2 0.6 collective-permute-start.9
  48.8 0.5 collective-permute-start.10
  49.3 0.9 collective-permute-start.11
  50.3 0.5 collective-permute-start.12
  50.8 0.7 collective-permute-start.33
  51.5 3.7 %shard_map.104 = (bf16[1024,1024]{1,0:T(8,128)(2,1)S(1)}, bf16[1024,1024]{1,0:T(8,128)(2,1)S(1)}) custom-call(s32[2]{0:T(128)S(1)} %pad_add_fusion.pos, bf16[1,2048,1024]{2,1,0:T(8,128)(2,1)} %w_in.5, bf16[1,2048,1024]{2,1,0:T(8,128)(2,1)} %w_out.3), custom_call_target="tpu_custom_call" | custom-call | bytes 12582912 | tf_op jit(solution)/shard_map/pallas_call | solution.py:289
  55.2 0.8 shard_map.111
  56.0 2.5 %collective-permute-done.33.refs_2_.refs_10_ = bf16[64,512]{1,0:T(8,128)(2,1)S(1)} collective-permute-done((bf16[64,512]{1,0:T(8,128)(2,1)S(1)}, bf16[64,512]{1,0:T(8,128)(2,1)S(1)}, u32[]{:S(2)}, u32[]{:S(2)}) %collective-permute-start.33) | collective-permute-done | bytes 65568 | tf_op jit(solution)/shard_map/ppermute | solution.py:350
  58.5 0.5 collective-permute-start.14
  59.1 2.3 %collective-permute-start.15 = (bf16[64,1024]{1,0:T(8,128)(2,1)S(1)}, bf16[64,1024]{1,0:T(8,128)(2,1)S(1)}, u32[]{:S(2)}, u32[]{:S(2)}) collective-permute-start(bf16[64,1024]{1,0:T(8,128)(2,1)S(1)} %get-tuple-element.96), channel_id=1, source_target_pairs={{0,28},{4,24},{8,20},{12,16},{16,12},{20,8},{24,4},{28,0},{1,29},{... | collective-permute-start | bytes 393224 | tf_op jit(solution)/shard_map/ppermute | solution.py:350
  61.6 0.5 collective-permute-start.25
  62.1 4.8 %shard_map.103 = (bf16[1024,512]{1,0:T(8,128)(2,1)S(1)}, bf16[1024,512]{1,0:T(8,128)(2,1)S(1)}) custom-call(s32[2]{0:T(128)S(1)} %pad_add_fusion.pos, bf16[1,2048,1024]{2,1,0:T(8,128)(2,1)} %w_in.5, bf16[64,1536]{1,0:T(8,128)(2,1)S(1)} %get-tuple-element.67.refs_0_, bf16[64,1536]{1,0:T(8,128)(2,1)S(1)} %collective-permute-done.refs_1_, ...), custom_call_target="tpu_custom_call" | custom-call | flops 1073741824 | bytes 7864320 | tf_op jit(solution)/shard_map/pallas_call | solution.py:289
  66.9 2.1 %shard_map.105 = (bf16[1024,512]{1,0:T(8,128)(2,1)S(1)}, bf16[1024,512]{1,0:T(8,128)(2,1)S(1)}) custom-call(bf16[1024,1024]{1,0:T(8,128)(2,1)S(1)} %get-tuple-element.77.w_in, bf16[64,1536]{1,0:T(8,128)(2,1)S(1)} %get-tuple-element.67.refs_0_, bf16[64,1536]{1,0:T(8,128)(2,1)S(1)} %collective-permute-done.refs_1_, ...), custom_call_target="tpu_custom_call" | custom-call | flops 1073741824 | bytes 5767168 | tf_op jit(solution)/shard_map/pallas_call | solution.py:307
  69.0 1.2 collective-permute-start.26
  70.3 1.5 %collective-permute-start.27 = (bf16[64,1024]{1,0:T(8,128)(2,1)S(1)}, bf16[64,1024]{1,0:T(8,128)(2,1)S(1)}, u32[]{:S(2)}, u32[]{:S(2)}) collective-permute-start(bf16[64,1024]{1,0:T(8,128)(2,1)S(1)} %get-tuple-element.114), channel_id=1, source_target_pairs={{0,16},{4,20},{8,24},{12,28},{16,0},{20,4},{24,8},{28,12},{1,17},{... | collective-permute-start | bytes 393224 | tf_op jit(solution)/shard_map/ppermute | solution.py:350
  72.1 1.4 collective-permute-start.29
  73.5 1.2 collective-permute-start.30
  74.7 2.6 %shard_map.108 = (bf16[1024,512]{1,0:T(8,128)(2,1)S(1)}, f32[512,1024]{1,0:T(8,128)S(1)}, f32[1,512]{1,0:T(1,128)S(1)}) custom-call(bf16[1024,1024]{1,0:T(8,128)(2,1)S(1)} %get-tuple-element.77.w_in, bf16[1024,1024]{1,0:T(8,128)(2,1)S(1)} %get-tuple-element.78.w_out, bf16[1024,512]{1,0:T(8,128)(2,1)S(1)} %get-tuple-element.79.act.own, ...), custom_call_target="tpu_custom_call" | custom-call | flops 2147483648 | bytes 12060672 | tf_op jit(solution)/shard_map/pallas_call | solution.py:307
  77.3 0.7 collective-permute-start.34
  78.0 4.3 %collective-permute-done.27.refs_4_.refs_12_ = bf16[64,1024]{1,0:T(8,128)(2,1)S(1)} collective-permute-done((bf16[64,1024]{1,0:T(8,128)(2,1)S(1)}, bf16[64,1024]{1,0:T(8,128)(2,1)S(1)}, u32[]{:S(2)}, u32[]{:S(2)}) %collective-permute-start.27) | collective-permute-done | bytes 131104 | tf_op jit(solution)/shard_map/ppermute | solution.py:350
  82.2 1.5 %collective-permute-start.35 = (bf16[64,512]{1,0:T(8,128)(2,1)S(1)}, bf16[64,512]{1,0:T(8,128)(2,1)S(1)}, u32[]{:S(2)}, u32[]{:S(2)}) collective-permute-start(bf16[64,512]{1,0:T(8,128)(2,1)S(1)} %get-tuple-element.123), channel_id=1, source_target_pairs={{0,16},{4,20},{8,24},{12,28},{16,0},{20,4},{24,8},{28,12},{1,17},{... | collective-permute-start | bytes 196616 | tf_op jit(solution)/shard_map/ppermute | solution.py:350
  84.1 1.9 %collective-permute-start.36 = (bf16[64,512]{1,0:T(8,128)(2,1)S(1)}, bf16[64,512]{1,0:T(8,128)(2,1)S(1)}, u32[]{:S(2)}, u32[]{:S(2)}) collective-permute-start(bf16[64,512]{1,0:T(8,128)(2,1)S(1)} %get-tuple-element.124), channel_id=1, source_target_pairs={{0,20},{4,16},{8,28},{12,24},{16,4},{20,0},{24,12},{28,8},{1,21},{... | collective-permute-start | bytes 196616 | tf_op jit(solution)/shard_map/ppermute | solution.py:350
  86.0 0.5 collective-permute-start.37
  86.5 1.2 collective-permute-start.38
  87.7 2.1 %shard_map.112 = (bf16[1024,512]{1,0:T(8,128)(2,1)S(1)}, bf16[1024,512]{1,0:T(8,128)(2,1)S(1)}) custom-call(bf16[1024,1024]{1,0:T(8,128)(2,1)S(1)} %get-tuple-element.77.w_in, bf16[64,1024]{1,0:T(8,128)(2,1)S(1)} %get-tuple-element.110.refs_0_.refs_8_, bf16[64,1024]{1,0:T(8,128)(2,1)S(1)} %collective-permute-done.24.refs_1_.refs_9_, ...), custom_call_target="tpu_custom_call" | custom-call | flops 1073741824 | bytes 5242880 | tf_op jit(solution)/shard_map/pallas_call | solution.py:307
  89.8 1.9 %collective-permute-done.37.refs_6_.refs_14_ = bf16[64,512]{1,0:T(8,128)(2,1)S(1)} collective-permute-done((bf16[64,512]{1,0:T(8,128)(2,1)S(1)}, bf16[64,512]{1,0:T(8,128)(2,1)S(1)}, u32[]{:S(2)}, u32[]{:S(2)}) %collective-permute-start.37) | collective-permute-done | bytes 65568 | tf_op jit(solution)/shard_map/ppermute | solution.py:350
  91.8 1.3 shard_map.114.other
  93.1 1.5 %shard_map.117 = bf16[512,768]{1,0:T(8,128)(2,1)S(1)} custom-call(s32[2]{0:T(128)S(1)} %pad_add_fusion.pos, bf16[1024,512]{1,0:T(8,128)(2,1)S(1)} %get-tuple-element.109.own, bf16[1024,512]{1,0:T(8,128)(2,1)S(1)} %shard_map.114.other, bf16[64,1536]{1,0:T(8,128)(2,1)S(1)} %get-tuple-element.67.refs_0_, bf16[64,1536]{1,0:T(8,128)(2,1)S(1)} %collective-permute-done.refs_1_, ...), custom_call_target="tpu_custom_call" | custom-call | flops 805306368 | bytes 5505024 | tf_op jit(solution)/shard_map/pallas_call | solution.py:307
  94.6 0.7 collective-permute-start.40
  95.3 6.5 %shard_map.109 = (bf16[64,1024]{1,0:T(8,128)(2,1)S(1)}, bf16[64,1024]{1,0:T(8,128)(2,1)S(1)}, bf16[64,1024]{1,0:T(8,128)(2,1)S(1)}, bf16[64,1024]{1,0:T(8,128)(2...) custom-call(s32[2]{0:T(128)S(1)} %pad_add_fusion.pos, ...), custom_call_target="tpu_custom_call" | custom-call | flops 2147483648 | bytes 16254976 | tf_op jit(solution)/shard_map/pallas_call | solution.py:289
  102.2 1.2 collective-permute-start.17
  103.8 1.2 shard_map.121
  105.0 1.5 %collective-permute-start.42 = (bf16[512,512]{1,0:T(8,128)(2,1)S(1)}, bf16[512,512]{1,0:T(8,128)(2,1)S(1)}, u32[]{:S(2)}, u32[]{:S(2)}) collective-permute-start(bf16[512,512]{1,0:T(8,128)(2,1)S(1)} %shard_map.121), channel_id=1, source_target_pairs={{0,1},{1,0},{2,3},{3,2},{4,5},{5,4},{6,7},{7,6},{8,9},{9,8},{10,11... | collective-permute-start | bytes 1572872 | tf_op jit(solution)/shard_map/ppermute | solution.py:356
  106.5 1.3 shard_map.120
  107.8 0.7 collective-permute-start.41
  108.5 1.2 collective-permute-start.19
  109.9 1.7 %collective-permute-start.20 = (bf16[64,1024]{1,0:T(8,128)(2,1)S(1)}, bf16[64,1024]{1,0:T(8,128)(2,1)S(1)}, u32[]{:S(2)}, u32[]{:S(2)}) collective-permute-start(bf16[64,1024]{1,0:T(8,128)(2,1)S(1)} %get-tuple-element.104), channel_id=1, source_target_pairs={{0,20},{4,16},{8,28},{12,24},{16,4},{20,0},{24,12},{28,8},{1,21},{... | collective-permute-start | bytes 393224 | tf_op jit(solution)/shard_map/ppermute | solution.py:350
  111.7 3.0 %collective-permute-done.19.refs_4_ = bf16[64,1024]{1,0:T(8,128)(2,1)S(1)} collective-permute-done((bf16[64,1024]{1,0:T(8,128)(2,1)S(1)}, bf16[64,1024]{1,0:T(8,128)(2,1)S(1)}, u32[]{:S(2)}, u32[]{:S(2)}) %collective-permute-start.19) | collective-permute-done | bytes 131104 | tf_op jit(solution)/shard_map/ppermute | solution.py:350
  114.7 1.3 collective-permute-start.21
  116.0 0.7 collective-permute-done.20.refs_5_
  116.7 2.7 %collective-permute-start.22 = (bf16[64,1024]{1,0:T(8,128)(2,1)S(1)}, bf16[64,1024]{1,0:T(8,128)(2,1)S(1)}, u32[]{:S(2)}, u32[]{:S(2)}) collective-permute-start(bf16[64,1024]{1,0:T(8,128)(2,1)S(1)} %get-tuple-element.106), channel_id=1, source_target_pairs={{0,28},{4,24},{8,20},{12,16},{16,12},{20,8},{24,4},{28,0},{1,29},{... | collective-permute-start | bytes 393224 | tf_op jit(solution)/shard_map/ppermute | solution.py:350
  119.4 1.0 shard_map.116
  120.6 1.4 collective-permute-start.39
  122.0 1.6 %shard_map.110 = (bf16[192,1024]{1,0:T(8,128)(2,1)}, bf16[2,192]{1,0:T(2,128)(2,1)}) custom-call(f32[8,192]{1,0:T(8,128)S(1)} %get-tuple-element.66.meta, bf16[64,1024]{1,0:T(8,128)(2,1)S(1)} %get-tuple-element.99.refs_0_, bf16[64,1024]{1,0:T(8,128)(2,1)S(1)} %collective-permute-done.16.refs_1_, bf16[64,1024]{1,0:T(8,128)(2,1)S(1)} %collective-permute-done.17.refs_2_, ...), custom_call_target="tpu_custom_call" | custom-call | flops 201326592 | bytes 1448704 | tf_op jit(solution)/shard_map/pallas_call | solution.py:289
  123.6 1.8 %shard_map.115.before = f32[512,1024]{1,0:T(8,128)S(1)} custom-call(s32[2]{0:T(128)S(1)} %pad_add_fusion.pos, bf16[1024,512]{1,0:T(8,128)(2,1)S(1)} %get-tuple-element.109.own, bf16[1024,512]{1,0:T(8,128)(2,1)S(1)} %shard_map.114.other, bf16[64,1536]{1,0:T(8,128)(2,1)S(1)} %get-tuple-element.67.refs_0_, bf16[64,1536]{1,0:T(8,128)(2,1)S(1)} %collective-permute-done.refs_1_, ...), custom_call_target="tpu_custom_call" | custom-call | flops 1073741824 | bytes 6815744 | tf_op jit(solution)/shard_map/pallas_call | solution.py:307
  125.4 1.0 collective-permute-done.42.refs_16_
  126.3 2.5 %shard_map.122.refs_17_ = f32[1,512,1024]{2,1,0:T(8,128)} custom-call(s32[2]{0:T(128)S(1)} %pad_add_fusion.pos, bf16[1024,512]{1,0:T(8,128)(2,1)S(1)} %get-tuple-element.79.act.own, bf16[1024,512]{1,0:T(8,128)(2,1)S(1)} %get-tuple-element.127.other, bf16[64,1536]{1,0:T(8,128)(2,1)S(1)} %get-tuple-element.67.refs_0_, ...), custom_call_target="tpu_custom_call" | custom-call | flops 536870912 | bytes 6815744 | tf_op jit(solution)/shard_map/pallas_call | solution.py:289
  128.8 8.7 %collective-permute-done.41.refs_16_ = bf16[512,512]{1,0:T(8,128)(2,1)S(1)} collective-permute-done((bf16[512,512]{1,0:T(8,128)(2,1)S(1)}, bf16[512,512]{1,0:T(8,128)(2,1)S(1)}, u32[]{:S(2)}, u32[]{:S(2)}) %collective-permute-start.41) | collective-permute-done | bytes 524320 | tf_op jit(solution)/shard_map/ppermute | solution.py:356
  137.6 2.6 %shard_map.123 = f32[1,512,1024]{2,1,0:T(8,128)} custom-call(s32[2]{0:T(128)S(1)} %pad_add_fusion.pos, bf16[1024,512]{1,0:T(8,128)(2,1)S(1)} %get-tuple-element.79.act.own, bf16[1024,512]{1,0:T(8,128)(2,1)S(1)} %get-tuple-element.127.other, bf16[64,1024]{1,0:T(8,128)(2,1)S(1)} %get-tuple-element.89.refs_8_.refs_0_, ...), custom_call_target="tpu_custom_call", output_to_operand_aliasing={{}: (20, {})} | custom-call | flops 536870912 | bytes 8912896 | tf_op jit(solution)/shard_map/pallas_call | solution.py:289
  140.2 1.8 %shard_map.118.refs_1_ = f32[1,512,1024]{2,1,0:T(8,128)} custom-call(f32[512,1024]{1,0:T(8,128)S(1)} %shard_map.115.before, bf16[512,768]{1,0:T(8,128)(2,1)S(1)} %collective-permute-done.40.refs_0_), custom_call_target="tpu_custom_call" | custom-call | bytes 4980736 | tf_op jit(solution)/shard_map/pallas_call | solution.py:289
  142.0 0.8 collective-permute-done.39.refs_0_
  142.8 0.8 shard_map.119
  (46 shorter events, 3.3 us)
Async XLA Ops:
  2.5 10.6 %collective-permute-start = (bf16[64,1536]{1,0:T(8,128)(2,1)S(1)}, bf16[64,1536]{1,0:T(8,128)(2,1)S(1)}, u32[]{:S(2)}, u32[]{:S(2)}) collective-permute-start(bf16[64,1536]{1,0:T(8,128)(2,1)S(1)} %get-tuple-element.68), channel_id=1, source_target_pairs={{0,4},{4,0},{8,12},{12,8},{16,20},{20,16},{24,28},{28,24},{1,5},{5... | collective-permute-start | bytes 589832 | tf_op jit(solution)/shard_map/ppermute | solution.py:350
  2.6 10.9 %collective-permute-start.1 = (bf16[64,1536]{1,0:T(8,128)(2,1)S(1)}, bf16[64,1536]{1,0:T(8,128)(2,1)S(1)}, u32[]{:S(2)}, u32[]{:S(2)}) collective-permute-start(bf16[64,1536]{1,0:T(8,128)(2,1)S(1)} %get-tuple-element.69), channel_id=1, source_target_pairs={{0,8},{4,12},{8,0},{12,4},{16,24},{20,28},{24,16},{28,20},{1,9},{5... | collective-permute-start | bytes 589832 | tf_op jit(solution)/shard_map/ppermute | solution.py:350
  2.7 13.4 %collective-permute-start.2 = (bf16[64,1536]{1,0:T(8,128)(2,1)S(1)}, bf16[64,1536]{1,0:T(8,128)(2,1)S(1)}, u32[]{:S(2)}, u32[]{:S(2)}) collective-permute-start(bf16[64,1536]{1,0:T(8,128)(2,1)S(1)} %get-tuple-element.70), channel_id=1, source_target_pairs={{0,12},{4,8},{8,4},{12,0},{16,28},{20,24},{24,20},{28,16},{1,13},{... | collective-permute-start | bytes 589832 | tf_op jit(solution)/shard_map/ppermute | solution.py:350
  4.5 11.6 %collective-permute-start.3 = (bf16[64,1536]{1,0:T(8,128)(2,1)S(1)}, bf16[64,1536]{1,0:T(8,128)(2,1)S(1)}, u32[]{:S(2)}, u32[]{:S(2)}) collective-permute-start(bf16[64,1536]{1,0:T(8,128)(2,1)S(1)} %get-tuple-element.71), channel_id=1, source_target_pairs={{0,16},{4,20},{8,24},{12,28},{16,0},{20,4},{24,8},{28,12},{1,17},{... | collective-permute-start | bytes 589832 | tf_op jit(solution)/shard_map/ppermute | solution.py:350
  6.0 4.5 %collective-permute-start.7 = (f32[8,192]{1,0:T(8,128)S(1)}, f32[8,192]{1,0:T(8,128)S(1)}, u32[]{:S(2)}, u32[]{:S(2)}) collective-permute-start(f32[8,192]{1,0:T(8,128)S(1)} %get-tuple-element.66.meta), channel_id=1, source_target_pairs={{0,2},{1,3},{2,0},{3,1},{4,6},{5,7},{6,4},{7,5},{8,10},{9,11},{10,... | collective-permute-start | bytes 18440 | tf_op jit(solution)/shard_map/ppermute | solution.py:346
  10.5 24.6 %collective-permute-start.31 = (bf16[192,512]{1,0:T(8,128)(2,1)S(1)}, bf16[192,512]{1,0:T(8,128)(2,1)S(1)}, u32[]{:S(2)}, u32[]{:S(2)}) collective-permute-start(bf16[192,512]{1,0:T(8,128)(2,1)S(1)} %get-tuple-element.128), channel_id=1, source_target_pairs={{0,2},{1,3},{2,0},{3,1},{4,6},{5,7},{6,4},{7,5},{8,10},{9,11},{10,... | collective-permute-start | bytes 589832 | tf_op jit(solution)/shard_map/ppermute | solution.py:346
  13.1 37.6 %collective-permute-start.23 = (bf16[192,1024]{1,0:T(8,128)(2,1)}, bf16[192,1024]{1,0:T(8,128)(2,1)S(1)}, u32[]{:S(2)}, u32[]{:S(2)}) collective-permute-start(bf16[192,1024]{1,0:T(8,128)(2,1)} %tokens.1), channel_id=1, source_target_pairs={{0,2},{1,3},{2,0},{3,1},{4,6},{5,7},{6,4},{7,5},{8,10},{9,11},{10,... | collective-permute-start | bytes 1179656 | tf_op jit(solution)/shard_map/ppermute | solution.py:346
  13.5 33.2 %collective-permute-start.8 = (bf16[192,512]{1,0:T(8,128)(2,1)S(1)}, bf16[192,512]{1,0:T(8,128)(2,1)S(1)}, u32[]{:S(2)}, u32[]{:S(2)}) collective-permute-start(bf16[192,512]{1,0:T(8,128)(2,1)S(1)} %get-tuple-element.129), channel_id=1, source_target_pairs={{0,2},{1,3},{2,0},{3,1},{4,6},{5,7},{6,4},{7,5},{8,10},{9,11},{10,... | collective-permute-start | bytes 589832 | tf_op jit(solution)/shard_map/ppermute | solution.py:346
  16.1 32.2 %collective-permute-start.4 = (bf16[64,1536]{1,0:T(8,128)(2,1)S(1)}, bf16[64,1536]{1,0:T(8,128)(2,1)S(1)}, u32[]{:S(2)}, u32[]{:S(2)}) collective-permute-start(bf16[64,1536]{1,0:T(8,128)(2,1)S(1)} %get-tuple-element.72), channel_id=1, source_target_pairs={{0,20},{4,16},{8,28},{12,24},{16,4},{20,0},{24,12},{28,8},{1,21},{... | collective-permute-start | bytes 589832 | tf_op jit(solution)/shard_map/ppermute | solution.py:350
  16.1 32.7 %collective-permute-start.5 = (bf16[64,1536]{1,0:T(8,128)(2,1)S(1)}, bf16[64,1536]{1,0:T(8,128)(2,1)S(1)}, u32[]{:S(2)}, u32[]{:S(2)}) collective-permute-start(bf16[64,1536]{1,0:T(8,128)(2,1)S(1)} %get-tuple-element.73), channel_id=1, source_target_pairs={{0,24},{4,28},{8,16},{12,20},{16,8},{20,12},{24,0},{28,4},{1,25},{... | collective-permute-start | bytes 589832 | tf_op jit(solution)/shard_map/ppermute | solution.py:350
  35.2 14.2 %collective-permute-start.6 = (bf16[64,1536]{1,0:T(8,128)(2,1)S(1)}, bf16[64,1536]{1,0:T(8,128)(2,1)S(1)}, u32[]{:S(2)}, u32[]{:S(2)}) collective-permute-start(bf16[64,1536]{1,0:T(8,128)(2,1)S(1)} %get-tuple-element.74), channel_id=1, source_target_pairs={{0,28},{4,24},{8,20},{12,16},{16,12},{20,8},{24,4},{28,0},{1,29},{... | collective-permute-start | bytes 589832 | tf_op jit(solution)/shard_map/ppermute | solution.py:350
  46.7 3.6 %collective-permute-start.32 = (bf16[64,512]{1,0:T(8,128)(2,1)S(1)}, bf16[64,512]{1,0:T(8,128)(2,1)S(1)}, u32[]{:S(2)}, u32[]{:S(2)}) collective-permute-start(bf16[64,512]{1,0:T(8,128)(2,1)S(1)} %get-tuple-element.120), channel_id=1, source_target_pairs={{0,4},{4,0},{8,12},{12,8},{16,20},{20,16},{24,28},{28,24},{1,5},{5... | collective-permute-start | bytes 196616 | tf_op jit(solution)/shard_map/ppermute | solution.py:350
  48.2 10.3 %collective-permute-start.9 = (bf16[64,1024]{1,0:T(8,128)(2,1)S(1)}, bf16[64,1024]{1,0:T(8,128)(2,1)S(1)}, u32[]{:S(2)}, u32[]{:S(2)}) collective-permute-start(bf16[64,1024]{1,0:T(8,128)(2,1)S(1)} %get-tuple-element.90), channel_id=1, source_target_pairs={{0,4},{4,0},{8,12},{12,8},{16,20},{20,16},{24,28},{28,24},{1,5},{5... | collective-permute-start | bytes 393224 | tf_op jit(solution)/shard_map/ppermute | solution.py:350
  48.8 10.2 %collective-permute-start.10 = (bf16[64,1024]{1,0:T(8,128)(2,1)S(1)}, bf16[64,1024]{1,0:T(8,128)(2,1)S(1)}, u32[]{:S(2)}, u32[]{:S(2)}) collective-permute-start(bf16[64,1024]{1,0:T(8,128)(2,1)S(1)} %get-tuple-element.91), channel_id=1, source_target_pairs={{0,8},{4,12},{8,0},{12,4},{16,24},{20,28},{24,16},{28,20},{1,9},{5... | collective-permute-start | bytes 393224 | tf_op jit(solution)/shard_map/ppermute | solution.py:350
  49.3 12.0 %collective-permute-start.11 = (bf16[64,1024]{1,0:T(8,128)(2,1)S(1)}, bf16[64,1024]{1,0:T(8,128)(2,1)S(1)}, u32[]{:S(2)}, u32[]{:S(2)}) collective-permute-start(bf16[64,1024]{1,0:T(8,128)(2,1)S(1)} %get-tuple-element.92), channel_id=1, source_target_pairs={{0,12},{4,8},{8,4},{12,0},{16,28},{20,24},{24,20},{28,16},{1,13},{... | collective-permute-start | bytes 393224 | tf_op jit(solution)/shard_map/ppermute | solution.py:350
  50.3 11.3 %collective-permute-start.12 = (bf16[64,1024]{1,0:T(8,128)(2,1)S(1)}, bf16[64,1024]{1,0:T(8,128)(2,1)S(1)}, u32[]{:S(2)}, u32[]{:S(2)}) collective-permute-start(bf16[64,1024]{1,0:T(8,128)(2,1)S(1)} %get-tuple-element.93), channel_id=1, source_target_pairs={{0,16},{4,20},{8,24},{12,28},{16,0},{20,4},{24,8},{28,12},{1,17},{... | collective-permute-start | bytes 393224 | tf_op jit(solution)/shard_map/ppermute | solution.py:350
  50.8 7.7 %collective-permute-start.33 = (bf16[64,512]{1,0:T(8,128)(2,1)S(1)}, bf16[64,512]{1,0:T(8,128)(2,1)S(1)}, u32[]{:S(2)}, u32[]{:S(2)}) collective-permute-start(bf16[64,512]{1,0:T(8,128)(2,1)S(1)} %get-tuple-element.121), channel_id=1, source_target_pairs={{0,8},{4,12},{8,0},{12,4},{16,24},{20,28},{24,16},{28,20},{1,9},{5... | collective-permute-start | bytes 196616 | tf_op jit(solution)/shard_map/ppermute | solution.py:350
  58.5 10.5 %collective-permute-start.13 = (bf16[64,1024]{1,0:T(8,128)(2,1)S(1)}, bf16[64,1024]{1,0:T(8,128)(2,1)S(1)}, u32[]{:S(2)}, u32[]{:S(2)}) collective-permute-start(bf16[64,1024]{1,0:T(8,128)(2,1)S(1)} %get-tuple-element.94), channel_id=1, source_target_pairs={{0,20},{4,16},{8,28},{12,24},{16,4},{20,0},{24,12},{28,8},{1,21},{... | collective-permute-start | bytes 393224 | tf_op jit(solution)/shard_map/ppermute | solution.py:350
  58.5 11.7 %collective-permute-start.14 = (bf16[64,1024]{1,0:T(8,128)(2,1)S(1)}, bf16[64,1024]{1,0:T(8,128)(2,1)S(1)}, u32[]{:S(2)}, u32[]{:S(2)}) collective-permute-start(bf16[64,1024]{1,0:T(8,128)(2,1)S(1)} %get-tuple-element.95), channel_id=1, source_target_pairs={{0,24},{4,28},{8,16},{12,20},{16,8},{20,12},{24,0},{28,4},{1,25},{... | collective-permute-start | bytes 393224 | tf_op jit(solution)/shard_map/ppermute | solution.py:350
  59.1 12.7 %collective-permute-start.15 = (bf16[64,1024]{1,0:T(8,128)(2,1)S(1)}, bf16[64,1024]{1,0:T(8,128)(2,1)S(1)}, u32[]{:S(2)}, u32[]{:S(2)}) collective-permute-start(bf16[64,1024]{1,0:T(8,128)(2,1)S(1)} %get-tuple-element.96), channel_id=1, source_target_pairs={{0,28},{4,24},{8,20},{12,16},{16,12},{20,8},{24,4},{28,0},{1,29},{... | collective-permute-start | bytes 393224 | tf_op jit(solution)/shard_map/ppermute | solution.py:350
  61.4 10.7 %collective-permute-start.24 = (bf16[64,1024]{1,0:T(8,128)(2,1)S(1)}, bf16[64,1024]{1,0:T(8,128)(2,1)S(1)}, u32[]{:S(2)}, u32[]{:S(2)}) collective-permute-start(bf16[64,1024]{1,0:T(8,128)(2,1)S(1)} %get-tuple-element.111), channel_id=1, source_target_pairs={{0,4},{4,0},{8,12},{12,8},{16,20},{20,16},{24,28},{28,24},{1,5},{5... | collective-permute-start | bytes 393224 | tf_op jit(solution)/shard_map/ppermute | solution.py:350
  61.6 11.9 %collective-permute-start.25 = (bf16[64,1024]{1,0:T(8,128)(2,1)S(1)}, bf16[64,1024]{1,0:T(8,128)(2,1)S(1)}, u32[]{:S(2)}, u32[]{:S(2)}) collective-permute-start(bf16[64,1024]{1,0:T(8,128)(2,1)S(1)} %get-tuple-element.112), channel_id=1, source_target_pairs={{0,8},{4,12},{8,0},{12,4},{16,24},{20,28},{24,16},{28,20},{1,9},{5... | collective-permute-start | bytes 393224 | tf_op jit(solution)/shard_map/ppermute | solution.py:350
  69.0 8.3 %collective-permute-start.26 = (bf16[64,1024]{1,0:T(8,128)(2,1)S(1)}, bf16[64,1024]{1,0:T(8,128)(2,1)S(1)}, u32[]{:S(2)}, u32[]{:S(2)}) collective-permute-start(bf16[64,1024]{1,0:T(8,128)(2,1)S(1)} %get-tuple-element.113), channel_id=1, source_target_pairs={{0,12},{4,8},{8,4},{12,0},{16,28},{20,24},{24,20},{28,16},{1,13},{... | collective-permute-start | bytes 393224 | tf_op jit(solution)/shard_map/ppermute | solution.py:350
  70.3 12.0 %collective-permute-start.27 = (bf16[64,1024]{1,0:T(8,128)(2,1)S(1)}, bf16[64,1024]{1,0:T(8,128)(2,1)S(1)}, u32[]{:S(2)}, u32[]{:S(2)}) collective-permute-start(bf16[64,1024]{1,0:T(8,128)(2,1)S(1)} %get-tuple-element.114), channel_id=1, source_target_pairs={{0,16},{4,20},{8,24},{12,28},{16,0},{20,4},{24,8},{28,12},{1,17},{... | collective-permute-start | bytes 393224 | tf_op jit(solution)/shard_map/ppermute | solution.py:350
  71.8 12.3 %collective-permute-start.28 = (bf16[64,1024]{1,0:T(8,128)(2,1)S(1)}, bf16[64,1024]{1,0:T(8,128)(2,1)S(1)}, u32[]{:S(2)}, u32[]{:S(2)}) collective-permute-start(bf16[64,1024]{1,0:T(8,128)(2,1)S(1)} %get-tuple-element.115), channel_id=1, source_target_pairs={{0,20},{4,16},{8,28},{12,24},{16,4},{20,0},{24,12},{28,8},{1,21},{... | collective-permute-start | bytes 393224 | tf_op jit(solution)/shard_map/ppermute | solution.py:350
  72.1 13.9 %collective-permute-start.29 = (bf16[64,1024]{1,0:T(8,128)(2,1)S(1)}, bf16[64,1024]{1,0:T(8,128)(2,1)S(1)}, u32[]{:S(2)}, u32[]{:S(2)}) collective-permute-start(bf16[64,1024]{1,0:T(8,128)(2,1)S(1)} %get-tuple-element.116), channel_id=1, source_target_pairs={{0,24},{4,28},{8,16},{12,20},{16,8},{20,12},{24,0},{28,4},{1,25},{... | collective-permute-start | bytes 393224 | tf_op jit(solution)/shard_map/ppermute | solution.py:350
  73.5 13.0 %collective-permute-start.30 = (bf16[64,1024]{1,0:T(8,128)(2,1)S(1)}, bf16[64,1024]{1,0:T(8,128)(2,1)S(1)}, u32[]{:S(2)}, u32[]{:S(2)}) collective-permute-start(bf16[64,1024]{1,0:T(8,128)(2,1)S(1)} %get-tuple-element.117), channel_id=1, source_target_pairs={{0,28},{4,24},{8,20},{12,16},{16,12},{20,8},{24,4},{28,0},{1,29},{... | collective-permute-start | bytes 393224 | tf_op jit(solution)/shard_map/ppermute | solution.py:350
  77.3 12.5 %collective-permute-start.34 = (bf16[64,512]{1,0:T(8,128)(2,1)S(1)}, bf16[64,512]{1,0:T(8,128)(2,1)S(1)}, u32[]{:S(2)}, u32[]{:S(2)}) collective-permute-start(bf16[64,512]{1,0:T(8,128)(2,1)S(1)} %get-tuple-element.122), channel_id=1, source_target_pairs={{0,12},{4,8},{8,4},{12,0},{16,28},{20,24},{24,20},{28,16},{1,13},{... | collective-permute-start | bytes 196616 | tf_op jit(solution)/shard_map/ppermute | solution.py:350
  82.2 7.6 %collective-permute-start.35 = (bf16[64,512]{1,0:T(8,128)(2,1)S(1)}, bf16[64,512]{1,0:T(8,128)(2,1)S(1)}, u32[]{:S(2)}, u32[]{:S(2)}) collective-permute-start(bf16[64,512]{1,0:T(8,128)(2,1)S(1)} %get-tuple-element.123), channel_id=1, source_target_pairs={{0,16},{4,20},{8,24},{12,28},{16,0},{20,4},{24,8},{28,12},{1,17},{... | collective-permute-start | bytes 196616 | tf_op jit(solution)/shard_map/ppermute | solution.py:350
  84.1 5.7 %collective-permute-start.36 = (bf16[64,512]{1,0:T(8,128)(2,1)S(1)}, bf16[64,512]{1,0:T(8,128)(2,1)S(1)}, u32[]{:S(2)}, u32[]{:S(2)}) collective-permute-start(bf16[64,512]{1,0:T(8,128)(2,1)S(1)} %get-tuple-element.124), channel_id=1, source_target_pairs={{0,20},{4,16},{8,28},{12,24},{16,4},{20,0},{24,12},{28,8},{1,21},{... | collective-permute-start | bytes 196616 | tf_op jit(solution)/shard_map/ppermute | solution.py:350
  86.0 5.8 %collective-permute-start.37 = (bf16[64,512]{1,0:T(8,128)(2,1)S(1)}, bf16[64,512]{1,0:T(8,128)(2,1)S(1)}, u32[]{:S(2)}, u32[]{:S(2)}) collective-permute-start(bf16[64,512]{1,0:T(8,128)(2,1)S(1)} %get-tuple-element.125), channel_id=1, source_target_pairs={{0,24},{4,28},{8,16},{12,20},{16,8},{20,12},{24,0},{28,4},{1,25},{... | collective-permute-start | bytes 196616 | tf_op jit(solution)/shard_map/ppermute | solution.py:350
  86.5 5.3 %collective-permute-start.38 = (bf16[64,512]{1,0:T(8,128)(2,1)S(1)}, bf16[64,512]{1,0:T(8,128)(2,1)S(1)}, u32[]{:S(2)}, u32[]{:S(2)}) collective-permute-start(bf16[64,512]{1,0:T(8,128)(2,1)S(1)} %get-tuple-element.126), channel_id=1, source_target_pairs={{0,28},{4,24},{8,20},{12,16},{16,12},{20,8},{24,4},{28,0},{1,29},{... | collective-permute-start | bytes 196616 | tf_op jit(solution)/shard_map/ppermute | solution.py:350
  94.6 45.5 %collective-permute-start.40 = (bf16[512,768]{1,0:T(8,128)(2,1)S(1)}, bf16[512,768]{1,0:T(8,128)(2,1)S(1)}, u32[]{:S(2)}, u32[]{:S(2)}) collective-permute-start(bf16[512,768]{1,0:T(8,128)(2,1)S(1)} %shard_map.117), channel_id=1, source_target_pairs={{0,1},{1,0},{2,3},{3,2},{4,5},{5,4},{6,7},{7,6},{8,9},{9,8},{10,11... | collective-permute-start | bytes 2359304 | tf_op jit(solution)/shard_map/ppermute | solution.py:356
  101.9 5.9 %collective-permute-start.16 = (bf16[64,1024]{1,0:T(8,128)(2,1)S(1)}, bf16[64,1024]{1,0:T(8,128)(2,1)S(1)}, u32[]{:S(2)}, u32[]{:S(2)}) collective-permute-start(bf16[64,1024]{1,0:T(8,128)(2,1)S(1)} %get-tuple-element.100), channel_id=1, source_target_pairs={{0,4},{4,0},{8,12},{12,8},{16,20},{20,16},{24,28},{28,24},{1,5},{5... | collective-permute-start | bytes 393224 | tf_op jit(solution)/shard_map/ppermute | solution.py:350
  102.2 6.4 %collective-permute-start.17 = (bf16[64,1024]{1,0:T(8,128)(2,1)S(1)}, bf16[64,1024]{1,0:T(8,128)(2,1)S(1)}, u32[]{:S(2)}, u32[]{:S(2)}) collective-permute-start(bf16[64,1024]{1,0:T(8,128)(2,1)S(1)} %get-tuple-element.101), channel_id=1, source_target_pairs={{0,8},{4,12},{8,0},{12,4},{16,24},{20,28},{24,16},{28,20},{1,9},{5... | collective-permute-start | bytes 393224 | tf_op jit(solution)/shard_map/ppermute | solution.py:350
  103.3 6.6 %collective-permute-start.18 = (bf16[64,1024]{1,0:T(8,128)(2,1)S(1)}, bf16[64,1024]{1,0:T(8,128)(2,1)S(1)}, u32[]{:S(2)}, u32[]{:S(2)}) collective-permute-start(bf16[64,1024]{1,0:T(8,128)(2,1)S(1)} %get-tuple-element.102), channel_id=1, source_target_pairs={{0,12},{4,8},{8,4},{12,0},{16,28},{20,24},{24,20},{28,16},{1,13},{... | collective-permute-start | bytes 393224 | tf_op jit(solution)/shard_map/ppermute | solution.py:350
  105.0 21.3 %collective-permute-start.42 = (bf16[512,512]{1,0:T(8,128)(2,1)S(1)}, bf16[512,512]{1,0:T(8,128)(2,1)S(1)}, u32[]{:S(2)}, u32[]{:S(2)}) collective-permute-start(bf16[512,512]{1,0:T(8,128)(2,1)S(1)} %shard_map.121), channel_id=1, source_target_pairs={{0,1},{1,0},{2,3},{3,2},{4,5},{5,4},{6,7},{7,6},{8,9},{9,8},{10,11... | collective-permute-start | bytes 1572872 | tf_op jit(solution)/shard_map/ppermute | solution.py:356
  107.8 29.8 %collective-permute-start.41 = (bf16[512,512]{1,0:T(8,128)(2,1)S(1)}, bf16[512,512]{1,0:T(8,128)(2,1)S(1)}, u32[]{:S(2)}, u32[]{:S(2)}) collective-permute-start(bf16[512,512]{1,0:T(8,128)(2,1)S(1)} %shard_map.120), channel_id=1, source_target_pairs={{0,1},{1,0},{2,3},{3,2},{4,5},{5,4},{6,7},{7,6},{8,9},{9,8},{10,11... | collective-permute-start | bytes 1572872 | tf_op jit(solution)/shard_map/ppermute | solution.py:356
  108.5 6.2 %collective-permute-start.19 = (bf16[64,1024]{1,0:T(8,128)(2,1)S(1)}, bf16[64,1024]{1,0:T(8,128)(2,1)S(1)}, u32[]{:S(2)}, u32[]{:S(2)}) collective-permute-start(bf16[64,1024]{1,0:T(8,128)(2,1)S(1)} %get-tuple-element.103), channel_id=1, source_target_pairs={{0,16},{4,20},{8,24},{12,28},{16,0},{20,4},{24,8},{28,12},{1,17},{... | collective-permute-start | bytes 393224 | tf_op jit(solution)/shard_map/ppermute | solution.py:350
  109.9 6.8 %collective-permute-start.20 = (bf16[64,1024]{1,0:T(8,128)(2,1)S(1)}, bf16[64,1024]{1,0:T(8,128)(2,1)S(1)}, u32[]{:S(2)}, u32[]{:S(2)}) collective-permute-start(bf16[64,1024]{1,0:T(8,128)(2,1)S(1)} %get-tuple-element.104), channel_id=1, source_target_pairs={{0,20},{4,16},{8,28},{12,24},{16,4},{20,0},{24,12},{28,8},{1,21},{... | collective-permute-start | bytes 393224 | tf_op jit(solution)/shard_map/ppermute | solution.py:350
  114.7 5.9 %collective-permute-start.21 = (bf16[64,1024]{1,0:T(8,128)(2,1)S(1)}, bf16[64,1024]{1,0:T(8,128)(2,1)S(1)}, u32[]{:S(2)}, u32[]{:S(2)}) collective-permute-start(bf16[64,1024]{1,0:T(8,128)(2,1)S(1)} %get-tuple-element.105), channel_id=1, source_target_pairs={{0,24},{4,28},{8,16},{12,20},{16,8},{20,12},{24,0},{28,4},{1,25},{... | collective-permute-start | bytes 393224 | tf_op jit(solution)/shard_map/ppermute | solution.py:350
  116.7 5.3 %collective-permute-start.22 = (bf16[64,1024]{1,0:T(8,128)(2,1)S(1)}, bf16[64,1024]{1,0:T(8,128)(2,1)S(1)}, u32[]{:S(2)}, u32[]{:S(2)}) collective-permute-start(bf16[64,1024]{1,0:T(8,128)(2,1)S(1)} %get-tuple-element.106), channel_id=1, source_target_pairs={{0,28},{4,24},{8,20},{12,16},{16,12},{20,8},{24,4},{28,0},{1,29},{... | collective-permute-start | bytes 393224 | tf_op jit(solution)/shard_map/ppermute | solution.py:350
  120.6 22.2 %collective-permute-start.39 = (bf16[512,256]{1,0:T(8,128)(2,1)S(1)}, bf16[512,256]{1,0:T(8,128)(2,1)S(1)}, u32[]{:S(2)}, u32[]{:S(2)}) collective-permute-start(bf16[512,256]{1,0:T(8,128)(2,1)S(1)} %shard_map.116), channel_id=1, source_target_pairs={{0,1},{1,0},{2,3},{3,2},{4,5},{5,4},{6,7},{7,6},{8,9},{9,8},{10,11... | collective-permute-start | bytes 786440 | tf_op jit(solution)/shard_map/ppermute | solution.py:356

commit v5 on v4

--- a/solution.py
+++ b/solution.py
@@ -34,8 +34,7 @@
 
 
 def steps(extent, most):
-    size = min(extent, most)
-    return [(at, size) for at in range(0, extent, size)]
+    return [(at, min(most, extent - at)) for at in range(0, extent, most)]
 
 
 def stack(refs, experts):
@@ -76,14 +75,20 @@
     return ids == first_flat.astype(jnp.int32), ids == second_flat.astype(jnp.int32)
 
 
-def place(pick, source, out_refs, block, left=0):
-    for at, size in steps(source.shape[1], 256):
-        rows = dot(pick, source[:, at : at + size]).astype(bf16)
+def place(pick, source, out_refs, block, left=0, begin=0, end=None):
+    end = source.shape[1] if end is None else end
+    for at, size in steps(end - begin, 256):
+        rows = dot(pick, source[:, begin + at : begin + at + size]).astype(bf16)
         for k, out in enumerate(out_refs):
             out[:, left + at : left + at + size] = rows[k * block : (k + 1) * block]
 
 
-def own_send_kernel(experts, block, capacity, routes, keep, combine, tokens, grad_out, meta, *outs):
+def own_send_kernel(
+    experts, block, capacity, routes, keep, combine, tokens, grad_out, meta, lefts, rights, *outs
+):
+    end = lefts.shape[1]
+    lefts[...] = grad_out[:, :end]
+    rights[...] = grad_out[:, end:]
     me = lax.axis_index("expert")
     a, b, c, d = slot_rows(routes[...], keep[...], combine[...], me, experts, block, capacity)
     meta[0:1, :] = a
@@ -94,7 +99,7 @@
     first, second = picks(a, b, experts * block)
     place(jnp.where(first | second, 1.0, 0.0).astype(bf16), tokens, outs, block)
     weighted = jnp.where(first, c, jnp.where(second, d, 0.0)).astype(bf16)
-    place(weighted, grad_out, outs, block, tokens.shape[1])
+    place(weighted, grad_out, outs, block, tokens.shape[1], 0, end)
 
 
 def load_kernel(pos, w_in, w_out, in_half, out_half):
@@ -107,10 +112,10 @@
     place(jnp.where(first | second, 1.0, 0.0).astype(bf16), tokens, outs, block)
 
 
-def send_s_kernel(experts, block, meta, grad_out, *refs):
+def send_s_kernel(experts, block, begin, meta, grad_out, *refs):
     first, second = picks(meta[0:1, :], meta[1:2, :], experts * block)
     weighted = jnp.where(first, meta[2:3, :], jnp.where(second, meta[3:4, :], 0.0))
-    place(weighted.astype(bf16), grad_out, refs[-experts:], block)
+    place(weighted.astype(bf16), grad_out, refs[-experts:], block, 0, begin)
 
 
 def gate_sums(active, up):
@@ -134,22 +139,17 @@
     act_rows(w_in[...], stack(refs[:-2], experts), *refs[-2:], 0, w_in.shape[0])
 
 
-def other_grad_kernel(experts, lefts, w_out, slope, *refs):
-    run = w_out.shape[1] // 2
-    s = jnp.concatenate(
-        [cut(refs[:experts], lefts[0], run), cut(refs[experts : 2 * experts], lefts[1], run)], axis=1
-    )
+def other_grad_kernel(experts, sa, sb, w_out, slope, *refs):
+    s = jnp.concatenate([cut(refs[:experts], *sa), cut(refs[experts : 2 * experts], *sb)], axis=1)
     for at, size in steps(w_out.shape[0], 256):
         up = dot(w_out[at : at + size, :], s, NT)
         refs[-1][at : at + size, :] = (up * slope[at : at + size, :].astype(f32)).astype(bf16)
 
 
-def own_grad_kernel(experts, lefts, w_in, w_out, act, slope, *refs):
-    blocks, (grad, total, gates) = refs[:-3], refs[-3:]
-    run = w_out.shape[1] // 2
-    s = jnp.concatenate(
-        [cut(blocks[:experts], lefts[0], run), cut(blocks[experts:], lefts[1], run)], axis=1
-    )
+def own_grad_kernel(experts, sa, sb, w_in, w_out, act, slope, *refs):
+    blocks, (grad, total, gates, scaled) = refs[:-4], refs[-4:]
+    s = jnp.concatenate([cut(blocks[:experts], *sa), cut(blocks[experts:], *sb)], axis=1)
+    scaled[...] = s
     sums = 0.0
     for at, size in steps(w_out.shape[0], 256):
         up = dot(w_out[at : at + size, :], s, NT)
@@ -160,8 +160,8 @@
         total[:, at : at + size] = dot(grad[...], w_in[:, at : at + size], TN)
 
 
-def far_kernel(experts, block, capacity, pos, w_in, w_out, act, slope, near_total, near_gates, *refs):
-    blocks, outs, (total, gates) = refs[: 2 * experts], refs[2 * experts : -2], refs[-2:]
+def far_kernel(block, capacity, pos, w_in, w_out, act, slope, near_total, near_gates, scaled, *refs):
+    outs, (total, gates) = refs[:-2], refs[-2:]
     step, last = pl.program_id(0), pl.num_programs(0) - 1
 
     @pl.when(step == 0)
@@ -169,7 +169,7 @@
         total[...] = near_total[...]
         gates[...] = near_gates[...]
 
-    up = dot(w_out[...], stack(blocks, experts), NT)
+    up = dot(w_out[...], scaled[...], NT)
     gates[...] += gate_sums(act[...], up)
     total[...] += dot((up * slope[...].astype(f32)).astype(bf16), w_in[...], TN)
 
@@ -184,12 +184,6 @@
 
 def cut(refs, left, size):
     return jnp.concatenate([ref[:, left : left + size] for ref in refs], axis=0)
-
-
-def outer_rows(experts, own, other, refs):
-    return dot(own[...], stack(refs[:experts], experts)) + dot(
-        other[...], stack(refs[experts : 2 * experts], experts)
-    )
 
 
 def away_kernel(experts, owners, r, left, right, pos, own, other, *refs):
@@ -202,11 +196,28 @@
         out[:, at : at + run] = total.astype(out.dtype)
 
 
-def home_kernel(experts, owners, pos, own, other, *refs):
-    total = outer_rows(experts, own, other, refs)
-    for ref in refs[2 * experts : 2 * experts + owners - 1]:
-        total = total + ref[...].astype(f32)
-    refs[-1][0] = total
+def home_kernel(experts, owners, parts, pos, own, other, *refs):
+    out, total, sems = refs[-3:]
+    size = own.shape[0] // owners
+    mine = pl.ds(pl.multiple_of(pos[1] * size, size), size)
+    per, column, copies = 2 * experts + owners - 1, 0, []
+    for number, (left, right, extent) in enumerate(parts):
+        blocks = refs[number * per : (number + 1) * per]
+        for at, run in steps(extent, 256):
+            rows = dot(own[mine, :], cut(blocks[:experts], left + at, run))
+            rows += dot(other[mine, :], cut(blocks[experts : 2 * experts], right + at, run))
+            for ref in blocks[2 * experts :]:
+                rows += ref[:, at : at + run].astype(f32)
+            total[:, column : column + run] = rows
+            here = slice(column, column + run)
+            copy = pltpu.make_async_copy(
+                total.at[:, here], out.at[0, :, here], sems.at[len(copies)]
+            )
+            copy.start()
+            copies.append(copy)
+            column += run
+    for copy in copies:
+        copy.wait()
 
 
 def after_kernel(owners, before, *refs):
@@ -267,12 +278,6 @@
 
 def rows(array, size):
     return pl.BlockSpec((size, array.shape[1]), lambda g, *pos: (g, 0))
-
-
-def share_rows(array, owners, r):
-    return pl.BlockSpec(
-        (array.shape[0] // owners, array.shape[1]), lambda g, pos: (lax.rem(pos[1] + r, owners), 0)
-    )
 
 
 def half_rows(array, parts, far=0):
@@ -345,11 +350,12 @@
     def across(value):
         return lax.ppermute(value, "dp", [(j, (j + owners) % planes) for j in range(planes)])
 
-    def exchange(values):
-        return [values[0]] + [
+    def exchange(values, which=None):
+        sent = [
             lax.ppermute(values[k], "expert", [(i, i ^ k) for i in range(experts)])
-            for k in range(1, experts)
+            for k in which or range(1, experts)
         ]
+        return sent if which else [values[0]] + sent
 
     def to_owners(values):
         return [
@@ -371,8 +377,9 @@
 
     other_x = across(tokens)
     half = width // 2
-    other_dya = across(grad_out[:, :half])
-    other_dyb = across(grad_out[:, half:])
+    rest = width - half
+    half = width // 2
+    rest = width - half
 
     def blocks(columns_of):
         return [shaped((block, columns_of))] * experts
@@ -381,13 +388,15 @@
     unit_parts = max(units // 256, 1)
     unit_rows = units // unit_parts
     meta_shape = shaped((8, count), f32)
-    meta, *own_xs = call(
+    meta, dya, dyb, *own_xs = call(
         bind(own_send_kernel, experts, block, capacity),
         1,
         [],
-        each([stay(a) for a in (routes_t, keep_t, combine_t, tokens)], full)
-        + window([stay(grad_out)], 0, half),
-        each([meta_shape] + blocks(width + half), full),
+        each([stay(a) for a in (routes_t, keep_t, combine_t, tokens, grad_out)], full),
+        each(
+            [meta_shape, shaped((count, half)), shaped((count, rest))] + blocks(width + half),
+            full,
+        ),
         flops=3 * slots * count * width,
     )
     own_xs = exchange(own_xs)
@@ -398,6 +407,8 @@
         each([stay(w_in), stay(w_out)], half_rows, 4),
         each([shaped((units, width))] * 2, rows, units // 4),
     )
+    other_dya = across(dya)
+    other_dyb = across(dyb)
     other_meta = across(meta)
     other_xb = call(
         bind(send_x_kernel, experts, block),
@@ -409,15 +420,15 @@
     )
     x_out = exchange(other_xb)
     sb_out = call(
-        bind(send_s_kernel, experts, block),
+        bind(send_s_kernel, experts, block, 0),
         1,
         [],
-        each([meta], full) + window([stay(grad_out)], half, half),
-        window(blocks(2 * half), 0, half),
+        each([meta, dyb], full),
+        window(blocks(2 * rest), 0, rest),
         flops=slots * count * width,
     )
     sa_out = call(
-        bind(send_s_kernel, experts, block),
+        bind(send_s_kernel, experts, block, 0),
         1,
         [],
         each([other_meta, other_dya], full),
@@ -426,19 +437,21 @@
     )
     sa_out = exchange(sa_out)
     sb_out = call(
-        bind(send_s_kernel, experts, block),
+        bind(send_s_kernel, experts, block, 0),
         1,
         [],
         each([other_meta, other_dyb], full)
         + [(a, pl.BlockSpec(memory_space=pl.ANY)) for a in sb_out],
-        window(blocks(2 * half), half, half),
+        window(blocks(2 * rest), rest, rest),
         flops=slots * count * width,
         alias={2 + k: k for k in range(experts)},
     )
-    sb_out = exchange(sb_out)
+    near = experts * 3 // 4
+    sb_far = exchange(sb_out, range(near, experts))
+    sb_out = [sb_out[0]] + exchange(sb_out, range(1, near)) + sb_far
     own_x, other_x = (own_xs, 0), (x_out, 0)
     own_sa, other_sa = (own_xs, width), (sa_out, 0)
-    own_sb, other_sb = (sb_out, 0), (sb_out, half)
+    own_sb, other_sb = (sb_out, 0), (sb_out, rest)
 
     def act(x):
         return direct(
@@ -458,16 +471,14 @@
     run = width // 4
     fed = slots * share * run
 
-    def away(acts, left, right, first, many):
+    def away(acts, left, right, first, extent):
         return [
             direct(
-                bind(
-                    away_kernel, experts, owners, r, left[1] + first * run, right[1] + first * run
-                ),
+                bind(away_kernel, experts, owners, r, left[1] + first, right[1] + first),
                 [pos],
                 acts + left[0] + right[0],
-                [shaped((share, many * run))],
-                4 * fed * many,
+                [shaped((share, extent))],
+                4 * slots * share * extent,
             )[0]
             for r in range(1, owners)
         ]
@@ -480,25 +491,6 @@
         return operands + [(array, pl.BlockSpec(memory_space=pl.ANY))], {
             len(operands) + prefetched: 0
         }
-
-    def home(acts, left, right, got, first, many, array=None):
-        operands, alias = into(
-            array,
-            each(acts, share_rows, owners, 0)
-            + runs_of(*left, run)
-            + runs_of(*right, run)
-            + each(got, columns, many),
-            1,
-        )
-        return call(
-            bind(home_kernel, experts, owners),
-            many,
-            [pos],
-            operands,
-            each([goal], columns, 4, first),
-            flops=4 * fed * many,
-            alias=alias,
-        )[0]
 
     def after(before, got, first, many, array=None):
         operands, alias = into(
@@ -514,47 +506,69 @@
         )[0]
 
     out_acts = [own_act, other_act]
-    away_oa = away(out_acts, own_sa, other_sa, 0, 2)
+    away_oa = away(out_acts, own_sa, other_sa, 0, half)
     got_oa = to_owners(away_oa)
-    away_ob = away(out_acts, own_sb, other_sb, 0, 2)
+    away_ob = away(out_acts, own_sb, other_sb, 0, rest)
     got_ob = to_owners(away_ob)
     total_shape, gate_shape = shaped((slots, width), f32), shaped((1, slots), f32)
-    own_grad, near_total, near_gates = direct(
-        bind(own_grad_kernel, experts, (own_sa[1], own_sb[1])),
+    own_grad, near_total, near_gates, own_scaled = direct(
+        bind(own_grad_kernel, experts, (own_sa[1], half), (own_sb[1], rest)),
         [],
         [half_in, half_out, own_act, own_slope] + own_sa[0] + own_sb[0],
-        [act_shape, total_shape, gate_shape],
+        [act_shape, total_shape, gate_shape, shaped((slots, width))],
         4 * slots * units * width,
     )
     other_grad = direct(
-        bind(other_grad_kernel, experts, (other_sa[1], other_sb[1])),
+        bind(other_grad_kernel, experts, (other_sa[1], half), (other_sb[1], rest)),
         [],
         [half_out, other_slope] + other_sa[0] + other_sb[0],
         [act_shape],
         2 * slots * units * width,
     )[0]
     own_back = call(
-        bind(far_kernel, experts, block, capacity),
+        bind(far_kernel, block, capacity),
         unit_parts,
         [pos],
         each([stay(w_in), stay(w_out)], half_rows, unit_parts, 1)
         + each([far_act, far_slope], rows, unit_rows)
-        + each([near_total, near_gates], full)
-        + window(*own_sa, half)
-        + window(*own_sb, half),
+        + each([near_total, near_gates, own_scaled], full),
         each(blocks(width), full),
         [pltpu.VMEM((slots, width), f32), pltpu.VMEM((1, slots), f32)],
         4 * slots * units * width,
     )
     in_acts = [own_grad, other_grad]
-    away_a = away(in_acts, own_x, other_x, 0, 3)
+    away_a = away(in_acts, own_x, other_x, 0, 3 * run)
     got_a = to_owners(away_a)
-    away_b = away(in_acts, own_x, other_x, 3, 1)
+    away_b = away(in_acts, own_x, other_x, 3 * run, run)
     got_b = to_owners(away_b)
     own_back = exchange(own_back)
 
-    grad_outw = home(out_acts, own_sa, other_sa, got_oa, 0, 2)
-    grad_outw = home(out_acts, own_sb, other_sb, got_ob, 2, 2, grad_outw)
+    operands = (
+        out_acts
+        + own_sa[0]
+        + other_sa[0]
+        + got_oa
+        + own_sb[0]
+        + other_sb[0]
+        + got_ob
+    )
+    parts = ((own_sa[1], other_sa[1], half), (own_sb[1], other_sb[1], rest))
+    grad_outw = pl.pallas_call(
+        bind(home_kernel, experts, owners, parts),
+        name="home_out",
+        out_shape=goal,
+        in_specs=[pl.BlockSpec(memory_space=pltpu.SMEM)]
+        + [pl.BlockSpec(memory_space=pltpu.VMEM)] * len(operands),
+        out_specs=pl.BlockSpec(memory_space=pl.ANY),
+        scratch_shapes=[
+            pltpu.VMEM((share, width), f32),
+            pltpu.SemaphoreType.DMA((len(steps(half, 256)) + len(steps(rest, 256)),)),
+        ],
+        compiler_params=pltpu.CompilerParams(vmem_limit_bytes=28 << 20),
+        cost_estimate=pl.CostEstimate(
+            flops=4 * slots * share * width, transcendentals=0, bytes_accessed=12 * share * width
+        ),
+    )(pos, *operands)
     grad_tokens, grad_combine = call(
         bind(collect_kernel, experts, block, capacity),
         2,

time: 146 us -> 144 us (0.986)
  waiting for transfers between devices: 54.5 us -> 58.7 us
  Pallas kernels: 43.7 us -> 40.6 us
  starting transfers between devices: 43.4 us -> 41.8 us
    ppermute x35, waiting for transfers between devices: 13.4 us -> 21.5 us  [exchange(): lax.ppermute(values[k], 'expert', [(i, i ^ k) for i in range(experts)])]
    pallas_call x13 -> x11, Pallas kernels: 28.7 us -> 22.7 us  [call(): pl.pallas_call(kernel, out_shape=outs, grid_spec=pltpu.PrefetchScalarGrid...]
    ppermute x4, waiting for transfers between devices: 10.5 us -> 7.38 us  [to_owners(): lax.ppermute(value, 'dp', [(j, j // owners * owners + (j + r + 1) % owner...]
    pallas_call x0 -> x1, Pallas kernels: none -> 2.9 us  [per_device(): pl.pallas_call(bind(home_kernel, experts, owners, parts), name='home_out'...]
  transfers between devices with their start and end apart: 43 -> 43, of which waited for: 16 -> 13; matrix products, arithmetic and copies ran while one was open for 1% -> 0% of each run, Pallas kernels for 27% -> 25%
where the time goes in v5:
time: 144 us; the launch traced here: 142 us
  waiting for transfers between devices  58.7 us (41%)
  starting transfers between devices  41.8 us (29%)
  Pallas kernels  40.6 us (28%)
    ppermute x4, waiting for transfers between devices, across(): lax.ppermute(value, 'dp', [(j, (j + owners) % planes) for j in range(plan...  29.7 us
    ppermute x35, starting transfers between devices, exchange(): lax.ppermute(values[k], 'expert', [(i, i ^ k) for i in range(experts)])  29.6 us
    pallas_call x11, Pallas kernels, call(): pl.pallas_call(kernel, out_shape=outs, grid_spec=pltpu.PrefetchScalarGrid...  22.7 us
    ppermute x35, waiting for transfers between devices, exchange(): lax.ppermute(values[k], 'expert', [(i, i ^ k) for i in range(experts)])  21.5 us
    pallas_call x9, Pallas kernels, direct(): pl.pallas_call(kernel, out_shape=outs, in_specs=[pl.BlockSpec(memory_spac...  15 us
    ppermute x4, starting transfers between devices, across(): lax.ppermute(value, 'dp', [(j, (j + owners) % planes) for j in range(plan...  8.12 us
    ppermute x4, waiting for transfers between devices, to_owners(): lax.ppermute(value, 'dp', [(j, j // owners * owners + (j + r + 1) % owner...  7.38 us
    ppermute x4, starting transfers between devices, to_owners(): lax.ppermute(value, 'dp', [(j, j // owners * owners + (j + r + 1) % owner...  4.06 us
  transfers between devices with their start and end apart: 43, of which 13 were waited for; matrix products, arithmetic and copies ran while one was open for 0% of the time, Pallas kernels for 25%

profile of v5, /device:TPU:2, one launch (start us, length us, event | category | flops | bytes accessed | tf_op | source)
XLA Modules:
  0.0 142.0 jit_solution(7352113164421080547)
XLA Ops:
  0.6 2.0 %shard_map.102 = (f32[8,192]{1,0:T(8,128)S(1)}, bf16[192,512]{1,0:T(8,128)(2,1)S(1)}, bf16[192,512]{1,0:T(8,128)(2,1)S(1)}, bf16[64,1536]{1,0:T(8,128)(2,1)S(1)}...) custom-call(s32[2,192]{1,0:T(2,128)} %bitcast.6, ...), custom_call_target="tpu_custom_call" | custom-call | flops 301989888 | bytes 2761728 | tf_op jit(solution)/shard_map/pallas_call | solution.py:294
  2.8 3.1 %collective-permute-start.7 = (f32[8,192]{1,0:T(8,128)S(1)}, f32[8,192]{1,0:T(8,128)S(1)}, u32[]{:S(2)}, u32[]{:S(2)}) collective-permute-start(f32[8,192]{1,0:T(8,128)S(1)} %get-tuple-element.69.meta), channel_id=1, source_target_pairs={{0,2},{1,3},{2,0},{3,1},{4,6},{5,7},{6,4},{7,5},{8,10},{9,11},{10,... | collective-permute-start | bytes 18440 | tf_op jit(solution)/shard_map/ppermute | solution.py:351
  5.9 1.0 collective-permute-start.2
  6.9 1.5 %collective-permute-start.3 = (bf16[64,1536]{1,0:T(8,128)(2,1)S(1)}, bf16[64,1536]{1,0:T(8,128)(2,1)S(1)}, u32[]{:S(2)}, u32[]{:S(2)}) collective-permute-start(bf16[64,1536]{1,0:T(8,128)(2,1)S(1)} %get-tuple-element.74), channel_id=1, source_target_pairs={{0,16},{4,20},{8,24},{12,28},{16,0},{20,4},{24,8},{28,12},{1,17},{... | collective-permute-start | bytes 589832 | tf_op jit(solution)/shard_map/ppermute | solution.py:355
  8.4 2.1 %collective-permute-start.31 = (bf16[192,512]{1,0:T(8,128)(2,1)S(1)}, bf16[192,512]{1,0:T(8,128)(2,1)S(1)}, u32[]{:S(2)}, u32[]{:S(2)}) collective-permute-start(bf16[192,512]{1,0:T(8,128)(2,1)S(1)} %get-tuple-element.124), channel_id=1, source_target_pairs={{0,2},{1,3},{2,0},{3,1},{4,6},{5,7},{6,4},{7,5},{8,10},{9,11},{10,... | collective-permute-start | bytes 589832 | tf_op jit(solution)/shard_map/ppermute | solution.py:351
  10.5 0.9 collective-permute-start.23
  11.3 2.1 %collective-permute-start.8 = (bf16[192,512]{1,0:T(8,128)(2,1)S(1)}, bf16[192,512]{1,0:T(8,128)(2,1)S(1)}, u32[]{:S(2)}, u32[]{:S(2)}) collective-permute-start(bf16[192,512]{1,0:T(8,128)(2,1)S(1)} %get-tuple-element.84.grad_out), channel_id=1, source_target_pairs={{0,2},{1,3},{2,0},{3,1},{4,6},{5,7},{6,4},{7,5},{8,10},{9,11},{10,... | collective-permute-start | bytes 589832 | tf_op jit(solution)/shard_map/ppermute | solution.py:351
  13.7 1.8 %collective-permute-start.4 = (bf16[64,1536]{1,0:T(8,128)(2,1)S(1)}, bf16[64,1536]{1,0:T(8,128)(2,1)S(1)}, u32[]{:S(2)}, u32[]{:S(2)}) collective-permute-start(bf16[64,1536]{1,0:T(8,128)(2,1)S(1)} %get-tuple-element.75), channel_id=1, source_target_pairs={{0,20},{4,16},{8,28},{12,24},{16,4},{20,0},{24,12},{28,8},{1,21},{... | collective-permute-start | bytes 589832 | tf_op jit(solution)/shard_map/ppermute | solution.py:355
  15.5 0.4 collective-permute-start.5
  15.9 18.0 %collective-permute-done.31.grad_out = bf16[192,512]{1,0:T(8,128)(2,1)S(1)} collective-permute-done((bf16[192,512]{1,0:T(8,128)(2,1)S(1)}, bf16[192,512]{1,0:T(8,128)(2,1)S(1)}, u32[]{:S(2)}, u32[]{:S(2)}) %collective-permute-start.31) | collective-permute-done | bytes 196640 | tf_op jit(solution)/shard_map/ppermute | solution.py:351
  34.2 11.7 %collective-permute-done.8.grad_out = bf16[192,512]{1,0:T(8,128)(2,1)S(1)} collective-permute-done((bf16[192,512]{1,0:T(8,128)(2,1)S(1)}, bf16[192,512]{1,0:T(8,128)(2,1)S(1)}, u32[]{:S(2)}, u32[]{:S(2)}) %collective-permute-start.8) | collective-permute-done | bytes 196640 | tf_op jit(solution)/shard_map/ppermute | solution.py:351
  46.2 0.3 shard_map.107
  46.6 0.6 collective-permute-start.9
  47.1 0.5 collective-permute-start.10
  47.7 0.9 collective-permute-start.11
  48.6 0.5 collective-permute-start.12
  49.1 0.7 collective-permute-start.33
  49.8 3.7 %shard_map.104 = (bf16[1024,1024]{1,0:T(8,128)(2,1)S(1)}, bf16[1024,1024]{1,0:T(8,128)(2,1)S(1)}) custom-call(s32[2]{0:T(128)S(1)} %pad_add_fusion.pos, bf16[1,2048,1024]{2,1,0:T(8,128)(2,1)} %w_in.5, bf16[1,2048,1024]{2,1,0:T(8,128)(2,1)} %w_out.3), custom_call_target="tpu_custom_call" | custom-call | bytes 12582912 | tf_op jit(solution)/shard_map/pallas_call | solution.py:294
  53.5 0.8 shard_map.111
  54.3 2.5 %collective-permute-done.33.refs_2_.refs_10_ = bf16[64,512]{1,0:T(8,128)(2,1)S(1)} collective-permute-done((bf16[64,512]{1,0:T(8,128)(2,1)S(1)}, bf16[64,512]{1,0:T(8,128)(2,1)S(1)}, u32[]{:S(2)}, u32[]{:S(2)}) %collective-permute-start.33) | collective-permute-done | bytes 65568 | tf_op jit(solution)/shard_map/ppermute | solution.py:355
  56.8 0.6 collective-permute-start.14
  57.4 2.3 %collective-permute-start.15 = (bf16[64,1024]{1,0:T(8,128)(2,1)S(1)}, bf16[64,1024]{1,0:T(8,128)(2,1)S(1)}, u32[]{:S(2)}, u32[]{:S(2)}) collective-permute-start(bf16[64,1024]{1,0:T(8,128)(2,1)S(1)} %get-tuple-element.100), channel_id=1, source_target_pairs={{0,28},{4,24},{8,20},{12,16},{16,12},{20,8},{24,4},{28,0},{1,29},{... | collective-permute-start | bytes 393224 | tf_op jit(solution)/shard_map/ppermute | solution.py:355
  59.9 0.5 collective-permute-start.25
  60.4 4.8 %shard_map.103 = (bf16[1024,512]{1,0:T(8,128)(2,1)S(1)}, bf16[1024,512]{1,0:T(8,128)(2,1)S(1)}) custom-call(s32[2]{0:T(128)S(1)} %pad_add_fusion.pos, bf16[1,2048,1024]{2,1,0:T(8,128)(2,1)} %w_in.5, bf16[64,1536]{1,0:T(8,128)(2,1)S(1)} %get-tuple-element.70.refs_0_, bf16[64,1536]{1,0:T(8,128)(2,1)S(1)} %collective-permute-done.refs_1_, ...), custom_call_target="tpu_custom_call" | custom-call | flops 1073741824 | bytes 7864320 | tf_op jit(solution)/shard_map/pallas_call | solution.py:294
  65.2 2.1 %shard_map.105 = (bf16[1024,512]{1,0:T(8,128)(2,1)S(1)}, bf16[1024,512]{1,0:T(8,128)(2,1)S(1)}) custom-call(bf16[1024,1024]{1,0:T(8,128)(2,1)S(1)} %get-tuple-element.80.w_in, bf16[64,1536]{1,0:T(8,128)(2,1)S(1)} %get-tuple-element.70.refs_0_, bf16[64,1536]{1,0:T(8,128)(2,1)S(1)} %collective-permute-done.refs_1_, ...), custom_call_target="tpu_custom_call" | custom-call | flops 1073741824 | bytes 5767168 | tf_op jit(solution)/shard_map/pallas_call | solution.py:312
  67.4 1.2 collective-permute-start.26
  68.6 1.5 %collective-permute-start.27 = (bf16[64,1024]{1,0:T(8,128)(2,1)S(1)}, bf16[64,1024]{1,0:T(8,128)(2,1)S(1)}, u32[]{:S(2)}, u32[]{:S(2)}) collective-permute-start(bf16[64,1024]{1,0:T(8,128)(2,1)S(1)} %get-tuple-element.119), channel_id=1, source_target_pairs={{0,16},{4,20},{8,24},{12,28},{16,0},{20,4},{24,8},{28,12},{1,17},{... | collective-permute-start | bytes 393224 | tf_op jit(solution)/shard_map/ppermute | solution.py:355
  70.4 1.4 collective-permute-start.29
  71.8 1.2 collective-permute-start.30
  73.0 2.7 %shard_map.108 = (bf16[1024,512]{1,0:T(8,128)(2,1)S(1)}, f32[512,1024]{1,0:T(8,128)S(1)}, f32[1,512]{1,0:T(1,128)S(1)}, bf16[512,1024]{1,0:T(8,128)(2,1)S(1)}) custom-call(bf16[1024,1024]{1,0:T(8,128)(2,1)S(1)} %get-tuple-element.80.w_in, bf16[1024,1024]{1,0:T(8,128)(2,1)S(1)} %get-tuple-element.81.w_out, bf16[1024,512]{1,0:T(8,128)(2,1)S(1)} %get-tuple-element.82.act.own, ...), custom_call_target="tpu_custom_call" | custom-call | flops 2147483648 | bytes 13109248 | tf_op jit(solution)/shard_map/pallas_call | solution.py:312
  75.7 0.7 collective-permute-start.34
  76.3 4.2 %collective-permute-done.27.refs_4_.refs_12_ = bf16[64,1024]{1,0:T(8,128)(2,1)S(1)} collective-permute-done((bf16[64,1024]{1,0:T(8,128)(2,1)S(1)}, bf16[64,1024]{1,0:T(8,128)(2,1)S(1)}, u32[]{:S(2)}, u32[]{:S(2)}) %collective-permute-start.27) | collective-permute-done | bytes 131104 | tf_op jit(solution)/shard_map/ppermute | solution.py:355
  80.6 1.5 %collective-permute-start.35 = (bf16[64,512]{1,0:T(8,128)(2,1)S(1)}, bf16[64,512]{1,0:T(8,128)(2,1)S(1)}, u32[]{:S(2)}, u32[]{:S(2)}) collective-permute-start(bf16[64,512]{1,0:T(8,128)(2,1)S(1)} %get-tuple-element.129), channel_id=1, source_target_pairs={{0,16},{4,20},{8,24},{12,28},{16,0},{20,4},{24,8},{28,12},{1,17},{... | collective-permute-start | bytes 196616 | tf_op jit(solution)/shard_map/ppermute | solution.py:355
  82.1 0.3 collective-permute-done.28.refs_5_.refs_13_
  82.4 1.9 %collective-permute-start.36 = (bf16[64,512]{1,0:T(8,128)(2,1)S(1)}, bf16[64,512]{1,0:T(8,128)(2,1)S(1)}, u32[]{:S(2)}, u32[]{:S(2)}) collective-permute-start(bf16[64,512]{1,0:T(8,128)(2,1)S(1)} %get-tuple-element.130), channel_id=1, source_target_pairs={{0,20},{4,16},{8,28},{12,24},{16,4},{20,0},{24,12},{28,8},{1,21},{... | collective-permute-start | bytes 196616 | tf_op jit(solution)/shard_map/ppermute | solution.py:355
  84.3 0.6 collective-permute-start.37
  84.9 1.1 collective-permute-start.38
  86.0 2.1 %shard_map.112 = (bf16[1024,512]{1,0:T(8,128)(2,1)S(1)}, bf16[1024,512]{1,0:T(8,128)(2,1)S(1)}) custom-call(bf16[1024,1024]{1,0:T(8,128)(2,1)S(1)} %get-tuple-element.80.w_in, bf16[64,1024]{1,0:T(8,128)(2,1)S(1)} %get-tuple-element.115.refs_0_.refs_8_, bf16[64,1024]{1,0:T(8,128)(2,1)S(1)} %collective-permute-done.24.refs_1_.refs_9_, ...), custom_call_target="tpu_custom_call" | custom-call | flops 1073741824 | bytes 5242880 | tf_op jit(solution)/shard_map/pallas_call | solution.py:312
  88.2 2.0 %collective-permute-done.37.refs_6_.refs_14_ = bf16[64,512]{1,0:T(8,128)(2,1)S(1)} collective-permute-done((bf16[64,512]{1,0:T(8,128)(2,1)S(1)}, bf16[64,512]{1,0:T(8,128)(2,1)S(1)}, u32[]{:S(2)}, u32[]{:S(2)}) %collective-permute-start.37) | collective-permute-done | bytes 65568 | tf_op jit(solution)/shard_map/ppermute | solution.py:355
  90.2 1.3 shard_map.114.other
  91.5 1.5 %shard_map.117 = bf16[512,768]{1,0:T(8,128)(2,1)S(1)} custom-call(s32[2]{0:T(128)S(1)} %pad_add_fusion.pos, bf16[1024,512]{1,0:T(8,128)(2,1)S(1)} %get-tuple-element.114.own, bf16[1024,512]{1,0:T(8,128)(2,1)S(1)} %shard_map.114.other, bf16[64,1536]{1,0:T(8,128)(2,1)S(1)} %get-tuple-element.70.refs_0_, bf16[64,1536]{1,0:T(8,128)(2,1)S(1)} %collective-permute-done.refs_1_, ...), custom_call_target="tpu_custom_call" | custom-call | flops 805306368 | bytes 5505024 | tf_op jit(solution)/shard_map/pallas_call | solution.py:312
  93.1 6.4 %shard_map.109 = (bf16[64,1024]{1,0:T(8,128)(2,1)S(1)}, bf16[64,1024]{1,0:T(8,128)(2,1)S(1)}, bf16[64,1024]{1,0:T(8,128)(2,1)S(1)}, bf16[64,1024]{1,0:T(8,128)(2...) custom-call(s32[2]{0:T(128)S(1)} %pad_add_fusion.pos, ...), custom_call_target="tpu_custom_call" | custom-call | flops 2147483648 | bytes 14682112 | tf_op jit(solution)/shard_map/pallas_call | solution.py:294
  99.6 0.6 collective-permute-start.16
  100.1 0.8 collective-permute-start.17
  100.9 1.2 shard_map.120
  102.2 2.1 %collective-permute-start.41 = (bf16[512,512]{1,0:T(8,128)(2,1)S(1)}, bf16[512,512]{1,0:T(8,128)(2,1)S(1)}, u32[]{:S(2)}, u32[]{:S(2)}) collective-permute-start(bf16[512,512]{1,0:T(8,128)(2,1)S(1)} %shard_map.120), channel_id=1, source_target_pairs={{0,1},{1,0},{2,3},{3,2},{4,5},{5,4},{6,7},{7,6},{8,9},{9,8},{10,11... | collective-permute-start | bytes 1572872 | tf_op jit(solution)/shard_map/ppermute | solution.py:362
  104.2 1.2 shard_map.121
  105.6 0.3 collective-permute-start.18
  105.9 1.2 collective-permute-start.19
  107.1 4.3 %collective-permute-done.18.refs_3_ = bf16[64,1024]{1,0:T(8,128)(2,1)S(1)} collective-permute-done((bf16[64,1024]{1,0:T(8,128)(2,1)S(1)}, bf16[64,1024]{1,0:T(8,128)(2,1)S(1)}, u32[]{:S(2)}, u32[]{:S(2)}) %collective-permute-start.18) | collective-permute-done | bytes 131104 | tf_op jit(solution)/shard_map/ppermute | solution.py:355
  111.4 0.8 collective-permute-start.20
  112.3 1.4 collective-permute-start.21
  113.7 6.0 %collective-permute-done.20.refs_5_ = bf16[64,1024]{1,0:T(8,128)(2,1)S(1)} collective-permute-done((bf16[64,1024]{1,0:T(8,128)(2,1)S(1)}, bf16[64,1024]{1,0:T(8,128)(2,1)S(1)}, u32[]{:S(2)}, u32[]{:S(2)}) %collective-permute-start.20) | collective-permute-done | bytes 131104 | tf_op jit(solution)/shard_map/ppermute | solution.py:355
  119.6 1.5 %collective-permute-start.22 = (bf16[64,1024]{1,0:T(8,128)(2,1)S(1)}, bf16[64,1024]{1,0:T(8,128)(2,1)S(1)}, u32[]{:S(2)}, u32[]{:S(2)}) collective-permute-start(bf16[64,1024]{1,0:T(8,128)(2,1)S(1)} %get-tuple-element.111), channel_id=1, source_target_pairs={{0,28},{4,24},{8,20},{12,16},{16,12},{20,8},{24,4},{28,0},{1,29},{... | collective-permute-start | bytes 393224 | tf_op jit(solution)/shard_map/ppermute | solution.py:355
  121.2 1.0 shard_map.116
  122.2 1.8 %collective-permute-start.39 = (bf16[512,256]{1,0:T(8,128)(2,1)S(1)}, bf16[512,256]{1,0:T(8,128)(2,1)S(1)}, u32[]{:S(2)}, u32[]{:S(2)}) collective-permute-start(bf16[512,256]{1,0:T(8,128)(2,1)S(1)} %shard_map.116), channel_id=1, source_target_pairs={{0,1},{1,0},{2,3},{3,2},{4,5},{5,4},{6,7},{7,6},{8,9},{9,8},{10,11... | collective-permute-start | bytes 786440 | tf_op jit(solution)/shard_map/ppermute | solution.py:362
  124.0 1.7 %collective-permute-done.22.refs_7_ = bf16[64,1024]{1,0:T(8,128)(2,1)S(1)} collective-permute-done((bf16[64,1024]{1,0:T(8,128)(2,1)S(1)}, bf16[64,1024]{1,0:T(8,128)(2,1)S(1)}, u32[]{:S(2)}, u32[]{:S(2)}) %collective-permute-start.22) | collective-permute-done | bytes 131104 | tf_op jit(solution)/shard_map/ppermute | solution.py:355
  125.7 1.6 %shard_map.110 = (bf16[192,1024]{1,0:T(8,128)(2,1)}, bf16[2,192]{1,0:T(2,128)(2,1)}) custom-call(f32[8,192]{1,0:T(8,128)S(1)} %get-tuple-element.69.meta, bf16[64,1024]{1,0:T(8,128)(2,1)S(1)} %get-tuple-element.104.refs_0_, bf16[64,1024]{1,0:T(8,128)(2,1)S(1)} %collective-permute-done.16.refs_1_, bf16[64,1024]{1,0:T(8,128)(2,1)S(1)} %collective-permute-done.17.refs_2_, ...), custom_call_target="tpu_custom_call" | custom-call | flops 201326592 | bytes 1448704 | tf_op jit(solution)/shard_map/pallas_call | solution.py:294
  127.2 1.8 %shard_map.115.before = f32[512,1024]{1,0:T(8,128)S(1)} custom-call(s32[2]{0:T(128)S(1)} %pad_add_fusion.pos, bf16[1024,512]{1,0:T(8,128)(2,1)S(1)} %get-tuple-element.114.own, bf16[1024,512]{1,0:T(8,128)(2,1)S(1)} %shard_map.114.other, bf16[64,1536]{1,0:T(8,128)(2,1)S(1)} %get-tuple-element.70.refs_0_, bf16[64,1536]{1,0:T(8,128)(2,1)S(1)} %collective-permute-done.refs_1_, ...), custom_call_target="tpu_custom_call" | custom-call | flops 1073741824 | bytes 6815744 | tf_op jit(solution)/shard_map/pallas_call | solution.py:312
  129.1 7.0 %collective-permute-done.42.refs_33_ = bf16[512,512]{1,0:T(8,128)(2,1)S(1)} collective-permute-done((bf16[512,512]{1,0:T(8,128)(2,1)S(1)}, bf16[512,512]{1,0:T(8,128)(2,1)S(1)}, u32[]{:S(2)}, u32[]{:S(2)}) %collective-permute-start.42) | collective-permute-done | bytes 524320 | tf_op jit(solution)/shard_map/ppermute | solution.py:362
  136.0 2.9 %home_out.1 = f32[1,512,1024]{2,1,0:T(8,128)} custom-call(s32[2]{0:T(128)S(1)} %pad_add_fusion.pos, bf16[1024,512]{1,0:T(8,128)(2,1)S(1)} %get-tuple-element.82.act.own, bf16[1024,512]{1,0:T(8,128)(2,1)S(1)} %get-tuple-element.133.other, bf16[64,1536]{1,0:T(8,128)(2,1)S(1)} %get-tuple-element.70.refs_0_, bf16[64,1536]{1,0:T(8,128)(2,1)S(1)} %collective-permute-done.refs_1_, ...), custom_call_target="tpu_custom_call" | custom-call | flops 1073741824 | bytes 6291456 | tf_op jit(solution)/shard_map/home_out/pallas_call | solution.py:556
  138.9 1.8 %shard_map.118.refs_1_ = f32[1,512,1024]{2,1,0:T(8,128)} custom-call(f32[512,1024]{1,0:T(8,128)S(1)} %shard_map.115.before, bf16[512,768]{1,0:T(8,128)(2,1)S(1)} %collective-permute-done.40.refs_0_), custom_call_target="tpu_custom_call" | custom-call | bytes 4980736 | tf_op jit(solution)/shard_map/pallas_call | solution.py:294
  140.7 0.4 collective-permute-done.39.refs_0_
  141.2 0.8 shard_map.119
  (44 shorter events, 1.9 us)
Async XLA Ops:
  2.6 7.8 %collective-permute-start = (bf16[64,1536]{1,0:T(8,128)(2,1)S(1)}, bf16[64,1536]{1,0:T(8,128)(2,1)S(1)}, u32[]{:S(2)}, u32[]{:S(2)}) collective-permute-start(bf16[64,1536]{1,0:T(8,128)(2,1)S(1)} %get-tuple-element.71), channel_id=1, source_target_pairs={{0,4},{4,0},{8,12},{12,8},{16,20},{20,16},{24,28},{28,24},{1,5},{5... | collective-permute-start | bytes 589832 | tf_op jit(solution)/shard_map/ppermute | solution.py:355
  2.7 8.6 %collective-permute-start.1 = (bf16[64,1536]{1,0:T(8,128)(2,1)S(1)}, bf16[64,1536]{1,0:T(8,128)(2,1)S(1)}, u32[]{:S(2)}, u32[]{:S(2)}) collective-permute-start(bf16[64,1536]{1,0:T(8,128)(2,1)S(1)} %get-tuple-element.72), channel_id=1, source_target_pairs={{0,8},{4,12},{8,0},{12,4},{16,24},{20,28},{24,16},{28,20},{1,9},{5... | collective-permute-start | bytes 589832 | tf_op jit(solution)/shard_map/ppermute | solution.py:355
  2.8 5.6 %collective-permute-start.7 = (f32[8,192]{1,0:T(8,128)S(1)}, f32[8,192]{1,0:T(8,128)S(1)}, u32[]{:S(2)}, u32[]{:S(2)}) collective-permute-start(f32[8,192]{1,0:T(8,128)S(1)} %get-tuple-element.69.meta), channel_id=1, source_target_pairs={{0,2},{1,3},{2,0},{3,1},{4,6},{5,7},{6,4},{7,5},{8,10},{9,11},{10,... | collective-permute-start | bytes 18440 | tf_op jit(solution)/shard_map/ppermute | solution.py:351
  5.9 7.8 %collective-permute-start.2 = (bf16[64,1536]{1,0:T(8,128)(2,1)S(1)}, bf16[64,1536]{1,0:T(8,128)(2,1)S(1)}, u32[]{:S(2)}, u32[]{:S(2)}) collective-permute-start(bf16[64,1536]{1,0:T(8,128)(2,1)S(1)} %get-tuple-element.73), channel_id=1, source_target_pairs={{0,12},{4,8},{8,4},{12,0},{16,28},{20,24},{24,20},{28,16},{1,13},{... | collective-permute-start | bytes 589832 | tf_op jit(solution)/shard_map/ppermute | solution.py:355
  6.9 8.6 %collective-permute-start.3 = (bf16[64,1536]{1,0:T(8,128)(2,1)S(1)}, bf16[64,1536]{1,0:T(8,128)(2,1)S(1)}, u32[]{:S(2)}, u32[]{:S(2)}) collective-permute-start(bf16[64,1536]{1,0:T(8,128)(2,1)S(1)} %get-tuple-element.74), channel_id=1, source_target_pairs={{0,16},{4,20},{8,24},{12,28},{16,0},{20,4},{24,8},{28,12},{1,17},{... | collective-permute-start | bytes 589832 | tf_op jit(solution)/shard_map/ppermute | solution.py:355
  8.4 25.5 %collective-permute-start.31 = (bf16[192,512]{1,0:T(8,128)(2,1)S(1)}, bf16[192,512]{1,0:T(8,128)(2,1)S(1)}, u32[]{:S(2)}, u32[]{:S(2)}) collective-permute-start(bf16[192,512]{1,0:T(8,128)(2,1)S(1)} %get-tuple-element.124), channel_id=1, source_target_pairs={{0,2},{1,3},{2,0},{3,1},{4,6},{5,7},{6,4},{7,5},{8,10},{9,11},{10,... | collective-permute-start | bytes 589832 | tf_op jit(solution)/shard_map/ppermute | solution.py:351
  10.5 38.6 %collective-permute-start.23 = (bf16[192,1024]{1,0:T(8,128)(2,1)}, bf16[192,1024]{1,0:T(8,128)(2,1)S(1)}, u32[]{:S(2)}, u32[]{:S(2)}) collective-permute-start(bf16[192,1024]{1,0:T(8,128)(2,1)} %tokens.1), channel_id=1, source_target_pairs={{0,2},{1,3},{2,0},{3,1},{4,6},{5,7},{6,4},{7,5},{8,10},{9,11},{10,... | collective-permute-start | bytes 1179656 | tf_op jit(solution)/shard_map/ppermute | solution.py:351
  11.3 34.6 %collective-permute-start.8 = (bf16[192,512]{1,0:T(8,128)(2,1)S(1)}, bf16[192,512]{1,0:T(8,128)(2,1)S(1)}, u32[]{:S(2)}, u32[]{:S(2)}) collective-permute-start(bf16[192,512]{1,0:T(8,128)(2,1)S(1)} %get-tuple-element.84.grad_out), channel_id=1, source_target_pairs={{0,2},{1,3},{2,0},{3,1},{4,6},{5,7},{6,4},{7,5},{8,10},{9,11},{10,... | collective-permute-start | bytes 589832 | tf_op jit(solution)/shard_map/ppermute | solution.py:351
  13.7 32.9 %collective-permute-start.4 = (bf16[64,1536]{1,0:T(8,128)(2,1)S(1)}, bf16[64,1536]{1,0:T(8,128)(2,1)S(1)}, u32[]{:S(2)}, u32[]{:S(2)}) collective-permute-start(bf16[64,1536]{1,0:T(8,128)(2,1)S(1)} %get-tuple-element.75), channel_id=1, source_target_pairs={{0,20},{4,16},{8,28},{12,24},{16,4},{20,0},{24,12},{28,8},{1,21},{... | collective-permute-start | bytes 589832 | tf_op jit(solution)/shard_map/ppermute | solution.py:355
  15.5 31.6 %collective-permute-start.5 = (bf16[64,1536]{1,0:T(8,128)(2,1)S(1)}, bf16[64,1536]{1,0:T(8,128)(2,1)S(1)}, u32[]{:S(2)}, u32[]{:S(2)}) collective-permute-start(bf16[64,1536]{1,0:T(8,128)(2,1)S(1)} %get-tuple-element.76), channel_id=1, source_target_pairs={{0,24},{4,28},{8,16},{12,20},{16,8},{20,12},{24,0},{28,4},{1,25},{... | collective-permute-start | bytes 589832 | tf_op jit(solution)/shard_map/ppermute | solution.py:355
  33.9 13.8 %collective-permute-start.6 = (bf16[64,1536]{1,0:T(8,128)(2,1)S(1)}, bf16[64,1536]{1,0:T(8,128)(2,1)S(1)}, u32[]{:S(2)}, u32[]{:S(2)}) collective-permute-start(bf16[64,1536]{1,0:T(8,128)(2,1)S(1)} %get-tuple-element.77), channel_id=1, source_target_pairs={{0,28},{4,24},{8,20},{12,16},{16,12},{20,8},{24,4},{28,0},{1,29},{... | collective-permute-start | bytes 589832 | tf_op jit(solution)/shard_map/ppermute | solution.py:355
  45.9 2.6 %collective-permute-start.32 = (bf16[64,512]{1,0:T(8,128)(2,1)S(1)}, bf16[64,512]{1,0:T(8,128)(2,1)S(1)}, u32[]{:S(2)}, u32[]{:S(2)}) collective-permute-start(bf16[64,512]{1,0:T(8,128)(2,1)S(1)} %get-tuple-element.126), channel_id=1, source_target_pairs={{0,4},{4,0},{8,12},{12,8},{16,20},{20,16},{24,28},{28,24},{1,5},{5... | collective-permute-start | bytes 196616 | tf_op jit(solution)/shard_map/ppermute | solution.py:355
  46.6 10.3 %collective-permute-start.9 = (bf16[64,1024]{1,0:T(8,128)(2,1)S(1)}, bf16[64,1024]{1,0:T(8,128)(2,1)S(1)}, u32[]{:S(2)}, u32[]{:S(2)}) collective-permute-start(bf16[64,1024]{1,0:T(8,128)(2,1)S(1)} %get-tuple-element.94), channel_id=1, source_target_pairs={{0,4},{4,0},{8,12},{12,8},{16,20},{20,16},{24,28},{28,24},{1,5},{5... | collective-permute-start | bytes 393224 | tf_op jit(solution)/shard_map/ppermute | solution.py:355
  47.1 10.3 %collective-permute-start.10 = (bf16[64,1024]{1,0:T(8,128)(2,1)S(1)}, bf16[64,1024]{1,0:T(8,128)(2,1)S(1)}, u32[]{:S(2)}, u32[]{:S(2)}) collective-permute-start(bf16[64,1024]{1,0:T(8,128)(2,1)S(1)} %get-tuple-element.95), channel_id=1, source_target_pairs={{0,8},{4,12},{8,0},{12,4},{16,24},{20,28},{24,16},{28,20},{1,9},{5... | collective-permute-start | bytes 393224 | tf_op jit(solution)/shard_map/ppermute | solution.py:355
  47.7 12.0 %collective-permute-start.11 = (bf16[64,1024]{1,0:T(8,128)(2,1)S(1)}, bf16[64,1024]{1,0:T(8,128)(2,1)S(1)}, u32[]{:S(2)}, u32[]{:S(2)}) collective-permute-start(bf16[64,1024]{1,0:T(8,128)(2,1)S(1)} %get-tuple-element.96), channel_id=1, source_target_pairs={{0,12},{4,8},{8,4},{12,0},{16,28},{20,24},{24,20},{28,16},{1,13},{... | collective-permute-start | bytes 393224 | tf_op jit(solution)/shard_map/ppermute | solution.py:355
  48.6 11.3 %collective-permute-start.12 = (bf16[64,1024]{1,0:T(8,128)(2,1)S(1)}, bf16[64,1024]{1,0:T(8,128)(2,1)S(1)}, u32[]{:S(2)}, u32[]{:S(2)}) collective-permute-start(bf16[64,1024]{1,0:T(8,128)(2,1)S(1)} %get-tuple-element.97), channel_id=1, source_target_pairs={{0,16},{4,20},{8,24},{12,28},{16,0},{20,4},{24,8},{28,12},{1,17},{... | collective-permute-start | bytes 393224 | tf_op jit(solution)/shard_map/ppermute | solution.py:355
  49.1 7.7 %collective-permute-start.33 = (bf16[64,512]{1,0:T(8,128)(2,1)S(1)}, bf16[64,512]{1,0:T(8,128)(2,1)S(1)}, u32[]{:S(2)}, u32[]{:S(2)}) collective-permute-start(bf16[64,512]{1,0:T(8,128)(2,1)S(1)} %get-tuple-element.127), channel_id=1, source_target_pairs={{0,8},{4,12},{8,0},{12,4},{16,24},{20,28},{24,16},{28,20},{1,9},{5... | collective-permute-start | bytes 196616 | tf_op jit(solution)/shard_map/ppermute | solution.py:355
  56.8 10.5 %collective-permute-start.13 = (bf16[64,1024]{1,0:T(8,128)(2,1)S(1)}, bf16[64,1024]{1,0:T(8,128)(2,1)S(1)}, u32[]{:S(2)}, u32[]{:S(2)}) collective-permute-start(bf16[64,1024]{1,0:T(8,128)(2,1)S(1)} %get-tuple-element.98), channel_id=1, source_target_pairs={{0,20},{4,16},{8,28},{12,24},{16,4},{20,0},{24,12},{28,8},{1,21},{... | collective-permute-start | bytes 393224 | tf_op jit(solution)/shard_map/ppermute | solution.py:355
  56.8 11.7 %collective-permute-start.14 = (bf16[64,1024]{1,0:T(8,128)(2,1)S(1)}, bf16[64,1024]{1,0:T(8,128)(2,1)S(1)}, u32[]{:S(2)}, u32[]{:S(2)}) collective-permute-start(bf16[64,1024]{1,0:T(8,128)(2,1)S(1)} %get-tuple-element.99), channel_id=1, source_target_pairs={{0,24},{4,28},{8,16},{12,20},{16,8},{20,12},{24,0},{28,4},{1,25},{... | collective-permute-start | bytes 393224 | tf_op jit(solution)/shard_map/ppermute | solution.py:355
  57.4 12.7 %collective-permute-start.15 = (bf16[64,1024]{1,0:T(8,128)(2,1)S(1)}, bf16[64,1024]{1,0:T(8,128)(2,1)S(1)}, u32[]{:S(2)}, u32[]{:S(2)}) collective-permute-start(bf16[64,1024]{1,0:T(8,128)(2,1)S(1)} %get-tuple-element.100), channel_id=1, source_target_pairs={{0,28},{4,24},{8,20},{12,16},{16,12},{20,8},{24,4},{28,0},{1,29},{... | collective-permute-start | bytes 393224 | tf_op jit(solution)/shard_map/ppermute | solution.py:355
  59.7 10.7 %collective-permute-start.24 = (bf16[64,1024]{1,0:T(8,128)(2,1)S(1)}, bf16[64,1024]{1,0:T(8,128)(2,1)S(1)}, u32[]{:S(2)}, u32[]{:S(2)}) collective-permute-start(bf16[64,1024]{1,0:T(8,128)(2,1)S(1)} %get-tuple-element.116), channel_id=1, source_target_pairs={{0,4},{4,0},{8,12},{12,8},{16,20},{20,16},{24,28},{28,24},{1,5},{5... | collective-permute-start | bytes 393224 | tf_op jit(solution)/shard_map/ppermute | solution.py:355
  59.9 11.9 %collective-permute-start.25 = (bf16[64,1024]{1,0:T(8,128)(2,1)S(1)}, bf16[64,1024]{1,0:T(8,128)(2,1)S(1)}, u32[]{:S(2)}, u32[]{:S(2)}) collective-permute-start(bf16[64,1024]{1,0:T(8,128)(2,1)S(1)} %get-tuple-element.117), channel_id=1, source_target_pairs={{0,8},{4,12},{8,0},{12,4},{16,24},{20,28},{24,16},{28,20},{1,9},{5... | collective-permute-start | bytes 393224 | tf_op jit(solution)/shard_map/ppermute | solution.py:355
  67.4 8.3 %collective-permute-start.26 = (bf16[64,1024]{1,0:T(8,128)(2,1)S(1)}, bf16[64,1024]{1,0:T(8,128)(2,1)S(1)}, u32[]{:S(2)}, u32[]{:S(2)}) collective-permute-start(bf16[64,1024]{1,0:T(8,128)(2,1)S(1)} %get-tuple-element.118), channel_id=1, source_target_pairs={{0,12},{4,8},{8,4},{12,0},{16,28},{20,24},{24,20},{28,16},{1,13},{... | collective-permute-start | bytes 393224 | tf_op jit(solution)/shard_map/ppermute | solution.py:355
  68.6 12.0 %collective-permute-start.27 = (bf16[64,1024]{1,0:T(8,128)(2,1)S(1)}, bf16[64,1024]{1,0:T(8,128)(2,1)S(1)}, u32[]{:S(2)}, u32[]{:S(2)}) collective-permute-start(bf16[64,1024]{1,0:T(8,128)(2,1)S(1)} %get-tuple-element.119), channel_id=1, source_target_pairs={{0,16},{4,20},{8,24},{12,28},{16,0},{20,4},{24,8},{28,12},{1,17},{... | collective-permute-start | bytes 393224 | tf_op jit(solution)/shard_map/ppermute | solution.py:355
  70.1 12.3 %collective-permute-start.28 = (bf16[64,1024]{1,0:T(8,128)(2,1)S(1)}, bf16[64,1024]{1,0:T(8,128)(2,1)S(1)}, u32[]{:S(2)}, u32[]{:S(2)}) collective-permute-start(bf16[64,1024]{1,0:T(8,128)(2,1)S(1)} %get-tuple-element.120), channel_id=1, source_target_pairs={{0,20},{4,16},{8,28},{12,24},{16,4},{20,0},{24,12},{28,8},{1,21},{... | collective-permute-start | bytes 393224 | tf_op jit(solution)/shard_map/ppermute | solution.py:355
  70.4 13.9 %collective-permute-start.29 = (bf16[64,1024]{1,0:T(8,128)(2,1)S(1)}, bf16[64,1024]{1,0:T(8,128)(2,1)S(1)}, u32[]{:S(2)}, u32[]{:S(2)}) collective-permute-start(bf16[64,1024]{1,0:T(8,128)(2,1)S(1)} %get-tuple-element.121), channel_id=1, source_target_pairs={{0,24},{4,28},{8,16},{12,20},{16,8},{20,12},{24,0},{28,4},{1,25},{... | collective-permute-start | bytes 393224 | tf_op jit(solution)/shard_map/ppermute | solution.py:355
  71.8 13.1 %collective-permute-start.30 = (bf16[64,1024]{1,0:T(8,128)(2,1)S(1)}, bf16[64,1024]{1,0:T(8,128)(2,1)S(1)}, u32[]{:S(2)}, u32[]{:S(2)}) collective-permute-start(bf16[64,1024]{1,0:T(8,128)(2,1)S(1)} %get-tuple-element.122), channel_id=1, source_target_pairs={{0,28},{4,24},{8,20},{12,16},{16,12},{20,8},{24,4},{28,0},{1,29},{... | collective-permute-start | bytes 393224 | tf_op jit(solution)/shard_map/ppermute | solution.py:355
  75.7 12.5 %collective-permute-start.34 = (bf16[64,512]{1,0:T(8,128)(2,1)S(1)}, bf16[64,512]{1,0:T(8,128)(2,1)S(1)}, u32[]{:S(2)}, u32[]{:S(2)}) collective-permute-start(bf16[64,512]{1,0:T(8,128)(2,1)S(1)} %get-tuple-element.128), channel_id=1, source_target_pairs={{0,12},{4,8},{8,4},{12,0},{16,28},{20,24},{24,20},{28,16},{1,13},{... | collective-permute-start | bytes 196616 | tf_op jit(solution)/shard_map/ppermute | solution.py:355
  80.6 7.6 %collective-permute-start.35 = (bf16[64,512]{1,0:T(8,128)(2,1)S(1)}, bf16[64,512]{1,0:T(8,128)(2,1)S(1)}, u32[]{:S(2)}, u32[]{:S(2)}) collective-permute-start(bf16[64,512]{1,0:T(8,128)(2,1)S(1)} %get-tuple-element.129), channel_id=1, source_target_pairs={{0,16},{4,20},{8,24},{12,28},{16,0},{20,4},{24,8},{28,12},{1,17},{... | collective-permute-start | bytes 196616 | tf_op jit(solution)/shard_map/ppermute | solution.py:355
  82.4 5.7 %collective-permute-start.36 = (bf16[64,512]{1,0:T(8,128)(2,1)S(1)}, bf16[64,512]{1,0:T(8,128)(2,1)S(1)}, u32[]{:S(2)}, u32[]{:S(2)}) collective-permute-start(bf16[64,512]{1,0:T(8,128)(2,1)S(1)} %get-tuple-element.130), channel_id=1, source_target_pairs={{0,20},{4,16},{8,28},{12,24},{16,4},{20,0},{24,12},{28,8},{1,21},{... | collective-permute-start | bytes 196616 | tf_op jit(solution)/shard_map/ppermute | solution.py:355
  84.3 5.9 %collective-permute-start.37 = (bf16[64,512]{1,0:T(8,128)(2,1)S(1)}, bf16[64,512]{1,0:T(8,128)(2,1)S(1)}, u32[]{:S(2)}, u32[]{:S(2)}) collective-permute-start(bf16[64,512]{1,0:T(8,128)(2,1)S(1)} %get-tuple-element.131), channel_id=1, source_target_pairs={{0,24},{4,28},{8,16},{12,20},{16,8},{20,12},{24,0},{28,4},{1,25},{... | collective-permute-start | bytes 196616 | tf_op jit(solution)/shard_map/ppermute | solution.py:355
  84.9 5.3 %collective-permute-start.38 = (bf16[64,512]{1,0:T(8,128)(2,1)S(1)}, bf16[64,512]{1,0:T(8,128)(2,1)S(1)}, u32[]{:S(2)}, u32[]{:S(2)}) collective-permute-start(bf16[64,512]{1,0:T(8,128)(2,1)S(1)} %get-tuple-element.132), channel_id=1, source_target_pairs={{0,28},{4,24},{8,20},{12,16},{16,12},{20,8},{24,4},{28,0},{1,29},{... | collective-permute-start | bytes 196616 | tf_op jit(solution)/shard_map/ppermute | solution.py:355
  93.1 45.9 %collective-permute-start.40 = (bf16[512,768]{1,0:T(8,128)(2,1)S(1)}, bf16[512,768]{1,0:T(8,128)(2,1)S(1)}, u32[]{:S(2)}, u32[]{:S(2)}) collective-permute-start(bf16[512,768]{1,0:T(8,128)(2,1)S(1)} %shard_map.117), channel_id=1, source_target_pairs={{0,1},{1,0},{2,3},{3,2},{4,5},{5,4},{6,7},{7,6},{8,9},{9,8},{10,11... | collective-permute-start | bytes 2359304 | tf_op jit(solution)/shard_map/ppermute | solution.py:362
  99.6 6.0 %collective-permute-start.16 = (bf16[64,1024]{1,0:T(8,128)(2,1)S(1)}, bf16[64,1024]{1,0:T(8,128)(2,1)S(1)}, u32[]{:S(2)}, u32[]{:S(2)}) collective-permute-start(bf16[64,1024]{1,0:T(8,128)(2,1)S(1)} %get-tuple-element.105), channel_id=1, source_target_pairs={{0,4},{4,0},{8,12},{12,8},{16,20},{20,16},{24,28},{28,24},{1,5},{5... | collective-permute-start | bytes 393224 | tf_op jit(solution)/shard_map/ppermute | solution.py:355
  100.1 5.8 %collective-permute-start.17 = (bf16[64,1024]{1,0:T(8,128)(2,1)S(1)}, bf16[64,1024]{1,0:T(8,128)(2,1)S(1)}, u32[]{:S(2)}, u32[]{:S(2)}) collective-permute-start(bf16[64,1024]{1,0:T(8,128)(2,1)S(1)} %get-tuple-element.106), channel_id=1, source_target_pairs={{0,8},{4,12},{8,0},{12,4},{16,24},{20,28},{24,16},{28,20},{1,9},{5... | collective-permute-start | bytes 393224 | tf_op jit(solution)/shard_map/ppermute | solution.py:355
  102.2 26.9 %collective-permute-start.41 = (bf16[512,512]{1,0:T(8,128)(2,1)S(1)}, bf16[512,512]{1,0:T(8,128)(2,1)S(1)}, u32[]{:S(2)}, u32[]{:S(2)}) collective-permute-start(bf16[512,512]{1,0:T(8,128)(2,1)S(1)} %shard_map.120), channel_id=1, source_target_pairs={{0,1},{1,0},{2,3},{3,2},{4,5},{5,4},{6,7},{7,6},{8,9},{9,8},{10,11... | collective-permute-start | bytes 1572872 | tf_op jit(solution)/shard_map/ppermute | solution.py:362
  105.5 30.5 %collective-permute-start.42 = (bf16[512,512]{1,0:T(8,128)(2,1)S(1)}, bf16[512,512]{1,0:T(8,128)(2,1)S(1)}, u32[]{:S(2)}, u32[]{:S(2)}) collective-permute-start(bf16[512,512]{1,0:T(8,128)(2,1)S(1)} %shard_map.121), channel_id=1, source_target_pairs={{0,1},{1,0},{2,3},{3,2},{4,5},{5,4},{6,7},{7,6},{8,9},{9,8},{10,11... | collective-permute-start | bytes 1572872 | tf_op jit(solution)/shard_map/ppermute | solution.py:362
  105.6 5.8 %collective-permute-start.18 = (bf16[64,1024]{1,0:T(8,128)(2,1)S(1)}, bf16[64,1024]{1,0:T(8,128)(2,1)S(1)}, u32[]{:S(2)}, u32[]{:S(2)}) collective-permute-start(bf16[64,1024]{1,0:T(8,128)(2,1)S(1)} %get-tuple-element.107), channel_id=1, source_target_pairs={{0,12},{4,8},{8,4},{12,0},{16,28},{20,24},{24,20},{28,16},{1,13},{... | collective-permute-start | bytes 393224 | tf_op jit(solution)/shard_map/ppermute | solution.py:355
  105.9 6.3 %collective-permute-start.19 = (bf16[64,1024]{1,0:T(8,128)(2,1)S(1)}, bf16[64,1024]{1,0:T(8,128)(2,1)S(1)}, u32[]{:S(2)}, u32[]{:S(2)}) collective-permute-start(bf16[64,1024]{1,0:T(8,128)(2,1)S(1)} %get-tuple-element.108), channel_id=1, source_target_pairs={{0,16},{4,20},{8,24},{12,28},{16,0},{20,4},{24,8},{28,12},{1,17},{... | collective-permute-start | bytes 393224 | tf_op jit(solution)/shard_map/ppermute | solution.py:355
  111.4 8.3 %collective-permute-start.20 = (bf16[64,1024]{1,0:T(8,128)(2,1)S(1)}, bf16[64,1024]{1,0:T(8,128)(2,1)S(1)}, u32[]{:S(2)}, u32[]{:S(2)}) collective-permute-start(bf16[64,1024]{1,0:T(8,128)(2,1)S(1)} %get-tuple-element.109), channel_id=1, source_target_pairs={{0,20},{4,16},{8,28},{12,24},{16,4},{20,0},{24,12},{28,8},{1,21},{... | collective-permute-start | bytes 393224 | tf_op jit(solution)/shard_map/ppermute | solution.py:355
  112.3 9.9 %collective-permute-start.21 = (bf16[64,1024]{1,0:T(8,128)(2,1)S(1)}, bf16[64,1024]{1,0:T(8,128)(2,1)S(1)}, u32[]{:S(2)}, u32[]{:S(2)}) collective-permute-start(bf16[64,1024]{1,0:T(8,128)(2,1)S(1)} %get-tuple-element.110), channel_id=1, source_target_pairs={{0,24},{4,28},{8,16},{12,20},{16,8},{20,12},{24,0},{28,4},{1,25},{... | collective-permute-start | bytes 393224 | tf_op jit(solution)/shard_map/ppermute | solution.py:355
  119.6 6.0 %collective-permute-start.22 = (bf16[64,1024]{1,0:T(8,128)(2,1)S(1)}, bf16[64,1024]{1,0:T(8,128)(2,1)S(1)}, u32[]{:S(2)}, u32[]{:S(2)}) collective-permute-start(bf16[64,1024]{1,0:T(8,128)(2,1)S(1)} %get-tuple-element.111), channel_id=1, source_target_pairs={{0,28},{4,24},{8,20},{12,16},{16,12},{20,8},{24,4},{28,0},{1,29},{... | collective-permute-start | bytes 393224 | tf_op jit(solution)/shard_map/ppermute | solution.py:355
  122.2 19.0 %collective-permute-start.39 = (bf16[512,256]{1,0:T(8,128)(2,1)S(1)}, bf16[512,256]{1,0:T(8,128)(2,1)S(1)}, u32[]{:S(2)}, u32[]{:S(2)}) collective-permute-start(bf16[512,256]{1,0:T(8,128)(2,1)S(1)} %shard_map.116), channel_id=1, source_target_pairs={{0,1},{1,0},{2,3},{3,2},{4,5},{5,4},{6,7},{7,6},{8,9},{9,8},{10,11... | collective-permute-start | bytes 786440 | tf_op jit(solution)/shard_map/ppermute | solution.py:362

commit v6 on v5

--- a/solution.py
+++ b/solution.py
@@ -508,8 +508,11 @@
     out_acts = [own_act, other_act]
     away_oa = away(out_acts, own_sa, other_sa, 0, half)
     got_oa = to_owners(away_oa)
-    away_ob = away(out_acts, own_sb, other_sb, 0, rest)
+    early = rest // 4
+    away_ob = away(out_acts, own_sb, other_sb, 0, early)
     got_ob = to_owners(away_ob)
+    away_oc = away(out_acts, own_sb, other_sb, early, rest - early)
+    got_oc = to_owners(away_oc)
     total_shape, gate_shape = shaped((slots, width), f32), shaped((1, slots), f32)
     own_grad, near_total, near_gates, own_scaled = direct(
         bind(own_grad_kernel, experts, (own_sa[1], half), (own_sb[1], rest)),
@@ -551,8 +554,15 @@
         + own_sb[0]
         + other_sb[0]
         + got_ob
-    )
-    parts = ((own_sa[1], other_sa[1], half), (own_sb[1], other_sb[1], rest))
+        + own_sb[0]
+        + other_sb[0]
+        + got_oc
+    )
+    parts = (
+        (own_sa[1], other_sa[1], half),
+        (own_sb[1], other_sb[1], early),
+        (own_sb[1] + early, other_sb[1] + early, rest - early),
+    )
     grad_outw = pl.pallas_call(
         bind(home_kernel, experts, owners, parts),
         name="home_out",
@@ -562,7 +572,7 @@
         out_specs=pl.BlockSpec(memory_space=pl.ANY),
         scratch_shapes=[
             pltpu.VMEM((share, width), f32),
-            pltpu.SemaphoreType.DMA((len(steps(half, 256)) + len(steps(rest, 256)),)),
+            pltpu.SemaphoreType.DMA((sum(len(steps(part[2], 256)) for part in parts),)),
         ],
         compiler_params=pltpu.CompilerParams(vmem_limit_bytes=28 << 20),
         cost_estimate=pl.CostEstimate(

time: 144 us -> 149 us (1.035)
  waiting for transfers between devices: 58.7 us -> 61.6 us
    ppermute x4 -> x5, waiting for transfers between devices: 7.38 us -> 17.4 us  [to_owners(): lax.ppermute(value, 'dp', [(j, j // owners * owners + (j + r + 1) % owner...]
    ppermute x35, waiting for transfers between devices: 21.5 us -> 14.5 us  [exchange(): lax.ppermute(values[k], 'expert', [(i, i ^ k) for i in range(experts)])]
    pallas_call x9 -> x10, Pallas kernels: 15 us -> 16 us  [direct(): pl.pallas_call(kernel, out_shape=outs, in_specs=[pl.BlockSpec(memory_spac...]
    ppermute x4 -> x5, starting transfers between devices: 4.06 us -> 4.92 us  [to_owners(): lax.ppermute(value, 'dp', [(j, j // owners * owners + (j + r + 1) % owner...]
  transfers between devices with their start and end apart: 43 -> 44, of which waited for: 13 -> 12; matrix products, arithmetic and copies ran while one was open for 0% -> 0% of each run, Pallas kernels for 25% -> 25%
where the time goes in v6:
time: 149 us; the launch traced here: 147 us
  waiting for transfers between devices  61.6 us (41%)
  starting transfers between devices  42.5 us (29%)
  Pallas kernels  41.8 us (28%)
    ppermute x4, waiting for transfers between devices, across(): lax.ppermute(value, 'dp', [(j, (j + owners) % planes) for j in range(plan...  29.7 us
    ppermute x35, starting transfers between devices, exchange(): lax.ppermute(values[k], 'expert', [(i, i ^ k) for i in range(experts)])  29.5 us
    pallas_call x11, Pallas kernels, call(): pl.pallas_call(kernel, out_shape=outs, grid_spec=pltpu.PrefetchScalarGrid...  22.7 us
    ppermute x5, waiting for transfers between devices, to_owners(): lax.ppermute(value, 'dp', [(j, j // owners * owners + (j + r + 1) % owner...  17.4 us
    pallas_call x10, Pallas kernels, direct(): pl.pallas_call(kernel, out_shape=outs, in_specs=[pl.BlockSpec(memory_spac...  16 us
    ppermute x35, waiting for transfers between devices, exchange(): lax.ppermute(values[k], 'expert', [(i, i ^ k) for i in range(experts)])  14.5 us
    ppermute x4, starting transfers between devices, across(): lax.ppermute(value, 'dp', [(j, (j + owners) % planes) for j in range(plan...  8.12 us
    ppermute x5, starting transfers between devices, to_owners(): lax.ppermute(value, 'dp', [(j, j // owners * owners + (j + r + 1) % owner...  4.92 us
  transfers between devices with their start and end apart: 44, of which 12 were waited for; matrix products, arithmetic and copies ran while one was open for 0% of the time, Pallas kernels for 25%

profile of v6, /device:TPU:2, one launch (start us, length us, event | category | flops | bytes accessed | tf_op | source)
XLA Modules:
  0.0 146.9 jit_solution(16872753361264589719)
XLA Ops:
  0.6 2.0 %shard_map.102 = (f32[8,192]{1,0:T(8,128)S(1)}, bf16[192,512]{1,0:T(8,128)(2,1)S(1)}, bf16[192,512]{1,0:T(8,128)(2,1)S(1)}, bf16[64,1536]{1,0:T(8,128)(2,1)S(1)}...) custom-call(s32[2,192]{1,0:T(2,128)} %bitcast.6, ...), custom_call_target="tpu_custom_call" | custom-call | flops 301989888 | bytes 2761728 | tf_op jit(solution)/shard_map/pallas_call | solution.py:294
  2.8 3.1 %collective-permute-start.7 = (f32[8,192]{1,0:T(8,128)S(1)}, f32[8,192]{1,0:T(8,128)S(1)}, u32[]{:S(2)}, u32[]{:S(2)}) collective-permute-start(f32[8,192]{1,0:T(8,128)S(1)} %get-tuple-element.69.meta), channel_id=1, source_target_pairs={{0,2},{1,3},{2,0},{3,1},{4,6},{5,7},{6,4},{7,5},{8,10},{9,11},{10,... | collective-permute-start | bytes 18440 | tf_op jit(solution)/shard_map/ppermute | solution.py:351
  5.9 1.0 collective-permute-start.2
  6.9 1.5 %collective-permute-start.3 = (bf16[64,1536]{1,0:T(8,128)(2,1)S(1)}, bf16[64,1536]{1,0:T(8,128)(2,1)S(1)}, u32[]{:S(2)}, u32[]{:S(2)}) collective-permute-start(bf16[64,1536]{1,0:T(8,128)(2,1)S(1)} %get-tuple-element.74), channel_id=1, source_target_pairs={{0,16},{4,20},{8,24},{12,28},{16,0},{20,4},{24,8},{28,12},{1,17},{... | collective-permute-start | bytes 589832 | tf_op jit(solution)/shard_map/ppermute | solution.py:355
  8.4 2.1 %collective-permute-start.31 = (bf16[192,512]{1,0:T(8,128)(2,1)S(1)}, bf16[192,512]{1,0:T(8,128)(2,1)S(1)}, u32[]{:S(2)}, u32[]{:S(2)}) collective-permute-start(bf16[192,512]{1,0:T(8,128)(2,1)S(1)} %get-tuple-element.124), channel_id=1, source_target_pairs={{0,2},{1,3},{2,0},{3,1},{4,6},{5,7},{6,4},{7,5},{8,10},{9,11},{10,... | collective-permute-start | bytes 589832 | tf_op jit(solution)/shard_map/ppermute | solution.py:351
  10.5 0.9 collective-permute-start.23
  11.3 2.1 %collective-permute-start.8 = (bf16[192,512]{1,0:T(8,128)(2,1)S(1)}, bf16[192,512]{1,0:T(8,128)(2,1)S(1)}, u32[]{:S(2)}, u32[]{:S(2)}) collective-permute-start(bf16[192,512]{1,0:T(8,128)(2,1)S(1)} %get-tuple-element.84.grad_out), channel_id=1, source_target_pairs={{0,2},{1,3},{2,0},{3,1},{4,6},{5,7},{6,4},{7,5},{8,10},{9,11},{10,... | collective-permute-start | bytes 589832 | tf_op jit(solution)/shard_map/ppermute | solution.py:351
  13.7 1.8 %collective-permute-start.4 = (bf16[64,1536]{1,0:T(8,128)(2,1)S(1)}, bf16[64,1536]{1,0:T(8,128)(2,1)S(1)}, u32[]{:S(2)}, u32[]{:S(2)}) collective-permute-start(bf16[64,1536]{1,0:T(8,128)(2,1)S(1)} %get-tuple-element.75), channel_id=1, source_target_pairs={{0,20},{4,16},{8,28},{12,24},{16,4},{20,0},{24,12},{28,8},{1,21},{... | collective-permute-start | bytes 589832 | tf_op jit(solution)/shard_map/ppermute | solution.py:355
  15.5 0.4 collective-permute-start.5
  15.9 18.0 %collective-permute-done.31.grad_out = bf16[192,512]{1,0:T(8,128)(2,1)S(1)} collective-permute-done((bf16[192,512]{1,0:T(8,128)(2,1)S(1)}, bf16[192,512]{1,0:T(8,128)(2,1)S(1)}, u32[]{:S(2)}, u32[]{:S(2)}) %collective-permute-start.31) | collective-permute-done | bytes 196640 | tf_op jit(solution)/shard_map/ppermute | solution.py:351
  34.2 11.7 %collective-permute-done.8.grad_out = bf16[192,512]{1,0:T(8,128)(2,1)S(1)} collective-permute-done((bf16[192,512]{1,0:T(8,128)(2,1)S(1)}, bf16[192,512]{1,0:T(8,128)(2,1)S(1)}, u32[]{:S(2)}, u32[]{:S(2)}) %collective-permute-start.8) | collective-permute-done | bytes 196640 | tf_op jit(solution)/shard_map/ppermute | solution.py:351
  46.6 0.6 collective-permute-start.9
  47.1 0.5 collective-permute-start.10
  47.7 0.9 collective-permute-start.11
  48.6 0.5 collective-permute-start.12
  49.1 0.7 collective-permute-start.33
  49.8 3.7 %shard_map.104 = (bf16[1024,1024]{1,0:T(8,128)(2,1)S(1)}, bf16[1024,1024]{1,0:T(8,128)(2,1)S(1)}) custom-call(s32[2]{0:T(128)S(1)} %pad_add_fusion.pos, bf16[1,2048,1024]{2,1,0:T(8,128)(2,1)} %w_in.5, bf16[1,2048,1024]{2,1,0:T(8,128)(2,1)} %w_out.3), custom_call_target="tpu_custom_call" | custom-call | bytes 12582912 | tf_op jit(solution)/shard_map/pallas_call | solution.py:294
  53.5 0.8 shard_map.111
  54.3 2.5 %collective-permute-done.33.refs_2_.refs_10_ = bf16[64,512]{1,0:T(8,128)(2,1)S(1)} collective-permute-done((bf16[64,512]{1,0:T(8,128)(2,1)S(1)}, bf16[64,512]{1,0:T(8,128)(2,1)S(1)}, u32[]{:S(2)}, u32[]{:S(2)}) %collective-permute-start.33) | collective-permute-done | bytes 65568 | tf_op jit(solution)/shard_map/ppermute | solution.py:355
  56.8 0.6 collective-permute-start.14
  57.4 2.3 %collective-permute-start.15 = (bf16[64,1024]{1,0:T(8,128)(2,1)S(1)}, bf16[64,1024]{1,0:T(8,128)(2,1)S(1)}, u32[]{:S(2)}, u32[]{:S(2)}) collective-permute-start(bf16[64,1024]{1,0:T(8,128)(2,1)S(1)} %get-tuple-element.100), channel_id=1, source_target_pairs={{0,28},{4,24},{8,20},{12,16},{16,12},{20,8},{24,4},{28,0},{1,29},{... | collective-permute-start | bytes 393224 | tf_op jit(solution)/shard_map/ppermute | solution.py:355
  59.9 0.5 collective-permute-start.25
  60.4 4.8 %shard_map.103 = (bf16[1024,512]{1,0:T(8,128)(2,1)S(1)}, bf16[1024,512]{1,0:T(8,128)(2,1)S(1)}) custom-call(s32[2]{0:T(128)S(1)} %pad_add_fusion.pos, bf16[1,2048,1024]{2,1,0:T(8,128)(2,1)} %w_in.5, bf16[64,1536]{1,0:T(8,128)(2,1)S(1)} %get-tuple-element.70.refs_0_, bf16[64,1536]{1,0:T(8,128)(2,1)S(1)} %collective-permute-done.refs_1_, ...), custom_call_target="tpu_custom_call" | custom-call | flops 1073741824 | bytes 7864320 | tf_op jit(solution)/shard_map/pallas_call | solution.py:294
  65.2 2.1 %shard_map.105 = (bf16[1024,512]{1,0:T(8,128)(2,1)S(1)}, bf16[1024,512]{1,0:T(8,128)(2,1)S(1)}) custom-call(bf16[1024,1024]{1,0:T(8,128)(2,1)S(1)} %get-tuple-element.80.w_in, bf16[64,1536]{1,0:T(8,128)(2,1)S(1)} %get-tuple-element.70.refs_0_, bf16[64,1536]{1,0:T(8,128)(2,1)S(1)} %collective-permute-done.refs_1_, ...), custom_call_target="tpu_custom_call" | custom-call | flops 1073741824 | bytes 5767168 | tf_op jit(solution)/shard_map/pallas_call | solution.py:312
  67.4 1.2 collective-permute-start.26
  68.6 1.5 %collective-permute-start.27 = (bf16[64,1024]{1,0:T(8,128)(2,1)S(1)}, bf16[64,1024]{1,0:T(8,128)(2,1)S(1)}, u32[]{:S(2)}, u32[]{:S(2)}) collective-permute-start(bf16[64,1024]{1,0:T(8,128)(2,1)S(1)} %get-tuple-element.119), channel_id=1, source_target_pairs={{0,16},{4,20},{8,24},{12,28},{16,0},{20,4},{24,8},{28,12},{1,17},{... | collective-permute-start | bytes 393224 | tf_op jit(solution)/shard_map/ppermute | solution.py:355
  70.4 1.4 collective-permute-start.29
  71.8 1.2 collective-permute-start.30
  73.0 2.7 %shard_map.108 = (bf16[1024,512]{1,0:T(8,128)(2,1)S(1)}, f32[512,1024]{1,0:T(8,128)S(1)}, f32[1,512]{1,0:T(1,128)S(1)}, bf16[512,1024]{1,0:T(8,128)(2,1)S(1)}) custom-call(bf16[1024,1024]{1,0:T(8,128)(2,1)S(1)} %get-tuple-element.80.w_in, bf16[1024,1024]{1,0:T(8,128)(2,1)S(1)} %get-tuple-element.81.w_out, bf16[1024,512]{1,0:T(8,128)(2,1)S(1)} %get-tuple-element.82.act.own, ...), custom_call_target="tpu_custom_call" | custom-call | flops 2147483648 | bytes 13109248 | tf_op jit(solution)/shard_map/pallas_call | solution.py:312
  75.7 0.7 collective-permute-start.34
  76.3 4.2 %collective-permute-done.27.refs_4_.refs_12_ = bf16[64,1024]{1,0:T(8,128)(2,1)S(1)} collective-permute-done((bf16[64,1024]{1,0:T(8,128)(2,1)S(1)}, bf16[64,1024]{1,0:T(8,128)(2,1)S(1)}, u32[]{:S(2)}, u32[]{:S(2)}) %collective-permute-start.27) | collective-permute-done | bytes 131104 | tf_op jit(solution)/shard_map/ppermute | solution.py:355
  80.6 1.5 %collective-permute-start.35 = (bf16[64,512]{1,0:T(8,128)(2,1)S(1)}, bf16[64,512]{1,0:T(8,128)(2,1)S(1)}, u32[]{:S(2)}, u32[]{:S(2)}) collective-permute-start(bf16[64,512]{1,0:T(8,128)(2,1)S(1)} %get-tuple-element.129), channel_id=1, source_target_pairs={{0,16},{4,20},{8,24},{12,28},{16,0},{20,4},{24,8},{28,12},{1,17},{... | collective-permute-start | bytes 196616 | tf_op jit(solution)/shard_map/ppermute | solution.py:355
  82.1 0.3 collective-permute-done.28.refs_5_.refs_13_
  82.4 1.9 %collective-permute-start.36 = (bf16[64,512]{1,0:T(8,128)(2,1)S(1)}, bf16[64,512]{1,0:T(8,128)(2,1)S(1)}, u32[]{:S(2)}, u32[]{:S(2)}) collective-permute-start(bf16[64,512]{1,0:T(8,128)(2,1)S(1)} %get-tuple-element.130), channel_id=1, source_target_pairs={{0,20},{4,16},{8,28},{12,24},{16,4},{20,0},{24,12},{28,8},{1,21},{... | collective-permute-start | bytes 196616 | tf_op jit(solution)/shard_map/ppermute | solution.py:355
  84.3 0.6 collective-permute-start.37
  84.9 1.1 collective-permute-start.38
  86.0 2.1 %shard_map.112 = (bf16[1024,512]{1,0:T(8,128)(2,1)S(1)}, bf16[1024,512]{1,0:T(8,128)(2,1)S(1)}) custom-call(bf16[1024,1024]{1,0:T(8,128)(2,1)S(1)} %get-tuple-element.80.w_in, bf16[64,1024]{1,0:T(8,128)(2,1)S(1)} %get-tuple-element.115.refs_0_.refs_8_, bf16[64,1024]{1,0:T(8,128)(2,1)S(1)} %collective-permute-done.24.refs_1_.refs_9_, ...), custom_call_target="tpu_custom_call" | custom-call | flops 1073741824 | bytes 5242880 | tf_op jit(solution)/shard_map/pallas_call | solution.py:312
  88.2 2.0 %collective-permute-done.37.refs_6_.refs_14_ = bf16[64,512]{1,0:T(8,128)(2,1)S(1)} collective-permute-done((bf16[64,512]{1,0:T(8,128)(2,1)S(1)}, bf16[64,512]{1,0:T(8,128)(2,1)S(1)}, u32[]{:S(2)}, u32[]{:S(2)}) %collective-permute-start.37) | collective-permute-done | bytes 65568 | tf_op jit(solution)/shard_map/ppermute | solution.py:355
  90.2 1.3 shard_map.114.other
  91.5 1.5 %shard_map.117 = bf16[512,768]{1,0:T(8,128)(2,1)S(1)} custom-call(s32[2]{0:T(128)S(1)} %pad_add_fusion.pos, bf16[1024,512]{1,0:T(8,128)(2,1)S(1)} %get-tuple-element.114.own, bf16[1024,512]{1,0:T(8,128)(2,1)S(1)} %shard_map.114.other, bf16[64,1536]{1,0:T(8,128)(2,1)S(1)} %get-tuple-element.70.refs_0_, bf16[64,1536]{1,0:T(8,128)(2,1)S(1)} %collective-permute-done.refs_1_, ...), custom_call_target="tpu_custom_call" | custom-call | flops 805306368 | bytes 5505024 | tf_op jit(solution)/shard_map/pallas_call | solution.py:312
  93.1 6.4 %shard_map.109 = (bf16[64,1024]{1,0:T(8,128)(2,1)S(1)}, bf16[64,1024]{1,0:T(8,128)(2,1)S(1)}, bf16[64,1024]{1,0:T(8,128)(2,1)S(1)}, bf16[64,1024]{1,0:T(8,128)(2...) custom-call(s32[2]{0:T(128)S(1)} %pad_add_fusion.pos, ...), custom_call_target="tpu_custom_call" | custom-call | flops 2147483648 | bytes 14682112 | tf_op jit(solution)/shard_map/pallas_call | solution.py:294
  99.6 0.6 collective-permute-start.16
  100.1 0.8 collective-permute-start.17
  100.9 0.6 collective-permute-start.18
  101.5 1.2 shard_map.120
  102.8 2.0 %collective-permute-start.41 = (bf16[512,512]{1,0:T(8,128)(2,1)S(1)}, bf16[512,512]{1,0:T(8,128)(2,1)S(1)}, u32[]{:S(2)}, u32[]{:S(2)}) collective-permute-start(bf16[512,512]{1,0:T(8,128)(2,1)S(1)} %shard_map.120), channel_id=1, source_target_pairs={{0,1},{1,0},{2,3},{3,2},{4,5},{5,4},{6,7},{7,6},{8,9},{9,8},{10,11... | collective-permute-start | bytes 1572872 | tf_op jit(solution)/shard_map/ppermute | solution.py:362
  104.8 1.2 collective-permute-start.19
  106.0 0.5 collective-permute-done.17.refs_2_
  106.5 1.2 shard_map.122
  107.8 1.9 %collective-permute-start.43 = (bf16[512,384]{1,0:T(8,128)(2,1)S(1)}, bf16[512,384]{1,0:T(8,128)(2,1)S(1)}, u32[]{:S(2)}, u32[]{:S(2)}) collective-permute-start(bf16[512,384]{1,0:T(8,128)(2,1)S(1)} %shard_map.122), channel_id=1, source_target_pairs={{0,1},{1,0},{2,3},{3,2},{4,5},{5,4},{6,7},{7,6},{8,9},{9,8},{10,11... | collective-permute-start | bytes 1179656 | tf_op jit(solution)/shard_map/ppermute | solution.py:362
  109.7 1.5 %collective-permute-done.19.refs_4_ = bf16[64,1024]{1,0:T(8,128)(2,1)S(1)} collective-permute-done((bf16[64,1024]{1,0:T(8,128)(2,1)S(1)}, bf16[64,1024]{1,0:T(8,128)(2,1)S(1)}, u32[]{:S(2)}, u32[]{:S(2)}) %collective-permute-start.19) | collective-permute-done | bytes 131104 | tf_op jit(solution)/shard_map/ppermute | solution.py:355
  111.2 1.7 %collective-permute-start.21 = (bf16[64,1024]{1,0:T(8,128)(2,1)S(1)}, bf16[64,1024]{1,0:T(8,128)(2,1)S(1)}, u32[]{:S(2)}, u32[]{:S(2)}) collective-permute-start(bf16[64,1024]{1,0:T(8,128)(2,1)S(1)} %get-tuple-element.110), channel_id=1, source_target_pairs={{0,24},{4,28},{8,16},{12,20},{16,8},{20,12},{24,0},{28,4},{1,25},{... | collective-permute-start | bytes 393224 | tf_op jit(solution)/shard_map/ppermute | solution.py:355
  112.9 1.6 %collective-permute-start.22 = (bf16[64,1024]{1,0:T(8,128)(2,1)S(1)}, bf16[64,1024]{1,0:T(8,128)(2,1)S(1)}, u32[]{:S(2)}, u32[]{:S(2)}) collective-permute-start(bf16[64,1024]{1,0:T(8,128)(2,1)S(1)} %get-tuple-element.111), channel_id=1, source_target_pairs={{0,28},{4,24},{8,20},{12,16},{16,12},{20,8},{24,4},{28,0},{1,29},{... | collective-permute-start | bytes 393224 | tf_op jit(solution)/shard_map/ppermute | solution.py:355
  114.5 1.0 shard_map.116
  115.5 1.8 %collective-permute-done.21.refs_6_ = bf16[64,1024]{1,0:T(8,128)(2,1)S(1)} collective-permute-done((bf16[64,1024]{1,0:T(8,128)(2,1)S(1)}, bf16[64,1024]{1,0:T(8,128)(2,1)S(1)}, u32[]{:S(2)}, u32[]{:S(2)}) %collective-permute-start.21) | collective-permute-done | bytes 131104 | tf_op jit(solution)/shard_map/ppermute | solution.py:355
  117.3 1.0 shard_map.121
  118.3 1.2 collective-permute-done.22.refs_7_
  119.5 0.9 collective-permute-start.42
  120.4 1.6 %shard_map.110 = (bf16[192,1024]{1,0:T(8,128)(2,1)}, bf16[2,192]{1,0:T(2,128)(2,1)}) custom-call(f32[8,192]{1,0:T(8,128)S(1)} %get-tuple-element.69.meta, bf16[64,1024]{1,0:T(8,128)(2,1)S(1)} %get-tuple-element.104.refs_0_, bf16[64,1024]{1,0:T(8,128)(2,1)S(1)} %collective-permute-done.16.refs_1_, bf16[64,1024]{1,0:T(8,128)(2,1)S(1)} %collective-permute-done.17.refs_2_, ...), custom_call_target="tpu_custom_call" | custom-call | flops 201326592 | bytes 1448704 | tf_op jit(solution)/shard_map/pallas_call | solution.py:294
  122.0 1.8 %shard_map.115.before = f32[512,1024]{1,0:T(8,128)S(1)} custom-call(s32[2]{0:T(128)S(1)} %pad_add_fusion.pos, bf16[1024,512]{1,0:T(8,128)(2,1)S(1)} %get-tuple-element.114.own, bf16[1024,512]{1,0:T(8,128)(2,1)S(1)} %shard_map.114.other, bf16[64,1536]{1,0:T(8,128)(2,1)S(1)} %get-tuple-element.70.refs_0_, bf16[64,1536]{1,0:T(8,128)(2,1)S(1)} %collective-permute-done.refs_1_, ...), custom_call_target="tpu_custom_call" | custom-call | flops 1073741824 | bytes 6815744 | tf_op jit(solution)/shard_map/pallas_call | solution.py:312
  123.8 17.4 %collective-permute-done.42.refs_33_ = bf16[512,128]{1,0:T(8,128)(2,1)S(1)} collective-permute-done((bf16[512,128]{1,0:T(8,128)(2,1)S(1)}, bf16[512,128]{1,0:T(8,128)(2,1)S(1)}, u32[]{:S(2)}, u32[]{:S(2)}) %collective-permute-start.42) | collective-permute-done | bytes 131104 | tf_op jit(solution)/shard_map/ppermute | solution.py:362
  141.2 3.1 %home_out.1 = f32[1,512,1024]{2,1,0:T(8,128)} custom-call(s32[2]{0:T(128)S(1)} %pad_add_fusion.pos, bf16[1024,512]{1,0:T(8,128)(2,1)S(1)} %get-tuple-element.82.act.own, bf16[1024,512]{1,0:T(8,128)(2,1)S(1)} %get-tuple-element.133.other, bf16[64,1536]{1,0:T(8,128)(2,1)S(1)} %get-tuple-element.70.refs_0_, bf16[64,1536]{1,0:T(8,128)(2,1)S(1)} %collective-permute-done.refs_1_, ...), custom_call_target="tpu_custom_call" | custom-call | flops 1073741824 | bytes 6291456 | tf_op jit(solution)/shard_map/home_out/pallas_call | solution.py:566
  144.3 1.8 %shard_map.118.refs_1_ = f32[1,512,1024]{2,1,0:T(8,128)} custom-call(f32[512,1024]{1,0:T(8,128)S(1)} %shard_map.115.before, bf16[512,768]{1,0:T(8,128)(2,1)S(1)} %collective-permute-done.40.refs_0_), custom_call_target="tpu_custom_call" | custom-call | bytes 4980736 | tf_op jit(solution)/shard_map/pallas_call | solution.py:294
  146.1 0.8 shard_map.119
  (47 shorter events, 2.0 us)
Async XLA Ops:
  2.6 7.8 %collective-permute-start = (bf16[64,1536]{1,0:T(8,128)(2,1)S(1)}, bf16[64,1536]{1,0:T(8,128)(2,1)S(1)}, u32[]{:S(2)}, u32[]{:S(2)}) collective-permute-start(bf16[64,1536]{1,0:T(8,128)(2,1)S(1)} %get-tuple-element.71), channel_id=1, source_target_pairs={{0,4},{4,0},{8,12},{12,8},{16,20},{20,16},{24,28},{28,24},{1,5},{5... | collective-permute-start | bytes 589832 | tf_op jit(solution)/shard_map/ppermute | solution.py:355
  2.7 8.6 %collective-permute-start.1 = (bf16[64,1536]{1,0:T(8,128)(2,1)S(1)}, bf16[64,1536]{1,0:T(8,128)(2,1)S(1)}, u32[]{:S(2)}, u32[]{:S(2)}) collective-permute-start(bf16[64,1536]{1,0:T(8,128)(2,1)S(1)} %get-tuple-element.72), channel_id=1, source_target_pairs={{0,8},{4,12},{8,0},{12,4},{16,24},{20,28},{24,16},{28,20},{1,9},{5... | collective-permute-start | bytes 589832 | tf_op jit(solution)/shard_map/ppermute | solution.py:355
  2.8 5.6 %collective-permute-start.7 = (f32[8,192]{1,0:T(8,128)S(1)}, f32[8,192]{1,0:T(8,128)S(1)}, u32[]{:S(2)}, u32[]{:S(2)}) collective-permute-start(f32[8,192]{1,0:T(8,128)S(1)} %get-tuple-element.69.meta), channel_id=1, source_target_pairs={{0,2},{1,3},{2,0},{3,1},{4,6},{5,7},{6,4},{7,5},{8,10},{9,11},{10,... | collective-permute-start | bytes 18440 | tf_op jit(solution)/shard_map/ppermute | solution.py:351
  5.9 7.8 %collective-permute-start.2 = (bf16[64,1536]{1,0:T(8,128)(2,1)S(1)}, bf16[64,1536]{1,0:T(8,128)(2,1)S(1)}, u32[]{:S(2)}, u32[]{:S(2)}) collective-permute-start(bf16[64,1536]{1,0:T(8,128)(2,1)S(1)} %get-tuple-element.73), channel_id=1, source_target_pairs={{0,12},{4,8},{8,4},{12,0},{16,28},{20,24},{24,20},{28,16},{1,13},{... | collective-permute-start | bytes 589832 | tf_op jit(solution)/shard_map/ppermute | solution.py:355
  6.9 8.6 %collective-permute-start.3 = (bf16[64,1536]{1,0:T(8,128)(2,1)S(1)}, bf16[64,1536]{1,0:T(8,128)(2,1)S(1)}, u32[]{:S(2)}, u32[]{:S(2)}) collective-permute-start(bf16[64,1536]{1,0:T(8,128)(2,1)S(1)} %get-tuple-element.74), channel_id=1, source_target_pairs={{0,16},{4,20},{8,24},{12,28},{16,0},{20,4},{24,8},{28,12},{1,17},{... | collective-permute-start | bytes 589832 | tf_op jit(solution)/shard_map/ppermute | solution.py:355
  8.4 25.5 %collective-permute-start.31 = (bf16[192,512]{1,0:T(8,128)(2,1)S(1)}, bf16[192,512]{1,0:T(8,128)(2,1)S(1)}, u32[]{:S(2)}, u32[]{:S(2)}) collective-permute-start(bf16[192,512]{1,0:T(8,128)(2,1)S(1)} %get-tuple-element.124), channel_id=1, source_target_pairs={{0,2},{1,3},{2,0},{3,1},{4,6},{5,7},{6,4},{7,5},{8,10},{9,11},{10,... | collective-permute-start | bytes 589832 | tf_op jit(solution)/shard_map/ppermute | solution.py:351
  10.5 38.6 %collective-permute-start.23 = (bf16[192,1024]{1,0:T(8,128)(2,1)}, bf16[192,1024]{1,0:T(8,128)(2,1)S(1)}, u32[]{:S(2)}, u32[]{:S(2)}) collective-permute-start(bf16[192,1024]{1,0:T(8,128)(2,1)} %tokens.1), channel_id=1, source_target_pairs={{0,2},{1,3},{2,0},{3,1},{4,6},{5,7},{6,4},{7,5},{8,10},{9,11},{10,... | collective-permute-start | bytes 1179656 | tf_op jit(solution)/shard_map/ppermute | solution.py:351
  11.3 34.6 %collective-permute-start.8 = (bf16[192,512]{1,0:T(8,128)(2,1)S(1)}, bf16[192,512]{1,0:T(8,128)(2,1)S(1)}, u32[]{:S(2)}, u32[]{:S(2)}) collective-permute-start(bf16[192,512]{1,0:T(8,128)(2,1)S(1)} %get-tuple-element.84.grad_out), channel_id=1, source_target_pairs={{0,2},{1,3},{2,0},{3,1},{4,6},{5,7},{6,4},{7,5},{8,10},{9,11},{10,... | collective-permute-start | bytes 589832 | tf_op jit(solution)/shard_map/ppermute | solution.py:351
  13.7 32.9 %collective-permute-start.4 = (bf16[64,1536]{1,0:T(8,128)(2,1)S(1)}, bf16[64,1536]{1,0:T(8,128)(2,1)S(1)}, u32[]{:S(2)}, u32[]{:S(2)}) collective-permute-start(bf16[64,1536]{1,0:T(8,128)(2,1)S(1)} %get-tuple-element.75), channel_id=1, source_target_pairs={{0,20},{4,16},{8,28},{12,24},{16,4},{20,0},{24,12},{28,8},{1,21},{... | collective-permute-start | bytes 589832 | tf_op jit(solution)/shard_map/ppermute | solution.py:355
  15.5 31.6 %collective-permute-start.5 = (bf16[64,1536]{1,0:T(8,128)(2,1)S(1)}, bf16[64,1536]{1,0:T(8,128)(2,1)S(1)}, u32[]{:S(2)}, u32[]{:S(2)}) collective-permute-start(bf16[64,1536]{1,0:T(8,128)(2,1)S(1)} %get-tuple-element.76), channel_id=1, source_target_pairs={{0,24},{4,28},{8,16},{12,20},{16,8},{20,12},{24,0},{28,4},{1,25},{... | collective-permute-start | bytes 589832 | tf_op jit(solution)/shard_map/ppermute | solution.py:355
  33.9 13.8 %collective-permute-start.6 = (bf16[64,1536]{1,0:T(8,128)(2,1)S(1)}, bf16[64,1536]{1,0:T(8,128)(2,1)S(1)}, u32[]{:S(2)}, u32[]{:S(2)}) collective-permute-start(bf16[64,1536]{1,0:T(8,128)(2,1)S(1)} %get-tuple-element.77), channel_id=1, source_target_pairs={{0,28},{4,24},{8,20},{12,16},{16,12},{20,8},{24,4},{28,0},{1,29},{... | collective-permute-start | bytes 589832 | tf_op jit(solution)/shard_map/ppermute | solution.py:355
  45.9 2.6 %collective-permute-start.32 = (bf16[64,512]{1,0:T(8,128)(2,1)S(1)}, bf16[64,512]{1,0:T(8,128)(2,1)S(1)}, u32[]{:S(2)}, u32[]{:S(2)}) collective-permute-start(bf16[64,512]{1,0:T(8,128)(2,1)S(1)} %get-tuple-element.126), channel_id=1, source_target_pairs={{0,4},{4,0},{8,12},{12,8},{16,20},{20,16},{24,28},{28,24},{1,5},{5... | collective-permute-start | bytes 196616 | tf_op jit(solution)/shard_map/ppermute | solution.py:355
  46.6 10.3 %collective-permute-start.9 = (bf16[64,1024]{1,0:T(8,128)(2,1)S(1)}, bf16[64,1024]{1,0:T(8,128)(2,1)S(1)}, u32[]{:S(2)}, u32[]{:S(2)}) collective-permute-start(bf16[64,1024]{1,0:T(8,128)(2,1)S(1)} %get-tuple-element.94), channel_id=1, source_target_pairs={{0,4},{4,0},{8,12},{12,8},{16,20},{20,16},{24,28},{28,24},{1,5},{5... | collective-permute-start | bytes 393224 | tf_op jit(solution)/shard_map/ppermute | solution.py:355
  47.1 10.3 %collective-permute-start.10 = (bf16[64,1024]{1,0:T(8,128)(2,1)S(1)}, bf16[64,1024]{1,0:T(8,128)(2,1)S(1)}, u32[]{:S(2)}, u32[]{:S(2)}) collective-permute-start(bf16[64,1024]{1,0:T(8,128)(2,1)S(1)} %get-tuple-element.95), channel_id=1, source_target_pairs={{0,8},{4,12},{8,0},{12,4},{16,24},{20,28},{24,16},{28,20},{1,9},{5... | collective-permute-start | bytes 393224 | tf_op jit(solution)/shard_map/ppermute | solution.py:355
  47.7 12.0 %collective-permute-start.11 = (bf16[64,1024]{1,0:T(8,128)(2,1)S(1)}, bf16[64,1024]{1,0:T(8,128)(2,1)S(1)}, u32[]{:S(2)}, u32[]{:S(2)}) collective-permute-start(bf16[64,1024]{1,0:T(8,128)(2,1)S(1)} %get-tuple-element.96), channel_id=1, source_target_pairs={{0,12},{4,8},{8,4},{12,0},{16,28},{20,24},{24,20},{28,16},{1,13},{... | collective-permute-start | bytes 393224 | tf_op jit(solution)/shard_map/ppermute | solution.py:355
  48.6 11.3 %collective-permute-start.12 = (bf16[64,1024]{1,0:T(8,128)(2,1)S(1)}, bf16[64,1024]{1,0:T(8,128)(2,1)S(1)}, u32[]{:S(2)}, u32[]{:S(2)}) collective-permute-start(bf16[64,1024]{1,0:T(8,128)(2,1)S(1)} %get-tuple-element.97), channel_id=1, source_target_pairs={{0,16},{4,20},{8,24},{12,28},{16,0},{20,4},{24,8},{28,12},{1,17},{... | collective-permute-start | bytes 393224 | tf_op jit(solution)/shard_map/ppermute | solution.py:355
  49.1 7.7 %collective-permute-start.33 = (bf16[64,512]{1,0:T(8,128)(2,1)S(1)}, bf16[64,512]{1,0:T(8,128)(2,1)S(1)}, u32[]{:S(2)}, u32[]{:S(2)}) collective-permute-start(bf16[64,512]{1,0:T(8,128)(2,1)S(1)} %get-tuple-element.127), channel_id=1, source_target_pairs={{0,8},{4,12},{8,0},{12,4},{16,24},{20,28},{24,16},{28,20},{1,9},{5... | collective-permute-start | bytes 196616 | tf_op jit(solution)/shard_map/ppermute | solution.py:355
  56.8 10.5 %collective-permute-start.13 = (bf16[64,1024]{1,0:T(8,128)(2,1)S(1)}, bf16[64,1024]{1,0:T(8,128)(2,1)S(1)}, u32[]{:S(2)}, u32[]{:S(2)}) collective-permute-start(bf16[64,1024]{1,0:T(8,128)(2,1)S(1)} %get-tuple-element.98), channel_id=1, source_target_pairs={{0,20},{4,16},{8,28},{12,24},{16,4},{20,0},{24,12},{28,8},{1,21},{... | collective-permute-start | bytes 393224 | tf_op jit(solution)/shard_map/ppermute | solution.py:355
  56.8 11.7 %collective-permute-start.14 = (bf16[64,1024]{1,0:T(8,128)(2,1)S(1)}, bf16[64,1024]{1,0:T(8,128)(2,1)S(1)}, u32[]{:S(2)}, u32[]{:S(2)}) collective-permute-start(bf16[64,1024]{1,0:T(8,128)(2,1)S(1)} %get-tuple-element.99), channel_id=1, source_target_pairs={{0,24},{4,28},{8,16},{12,20},{16,8},{20,12},{24,0},{28,4},{1,25},{... | collective-permute-start | bytes 393224 | tf_op jit(solution)/shard_map/ppermute | solution.py:355
  57.4 12.7 %collective-permute-start.15 = (bf16[64,1024]{1,0:T(8,128)(2,1)S(1)}, bf16[64,1024]{1,0:T(8,128)(2,1)S(1)}, u32[]{:S(2)}, u32[]{:S(2)}) collective-permute-start(bf16[64,1024]{1,0:T(8,128)(2,1)S(1)} %get-tuple-element.100), channel_id=1, source_target_pairs={{0,28},{4,24},{8,20},{12,16},{16,12},{20,8},{24,4},{28,0},{1,29},{... | collective-permute-start | bytes 393224 | tf_op jit(solution)/shard_map/ppermute | solution.py:355
  59.7 10.7 %collective-permute-start.24 = (bf16[64,1024]{1,0:T(8,128)(2,1)S(1)}, bf16[64,1024]{1,0:T(8,128)(2,1)S(1)}, u32[]{:S(2)}, u32[]{:S(2)}) collective-permute-start(bf16[64,1024]{1,0:T(8,128)(2,1)S(1)} %get-tuple-element.116), channel_id=1, source_target_pairs={{0,4},{4,0},{8,12},{12,8},{16,20},{20,16},{24,28},{28,24},{1,5},{5... | collective-permute-start | bytes 393224 | tf_op jit(solution)/shard_map/ppermute | solution.py:355
  59.9 11.9 %collective-permute-start.25 = (bf16[64,1024]{1,0:T(8,128)(2,1)S(1)}, bf16[64,1024]{1,0:T(8,128)(2,1)S(1)}, u32[]{:S(2)}, u32[]{:S(2)}) collective-permute-start(bf16[64,1024]{1,0:T(8,128)(2,1)S(1)} %get-tuple-element.117), channel_id=1, source_target_pairs={{0,8},{4,12},{8,0},{12,4},{16,24},{20,28},{24,16},{28,20},{1,9},{5... | collective-permute-start | bytes 393224 | tf_op jit(solution)/shard_map/ppermute | solution.py:355
  67.4 8.3 %collective-permute-start.26 = (bf16[64,1024]{1,0:T(8,128)(2,1)S(1)}, bf16[64,1024]{1,0:T(8,128)(2,1)S(1)}, u32[]{:S(2)}, u32[]{:S(2)}) collective-permute-start(bf16[64,1024]{1,0:T(8,128)(2,1)S(1)} %get-tuple-element.118), channel_id=1, source_target_pairs={{0,12},{4,8},{8,4},{12,0},{16,28},{20,24},{24,20},{28,16},{1,13},{... | collective-permute-start | bytes 393224 | tf_op jit(solution)/shard_map/ppermute | solution.py:355
  68.6 12.0 %collective-permute-start.27 = (bf16[64,1024]{1,0:T(8,128)(2,1)S(1)}, bf16[64,1024]{1,0:T(8,128)(2,1)S(1)}, u32[]{:S(2)}, u32[]{:S(2)}) collective-permute-start(bf16[64,1024]{1,0:T(8,128)(2,1)S(1)} %get-tuple-element.119), channel_id=1, source_target_pairs={{0,16},{4,20},{8,24},{12,28},{16,0},{20,4},{24,8},{28,12},{1,17},{... | collective-permute-start | bytes 393224 | tf_op jit(solution)/shard_map/ppermute | solution.py:355
  70.1 12.3 %collective-permute-start.28 = (bf16[64,1024]{1,0:T(8,128)(2,1)S(1)}, bf16[64,1024]{1,0:T(8,128)(2,1)S(1)}, u32[]{:S(2)}, u32[]{:S(2)}) collective-permute-start(bf16[64,1024]{1,0:T(8,128)(2,1)S(1)} %get-tuple-element.120), channel_id=1, source_target_pairs={{0,20},{4,16},{8,28},{12,24},{16,4},{20,0},{24,12},{28,8},{1,21},{... | collective-permute-start | bytes 393224 | tf_op jit(solution)/shard_map/ppermute | solution.py:355
  70.4 13.9 %collective-permute-start.29 = (bf16[64,1024]{1,0:T(8,128)(2,1)S(1)}, bf16[64,1024]{1,0:T(8,128)(2,1)S(1)}, u32[]{:S(2)}, u32[]{:S(2)}) collective-permute-start(bf16[64,1024]{1,0:T(8,128)(2,1)S(1)} %get-tuple-element.121), channel_id=1, source_target_pairs={{0,24},{4,28},{8,16},{12,20},{16,8},{20,12},{24,0},{28,4},{1,25},{... | collective-permute-start | bytes 393224 | tf_op jit(solution)/shard_map/ppermute | solution.py:355
  71.8 13.1 %collective-permute-start.30 = (bf16[64,1024]{1,0:T(8,128)(2,1)S(1)}, bf16[64,1024]{1,0:T(8,128)(2,1)S(1)}, u32[]{:S(2)}, u32[]{:S(2)}) collective-permute-start(bf16[64,1024]{1,0:T(8,128)(2,1)S(1)} %get-tuple-element.122), channel_id=1, source_target_pairs={{0,28},{4,24},{8,20},{12,16},{16,12},{20,8},{24,4},{28,0},{1,29},{... | collective-permute-start | bytes 393224 | tf_op jit(solution)/shard_map/ppermute | solution.py:355
  75.7 12.5 %collective-permute-start.34 = (bf16[64,512]{1,0:T(8,128)(2,1)S(1)}, bf16[64,512]{1,0:T(8,128)(2,1)S(1)}, u32[]{:S(2)}, u32[]{:S(2)}) collective-permute-start(bf16[64,512]{1,0:T(8,128)(2,1)S(1)} %get-tuple-element.128), channel_id=1, source_target_pairs={{0,12},{4,8},{8,4},{12,0},{16,28},{20,24},{24,20},{28,16},{1,13},{... | collective-permute-start | bytes 196616 | tf_op jit(solution)/shard_map/ppermute | solution.py:355
  80.6 7.6 %collective-permute-start.35 = (bf16[64,512]{1,0:T(8,128)(2,1)S(1)}, bf16[64,512]{1,0:T(8,128)(2,1)S(1)}, u32[]{:S(2)}, u32[]{:S(2)}) collective-permute-start(bf16[64,512]{1,0:T(8,128)(2,1)S(1)} %get-tuple-element.129), channel_id=1, source_target_pairs={{0,16},{4,20},{8,24},{12,28},{16,0},{20,4},{24,8},{28,12},{1,17},{... | collective-permute-start | bytes 196616 | tf_op jit(solution)/shard_map/ppermute | solution.py:355
  82.4 5.7 %collective-permute-start.36 = (bf16[64,512]{1,0:T(8,128)(2,1)S(1)}, bf16[64,512]{1,0:T(8,128)(2,1)S(1)}, u32[]{:S(2)}, u32[]{:S(2)}) collective-permute-start(bf16[64,512]{1,0:T(8,128)(2,1)S(1)} %get-tuple-element.130), channel_id=1, source_target_pairs={{0,20},{4,16},{8,28},{12,24},{16,4},{20,0},{24,12},{28,8},{1,21},{... | collective-permute-start | bytes 196616 | tf_op jit(solution)/shard_map/ppermute | solution.py:355
  84.3 5.9 %collective-permute-start.37 = (bf16[64,512]{1,0:T(8,128)(2,1)S(1)}, bf16[64,512]{1,0:T(8,128)(2,1)S(1)}, u32[]{:S(2)}, u32[]{:S(2)}) collective-permute-start(bf16[64,512]{1,0:T(8,128)(2,1)S(1)} %get-tuple-element.131), channel_id=1, source_target_pairs={{0,24},{4,28},{8,16},{12,20},{16,8},{20,12},{24,0},{28,4},{1,25},{... | collective-permute-start | bytes 196616 | tf_op jit(solution)/shard_map/ppermute | solution.py:355
  84.9 5.3 %collective-permute-start.38 = (bf16[64,512]{1,0:T(8,128)(2,1)S(1)}, bf16[64,512]{1,0:T(8,128)(2,1)S(1)}, u32[]{:S(2)}, u32[]{:S(2)}) collective-permute-start(bf16[64,512]{1,0:T(8,128)(2,1)S(1)} %get-tuple-element.132), channel_id=1, source_target_pairs={{0,28},{4,24},{8,20},{12,16},{16,12},{20,8},{24,4},{28,0},{1,29},{... | collective-permute-start | bytes 196616 | tf_op jit(solution)/shard_map/ppermute | solution.py:355
  93.1 51.2 %collective-permute-start.40 = (bf16[512,768]{1,0:T(8,128)(2,1)S(1)}, bf16[512,768]{1,0:T(8,128)(2,1)S(1)}, u32[]{:S(2)}, u32[]{:S(2)}) collective-permute-start(bf16[512,768]{1,0:T(8,128)(2,1)S(1)} %shard_map.117), channel_id=1, source_target_pairs={{0,1},{1,0},{2,3},{3,2},{4,5},{5,4},{6,7},{7,6},{8,9},{9,8},{10,11... | collective-permute-start | bytes 2359304 | tf_op jit(solution)/shard_map/ppermute | solution.py:362
  99.6 5.2 %collective-permute-start.16 = (bf16[64,1024]{1,0:T(8,128)(2,1)S(1)}, bf16[64,1024]{1,0:T(8,128)(2,1)S(1)}, u32[]{:S(2)}, u32[]{:S(2)}) collective-permute-start(bf16[64,1024]{1,0:T(8,128)(2,1)S(1)} %get-tuple-element.105), channel_id=1, source_target_pairs={{0,4},{4,0},{8,12},{12,8},{16,20},{20,16},{24,28},{28,24},{1,5},{5... | collective-permute-start | bytes 393224 | tf_op jit(solution)/shard_map/ppermute | solution.py:355
  100.1 6.4 %collective-permute-start.17 = (bf16[64,1024]{1,0:T(8,128)(2,1)S(1)}, bf16[64,1024]{1,0:T(8,128)(2,1)S(1)}, u32[]{:S(2)}, u32[]{:S(2)}) collective-permute-start(bf16[64,1024]{1,0:T(8,128)(2,1)S(1)} %get-tuple-element.106), channel_id=1, source_target_pairs={{0,8},{4,12},{8,0},{12,4},{16,24},{20,28},{24,16},{28,20},{1,9},{5... | collective-permute-start | bytes 393224 | tf_op jit(solution)/shard_map/ppermute | solution.py:355
  100.9 6.8 %collective-permute-start.18 = (bf16[64,1024]{1,0:T(8,128)(2,1)S(1)}, bf16[64,1024]{1,0:T(8,128)(2,1)S(1)}, u32[]{:S(2)}, u32[]{:S(2)}) collective-permute-start(bf16[64,1024]{1,0:T(8,128)(2,1)S(1)} %get-tuple-element.107), channel_id=1, source_target_pairs={{0,12},{4,8},{8,4},{12,0},{16,28},{20,24},{24,20},{28,16},{1,13},{... | collective-permute-start | bytes 393224 | tf_op jit(solution)/shard_map/ppermute | solution.py:355
  102.8 38.4 %collective-permute-start.41 = (bf16[512,512]{1,0:T(8,128)(2,1)S(1)}, bf16[512,512]{1,0:T(8,128)(2,1)S(1)}, u32[]{:S(2)}, u32[]{:S(2)}) collective-permute-start(bf16[512,512]{1,0:T(8,128)(2,1)S(1)} %shard_map.120), channel_id=1, source_target_pairs={{0,1},{1,0},{2,3},{3,2},{4,5},{5,4},{6,7},{7,6},{8,9},{9,8},{10,11... | collective-permute-start | bytes 1572872 | tf_op jit(solution)/shard_map/ppermute | solution.py:362
  104.8 6.4 %collective-permute-start.19 = (bf16[64,1024]{1,0:T(8,128)(2,1)S(1)}, bf16[64,1024]{1,0:T(8,128)(2,1)S(1)}, u32[]{:S(2)}, u32[]{:S(2)}) collective-permute-start(bf16[64,1024]{1,0:T(8,128)(2,1)S(1)} %get-tuple-element.108), channel_id=1, source_target_pairs={{0,16},{4,20},{8,24},{12,28},{16,0},{20,4},{24,8},{28,12},{1,17},{... | collective-permute-start | bytes 393224 | tf_op jit(solution)/shard_map/ppermute | solution.py:355
  106.5 6.4 %collective-permute-start.20 = (bf16[64,1024]{1,0:T(8,128)(2,1)S(1)}, bf16[64,1024]{1,0:T(8,128)(2,1)S(1)}, u32[]{:S(2)}, u32[]{:S(2)}) collective-permute-start(bf16[64,1024]{1,0:T(8,128)(2,1)S(1)} %get-tuple-element.109), channel_id=1, source_target_pairs={{0,20},{4,16},{8,28},{12,24},{16,4},{20,0},{24,12},{28,8},{1,21},{... | collective-permute-start | bytes 393224 | tf_op jit(solution)/shard_map/ppermute | solution.py:355
  107.8 33.4 %collective-permute-start.43 = (bf16[512,384]{1,0:T(8,128)(2,1)S(1)}, bf16[512,384]{1,0:T(8,128)(2,1)S(1)}, u32[]{:S(2)}, u32[]{:S(2)}) collective-permute-start(bf16[512,384]{1,0:T(8,128)(2,1)S(1)} %shard_map.122), channel_id=1, source_target_pairs={{0,1},{1,0},{2,3},{3,2},{4,5},{5,4},{6,7},{7,6},{8,9},{9,8},{10,11... | collective-permute-start | bytes 1179656 | tf_op jit(solution)/shard_map/ppermute | solution.py:362
  111.2 6.1 %collective-permute-start.21 = (bf16[64,1024]{1,0:T(8,128)(2,1)S(1)}, bf16[64,1024]{1,0:T(8,128)(2,1)S(1)}, u32[]{:S(2)}, u32[]{:S(2)}) collective-permute-start(bf16[64,1024]{1,0:T(8,128)(2,1)S(1)} %get-tuple-element.110), channel_id=1, source_target_pairs={{0,24},{4,28},{8,16},{12,20},{16,8},{20,12},{24,0},{28,4},{1,25},{... | collective-permute-start | bytes 393224 | tf_op jit(solution)/shard_map/ppermute | solution.py:355
  112.9 6.6 %collective-permute-start.22 = (bf16[64,1024]{1,0:T(8,128)(2,1)S(1)}, bf16[64,1024]{1,0:T(8,128)(2,1)S(1)}, u32[]{:S(2)}, u32[]{:S(2)}) collective-permute-start(bf16[64,1024]{1,0:T(8,128)(2,1)S(1)} %get-tuple-element.111), channel_id=1, source_target_pairs={{0,28},{4,24},{8,20},{12,16},{16,12},{20,8},{24,4},{28,0},{1,29},{... | collective-permute-start | bytes 393224 | tf_op jit(solution)/shard_map/ppermute | solution.py:355
  117.3 28.8 %collective-permute-start.39 = (bf16[512,256]{1,0:T(8,128)(2,1)S(1)}, bf16[512,256]{1,0:T(8,128)(2,1)S(1)}, u32[]{:S(2)}, u32[]{:S(2)}) collective-permute-start(bf16[512,256]{1,0:T(8,128)(2,1)S(1)} %shard_map.116), channel_id=1, source_target_pairs={{0,1},{1,0},{2,3},{3,2},{4,5},{5,4},{6,7},{7,6},{8,9},{9,8},{10,11... | collective-permute-start | bytes 786440 | tf_op jit(solution)/shard_map/ppermute | solution.py:362
  119.5 21.7 %collective-permute-start.42 = (bf16[512,128]{1,0:T(8,128)(2,1)S(1)}, bf16[512,128]{1,0:T(8,128)(2,1)S(1)}, u32[]{:S(2)}, u32[]{:S(2)}) collective-permute-start(bf16[512,128]{1,0:T(8,128)(2,1)S(1)} %shard_map.121), channel_id=1, source_target_pairs={{0,1},{1,0},{2,3},{3,2},{4,5},{5,4},{6,7},{7,6},{8,9},{9,8},{10,11... | collective-permute-start | bytes 393224 | tf_op jit(solution)/shard_map/ppermute | solution.py:362
